TPU v7x, 32 devices: a whole 2x2x4 slice. The times are simulated.
32 devices in a mesh: batch: 8 (over z, y), ctx: 4 (over x, core).
Axes of the slice: x: 2, y: 2, z: 4, core: 2. Of those that a mesh axis runs over, the one named last changes fastest.
Arguments:
- tokens: bfloat16 [16, 256, 2048], P('batch', 'ctx'), may hold values from -50 to 50
- cotangent: bfloat16 [16, 256, 2048], P('batch', 'ctx'), may hold values from -6 to 6
- lengths: int32 [16], replicated, may hold values from 64 to 256, as said below
- slot_sequence: int32 [16], replicated, may hold values from 0 to 15, each once
- proj_in: bfloat16 [2048, 1536], P(('batch', 'ctx')), may hold values from -0.125 to 0.125
- query_up: bfloat16 [1024, 4096], P(('batch', 'ctx')), may hold values from -0.1875 to 0.1875
- proj_out: bfloat16 [4096, 2048], P(('batch', 'ctx')), may hold values from -0.75 to 0.75
- attn_gain: bfloat16 [2048], P(('batch', 'ctx')), may hold values from 0.5 to 1.5
- query_gain: bfloat16 [1024], P(('batch', 'ctx')), may hold values from 0.5 to 1.5
- mlp_gain: bfloat16 [2048], P(('batch', 'ctx')), may hold values from 0.5 to 1.5
- gate_up: bfloat16 [2048, 11264], P(('batch', 'ctx')), may hold values from -0.125 to 0.125
- down_proj: bfloat16 [5632, 2048], P(('batch', 'ctx')), may hold values from -0.109375 to 0.109375
Outputs:
- layer_out: bfloat16 [16, 256, 2048], P('batch', 'ctx')
- tokens_grad: bfloat16 [16, 256, 2048], P('batch', 'ctx')
- grad_proj_in: float32 [2048, 1536], P(('batch', 'ctx'))
- grad_query_up: float32 [1024, 4096], P(('batch', 'ctx'))
- grad_proj_out: float32 [4096, 2048], P(('batch', 'ctx'))
- grad_attn_gain: float32 [2048], P(('batch', 'ctx'))
- grad_query_gain: float32 [1024], P(('batch', 'ctx'))
- grad_mlp_gain: float32 [2048], P(('batch', 'ctx'))
- grad_gate_up: float32 [2048, 11264], P(('batch', 'ctx'))
- grad_down_proj: float32 [5632, 2048], P(('batch', 'ctx'))
Inputs may be any that keep to these rules, and one draw needn't show every extreme that they name: `lengths`: valid tokens of each sequence, counted from its start; the longest equals 256 in every draw. Slot s holds the sequence numbered slot_sequence[s]; every sequence fills exactly one slot.
All inputs are finite; a program needn't handle non-finite values.
Results may differ from a plain program's by a relative error of at most 0.017.
Values may be sent and summed in bfloat16 or wider, within the bound.
A program may use at most 448 MiB of HBM per device.

v0:
```python
import math

import jax
import jax.numpy as jnp
from jax import lax
from jax.sharding import PartitionSpec as P

H = 16
HD = 256
QR = 1024
FF = 5632
MICRO = 2
POS_DEV = 64


EPSILON = 1e-06


def rms_scale(values):
    return lax.rsqrt(jnp.mean(values * values, axis=-1, keepdims=True) + EPSILON)


def rope_tables(positions):
    half_size = HD // 2
    frequency = 10000.0 ** (-(jnp.arange(half_size, dtype=jnp.float32) * 2.0 / HD))
    angles = positions.astype(jnp.float32)[:, None] * frequency[None, :]
    return (jnp.cos(angles), jnp.sin(angles))


def rotate(values, cosine_table, sine_table):
    half_size = values.shape[-1] // 2
    front_half = values[..., :half_size]
    back_half = values[..., half_size:]
    return jnp.concatenate(
        [
            front_half * cosine_table - back_half * sine_table,
            back_half * cosine_table + front_half * sine_table,
        ],
        axis=-1,
    )


def rotate_back(values, cosine_table, sine_table):
    half_size = values.shape[-1] // 2
    front_half = values[..., :half_size]
    back_half = values[..., half_size:]
    return jnp.concatenate(
        [
            front_half * cosine_table + back_half * sine_table,
            back_half * cosine_table - front_half * sine_table,
        ],
        axis=-1,
    )


def dot_right_t(left_side, right_side):
    return lax.dot_general(
        left_side, right_side, (((1,), (1,)), ((), ())), preferred_element_type=jnp.float32
    )


def dot_left_t(left_side, right_side):
    return lax.dot_general(
        left_side, right_side, (((0,), (0,)), ((), ())), preferred_element_type=jnp.float32
    )


def norm_back(grad_normed, normed, inv_rms):
    return inv_rms * (grad_normed - normed * jnp.mean(grad_normed * normed, axis=-1, keepdims=True))


def joined_member(stored_list, member):
    return jnp.concatenate([stored[member] for stored in stored_list], axis=0)


def summed_member(stored_list, member):
    return jnp.sum(jnp.stack([stored[member] for stored in stored_list], axis=0), axis=0)


def attn_terms(stored_list):
    return (
        dot_left_t(joined_member(stored_list, 0), joined_member(stored_list, 1)),
        dot_left_t(joined_member(stored_list, 2), joined_member(stored_list, 3)),
        dot_left_t(joined_member(stored_list, 4), joined_member(stored_list, 5)),
        summed_member(stored_list, 10),
        summed_member(stored_list, 11),
    )


def mlp_terms(stored_list):
    return (
        dot_left_t(joined_member(stored_list, 6), joined_member(stored_list, 7)),
        dot_left_t(joined_member(stored_list, 8), joined_member(stored_list, 9)),
        summed_member(stored_list, 12),
    )


def shards(
    tokens,
    cotangent,
    lengths,
    slot_sequence,
    proj_in,
    query_up,
    proj_out,
    attn_gain,
    query_gain,
    mlp_gain,
    gate_up,
    down_proj,
):
    ctx_size = lax.axis_size("ctx")
    ctx_rank = lax.axis_index("ctx")
    batch_rank = lax.axis_index("batch")
    full_length = POS_DEV * ctx_size
    slot_total = lengths.shape[0]
    slot_ids = jnp.arange(slot_total, dtype=jnp.int32)
    seq_lengths = jnp.sum(
        jnp.where(slot_sequence[:, None] == slot_ids[None, :], lengths[None, :], 0), axis=1
    )
    own_lengths = lax.dynamic_slice_in_dim(seq_lengths, batch_rank * MICRO, MICRO)
    query_pos = ctx_rank * POS_DEV + jnp.arange(POS_DEV, dtype=jnp.int32)
    key_pos = jnp.arange(full_length, dtype=jnp.int32)
    cosine_table, sine_table = rope_tables(query_pos)
    score_scale = 1.0 / math.sqrt(HD)
    causal = key_pos[None, :] <= query_pos[:, None]
    kept_items = []
    outputs = []
    input_grads = []
    for micro_index in range(MICRO):
        full_in, full_qup, full_out, gain_norm, gain_query = (
            lax.all_gather(proj_in, ("batch", "ctx"), axis=0, tiled=True),
            lax.all_gather(query_up, ("batch", "ctx"), axis=0, tiled=True),
            lax.all_gather(proj_out, ("batch", "ctx"), axis=0, tiled=True),
            lax.all_gather(attn_gain, ("batch", "ctx"), axis=0, tiled=True),
            lax.all_gather(query_gain, ("batch", "ctx"), axis=0, tiled=True),
        )
        residual = tokens[micro_index].astype(jnp.float32)
        seq_limit = own_lengths[micro_index]
        allowed = causal & (key_pos[None, :] < seq_limit)
        scale_one = rms_scale(residual)
        normed_one = residual * scale_one
        attn_in = (normed_one * gain_norm.astype(jnp.float32)).astype(jnp.bfloat16)
        projected = jnp.dot(attn_in, full_in, preferred_element_type=jnp.float32)
        q_latent = projected[:, :QR]
        scale_query = rms_scale(q_latent)
        normed_query = q_latent * scale_query
        q_normed = (normed_query * gain_query.astype(jnp.float32)).astype(jnp.bfloat16)
        queries = jnp.dot(q_normed, full_qup, preferred_element_type=jnp.float32).reshape(
            POS_DEV, H, HD
        )
        q_rot = rotate(queries, cosine_table[:, None, :], sine_table[:, None, :]).astype(
            jnp.bfloat16
        )
        k_rot = rotate(projected[:, QR : QR + HD], cosine_table, sine_table).astype(jnp.bfloat16)
        v_low = projected[:, QR + HD :].astype(jnp.bfloat16)
        kv_all = lax.all_gather(jnp.concatenate([k_rot, v_low], axis=1), "ctx", axis=0, tiled=True)
        keys_all = kv_all[:, :HD]
        values_all = kv_all[:, HD:]
        scores = (
            jnp.einsum("thd,ud->htu", q_rot, keys_all, preferred_element_type=jnp.float32)
            * score_scale
        )
        masked = jnp.where(allowed[None], scores, -1e30)
        row_max = jnp.max(masked, axis=-1, keepdims=True)
        weights_raw = jnp.exp(masked - row_max)
        row_total = jnp.sum(weights_raw, axis=-1, keepdims=True)
        log_total = row_max + jnp.log(row_total)
        weights_low = (weights_raw / row_total).astype(jnp.bfloat16)
        mixed = (
            jnp.einsum("htu,ud->thd", weights_low, values_all, preferred_element_type=jnp.float32)
            .reshape(POS_DEV, H * HD)
            .astype(jnp.bfloat16)
        )
        hidden_res = residual + jnp.dot(mixed, full_out, preferred_element_type=jnp.float32)
        full_gu, full_down, gain_mlp = (
            lax.all_gather(gate_up, ("batch", "ctx"), axis=0, tiled=True),
            lax.all_gather(down_proj, ("batch", "ctx"), axis=0, tiled=True),
            lax.all_gather(mlp_gain, ("batch", "ctx"), axis=0, tiled=True),
        )
        scale_two = rms_scale(hidden_res)
        normed_two = hidden_res * scale_two
        mlp_in = (normed_two * gain_mlp.astype(jnp.float32)).astype(jnp.bfloat16)
        gate_mix = jnp.dot(mlp_in, full_gu, preferred_element_type=jnp.float32)
        gate_part = gate_mix[:, :FF]
        up_part = gate_mix[:, FF:]
        sigmoid_gate = jax.nn.sigmoid(gate_part)
        silu_gate = gate_part * sigmoid_gate
        activated = (silu_gate * up_part).astype(jnp.bfloat16)
        layer_out = hidden_res + jnp.dot(activated, full_down, preferred_element_type=jnp.float32)
        outputs.append(layer_out.astype(jnp.bfloat16))
        valid_rows = (query_pos < seq_limit).astype(jnp.float32)
        grad_out = cotangent[micro_index].astype(jnp.float32) * valid_rows[:, None]
        grad_mo = grad_out.astype(jnp.bfloat16)
        full_gu, full_down, gain_mlp = (
            lax.all_gather(gate_up, ("batch", "ctx"), axis=0, tiled=True),
            lax.all_gather(down_proj, ("batch", "ctx"), axis=0, tiled=True),
            lax.all_gather(mlp_gain, ("batch", "ctx"), axis=0, tiled=True),
        )
        grad_act = dot_right_t(grad_mo, full_down)
        grad_gate = grad_act * up_part * (sigmoid_gate * (1.0 + gate_part * (1.0 - sigmoid_gate)))
        grad_up = grad_act * silu_gate
        grad_gu = jnp.concatenate([grad_gate, grad_up], axis=1).astype(jnp.bfloat16)
        grad_mlp_in = dot_right_t(grad_gu, full_gu)
        gain_mlp_term = jnp.sum(grad_mlp_in * normed_two, axis=0)
        grad_hidden = grad_out + norm_back(
            grad_mlp_in * gain_mlp.astype(jnp.float32), normed_two, scale_two
        )
        grad_att = grad_hidden.astype(jnp.bfloat16)
        full_in, full_qup, full_out, gain_norm, gain_query = (
            lax.all_gather(proj_in, ("batch", "ctx"), axis=0, tiled=True),
            lax.all_gather(query_up, ("batch", "ctx"), axis=0, tiled=True),
            lax.all_gather(proj_out, ("batch", "ctx"), axis=0, tiled=True),
            lax.all_gather(attn_gain, ("batch", "ctx"), axis=0, tiled=True),
            lax.all_gather(query_gain, ("batch", "ctx"), axis=0, tiled=True),
        )
        grad_mixed = dot_right_t(grad_att, full_out).astype(jnp.bfloat16).reshape(POS_DEV, H, HD)
        scores_again = (
            jnp.einsum("thd,ud->htu", q_rot, keys_all, preferred_element_type=jnp.float32)
            * score_scale
        )
        weights_full = jnp.where(allowed[None], jnp.exp(scores_again - log_total), 0.0)
        grad_probs = jnp.einsum(
            "thd,ud->htu", grad_mixed, values_all, preferred_element_type=jnp.float32
        )
        row_dot = jnp.sum(weights_full * grad_probs, axis=-1, keepdims=True)
        grad_scores = (weights_full * (grad_probs - row_dot)).astype(jnp.bfloat16)
        grad_q_rot = (
            jnp.einsum("htu,ud->thd", grad_scores, keys_all, preferred_element_type=jnp.float32)
            * score_scale
        )
        grad_keys = (
            jnp.einsum("htu,thd->ud", grad_scores, q_rot, preferred_element_type=jnp.float32)
            * score_scale
        )
        grad_values = jnp.einsum(
            "htu,thd->ud",
            weights_full.astype(jnp.bfloat16),
            grad_mixed,
            preferred_element_type=jnp.float32,
        )
        grad_kv = lax.psum_scatter(
            jnp.concatenate([grad_keys, grad_values], axis=1).astype(jnp.bfloat16),
            "ctx",
            scatter_dimension=0,
            tiled=True,
        ).astype(jnp.float32)
        grad_key_raw = rotate_back(grad_kv[:, :HD], cosine_table, sine_table)
        grad_value_raw = grad_kv[:, HD:]
        grad_query = (
            rotate_back(grad_q_rot, cosine_table[:, None, :], sine_table[:, None, :])
            .reshape(POS_DEV, H * HD)
            .astype(jnp.bfloat16)
        )
        grad_qn = dot_right_t(grad_query, full_qup)
        gain_query_term = jnp.sum(grad_qn * normed_query, axis=0)
        grad_latent = norm_back(grad_qn * gain_query.astype(jnp.float32), normed_query, scale_query)
        grad_project = jnp.concatenate([grad_latent, grad_key_raw, grad_value_raw], axis=1).astype(
            jnp.bfloat16
        )
        grad_attn_in = dot_right_t(grad_project, full_in)
        gain_norm_term = jnp.sum(grad_attn_in * normed_one, axis=0)
        grad_tokens = grad_hidden + norm_back(
            grad_attn_in * gain_norm.astype(jnp.float32), normed_one, scale_one
        )
        input_grads.append(grad_tokens.astype(jnp.bfloat16))
        stored_now = (
            attn_in,
            grad_project,
            q_normed,
            grad_query,
            mixed,
            grad_att,
            mlp_in,
            grad_gu,
            activated,
            grad_mo,
            gain_norm_term,
            gain_query_term,
            gain_mlp_term,
        )
        kept_items.append(stored_now)
    attn_all = attn_terms(kept_items)
    attn_sums = (
        lax.psum_scatter(attn_all[0], ("batch", "ctx"), scatter_dimension=0, tiled=True),
        lax.psum_scatter(attn_all[1], ("batch", "ctx"), scatter_dimension=0, tiled=True),
        lax.psum_scatter(attn_all[2], ("batch", "ctx"), scatter_dimension=0, tiled=True),
        lax.psum_scatter(attn_all[3], ("batch", "ctx"), scatter_dimension=0, tiled=True),
        lax.psum_scatter(attn_all[4], ("batch", "ctx"), scatter_dimension=0, tiled=True),
    )
    mlp_all = mlp_terms(kept_items)
    mlp_sums = (
        lax.psum_scatter(mlp_all[0], ("batch", "ctx"), scatter_dimension=0, tiled=True),
        lax.psum_scatter(mlp_all[1], ("batch", "ctx"), scatter_dimension=0, tiled=True),
        lax.psum_scatter(mlp_all[2], ("batch", "ctx"), scatter_dimension=0, tiled=True),
    )
    layer_stack = jnp.stack(outputs, axis=0)
    grad_stack = jnp.stack(input_grads, axis=0)
    return (
        layer_stack,
        grad_stack,
        attn_sums[0],
        attn_sums[1],
        attn_sums[2],
        attn_sums[3],
        attn_sums[4],
        mlp_sums[2],
        mlp_sums[0],
        mlp_sums[1],
    )


def solution(mesh):
    placed = (
        P("batch", "ctx", None),
        P("batch", "ctx", None),
        P(),
        P(),
        P(("batch", "ctx"), None),
        P(("batch", "ctx"), None),
        P(("batch", "ctx"), None),
        P(("batch", "ctx")),
        P(("batch", "ctx")),
        P(("batch", "ctx")),
        P(("batch", "ctx"), None),
        P(("batch", "ctx"), None),
    )
    return jax.shard_map(
        shards,
        mesh=mesh,
        in_specs=placed,
        out_specs=(
            P("batch", "ctx", None),
            P("batch", "ctx", None),
            P(("batch", "ctx"), None),
            P(("batch", "ctx"), None),
            P(("batch", "ctx"), None),
            P(("batch", "ctx")),
            P(("batch", "ctx")),
            P(("batch", "ctx")),
            P(("batch", "ctx"), None),
            P(("batch", "ctx"), None),
        ),
        check_vma=False,
    )
```

profile of v0, /device:TPU:4, one launch (start us, length us, event | category | flops | bytes accessed | tf_op | source)
XLA Modules:
  0.0 3028.1 jit_solution(7683003624652409945)
XLA Ops:
  13.2 41.6 %all-reduce.7 = (bf16[2048]{0:T(1024)(128)(2,1)S(1)}, bf16[1024]{0:T(1024)(128)(2,1)S(1)}, bf16[2048]{0:T(1024)(128)(2,1)S(1)}) all-reduce(bf16[2048]{0:T(1024)(128)(2,1)S(1)} %dynamic-update-slice, bf16[1024]{0:T(1024)(128)(2,1)S(1)} %dynamic-update-slice.1, ...), channel_id=1, replica_groups=mesh['batch'=8,'ctx'=4] {'batch','ctx'}, use_global_device_ids=true, to_apply=%add | all-reduce | flops 5120 | bytes 20480
  63.6 17.9 all-gather.6.cloned.1.call-done
  99.9 60.5 %all-gather.8.cloned.1.call-done = bf16[1024,4096]{1,0:T(8,128)(2,1)} async-done(((bf16[32,4096]{1,0:T(8,128)(2,1)}), bf16[1024,4096]{1,0:T(8,128)(2,1)}) %all-gather.8.cloned.1.call-update) | async-done | bytes 8388624 | tf_op jit(solution)/shard_map/all_gather | solution.py:133
  171.8 104.9 %all-gather.10.cloned.1.call-done = bf16[4096,2048]{1,0:T(8,128)(2,1)} async-done(((bf16[128,2048]{1,0:T(8,128)(2,1)}), bf16[4096,2048]{1,0:T(8,128)(2,1)}) %all-gather.10.cloned.1.call-update) | async-done | bytes 16777232 | tf_op jit(solution)/shard_map/all_gather | solution.py:134
  291.7 241.2 %all-gather.12.cloned.1.call-done = bf16[2048,11264]{1,0:T(8,128)(2,1)} async-done(((bf16[64,11264]{1,0:T(8,128)(2,1)}), bf16[2048,11264]{1,0:T(8,128)(2,1)}) %all-gather.12.cloned.1.call-update) | async-done | bytes 46137360 | tf_op jit(solution)/shard_map/all_gather | solution.py:177
  532.9 20.9 fusion.206
  553.9 124.6 %all-gather.14.cloned.1.call-done = bf16[5632,2048]{1,0:T(8,128)(2,1)} async-done(((bf16[176,2048]{1,0:T(8,128)(2,1)}), bf16[5632,2048]{1,0:T(8,128)(2,1)}) %all-gather.14.cloned.1.call-update) | async-done | bytes 23068688 | tf_op jit(solution)/shard_map/all_gather | solution.py:178
  678.5 12.1 multiply_convert_fusion.3
  690.6 21.6 multiply_reduce_fusion.3
  712.2 20.0 fusion.209
  732.1 12.9 multiply_convert_fusion.1
  745.0 21.5 multiply_reduce_fusion.2
  769.3 11.1 convolution_convert_fusion
  783.1 11.0 convolution_convert_fusion.1
  818.8 20.8 reduce-scatter.10.cloned.1.call-done
  859.8 15.0 fusion.42
  876.1 20.2 fusion.20
  897.5 35.0 %fusion = f32[2048,11264]{1,0:T(8,128)} fusion(bf16[64,5632]{1,0:T(8,128)(2,1)} %copy-done.14, bf16[64,5632]{1,0:T(8,128)(2,1)S(1)} %copy-done.13, bf16[64,5632]{1,0:T(8,128)(2,1)} %copy-done.16, bf16[64,5632]{1,0:T(8,128)(2,1)} %copy-done.15, bf16[64,2048]{1,0:T(8,128)(2,1)S(1)} %copy-done.30, bf16[64,2048]{1,0:T(8,128)(2,1)S(1)} %copy-done.32), kind=kOutput, calls=%fused_computation.2 | convolution fusion | flops 5918162944 | bytes 95682560 | tf_op jit(solution)/shard_map/dot_general | solution.py:63
  934.4 10.5 fusion.10
  960.4 42.1 %all-reduce.6 = (f32[2048]{0:T(1024)S(1)}, f32[1024]{0:T(1024)S(1)}, f32[2048]{0:T(1024)S(1)}) all-reduce(f32[2048]{0:T(1024)S(1)} %reduce_sum.247, f32[1024]{0:T(1024)S(1)} %copy-done.69, f32[2048]{0:T(1024)S(1)} %copy-done.66), channel_id=7, replica_groups=mesh['batch'=8,'ctx'=4] {'batch','ctx'}, use_global_device_ids=true, to_apply=%region_26.27.clone | all-reduce | flops 5120 | bytes 40960
  1005.6 183.1 %reduce-scatter.14.cloned.1.call-done = f32[32,4096]{1,0:T(8,128)} async-done(((f32[1024,4096]{1,0:T(8,128)}), f32[32,4096]{1,0:T(8,128)}) %reduce-scatter.14.cloned.1.call-update) | async-done | bytes 524304 | tf_op jit(solution)/shard_map/reduce_scatter | solution.py:286
  1188.7 361.5 %reduce-scatter.16.cloned.1.call-done = f32[128,2048]{1,0:T(8,128)} async-done(((f32[4096,2048]{1,0:T(8,128)}), f32[128,2048]{1,0:T(8,128)}) %reduce-scatter.16.cloned.1.call-update) | async-done | bytes 1048592 | tf_op jit(solution)/shard_map/reduce_scatter | solution.py:287
  1550.3 496.0 %reduce-scatter.20.cloned.1.call-done = f32[176,2048]{1,0:T(8,128)} async-done(((f32[5632,2048]{1,0:T(8,128)}), f32[176,2048]{1,0:T(8,128)}) %reduce-scatter.20.cloned.1.call-update) | async-done | bytes 1441808 | tf_op jit(solution)/shard_map/reduce_scatter | solution.py:294
  2046.3 974.8 %reduce-scatter.18.cloned.1.call-done = f32[64,11264]{1,0:T(8,128)} async-done(((f32[2048,11264]{1,0:T(8,128)}), f32[64,11264]{1,0:T(8,128)}) %reduce-scatter.18.cloned.1.call-update) | async-done | bytes 2883600 | tf_op jit(solution)/shard_map/reduce_scatter | solution.py:293
  (292 shorter events, 131.6 us)
Async XLA Ops:
  7.2 74.4 %all-gather.6.cloned.1.call-start = ((), (), s32[]{:S(2)}) async-start(), calls=%async_computation.7 | async-start | bytes 6488064 | tf_op jit(solution)/shard_map/all_gather | solution.py:132
  7.9 152.5 %all-gather.8.cloned.1.call-start = ((), (), s32[]{:S(2)}) async-start(), calls=%async_computation.8 | async-start | bytes 8650752 | tf_op jit(solution)/shard_map/all_gather | solution.py:133
  8.7 268.1 %all-gather.10.cloned.1.call-start = ((), (), s32[]{:S(2)}) async-start(), calls=%async_computation.9 | async-start | bytes 17301504 | tf_op jit(solution)/shard_map/all_gather | solution.py:134
  9.4 523.5 %all-gather.12.cloned.1.call-start = ((), (), s32[]{:S(2)}) async-start(), calls=%async_computation.10 | async-start | bytes 47579136 | tf_op jit(solution)/shard_map/all_gather | solution.py:177
  10.0 668.5 %all-gather.14.cloned.1.call-start = ((), (), s32[]{:S(2)}) async-start(), calls=%async_computation.11 | async-start | bytes 23789568 | tf_op jit(solution)/shard_map/all_gather | solution.py:178
  10.6 807.4 %reduce-scatter.8.cloned.1.call-start = ((), (), s32[]{:S(2)}) async-start(), calls=%async_computation.12 | async-start | bytes 327680 | tf_op jit(solution)/shard_map/reduce_scatter | solution.py:242
  93.4 77.2 %copy-start.47 = (bf16[256,512]{1,0:T(8,128)(2,1)}, bf16[256,512]{1,0:T(8,128)(2,1)S(1)}, u32[]{:S(2)}) copy-start(bf16[256,512]{1,0:T(8,128)(2,1)S(1)} %all_gather.29) | copy-start | bytes 786436
  99.5 71.7 %copy-start.49 = (bf16[256,512]{1,0:T(8,128)(2,1)}, bf16[256,512]{1,0:T(8,128)(2,1)S(1)}, u32[]{:S(2)}) copy-start(bf16[256,512]{1,0:T(8,128)(2,1)S(1)} %all_gather.22) | copy-start | bytes 786436
  99.9 65.6 %copy-start.43 = (bf16[64,1024]{1,0:T(8,128)(2,1)}, bf16[64,1024]{1,0:T(8,128)(2,1)S(1)}, u32[]{:S(2)}) copy-start(bf16[64,1024]{1,0:T(8,128)(2,1)S(1)} %get-tuple-element.76) | copy-start | bytes 393220
  99.9 65.9 %copy-start.45 = (bf16[64,1024]{1,0:T(8,128)(2,1)}, bf16[64,1024]{1,0:T(8,128)(2,1)S(1)}, u32[]{:S(2)}) copy-start(bf16[64,1024]{1,0:T(8,128)(2,1)S(1)} %get-tuple-element.77) | copy-start | bytes 393220
  170.7 106.1 %copy-start.7 = (bf16[2,64,2048]{2,1,0:T(8,128)(2,1)S(1)}, bf16[2,64,2048]{2,1,0:T(8,128)(2,1)}, u32[]{:S(2)}) copy-start(bf16[2,64,2048]{2,1,0:T(8,128)(2,1)} %param.12) | copy-start | bytes 1572868
  171.2 114.6 %copy-start.21 = (bf16[16,8,8,256]{3,2,0,1:T(8,128)(2,1)}, bf16[16,8,8,256]{3,2,0,1:T(8,128)(2,1)S(1)}, u32[]{:S(2)}) copy-start(bf16[16,8,8,256]{3,2,0,1:T(8,128)(2,1)S(1)} %copy.95) | copy-start | bytes 1572868
  171.8 114.1 %copy-start.23 = (bf16[16,8,8,256]{3,2,0,1:T(8,128)(2,1)}, bf16[16,8,8,256]{3,2,0,1:T(8,128)(2,1)S(1)}, u32[]{:S(2)}) copy-start(bf16[16,8,8,256]{3,2,0,1:T(8,128)(2,1)S(1)} %copy.94) | copy-start | bytes 1572868
  285.8 480.8 %copy-start.5 = (f32[64,2048]{1,0:T(8,128)}, f32[64,2048]{1,0:T(8,128)S(1)}, u32[]{:S(2)}) copy-start(f32[64,2048]{1,0:T(8,128)S(1)} %get-tuple-element.93) | copy-start | bytes 1572868
  291.5 475.1 %copy-start.3 = (f32[64,2048]{1,0:T(8,128)}, f32[64,2048]{1,0:T(8,128)S(1)}, u32[]{:S(2)}) copy-start(f32[64,2048]{1,0:T(8,128)S(1)} %get-tuple-element.95) | copy-start | bytes 1572868
  291.7 262.2 %copy-start.31 = (bf16[64,2048]{1,0:T(8,128)(2,1)}, bf16[64,2048]{1,0:T(8,128)(2,1)S(1)}, u32[]{:S(2)}) copy-start(bf16[64,2048]{1,0:T(8,128)(2,1)S(1)} %multiply_convert_fusion.9) | copy-start | bytes 786436
  291.7 386.8 %copy-start.25 = (bf16[64,2048]{1,0:T(8,128)(2,1)S(1)}, bf16[64,2048]{1,0:T(8,128)(2,1)}, u32[]{:S(2)}) copy-start(bf16[64,2048]{1,0:T(8,128)(2,1)} %get-tuple-element.60) | copy-start | bytes 786436
  798.0 41.6 %reduce-scatter.10.cloned.1.call-start = ((), (), s32[]{:S(2)}) async-start(), calls=%async_computation.13 | async-start | bytes 327680 | tf_op jit(solution)/shard_map/reduce_scatter | solution.py:242
  811.0 194.6 %reduce-scatter.12.cloned.1.call-start = ((), (), s32[]{:S(2)}) async-start(), calls=%async_computation.14 | async-start | bytes 12976128 | tf_op jit(solution)/shard_map/reduce_scatter | solution.py:285
  848.7 340.1 %reduce-scatter.14.cloned.1.call-start = ((), (), s32[]{:S(2)}) async-start(), calls=%async_computation.15 | async-start | bytes 17301504 | tf_op jit(solution)/shard_map/reduce_scatter | solution.py:286
  858.4 691.9 %reduce-scatter.16.cloned.1.call-start = ((), (), s32[]{:S(2)}) async-start(), calls=%async_computation.16 | async-start | bytes 34603008 | tf_op jit(solution)/shard_map/reduce_scatter | solution.py:287
  874.8 1171.4 %reduce-scatter.20.cloned.1.call-start = ((), (), s32[]{:S(2)}) async-start(), calls=%async_computation.18 | async-start | bytes 47579136 | tf_op jit(solution)/shard_map/reduce_scatter | solution.py:294
  896.3 2124.8 %reduce-scatter.18.cloned.1.call-start = ((), (), s32[]{:S(2)}) async-start(), calls=%async_computation.17 | async-start | bytes 95158272 | tf_op jit(solution)/shard_map/reduce_scatter | solution.py:293
  956.2 48.1 %copy-start.41 = (f32[64,2048]{1,0:T(8,128)S(1)}, f32[64,2048]{1,0:T(8,128)}, u32[]{:S(2)}) copy-start(f32[64,2048]{1,0:T(8,128)} %get-tuple-element.33) | copy-start | bytes 1572868
  (68 other events, 743.9 us)
Sparse Core Ops, SparseCore 0:
  10.9 70.6 all-gather.5
  84.4 75.9 all-gather.7
  163.3 113.4 all-gather.9
  279.5 253.4 all-gather.11
  535.6 142.7 all-gather.13
  798.1 18.2 reduce-scatter.7
  819.5 20.0 reduce-scatter.9
  848.8 156.7 reduce-scatter.11
  1008.6 180.1 reduce-scatter.13
  1191.6 358.6 reduce-scatter.15
  1553.3 492.9 reduce-scatter.19
  2049.2 971.8 reduce-scatter.17
where the time goes:
time: 3040 us; the launch traced here: 3030 us
  waiting for transfers between devices  2590 us (85%)
  matrix products  288 us (9%)
  blocking collectives  95.5 us (3%)
    reduce_scatter x1, waiting for transfers between devices, shards(): lax.psum_scatter(mlp_all[0], ('batch', 'ctx'), scatter_dimension=0, tiled...  975 us
    reduce_scatter x1, waiting for transfers between devices, shards(): lax.psum_scatter(mlp_all[1], ('batch', 'ctx'), scatter_dimension=0, tiled...  496 us
    reduce_scatter x1, waiting for transfers between devices, shards(): lax.psum_scatter(attn_all[2], ('batch', 'ctx'), scatter_dimension=0, tile...  362 us
    all_gather x1, waiting for transfers between devices, shards(): lax.all_gather(gate_up, ('batch', 'ctx'), axis=0, tiled=True)  241 us
    reduce_scatter x1, waiting for transfers between devices, shards(): lax.psum_scatter(attn_all[1], ('batch', 'ctx'), scatter_dimension=0, tile...  183 us
    all_gather x1, waiting for transfers between devices, shards(): lax.all_gather(down_proj, ('batch', 'ctx'), axis=0, tiled=True)  125 us
    dot_general x10, matrix products, dot_right_t(): lax.dot_general(left_side, right_side, (((1,), (1,)), ((), ())), preferre...  108 us
    all_gather x1, waiting for transfers between devices, shards(): lax.all_gather(proj_out, ('batch', 'ctx'), axis=0, tiled=True)  105 us
  transfers between devices with their start and end apart: 12, of which 11 were waited for; matrix products, arithmetic and copies ran while one was open for 6% of the time, Pallas kernels for 0%

commit v1 on v0

v1 whole, which is shorter than its diff:
```python
import math

import jax
import jax.numpy as jnp
from jax import lax
from jax.sharding import PartitionSpec as P

H = 16
HD = 256
QR = 1024
EPSILON = 1e-06
BF = jnp.bfloat16
F32 = jnp.float32


def rms_scale(values):
    return lax.rsqrt(jnp.mean(values * values, axis=-1, keepdims=True) + EPSILON)


def rope_tables(positions):
    half_size = HD // 2
    frequency = 10000.0 ** (-(jnp.arange(half_size, dtype=F32) * 2.0 / HD))
    angles = positions.astype(F32)[:, None] * frequency[None, :]
    return (jnp.cos(angles), jnp.sin(angles))


def rotate(values, cosine_table, sine_table):
    half_size = values.shape[-1] // 2
    front_half = values[..., :half_size]
    back_half = values[..., half_size:]
    return jnp.concatenate(
        [
            front_half * cosine_table - back_half * sine_table,
            back_half * cosine_table + front_half * sine_table,
        ],
        axis=-1,
    )


def rotate_back(values, cosine_table, sine_table):
    return rotate(values, cosine_table, -sine_table)


def dot(left_side, right_side):
    return jnp.dot(left_side, right_side, preferred_element_type=F32)


def dot_right_t(left_side, right_side):
    return lax.dot_general(
        left_side, right_side, (((1,), (1,)), ((), ())), preferred_element_type=F32
    )


def dot_left_t(left_side, right_side):
    return lax.dot_general(
        left_side, right_side, (((0,), (0,)), ((), ())), preferred_element_type=F32
    )


def norm_back(grad_normed, normed, inv_rms):
    return inv_rms * (grad_normed - normed * jnp.mean(grad_normed * normed, axis=-1, keepdims=True))


def pick(array, index, axis=0):
    return lax.dynamic_index_in_dim(array, index, axis, keepdims=False)


def place(array, block, index, axis=0):
    return lax.dynamic_update_index_in_dim(array, block, index, axis)


class Ring:
    def __init__(self):
        self.n = lax.axis_size("batch")
        self.h = self.n // 2
        rank = lax.axis_index("batch")
        self.at = jnp.where(rank % 2 == 0, rank // 2, self.n - 1 - rank // 2)
        order = [2 * i for i in range(self.h)] + [2 * i + 1 for i in reversed(range(self.h))]
        self.up = [(order[i], order[(i + 1) % self.n]) for i in range(self.n)]
        self.down = [(there, here) for here, there in self.up]

    def rank_of(self, step):
        spot = (self.at + step) % self.n
        return jnp.where(spot < self.h, 2 * spot, 2 * (self.n - 1 - spot) + 1)

    def spread(self, block):
        found = {0: block}
        upward = downward = block
        for step in range(1, self.h):
            upward = lax.ppermute(upward, "batch", self.up)
            downward = lax.ppermute(downward, "batch", self.down)
            found[-step] = upward
            found[step] = downward
        cut = block.shape[0] // 2
        found[self.h] = jnp.concatenate(
            [
                lax.ppermute(upward[:cut], "batch", self.up),
                lax.ppermute(downward[cut:], "batch", self.down),
            ],
            axis=0,
        )
        return found

    def gather(self, block):
        found = self.spread(block)
        whole = jnp.zeros((self.n,) + block.shape, block.dtype)
        for step, part in found.items():
            whole = place(whole, part, self.rank_of(step))
        return whole

    def collect(self, term):
        far = term(self.h)
        cut = far.shape[0] // 2
        downward = lax.ppermute(far[:cut].astype(BF), "batch", self.down)
        upward = lax.ppermute(far[cut:].astype(BF), "batch", self.up)
        for step in range(self.h - 1, 0, -1):
            for_lower = term(-step).astype(F32)
            for_upper = term(step).astype(F32)
            if step == self.h - 1:
                for_lower = jnp.concatenate(
                    [for_lower[:cut] + downward.astype(F32), for_lower[cut:]], axis=0
                )
                for_upper = jnp.concatenate(
                    [for_upper[:cut], for_upper[cut:] + upward.astype(F32)], axis=0
                )
            else:
                for_lower = for_lower + downward.astype(F32)
                for_upper = for_upper + upward.astype(F32)
            downward = lax.ppermute(for_lower.astype(BF), "batch", self.down)
            upward = lax.ppermute(for_upper.astype(BF), "batch", self.up)
        own = term(0).astype(F32)
        return own + downward.astype(F32) + upward.astype(F32)

    def collect_rows(self, stacked):
        return self.collect(lambda step: pick(stacked, self.rank_of(step)))


def batch_exchange(stacked):
    n = lax.axis_size("batch")
    rank = lax.axis_index("batch")
    swapped = stacked
    for offset in range(1, n):
        pairs = [(i, i ^ offset) for i in range(n)]
        other = rank ^ offset
        swapped = place(swapped, lax.ppermute(pick(stacked, other), "batch", pairs), other)
    return swapped


FAR = [(0, 2), (1, 3), (2, 0), (3, 1)]
NEAR = [(0, 1), (1, 0), (2, 3), (3, 2)]


def ctx_place():
    rank = lax.axis_index("ctx")
    return rank // 2, rank % 2


def in_order(mine, theirs, at):
    return jnp.where(at == 0, jnp.stack([mine, theirs]), jnp.stack([theirs, mine]))


def ctx_gather(block):
    outer, inner = ctx_place()
    pair = in_order(block, lax.ppermute(block, "ctx", FAR), outer)
    whole = in_order(pair, lax.ppermute(pair, "ctx", NEAR), inner)
    whole = jnp.swapaxes(whole, 0, 1)
    return whole.reshape((4,) + block.shape)


def ctx_collect(stacked):
    outer, inner = ctx_place()
    parts = stacked.reshape((2, 2) + stacked.shape[1:])
    got = lax.ppermute(pick(parts, 1 - inner, 1).astype(BF), "ctx", NEAR)
    half = pick(parts, inner, 1).astype(F32) + got.astype(F32)
    got = lax.ppermute(pick(half, 1 - outer).astype(BF), "ctx", FAR)
    return pick(half, outer) + got.astype(F32)


def ctx_exchange(stacked):
    outer, inner = ctx_place()
    parts = stacked.reshape((2, 2) + stacked.shape[1:])
    got = lax.ppermute(pick(parts, 1 - outer), "ctx", FAR)
    parts = in_order(pick(parts, outer), got, outer)
    got = lax.ppermute(pick(parts, 1 - inner, 1), "ctx", NEAR)
    whole = in_order(pick(parts, inner, 1), got, inner)
    return jnp.swapaxes(whole, 0, 1).reshape(stacked.shape)


def slab_pairs(n_batch, n_ctx):
    return [(i, (i % n_batch) * n_ctx + i // n_batch) for i in range(n_batch * n_ctx)]


def shards(
    tokens,
    cotangent,
    lengths,
    slot_sequence,
    proj_in,
    query_up,
    proj_out,
    attn_gain,
    query_gain,
    mlp_gain,
    gate_up,
    down_proj,
):
    n_ctx = lax.axis_size("ctx")
    n_batch = lax.axis_size("batch")
    ctx_rank = lax.axis_index("ctx")
    batch_rank = lax.axis_index("batch")
    ring = Ring()
    micro, pos_dev, width = tokens.shape
    n_tok = micro * pos_dev
    full_length = pos_dev * n_ctx
    heads = H // n_ctx
    score_scale = 1.0 / math.sqrt(HD)
    in_cols = proj_in.shape[1]

    slot_total = lengths.shape[0]
    slot_ids = jnp.arange(slot_total, dtype=jnp.int32)
    seq_lengths = jnp.sum(
        jnp.where(slot_sequence[:, None] == slot_ids[None, :], lengths[None, :], 0), axis=1
    )
    own_lengths = lax.dynamic_slice_in_dim(seq_lengths, batch_rank * micro, micro)
    query_pos = ctx_rank * pos_dev + jnp.arange(pos_dev, dtype=jnp.int32)
    key_pos = jnp.arange(full_length, dtype=jnp.int32)
    cos_all, sin_all = rope_tables(key_pos)
    cos_own, sin_own = rope_tables(query_pos)

    own_rows = proj_in.shape[0]
    gain_rows = query_gain.shape[0]
    gains = jnp.stack(
        [attn_gain, mlp_gain, jnp.pad(query_gain, (0, own_rows - gain_rows))], axis=1
    )
    packed = jnp.concatenate([proj_in, jnp.pad(gains, ((0, 0), (0, 125)))], axis=1)
    packed = ctx_gather(ring.gather(packed))
    packed = jnp.swapaxes(packed, 0, 1).reshape(width, in_cols + 128)
    full_in = packed[:, :in_cols]
    gains = packed[:, in_cols : in_cols + 3].T.astype(F32)
    gain_norm = gains[0]
    gain_mlp = gains[1]
    gain_query = gains[2].reshape(n_batch * n_ctx, own_rows)[:, :gain_rows].reshape(QR)

    up_parts = query_up.reshape(gain_rows, n_ctx, heads * HD).swapaxes(0, 1)
    up_block = ctx_exchange(up_parts).reshape(n_ctx * gain_rows, heads * HD)
    own_qup = ring.gather(up_block).reshape(QR, heads * HD)
    slabs = slab_pairs(n_batch, n_ctx)
    out_block = lax.ppermute(proj_out, ("batch", "ctx"), slabs)
    own_out = ring.gather(out_block).reshape(heads * HD, width)

    ff_all = gate_up.shape[1] // 2
    ff = ff_all // n_batch
    gu_parts = gate_up.reshape(own_rows, 2, n_batch, ff).transpose(2, 1, 0, 3)
    gu_rows = ctx_gather(batch_exchange(gu_parts))
    gu_rows = gu_rows.transpose(2, 1, 0, 3, 4).reshape(2, width, ff)
    own_gate, own_up = gu_rows[0], gu_rows[1]
    own_down = ctx_gather(down_proj).reshape(ff, width)

    residual = tokens.reshape(n_tok, width).astype(F32)
    valid_rows = (query_pos[None, :] < own_lengths[:, None]).astype(F32).reshape(n_tok, 1)
    grad_out = cotangent.reshape(n_tok, width).astype(F32) * valid_rows
    grad_mo = ring.spread(grad_out.astype(BF))

    scale_one = rms_scale(residual)
    normed_one = residual * scale_one
    attn_in = (normed_one * gain_norm).astype(BF)
    attn_in_all = ctx_gather(attn_in).reshape(n_ctx * n_tok, width)
    projected = dot(attn_in, full_in)
    q_latent = projected[:, :QR]
    scale_query = rms_scale(q_latent)
    normed_query = q_latent * scale_query
    q_normed = (normed_query * gain_query).astype(BF)
    k_rot = rotate(
        projected[:, QR : QR + HD].reshape(micro, pos_dev, HD), cos_own, sin_own
    ).astype(BF)
    v_low = projected[:, QR + HD :].astype(BF)
    qkv_all = ctx_gather(jnp.concatenate([q_normed, k_rot.reshape(n_tok, HD), v_low], axis=1))
    q_normed_all = qkv_all[..., :QR].reshape(n_ctx * n_tok, QR)

    def by_sequence(values):
        return (
            values.reshape(n_ctx, micro, pos_dev, -1)
            .swapaxes(0, 1)
            .reshape(micro, full_length, -1)
        )

    def by_position(values):
        return (
            values.reshape(micro, n_ctx, pos_dev, -1)
            .swapaxes(0, 1)
            .reshape(n_ctx * n_tok, -1)
        )

    def split_heads(values):
        return by_sequence(values).reshape(micro, full_length, heads, HD).swapaxes(1, 2)

    def join_heads(values):
        return by_position(values.swapaxes(1, 2).reshape(micro, full_length, heads * HD))

    kv_all = by_sequence(qkv_all[..., QR:])
    keys_all = kv_all[..., :HD]
    values_all = kv_all[..., HD:]
    queries = split_heads(dot(q_normed_all, own_qup))
    q_rot = rotate(queries, cos_all, sin_all).astype(BF)
    allowed = (key_pos[None, :] <= key_pos[:, None])[None, None] & (
        key_pos[None, None, None, :] < own_lengths[:, None, None, None]
    )
    scores = jnp.einsum("shtd,sud->shtu", q_rot, keys_all, preferred_element_type=F32) * score_scale
    masked = jnp.where(allowed, scores, -1e30)
    row_max = jnp.max(masked, axis=-1, keepdims=True)
    raised = jnp.exp(masked - row_max)
    weights = raised / jnp.sum(raised, axis=-1, keepdims=True)
    weights_low = weights.astype(BF)
    mixed = join_heads(
        jnp.einsum("shtu,sud->shtd", weights_low, values_all, preferred_element_type=F32).astype(BF)
    )
    attended = ctx_collect(dot(mixed, own_out).reshape(n_ctx, n_tok, width))
    hidden_res = residual + attended

    scale_two = rms_scale(hidden_res)
    normed_two = hidden_res * scale_two
    mlp_in = ring.spread((normed_two * gain_mlp).astype(BF))
    far = ring.h
    groups = [[0]] + [[-step, step] for step in range(1, far)] + [[far]]
    out_terms = {}
    in_terms = {}
    kept = []
    for group in groups:
        rows = jnp.concatenate([mlp_in[step] for step in group], axis=0)
        grad_rows = jnp.concatenate([grad_mo[step] for step in group], axis=0)
        gate_part = dot(rows, own_gate)
        up_part = dot(rows, own_up)
        sigmoid_gate = jax.nn.sigmoid(gate_part)
        silu_gate = gate_part * sigmoid_gate
        activated = (silu_gate * up_part).astype(BF)
        grad_act = dot_right_t(grad_rows, own_down)
        grad_gate = (
            grad_act * up_part * (sigmoid_gate * (1.0 + gate_part * (1.0 - sigmoid_gate)))
        ).astype(BF)
        grad_up = (grad_act * silu_gate).astype(BF)
        in_term = dot_right_t(grad_gate, own_gate) + dot_right_t(grad_up, own_up)
        out_term = dot(activated, own_down)
        for place_in, step in enumerate(group):
            cut = slice(place_in * n_tok, (place_in + 1) * n_tok)
            in_terms[step] = in_term[cut]
            out_terms[step] = out_term[cut]
        kept.append((rows, grad_rows, activated, grad_gate, grad_up))
    rows, grad_rows, activated, grad_gate, grad_up = (
        jnp.concatenate(items, axis=0) for items in zip(*kept)
    )
    grad_mlp_in = ring.collect(lambda step: in_terms[step])
    gain_mlp_term = jnp.sum(grad_mlp_in * normed_two, axis=0)
    grad_hidden = grad_out + norm_back(grad_mlp_in * gain_mlp, normed_two, scale_two)
    layer_out = hidden_res + ring.collect(lambda step: out_terms[step])

    grad_gu_own = jnp.stack([dot_left_t(rows, grad_gate), dot_left_t(rows, grad_up)])
    grad_gu_own = grad_gu_own.reshape(2, n_batch, n_ctx, own_rows, ff).transpose(2, 1, 0, 3, 4)
    grad_gu_own = batch_exchange(ctx_collect(grad_gu_own).astype(BF))
    grad_gate_up = grad_gu_own.transpose(2, 1, 0, 3).reshape(own_rows, 2 * ff_all).astype(F32)
    grad_down_own = dot_left_t(activated, grad_rows)
    grad_down = ctx_collect(grad_down_own.reshape(n_ctx, ff // n_ctx, width))

    grad_att_all = ctx_gather(grad_hidden.astype(BF)).reshape(n_ctx * n_tok, width)
    grad_out_own = dot_left_t(mixed, grad_att_all)
    grad_out_own = ring.collect_rows(grad_out_own.reshape(n_batch, -1, width)).astype(BF)
    grad_proj_out = lax.ppermute(
        grad_out_own, ("batch", "ctx"), [(there, here) for here, there in slabs]
    ).astype(F32)
    grad_mixed = split_heads(dot_right_t(grad_att_all, own_out).astype(BF))
    grad_probs = jnp.einsum(
        "shtd,sud->shtu", grad_mixed, values_all, preferred_element_type=F32
    )
    row_dot = jnp.sum(weights * grad_probs, axis=-1, keepdims=True)
    grad_scores = (weights * (grad_probs - row_dot)).astype(BF)
    grad_q_rot = (
        jnp.einsum("shtu,sud->shtd", grad_scores, keys_all, preferred_element_type=F32)
        * score_scale
    )
    grad_keys = (
        jnp.einsum("shtu,shtd->sud", grad_scores, q_rot, preferred_element_type=F32)
        * score_scale
    )
    grad_values = jnp.einsum(
        "shtu,shtd->sud", weights_low, grad_mixed, preferred_element_type=F32
    )
    grad_q = join_heads(rotate_back(grad_q_rot, cos_all, sin_all).astype(BF))
    grad_qn_part = dot_right_t(grad_q, own_qup)
    grad_kv_part = by_position(jnp.concatenate([grad_keys, grad_values], axis=-1))
    back_parts = jnp.concatenate([grad_qn_part, grad_kv_part], axis=1).astype(BF)
    back_own = ctx_collect(back_parts.reshape(n_ctx, n_tok, in_cols))
    grad_qn = back_own[:, :QR]
    gain_query_term = jnp.sum(grad_qn * normed_query, axis=0)
    grad_latent = norm_back(grad_qn * gain_query, normed_query, scale_query)
    grad_key_raw = rotate_back(
        back_own[:, QR : QR + HD].reshape(micro, pos_dev, HD), cos_own, sin_own
    ).reshape(n_tok, HD)
    grad_project = jnp.concatenate(
        [grad_latent, grad_key_raw, back_own[:, QR + HD :]], axis=1
    ).astype(BF)
    grad_attn_in = dot_right_t(grad_project, full_in)
    gain_norm_term = jnp.sum(grad_attn_in * normed_one, axis=0)
    grad_tokens = grad_hidden + norm_back(grad_attn_in * gain_norm, normed_one, scale_one)

    grad_up_own = dot_left_t(q_normed_all, grad_q)
    grad_up_own = ring.collect_rows(grad_up_own.reshape(n_batch, -1, heads * HD)).astype(BF)
    grad_query_up = (
        ctx_exchange(grad_up_own.reshape(n_ctx, gain_rows, heads * HD))
        .swapaxes(0, 1)
        .reshape(gain_rows, H * HD)
        .astype(F32)
    )
    part_cols = in_cols // n_ctx
    project_parts = grad_project.reshape(n_tok, n_ctx, part_cols).swapaxes(0, 1)
    project_all = ctx_exchange(project_parts).reshape(n_ctx * n_tok, part_cols)
    grad_in_own = dot_left_t(attn_in_all, project_all).reshape(
        n_batch, n_ctx, own_rows, part_cols
    )
    gain_terms = jnp.stack(
        [
            gain_norm_term.reshape(n_batch, n_ctx, own_rows),
            gain_mlp_term.reshape(n_batch, n_ctx, own_rows),
            jnp.pad(
                gain_query_term.reshape(n_batch, n_ctx, gain_rows),
                ((0, 0), (0, 0), (0, own_rows - gain_rows)),
            ),
        ],
        axis=2,
    )
    gain_terms = jnp.pad(gain_terms, ((0, 0), (0, 0), (0, 13), (0, part_cols - own_rows)))
    joined = jnp.concatenate([grad_in_own, gain_terms], axis=2).reshape(n_batch, -1, part_cols)
    joined = ring.collect_rows(joined).astype(BF)
    joined = ctx_exchange(joined.reshape(n_ctx, own_rows + 16, part_cols)).astype(F32)
    grad_proj_in = joined[:, :own_rows].swapaxes(0, 1).reshape(own_rows, in_cols)
    gain_sums = jnp.sum(joined[:, own_rows : own_rows + 3, :own_rows], axis=0)

    return (
        layer_out.reshape(tokens.shape).astype(BF),
        grad_tokens.reshape(tokens.shape).astype(BF),
        grad_proj_in,
        grad_query_up,
        grad_proj_out,
        gain_sums[0],
        gain_sums[2, :gain_rows],
        gain_sums[1],
        grad_gate_up,
        grad_down,
    )


def solution(mesh):
    rows = P(("batch", "ctx"), None)
    vector = P(("batch", "ctx"))
    acts = P("batch", "ctx", None)
    return jax.shard_map(
        shards,
        mesh=mesh,
        in_specs=(acts, acts, P(), P(), rows, rows, rows, vector, vector, vector, rows, rows),
        out_specs=(acts, acts, rows, rows, rows, vector, vector, vector, rows, rows),
        check_vma=False,
    )
```

time: 3040 us -> 835 us (0.27)
  waiting for transfers between devices: 2590 us -> 304 us
  matrix products: 288 us -> 101 us
  local copies, waits for them, and re-layouts: 16.1 us -> 185 us
  starting transfers between devices: 1.06 us -> 135 us
  blocking collectives: 95.5 us -> 0 us
  other arithmetic: 23.3 us -> 92 us
    reduce_scatter x7 -> x0, waiting for transfers between devices: 2040 us -> none  [the longest x1 975 us: shards(): lax.psum_scatter(mlp_all[0], ('batch', 'ctx'), scatter_dimension=0, tiled...]
    all_gather x5 -> x0, waiting for transfers between devices: 549 us -> none  [the longest x1 241 us: shards(): lax.all_gather(gate_up, ('batch', 'ctx'), axis=0, tiled=True)]
    ppermute x0 -> x124, waiting for transfers between devices: none -> 304 us  [the longest x15 64.6 us: collect(): downward = lax.ppermute(for_lower.astype(BF), 'batch', self.down)]
    ppermute x0 -> x124, starting transfers between devices: none -> 135 us  [the longest x14 22.9 us: batch_exchange(): lax.ppermute(pick(stacked, other), 'batch', pairs)]
    unnamed x2 -> x0, blocking collectives: 83.7 us -> none
    dot_general x10 -> x18, matrix products: 108 us -> 30.1 us  [dot_right_t(): lax.dot_general(left_side, right_side, (((1,), (1,)), ((), ())), preferre...]
    dynamic_update_slice x0 -> x33, local copies, waits for them, and re-layouts: none -> 70.6 us  [place(): return lax.dynamic_update_index_in_dim(array, block, index, axis)]
    dot_general x5 -> x6, matrix products: 85.3 us -> 20.5 us  [dot_left_t(): lax.dot_general(left_side, right_side, (((0,), (0,)), ((), ())), preferre...]
  transfers between devices with their start and end apart: 12 -> 124, of which waited for: 11 -> 50; matrix products, arithmetic and copies ran while one was open for 6% -> 44% of each run, Pallas kernels for 0% -> 0%
where the time goes in v1:
time: 835 us; the launch traced here: 821 us
  waiting for transfers between devices  304 us (36%)
  local copies, waits for them, and re-layouts  185 us (22%)
  starting transfers between devices  135 us (16%)
  matrix products  101 us (12%)
  other arithmetic  92 us (11%)
    dynamic_update_slice x33, local copies, waits for them, and re-layouts, place(): return lax.dynamic_update_index_in_dim(array, block, index, axis)  70.6 us
    ppermute x15, waiting for transfers between devices, collect(): downward = lax.ppermute(for_lower.astype(BF), 'batch', self.down)  64.6 us
    ppermute x6, waiting for transfers between devices, ctx_gather(): pair = in_order(block, lax.ppermute(block, 'ctx', FAR), outer)  50.8 us
    ppermute x14, waiting for transfers between devices, batch_exchange(): lax.ppermute(pick(stacked, other), 'batch', pairs)  44.5 us
    ppermute x15, waiting for transfers between devices, spread(): upward = lax.ppermute(upward, 'batch', self.up)  36.1 us
    ppermute x15, waiting for transfers between devices, collect(): upward = lax.ppermute(for_upper.astype(BF), 'batch', self.up)  35.3 us
    dot_general x18, matrix products, dot_right_t(): lax.dot_general(left_side, right_side, (((1,), (1,)), ((), ())), preferre...  30.1 us
    dot_general x18, matrix products, dot(): return jnp.dot(left_side, right_side, preferred_element_type=F32)  29.8 us
  transfers between devices with their start and end apart: 124, of which 50 were waited for; matrix products, arithmetic and copies ran while one was open for 44% of the time, Pallas kernels for 0%

profile of v1, /device:TPU:4, one launch (start us, length us, event | category | flops | bytes accessed | tf_op | source)
XLA Modules:
  0.0 821.2 jit_solution(282900905526429068)
XLA Ops:
  50.0 8.8 %collective-permute-done.36 = bf16[2,64,704]{2,1,0:T(8,128)(2,1)S(1)} collective-permute-done((bf16[2,64,704]{2,1,0:T(8,128)(2,1)S(1)}, bf16[2,64,704]{2,1,0:T(8,128)(2,1)S(1)}, u32[]{:S(2)}, u32[]{:S(2)}) %collective-permute-start.36) | collective-permute-done | bytes 180256 | tf_op jit(solution)/shard_map/ppermute | solution.py:145
  77.3 8.5 %dynamic_update_slice.142 = bf16[8,2,64,704]{3,0,1,2:T(8,128)(2,1)S(1)} dynamic-update-slice(bf16[8,2,64,704]{3,0,1,2:T(8,128)(2,1)S(1)} %bitcast.710, bf16[1,2,64,704]{3,0,1,2:T(2,128)(2,1)} %copy.239, s32[]{:T(128)S(6)} %select_n.672, s32[]{:T(128)} %constant.507.clone.1, s32[]{:T(128)} %constant.507.clone.1, s32[]{:T(128)} %constant.507.clone.1) | dynamic-update-slice | bytes 360452 | tf_op jit(solution)/shard_map/jit(dynamic_update_index_in_dim)/dynamic_update_slice | solution.py:69
  85.9 8.6 %dynamic_update_slice.143 = bf16[8,2,64,704]{3,0,1,2:T(8,128)(2,1)S(1)} dynamic-update-slice(bf16[8,2,64,704]{3,0,1,2:T(8,128)(2,1)S(1)} %dynamic_update_slice.142, bf16[1,2,64,704]{3,0,1,2:T(2,128)(2,1)} %copy.241, s32[]{:T(128)S(6)} %select_n.673, s32[]{:T(128)} %constant.507.clone.1, s32[]{:T(128)} %constant.507.clone.1, s32[]{:T(128)} %constant.507.clone.1) | dynamic-update-slice | bytes 360452 | tf_op jit(solution)/shard_map/jit(dynamic_update_index_in_dim)/dynamic_update_slice | solution.py:69
  94.4 8.6 %dynamic_update_slice.144 = bf16[8,2,64,704]{3,0,1,2:T(8,128)(2,1)S(1)} dynamic-update-slice(bf16[8,2,64,704]{3,0,1,2:T(8,128)(2,1)S(1)} %dynamic_update_slice.143, bf16[1,2,64,704]{3,0,1,2:T(2,128)(2,1)} %copy.243, s32[]{:T(128)S(6)} %select_n.674, s32[]{:T(128)} %constant.507.clone.1, s32[]{:T(128)} %constant.507.clone.1, s32[]{:T(128)} %constant.507.clone.1) | dynamic-update-slice | bytes 360452 | tf_op jit(solution)/shard_map/jit(dynamic_update_index_in_dim)/dynamic_update_slice | solution.py:69
  103.0 8.6 %dynamic_update_slice.145 = bf16[8,2,64,704]{3,0,1,2:T(8,128)(2,1)S(1)} dynamic-update-slice(bf16[8,2,64,704]{3,0,1,2:T(8,128)(2,1)S(1)} %dynamic_update_slice.144, bf16[1,2,64,704]{3,0,1,2:T(2,128)(2,1)} %copy.245, s32[]{:T(128)S(6)} %select_n.675, s32[]{:T(128)} %constant.507.clone.1, s32[]{:T(128)} %constant.507.clone.1, s32[]{:T(128)} %constant.507.clone.1) | dynamic-update-slice | bytes 360452 | tf_op jit(solution)/shard_map/jit(dynamic_update_index_in_dim)/dynamic_update_slice | solution.py:69
  111.6 8.6 %dynamic_update_slice.146 = bf16[8,2,64,704]{3,0,1,2:T(8,128)(2,1)S(1)} dynamic-update-slice(bf16[8,2,64,704]{3,0,1,2:T(8,128)(2,1)S(1)} %dynamic_update_slice.145, bf16[1,2,64,704]{3,0,1,2:T(2,128)(2,1)} %copy.247, s32[]{:T(128)S(6)} %select_n.676, s32[]{:T(128)} %constant.507.clone.1, s32[]{:T(128)} %constant.507.clone.1, s32[]{:T(128)} %constant.507.clone.1) | dynamic-update-slice | bytes 360452 | tf_op jit(solution)/shard_map/jit(dynamic_update_index_in_dim)/dynamic_update_slice | solution.py:69
  120.2 8.6 %dynamic_update_slice.147 = bf16[8,2,64,704]{3,0,1,2:T(8,128)(2,1)S(1)} dynamic-update-slice(bf16[8,2,64,704]{3,0,1,2:T(8,128)(2,1)S(1)} %dynamic_update_slice.146, bf16[1,2,64,704]{3,0,1,2:T(2,128)(2,1)} %copy.249, s32[]{:T(128)S(6)} %select_n.677, s32[]{:T(128)} %constant.507.clone.1, s32[]{:T(128)} %constant.507.clone.1, s32[]{:T(128)} %constant.507.clone.1) | dynamic-update-slice | bytes 360452 | tf_op jit(solution)/shard_map/jit(dynamic_update_index_in_dim)/dynamic_update_slice | solution.py:69
  128.8 8.6 %dynamic_update_slice.148 = bf16[8,2,64,704]{3,0,1,2:T(8,128)(2,1)S(1)} dynamic-update-slice(bf16[8,2,64,704]{3,0,1,2:T(8,128)(2,1)S(1)} %dynamic_update_slice.147, bf16[1,2,64,704]{3,0,1,2:T(2,128)(2,1)} %copy.251, s32[]{:T(128)S(6)} %select_n.678, s32[]{:T(128)} %constant.507.clone.1, s32[]{:T(128)} %constant.507.clone.1, s32[]{:T(128)} %constant.507.clone.1) | dynamic-update-slice | bytes 360452 | tf_op jit(solution)/shard_map/jit(dynamic_update_index_in_dim)/dynamic_update_slice | solution.py:69
  195.5 10.7 %collective-permute-done.63 = bf16[128,2048]{1,0:T(8,128)(2,1)S(1)} collective-permute-done((bf16[128,2048]{1,0:T(8,128)(2,1)}, bf16[128,2048]{1,0:T(8,128)(2,1)S(1)}, u32[]{:S(2)}, u32[]{:S(2)}) %collective-permute-start.63) | collective-permute-done | bytes 524320 | tf_op jit(solution)/shard_map/ppermute | solution.py:91
  208.3 9.3 %collective-permute-done.8 = bf16[8,64,1664]{2,1,0:T(8,128)(2,1)S(1)} collective-permute-done((bf16[8,64,1664]{2,1,0:T(8,128)(2,1)S(1)}, bf16[8,64,1664]{2,1,0:T(8,128)(2,1)S(1)}, u32[]{:S(2)}, u32[]{:S(2)}) %collective-permute-start.8) | collective-permute-done | bytes 1703968 | tf_op jit(solution)/shard_map/ppermute | solution.py:164
  226.4 10.1 %collective-permute-done.26 = bf16[128,2048]{1,0:T(8,128)(2,1)S(1)} collective-permute-done((bf16[128,2048]{1,0:T(8,128)(2,1)S(1)}, bf16[128,2048]{1,0:T(8,128)(2,1)S(1)}, u32[]{:S(2)}, u32[]{:S(2)}) %collective-permute-start.26) | collective-permute-done | bytes 524320 | tf_op jit(solution)/shard_map/ppermute | solution.py:91
  238.8 18.1 %collective-permute-done.40 = bf16[8,2,64,704]{3,0,1,2:T(8,128)(2,1)S(1)} collective-permute-done((bf16[8,2,64,704]{3,0,1,2:T(8,128)(2,1)S(1)}, bf16[8,2,64,704]{3,0,1,2:T(8,128)(2,1)S(1)}, u32[]{:S(2)}, u32[]{:S(2)}) %collective-permute-start.40) | collective-permute-done | bytes 1441824 | tf_op jit(solution)/shard_map/ppermute | solution.py:164
  344.7 9.4 %collective-permute-done.80 = bf16[128,2048]{1,0:T(8,128)(2,1)S(1)} collective-permute-done((bf16[128,2048]{1,0:T(8,128)(2,1)S(1)}, bf16[128,2048]{1,0:T(8,128)(2,1)S(1)}, u32[]{:S(2)}, u32[]{:S(2)}) %collective-permute-start.80) | collective-permute-done | bytes 524320 | tf_op jit(solution)/shard_map/ppermute | solution.py:164
  355.3 9.6 %collective-permute-done.32 = bf16[128,2048]{1,0:T(8,128)(2,1)S(1)} collective-permute-done((bf16[128,2048]{1,0:T(8,128)(2,1)S(1)}, bf16[128,2048]{1,0:T(8,128)(2,1)S(1)}, u32[]{:S(2)}, u32[]{:S(2)}) %collective-permute-start.32) | collective-permute-done | bytes 524320 | tf_op jit(solution)/shard_map/ppermute | solution.py:175
  463.5 10.6 %pad_maximum_fusion = f32[2,8,4,64,704]{4,3,2,1,0:T(8,128)} fusion(f32[1,8,4,64,704]{4,3,2,1,0:T(8,128)} %bitcast.740, f32[1,8,4,64,704]{4,3,2,1,0:T(8,128)} %bitcast.741), kind=kLoop, calls=%fused_computation.1 | loop fusion | flops 2883584 | bytes 23068672 | tf_op jit(solution)/shard_map/stack | solution.py:356
  485.6 9.7 %collective-permute-done.57 = bf16[128,2048]{1,0:T(8,128)(2,1)S(1)} collective-permute-done((bf16[128,2048]{1,0:T(8,128)(2,1)S(1)}, bf16[128,2048]{1,0:T(8,128)(2,1)S(1)}, u32[]{:S(2)}, u32[]{:S(2)}) %collective-permute-start.57) | collective-permute-done | bytes 524320 | tf_op jit(solution)/shard_map/ppermute | solution.py:130
  497.7 9.9 %collective-permute-done.73 = bf16[128,2048]{1,0:T(8,128)(2,1)S(1)} collective-permute-done((bf16[128,2048]{1,0:T(8,128)(2,1)S(1)}, bf16[128,2048]{1,0:T(8,128)(2,1)S(1)}, u32[]{:S(2)}, u32[]{:S(2)}) %collective-permute-start.73) | collective-permute-done | bytes 524320 | tf_op jit(solution)/shard_map/ppermute | solution.py:130
  509.9 9.7 %collective-permute-done.54 = bf16[128,2048]{1,0:T(8,128)(2,1)S(1)} collective-permute-done((bf16[128,2048]{1,0:T(8,128)(2,1)S(1)}, bf16[128,2048]{1,0:T(8,128)(2,1)S(1)}, u32[]{:S(2)}, u32[]{:S(2)}) %collective-permute-start.54) | collective-permute-done | bytes 524320 | tf_op jit(solution)/shard_map/ppermute | solution.py:129
  522.0 9.7 %collective-permute-done.70 = bf16[128,2048]{1,0:T(8,128)(2,1)S(1)} collective-permute-done((bf16[128,2048]{1,0:T(8,128)(2,1)S(1)}, bf16[128,2048]{1,0:T(8,128)(2,1)S(1)}, u32[]{:S(2)}, u32[]{:S(2)}) %collective-permute-start.70) | collective-permute-done | bytes 524320 | tf_op jit(solution)/shard_map/ppermute | solution.py:129
  536.5 16.6 %collective-permute-done.71 = bf16[128,2048]{1,0:T(8,128)(2,1)S(1)} collective-permute-done((bf16[128,2048]{1,0:T(8,128)(2,1)S(1)}, bf16[128,2048]{1,0:T(8,128)(2,1)S(1)}, u32[]{:S(2)}, u32[]{:S(2)}) %collective-permute-start.71) | collective-permute-done | bytes 524320 | tf_op jit(solution)/shard_map/ppermute | solution.py:129
  673.1 10.8 %collective-permute-done.115 = bf16[2,64,704]{2,1,0:T(8,128)(2,1)S(1)} collective-permute-done((bf16[2,64,704]{2,1,0:T(8,128)(2,1)S(1)}, bf16[2,64,704]{2,1,0:T(8,128)(2,1)S(1)}, u32[]{:S(2)}, u32[]{:S(2)}) %collective-permute-start.115) | collective-permute-done | bytes 180256 | tf_op jit(solution)/shard_map/ppermute | solution.py:145
  714.8 9.1 %collective-permute-done.118 = bf16[2,64,704]{2,1,0:T(8,128)(2,1)S(1)} collective-permute-done((bf16[2,64,704]{2,1,0:T(8,128)(2,1)S(1)}, bf16[2,64,704]{2,1,0:T(8,128)(2,1)S(1)}, u32[]{:S(2)}, u32[]{:S(2)}) %collective-permute-start.118) | collective-permute-done | bytes 180256 | tf_op jit(solution)/shard_map/ppermute | solution.py:145
  794.9 11.5 %collective-permute-done.92 = bf16[2,80,384]{2,1,0:T(8,128)(2,1)S(1)} collective-permute-done((bf16[2,80,384]{2,1,0:T(8,128)(2,1)S(1)}, bf16[2,80,384]{2,1,0:T(8,128)(2,1)S(1)}, u32[]{:S(2)}, u32[]{:S(2)}) %collective-permute-start.92) | collective-permute-done | bytes 122912 | tf_op jit(solution)/shard_map/ppermute | solution.py:182
  807.4 10.3 %collective-permute-done.112 = bf16[128,2048]{1,0:T(8,128)(2,1)S(1)} collective-permute-done((bf16[128,2048]{1,0:T(8,128)(2,1)S(1)}, bf16[128,2048]{1,0:T(8,128)(2,1)S(1)}, u32[]{:S(2)}, u32[]{:S(2)}) %collective-permute-start.112) | collective-permute-done | bytes 524320 | tf_op jit(solution)/shard_map/ppermute | solution.py:366
  (777 shorter events, 573.3 us)
Async XLA Ops:
  3.9 133.5 %collective-permute-start = (bf16[64,1664]{1,0:T(8,128)(2,1)}, bf16[64,1664]{1,0:T(8,128)(2,1)}, u32[]{:S(2)}, u32[]{:S(2)}) collective-permute-start(bf16[64,1664]{1,0:T(8,128)(2,1)} %fusion.109), channel_id=1, source_target_pairs={{0,8},{8,16},{16,24},{24,28},{28,20},{20,12},{12,4},{4,0},{1,9},{9... | collective-permute-start | bytes 638984 | tf_op jit(solution)/shard_map/ppermute | solution.py:90
  58.8 79.8 %collective-permute-start.1 = (bf16[64,1664]{1,0:T(8,128)(2,1)}, bf16[64,1664]{1,0:T(8,128)(2,1)}, u32[]{:S(2)}, u32[]{:S(2)}) collective-permute-start(bf16[64,1664]{1,0:T(8,128)(2,1)} %fusion.109), channel_id=1, source_target_pairs={{8,0},{16,8},{24,16},{28,24},{20,28},{12,20},{4,12},{0,4},{9,1},{1... | collective-permute-start | bytes 638984 | tf_op jit(solution)/shard_map/ppermute | solution.py:91
  64.1 98.1 %collective-permute-start.61 = (bf16[128,2048]{1,0:T(8,128)(2,1)}, bf16[128,2048]{1,0:T(8,128)(2,1)}, u32[]{:S(2)}, u32[]{:S(2)}) collective-permute-start(bf16[128,2048]{1,0:T(8,128)(2,1)} %get-tuple-element.198), channel_id=1, source_target_pairs={{8,0},{16,8},{24,16},{28,24},{20,28},{12,20},{4,12},{0,4},{9,1},{1... | collective-permute-start | bytes 1572872 | tf_op jit(solution)/shard_map/ppermute | solution.py:91
  65.2 91.5 %collective-permute-start.60 = (bf16[128,2048]{1,0:T(8,128)(2,1)}, bf16[128,2048]{1,0:T(8,128)(2,1)}, u32[]{:S(2)}, u32[]{:S(2)}) collective-permute-start(bf16[128,2048]{1,0:T(8,128)(2,1)} %get-tuple-element.198), channel_id=1, source_target_pairs={{0,8},{8,16},{16,24},{24,28},{28,20},{20,12},{12,4},{4,0},{1,9},{9... | collective-permute-start | bytes 1572872 | tf_op jit(solution)/shard_map/ppermute | solution.py:90
  68.3 91.7 %collective-permute-start.22 = (bf16[128,2048]{1,0:T(8,128)(2,1)}, bf16[128,2048]{1,0:T(8,128)(2,1)}, u32[]{:S(2)}, u32[]{:S(2)}) collective-permute-start(bf16[128,2048]{1,0:T(8,128)(2,1)} %param.18), channel_id=1, source_target_pairs={{0,0},{1,4},{2,8},{3,12},{4,16},{5,20},{6,24},{7,28},{8,1},{9,5},{... | collective-permute-start | bytes 1572872 | tf_op jit(solution)/shard_map/ppermute | solution.py:248
  180.9 36.7 %collective-permute-start.8 = (bf16[8,64,1664]{2,1,0:T(8,128)(2,1)S(1)}, bf16[8,64,1664]{2,1,0:T(8,128)(2,1)S(1)}, u32[]{:S(2)}, u32[]{:S(2)}) collective-permute-start(bf16[8,64,1664]{2,1,0:T(8,128)(2,1)S(1)} %fusion.110), channel_id=1, source_target_pairs={{0,2},{1,3},{2,0},{3,1},{4,6},{5,7},{6,4},{7,5},{8,10},{9,11},{10,... | collective-permute-start | bytes 5111816 | tf_op jit(solution)/shard_map/ppermute | solution.py:164
  218.3 54.5 %collective-permute-start.9 = (bf16[2,8,64,1664]{3,2,1,0:T(8,128)(2,1)S(1)}, bf16[2,8,64,1664]{3,2,1,0:T(8,128)(2,1)S(1)}, u32[]{:S(2)}, u32[]{:S(2)}) collective-permute-start(bf16[2,8,64,1664]{3,2,1,0:T(8,128)(2,1)S(1)} %maximum_select_fusion.2), channel_id=1, source_target_pairs={{0,1},{1,0},{2,3},{3,2},{4,5},{5,4},{6,7},{7,6},{8,9},{9,8},{10,11... | collective-permute-start | bytes 10223624 | tf_op jit(solution)/shard_map/ppermute | solution.py:165
  220.1 36.8 %collective-permute-start.40 = (bf16[8,2,64,704]{3,0,1,2:T(8,128)(2,1)S(1)}, bf16[8,2,64,704]{3,0,1,2:T(8,128)(2,1)S(1)}, u32[]{:S(2)}, u32[]{:S(2)}) collective-permute-start(bf16[8,2,64,704]{3,0,1,2:T(8,128)(2,1)S(1)} %dynamic_update_slice.148), channel_id=1, source_target_pairs={{0,2},{1,3},{2,0},{3,1},{4,6},{5,7},{6,4},{7,5},{8,10},{9,11},{10,... | collective-permute-start | bytes 4325384 | tf_op jit(solution)/shard_map/ppermute | solution.py:164
  223.9 38.5 %collective-permute-start.67 = (bf16[64,2048]{1,0:T(8,128)(2,1)S(1)}, bf16[64,2048]{1,0:T(8,128)(2,1)S(1)}, u32[]{:S(2)}, u32[]{:S(2)}) collective-permute-start(bf16[64,2048]{1,0:T(8,128)(2,1)S(1)} %slice.446), channel_id=1, source_target_pairs={{8,0},{16,8},{24,16},{28,24},{20,28},{12,20},{4,12},{0,4},{9,1},{1... | collective-permute-start | bytes 786440 | tf_op jit(solution)/shard_map/ppermute | solution.py:98
  262.5 67.6 %collective-permute-start.41 = (bf16[2,8,2,64,704]{4,1,2,3,0:T(8,128)(2,1)}, bf16[2,8,2,64,704]{4,1,2,3,0:T(8,128)(2,1)}, u32[]{:S(2)}, u32[]{:S(2)}) collective-permute-start(bf16[2,8,2,64,704]{4,1,2,3,0:T(8,128)(2,1)} %maximum_select_fusion.4), channel_id=1, source_target_pairs={{0,1},{1,0},{2,3},{3,2},{4,5},{5,4},{6,7},{7,6},{8,9},{9,8},{10,11... | collective-permute-start | bytes 8650760 | tf_op jit(solution)/shard_map/ppermute | solution.py:165
  355.3 214.4 %collective-permute-start.81 = (bf16[2,128,2048]{2,1,0:T(8,128)(2,1)}, bf16[2,128,2048]{2,1,0:T(8,128)(2,1)}, u32[]{:S(2)}, u32[]{:S(2)}) collective-permute-start(bf16[2,128,2048]{2,1,0:T(8,128)(2,1)} %maximum_select_fusion.13), channel_id=1, source_target_pairs={{0,1},{1,0},{2,3},{3,2},{4,5},{5,4},{6,7},{7,6},{8,9},{9,8},{10,11... | collective-permute-start | bytes 3145736 | tf_op jit(solution)/shard_map/ppermute | solution.py:165
  440.2 39.3 %collective-permute-start.52 = (bf16[64,2048]{1,0:T(8,128)(2,1)S(1)}, bf16[64,2048]{1,0:T(8,128)(2,1)S(1)}, u32[]{:S(2)}, u32[]{:S(2)}) collective-permute-start(bf16[64,2048]{1,0:T(8,128)(2,1)S(1)} %get-tuple-element.146), channel_id=1, source_target_pairs={{8,0},{16,8},{24,16},{28,24},{20,28},{12,20},{4,12},{0,4},{9,1},{1... | collective-permute-start | bytes 786440 | tf_op jit(solution)/shard_map/ppermute | solution.py:114
  441.2 38.4 %collective-permute-start.56 = (bf16[64,2048]{1,0:T(8,128)(2,1)S(1)}, bf16[64,2048]{1,0:T(8,128)(2,1)}, u32[]{:S(2)}, u32[]{:S(2)}) collective-permute-start(bf16[64,2048]{1,0:T(8,128)(2,1)S(1)} %get-tuple-element.147), channel_id=1, source_target_pairs={{0,8},{8,16},{16,24},{24,28},{28,20},{20,12},{12,4},{4,0},{1,9},{9... | collective-permute-start | bytes 786440 | tf_op jit(solution)/shard_map/ppermute | solution.py:115
  445.4 36.7 %collective-permute-start.68 = (bf16[64,2048]{1,0:T(8,128)(2,1)}, bf16[64,2048]{1,0:T(8,128)(2,1)}, u32[]{:S(2)}, u32[]{:S(2)}) collective-permute-start(bf16[64,2048]{1,0:T(8,128)(2,1)} %get-tuple-element.144), channel_id=1, source_target_pairs={{8,0},{16,8},{24,16},{28,24},{20,28},{12,20},{4,12},{0,4},{9,1},{1... | collective-permute-start | bytes 786440 | tf_op jit(solution)/shard_map/ppermute | solution.py:114
  446.4 36.7 %collective-permute-start.72 = (bf16[64,2048]{1,0:T(8,128)(2,1)}, bf16[64,2048]{1,0:T(8,128)(2,1)}, u32[]{:S(2)}, u32[]{:S(2)}) collective-permute-start(bf16[64,2048]{1,0:T(8,128)(2,1)} %get-tuple-element.145), channel_id=1, source_target_pairs={{0,8},{8,16},{16,24},{24,28},{28,20},{20,12},{12,4},{4,0},{1,9},{9... | collective-permute-start | bytes 786440 | tf_op jit(solution)/shard_map/ppermute | solution.py:115
  479.5 54.9 %collective-permute-start.122 = (bf16[2,176,2048]{2,1,0:T(8,128)(2,1)S(1)}, bf16[2,176,2048]{2,1,0:T(8,128)(2,1)S(1)}, u32[]{:S(2)}, u32[]{:S(2)}) collective-permute-start(bf16[2,176,2048]{2,1,0:T(8,128)(2,1)S(1)} %fusion.15), channel_id=1, source_target_pairs={{0,1},{1,0},{2,3},{3,2},{4,5},{5,4},{6,7},{7,6},{8,9},{9,8},{10,11... | collective-permute-start | bytes 4325384 | tf_op jit(solution)/shard_map/ppermute | solution.py:173
  479.6 102.9 %collective-permute-start.113 = (bf16[2,8,2,64,704]{4,3,2,1,0:T(8,128)(2,1)}, bf16[2,8,2,64,704]{4,3,2,1,0:T(8,128)(2,1)}, u32[]{:S(2)}, u32[]{:S(2)}) collective-permute-start(bf16[2,8,2,64,704]{4,3,2,1,0:T(8,128)(2,1)} %fusion.7), channel_id=1, source_target_pairs={{0,1},{1,0},{2,3},{3,2},{4,5},{5,4},{6,7},{7,6},{8,9},{9,8},{10,11... | collective-permute-start | bytes 8650760 | tf_op jit(solution)/shard_map/ppermute | solution.py:173
  588.6 79.4 %collective-permute-start.114 = (bf16[8,2,64,704]{3,2,1,0:T(8,128)(2,1)}, bf16[8,2,64,704]{3,2,1,0:T(8,128)(2,1)}, u32[]{:S(2)}, u32[]{:S(2)}) collective-permute-start(bf16[8,2,64,704]{3,2,1,0:T(8,128)(2,1)} %fusion.13), channel_id=1, source_target_pairs={{0,2},{1,3},{2,0},{3,1},{4,6},{5,7},{6,4},{7,5},{8,10},{9,11},{10,... | collective-permute-start | bytes 4325384 | tf_op jit(solution)/shard_map/ppermute | solution.py:175
  646.4 98.6 %collective-permute-start.109 = (bf16[128,2048]{1,0:T(8,128)(2,1)}, bf16[128,2048]{1,0:T(8,128)(2,1)S(1)}, u32[]{:S(2)}, u32[]{:S(2)}) collective-permute-start(bf16[128,2048]{1,0:T(8,128)(2,1)} %pad_maximum_fusion.11), channel_id=1, source_target_pairs={{0,8},{8,16},{16,24},{24,28},{28,20},{20,12},{12,4},{4,0},{1,9},{9... | collective-permute-start | bytes 1572872 | tf_op jit(solution)/shard_map/ppermute | solution.py:130
  655.3 38.7 %collective-permute-start.97 = (bf16[128,1024]{1,0:T(8,128)(2,1)}, bf16[128,1024]{1,0:T(8,128)(2,1)}, u32[]{:S(2)}, u32[]{:S(2)}) collective-permute-start(bf16[128,1024]{1,0:T(8,128)(2,1)} %get-tuple-element.63), channel_id=1, source_target_pairs={{8,0},{16,8},{24,16},{28,24},{20,28},{12,20},{4,12},{0,4},{9,1},{1... | collective-permute-start | bytes 786440 | tf_op jit(solution)/shard_map/ppermute | solution.py:129
  668.1 78.9 %collective-permute-start.106 = (bf16[128,2048]{1,0:T(8,128)(2,1)}, bf16[128,2048]{1,0:T(8,128)(2,1)}, u32[]{:S(2)}, u32[]{:S(2)}) collective-permute-start(bf16[128,2048]{1,0:T(8,128)(2,1)} %fusion.44), channel_id=1, source_target_pairs={{8,0},{16,8},{24,16},{28,24},{20,28},{12,20},{4,12},{0,4},{9,1},{1... | collective-permute-start | bytes 1572872 | tf_op jit(solution)/shard_map/ppermute | solution.py:129
  685.3 66.7 %collective-permute-start.121 = (bf16[2,64,704]{2,1,0:T(8,128)(2,1)}, bf16[2,64,704]{2,1,0:T(8,128)(2,1)}, u32[]{:S(2)}, u32[]{:S(2)}) collective-permute-start(bf16[2,64,704]{2,1,0:T(8,128)(2,1)} %get-tuple-element.91), channel_id=1, source_target_pairs={{0,28},{4,24},{8,20},{12,16},{16,12},{20,8},{24,4},{28,0},{1,29},{... | collective-permute-start | bytes 540680 | tf_op jit(solution)/shard_map/ppermute | solution.py:145
  694.0 47.6 %collective-permute-start.120 = (bf16[2,64,704]{2,1,0:T(8,128)(2,1)}, bf16[2,64,704]{2,1,0:T(8,128)(2,1)}, u32[]{:S(2)}, u32[]{:S(2)}) collective-permute-start(bf16[2,64,704]{2,1,0:T(8,128)(2,1)} %get-tuple-element.92), channel_id=1, source_target_pairs={{0,24},{4,28},{8,16},{12,20},{16,8},{20,12},{24,0},{28,4},{1,25},{... | collective-permute-start | bytes 540680 | tf_op jit(solution)/shard_map/ppermute | solution.py:145
  738.1 55.7 %collective-permute-start.102 = (bf16[2,32,1024]{2,1,0:T(8,128)(2,1)}, bf16[2,32,1024]{2,1,0:T(8,128)(2,1)}, u32[]{:S(2)}, u32[]{:S(2)}) collective-permute-start(bf16[2,32,1024]{2,1,0:T(8,128)(2,1)} %get-tuple-element.162), channel_id=1, source_target_pairs={{0,2},{1,3},{2,0},{3,1},{4,6},{5,7},{6,4},{7,5},{8,10},{9,11},{10,... | collective-permute-start | bytes 393224 | tf_op jit(solution)/shard_map/ppermute | solution.py:182
  (209 other events, 2732.4 us)

commit v2 on v1

--- a/solution.py
+++ b/solution.py
@@ -1,8 +1,11 @@
+import functools
 import math
 
 import jax
 import jax.numpy as jnp
 from jax import lax
+from jax.experimental import pallas as pl
+from jax.experimental.pallas import tpu as pltpu
 from jax.sharding import PartitionSpec as P
 
 H = 16
@@ -138,7 +141,7 @@
 def batch_exchange(stacked):
     n = lax.axis_size("batch")
     rank = lax.axis_index("batch")
-    swapped = stacked
+    swapped = place(jnp.zeros_like(stacked), pick(stacked, rank), rank)
     for offset in range(1, n):
         pairs = [(i, i ^ offset) for i in range(n)]
         other = rank ^ offset
@@ -188,6 +191,301 @@
 
 def slab_pairs(n_batch, n_ctx):
     return [(i, (i % n_batch) * n_ctx + i // n_batch) for i in range(n_batch * n_ctx)]
+
+
+MESH = pl.DeviceIdType.MESH
+
+
+class Place:
+    def __init__(self, n_batch):
+        self.n = n_batch
+        self.h = n_batch // 2
+        self.b = lax.axis_index("batch")
+        self.c = lax.axis_index("ctx")
+        self.outer = lax.div(self.c, 2)
+        self.inner = lax.rem(self.c, 2)
+        self.far = lax.rem(self.c + 2, 4)
+        self.near = self.c + 1 - 2 * self.inner
+        odd = lax.rem(self.b, 2)
+        half = lax.div(self.b, 2)
+        self.at = half + odd * (self.n - 1 - 2 * half)
+
+    def rank_of(self, step):
+        spot = lax.rem(self.at + step + 2 * self.n, self.n)
+        back = lax.div(spot, self.h)
+        return (1 - back) * 2 * spot + back * (2 * (self.n - 1 - spot) + 1)
+
+    def up(self):
+        return (self.rank_of(1), self.c)
+
+    def down(self):
+        return (self.rank_of(-1), self.c)
+
+
+class Copies:
+    def __init__(self, send_sems, recv_sems):
+        self.send_sems = send_sems
+        self.recv_sems = recv_sems
+        self.count = 0
+        self.open_sends = []
+        self.open_recvs = []
+
+    def remote(self, source, target, device):
+        index = self.count
+        self.count += 1
+        copy = pltpu.make_async_remote_copy(
+            src_ref=source,
+            dst_ref=target,
+            send_sem=self.send_sems.at[index],
+            recv_sem=self.recv_sems.at[index],
+            device_id=device,
+            device_id_type=MESH,
+        )
+        copy.start()
+        self.open_sends.append(copy)
+        self.open_recvs.append(copy)
+        return copy
+
+    def local(self, source, target):
+        index = self.count
+        self.count += 1
+        copy = pltpu.make_async_copy(source, target, self.recv_sems.at[index])
+        copy.start()
+        self.open_recvs.append(copy)
+        return copy
+
+    def arrive(self, copy):
+        if any(copy is other for other in self.open_recvs):
+            self.open_recvs = [other for other in self.open_recvs if other is not copy]
+            if any(copy is other for other in self.open_sends):
+                copy.wait_recv()
+            else:
+                copy.wait()
+
+    def drain(self):
+        for copy in list(self.open_recvs):
+            self.arrive(copy)
+        for copy in self.open_sends:
+            copy.wait_send()
+
+
+def greet(place, others):
+    barrier = pltpu.get_barrier_semaphore()
+    for device in others:
+        pl.semaphore_signal(barrier, inc=1, device_id=device, device_id_type=MESH)
+    return barrier
+
+
+class RingGather:
+    def __init__(self, place, copies, rows, slot):
+        self.place, self.copies, self.rows, self.slot = place, copies, rows, slot
+        self.step = 0
+        self.moving = ()
+
+    def advance(self):
+        place, copies = self.place, self.copies
+        for copy in self.moving:
+            copies.arrive(copy)
+        self.moving = ()
+        self.step += 1
+        cut = self.rows // 2
+        if self.step > place.h:
+            return
+        lower = place.rank_of(1 - self.step)
+        upper = place.rank_of(self.step - 1)
+        if self.step < place.h:
+            whole = pl.ds(0, self.rows)
+            pieces = (whole, whole)
+        else:
+            pieces = (pl.ds(0, cut), pl.ds(cut, self.rows - cut))
+        upward, downward = self.slot(lower, pieces[0]), self.slot(upper, pieces[1])
+        self.moving = (
+            copies.remote(upward, upward, place.up()),
+            copies.remote(downward, downward, place.down()),
+        )
+
+    def arrived(self):
+        step = self.step - 1
+        if step == 0:
+            return []
+        if step == self.place.h:
+            return [self.place.rank_of(step)]
+        return [self.place.rank_of(-step), self.place.rank_of(step)]
+
+
+def weights_kernel(
+    n_batch,
+    packed_ref,
+    up_ref,
+    out_ref,
+    gu_ref,
+    down_ref,
+    packed_all,
+    up_all,
+    out_all,
+    gu_all,
+    down_all,
+    send_sems,
+    recv_sems,
+    out_sems,
+):
+    place = Place(n_batch)
+    copies = Copies(send_sems, recv_sems)
+    b, c, n = place.b, place.c, n_batch
+    own_rows = packed_ref.shape[0]
+    out_rows = out_ref.shape[0]
+    index = b * 4 + c
+    target = (lax.rem(index, n), lax.div(index, n))
+    slab = c * n + b
+    source = (lax.div(slab, 4), lax.rem(slab, 4))
+    stays = slab == index
+    peers = [(lax.rem(b + k, n), c) for k in range(1, n)]
+    ctx_peers = [(b, place.far), (b, place.near), (b, lax.rem(place.near + 2, 4))]
+
+    barrier = greet(place, peers + ctx_peers)
+
+    @pl.when(jnp.logical_not(stays))
+    def _():
+        for device in (target, source):
+            pl.semaphore_signal(barrier, inc=1, device_id=device, device_id_type=MESH)
+
+    pl.semaphore_wait(barrier, n + 4 - 2 * stays.astype(jnp.int32))
+
+    own = [
+        copies.local(packed_ref, packed_all.at[b, c]),
+        copies.local(up_ref.at[c], up_all.at[b, c]),
+        copies.local(gu_ref.at[b], gu_all.at[:, b, c]),
+        copies.local(down_ref, down_all.at[c]),
+    ]
+    out_copy = pltpu.make_async_remote_copy(
+        src_ref=out_ref,
+        dst_ref=out_all.at[target[0]],
+        send_sem=out_sems.at[0],
+        recv_sem=out_sems.at[1],
+        device_id=target,
+        device_id_type=MESH,
+    )
+    out_stay = pltpu.make_async_copy(out_ref, out_all.at[b], out_sems.at[0])
+
+    @pl.when(jnp.logical_not(stays))
+    def _():
+        out_copy.start()
+
+    @pl.when(stays)
+    def _():
+        out_stay.start()
+
+    up_copies = [
+        copies.remote(up_ref.at[peer[1]], up_all.at[b, c], peer) for peer in ctx_peers
+    ]
+    far_device, near_device = ctx_peers[0], ctx_peers[1]
+    down_far = copies.remote(down_ref, down_all.at[c], far_device)
+
+    copies.arrive(own[0])
+    packed_ring = RingGather(
+        place, copies, own_rows, lambda rank, rows: packed_all.at[rank, c, rows]
+    )
+    up_ring = RingGather(
+        place, copies, up_ref.shape[1], lambda rank, rows: up_all.at[rank, :, rows]
+    )
+    out_ring = RingGather(place, copies, out_rows, lambda rank, rows: out_all.at[rank, rows])
+
+    packed_far = []
+
+    def packed_step():
+        packed_ring.advance()
+        ranks = packed_ring.arrived() if packed_ring.step > 1 else [b]
+        for rank in ranks:
+            block = packed_all.at[rank, c]
+            packed_far.append((rank, copies.remote(block, block, far_device)))
+
+    packed_step()
+    gu_copies = [
+        (
+            lax.rem(b - k + n, n),
+            copies.remote(gu_ref.at[peer[0]], gu_all.at[:, b, c], peer),
+        )
+        for k, peer in zip(range(1, n), peers)
+    ]
+    for copy in own[1:2] + up_copies:
+        copies.arrive(copy)
+    up_ring.advance()
+    packed_step()
+
+    @pl.when(jnp.logical_not(stays))
+    def _():
+        out_copy.wait()
+
+    @pl.when(stays)
+    def _():
+        out_stay.wait()
+
+    out_ring.advance()
+    gu_far = []
+    copies.arrive(own[2])
+    own_gu = gu_all.at[:, b, c]
+    gu_far.append(copies.remote(own_gu, own_gu, far_device))
+    waiting = list(gu_copies)
+    copies.arrive(own[3])
+    down_near = [copies.remote(down_all.at[c], down_all.at[c], near_device)]
+
+    def forward_gu(count):
+        for _ in range(min(count, len(waiting))):
+            rank, copy = waiting.pop(0)
+            copies.arrive(copy)
+            block = gu_all.at[:, rank, c]
+            gu_far.append(copies.remote(block, block, far_device))
+
+    for _ in range(place.h):
+        up_ring.advance()
+        if packed_ring.step <= place.h:
+            packed_step()
+        forward_gu(2)
+        out_ring.advance()
+    copies.arrive(down_far)
+    far = place.far
+    down_near.append(copies.remote(down_all.at[far], down_all.at[far], near_device))
+    forward_gu(n)
+    own_packed = packed_all.at[:, c]
+    copies.remote(own_packed, own_packed, near_device)
+    own_gu = gu_all.at[:, :, c]
+    copies.remote(own_gu, own_gu, near_device)
+    for _, copy in packed_far:
+        copies.arrive(copy)
+    far_packed = packed_all.at[:, far]
+    copies.remote(far_packed, far_packed, near_device)
+    for copy in gu_far:
+        copies.arrive(copy)
+    far_gu = gu_all.at[:, :, far]
+    copies.remote(far_gu, far_gu, near_device)
+    copies.drain()
+
+
+def spread_weights(n_batch, packed, up_parts, out_rows, gu_parts, down_rows):
+    own_rows, packed_cols = packed.shape
+    _, gain_rows, up_cols = up_parts.shape
+    ff = gu_parts.shape[-1]
+    shapes = (
+        jax.ShapeDtypeStruct((n_batch, 4, own_rows, packed_cols), BF),
+        jax.ShapeDtypeStruct((n_batch, 4, gain_rows, up_cols), BF),
+        jax.ShapeDtypeStruct((n_batch,) + out_rows.shape, BF),
+        jax.ShapeDtypeStruct((2, n_batch, 4, own_rows, ff), BF),
+        jax.ShapeDtypeStruct((4,) + down_rows.shape, BF),
+    )
+    sems = 6 * n_batch + 3 * n_batch + 32
+    return pl.pallas_call(
+        functools.partial(weights_kernel, n_batch),
+        out_shape=shapes,
+        in_specs=[pl.BlockSpec(memory_space=pl.ANY)] * 5,
+        out_specs=[pl.BlockSpec(memory_space=pl.ANY)] * 5,
+        scratch_shapes=[
+            pltpu.SemaphoreType.DMA((sems,)),
+            pltpu.SemaphoreType.DMA((sems,)),
+            pltpu.SemaphoreType.DMA((2,)),
+        ],
+        compiler_params=pltpu.CompilerParams(collective_id=0, has_side_effects=True),
+        name="spread_weights",
+    )(packed, up_parts, out_rows, gu_parts, down_rows)
 
 
 def shards(
@@ -233,38 +531,36 @@
         [attn_gain, mlp_gain, jnp.pad(query_gain, (0, own_rows - gain_rows))], axis=1
     )
     packed = jnp.concatenate([proj_in, jnp.pad(gains, ((0, 0), (0, 125)))], axis=1)
-    packed = ctx_gather(ring.gather(packed))
-    packed = jnp.swapaxes(packed, 0, 1).reshape(width, in_cols + 128)
+    up_parts = query_up.reshape(gain_rows, n_ctx, heads * HD).swapaxes(0, 1)
+    ff_all = gate_up.shape[1] // 2
+    ff = ff_all // n_batch
+    gu_parts = gate_up.reshape(own_rows, 2, n_batch, ff).transpose(2, 1, 0, 3)
+    packed, own_qup, own_out, gu_rows, own_down = spread_weights(
+        n_batch, packed, up_parts, proj_out, gu_parts, down_proj
+    )
+    packed = packed.reshape(width, in_cols + 128)
+    own_qup = own_qup.reshape(QR, heads * HD)
+    own_out = own_out.reshape(heads * HD, width)
+    own_gate, own_up = gu_rows.reshape(2, width, ff)
+    own_down = own_down.reshape(ff, width)
+    slabs = slab_pairs(n_batch, n_ctx)
     full_in = packed[:, :in_cols]
     gains = packed[:, in_cols : in_cols + 3].T.astype(F32)
     gain_norm = gains[0]
     gain_mlp = gains[1]
     gain_query = gains[2].reshape(n_batch * n_ctx, own_rows)[:, :gain_rows].reshape(QR)
 
-    up_parts = query_up.reshape(gain_rows, n_ctx, heads * HD).swapaxes(0, 1)
-    up_block = ctx_exchange(up_parts).reshape(n_ctx * gain_rows, heads * HD)
-    own_qup = ring.gather(up_block).reshape(QR, heads * HD)
-    slabs = slab_pairs(n_batch, n_ctx)
-    out_block = lax.ppermute(proj_out, ("batch", "ctx"), slabs)
-    own_out = ring.gather(out_block).reshape(heads * HD, width)
-
-    ff_all = gate_up.shape[1] // 2
-    ff = ff_all // n_batch
-    gu_parts = gate_up.reshape(own_rows, 2, n_batch, ff).transpose(2, 1, 0, 3)
-    gu_rows = ctx_gather(batch_exchange(gu_parts))
-    gu_rows = gu_rows.transpose(2, 1, 0, 3, 4).reshape(2, width, ff)
-    own_gate, own_up = gu_rows[0], gu_rows[1]
-    own_down = ctx_gather(down_proj).reshape(ff, width)
-
     residual = tokens.reshape(n_tok, width).astype(F32)
     valid_rows = (query_pos[None, :] < own_lengths[:, None]).astype(F32).reshape(n_tok, 1)
     grad_out = cotangent.reshape(n_tok, width).astype(F32) * valid_rows
-    grad_mo = ring.spread(grad_out.astype(BF))
+    with jax.named_scope('cotangent_spread'):
+        grad_mo = ring.spread(grad_out.astype(BF))
 
     scale_one = rms_scale(residual)
     normed_one = residual * scale_one
     attn_in = (normed_one * gain_norm).astype(BF)
-    attn_in_all = ctx_gather(attn_in).reshape(n_ctx * n_tok, width)
+    with jax.named_scope('attn_in_gather'):
+        attn_in_all = ctx_gather(attn_in).reshape(n_ctx * n_tok, width)
     projected = dot(attn_in, full_in)
     q_latent = projected[:, :QR]
     scale_query = rms_scale(q_latent)
@@ -274,7 +570,8 @@
         projected[:, QR : QR + HD].reshape(micro, pos_dev, HD), cos_own, sin_own
     ).astype(BF)
     v_low = projected[:, QR + HD :].astype(BF)
-    qkv_all = ctx_gather(jnp.concatenate([q_normed, k_rot.reshape(n_tok, HD), v_low], axis=1))
+    with jax.named_scope('qkv_gather'):
+        qkv_all = ctx_gather(jnp.concatenate([q_normed, k_rot.reshape(n_tok, HD), v_low], axis=1))
     q_normed_all = qkv_all[..., :QR].reshape(n_ctx * n_tok, QR)
 
     def by_sequence(values):
@@ -314,12 +611,14 @@
     mixed = join_heads(
         jnp.einsum("shtu,sud->shtd", weights_low, values_all, preferred_element_type=F32).astype(BF)
     )
-    attended = ctx_collect(dot(mixed, own_out).reshape(n_ctx, n_tok, width))
+    with jax.named_scope('attended_collect'):
+        attended = ctx_collect(dot(mixed, own_out).reshape(n_ctx, n_tok, width))
     hidden_res = residual + attended
 
     scale_two = rms_scale(hidden_res)
     normed_two = hidden_res * scale_two
-    mlp_in = ring.spread((normed_two * gain_mlp).astype(BF))
+    with jax.named_scope('mlp_in_spread'):
+        mlp_in = ring.spread((normed_two * gain_mlp).astype(BF))
     far = ring.h
     groups = [[0]] + [[-step, step] for step in range(1, far)] + [[far]]
     out_terms = {}
@@ -348,24 +647,32 @@
     rows, grad_rows, activated, grad_gate, grad_up = (
         jnp.concatenate(items, axis=0) for items in zip(*kept)
     )
-    grad_mlp_in = ring.collect(lambda step: in_terms[step])
+    with jax.named_scope('grad_mlp_in_collect'):
+        grad_mlp_in = ring.collect(lambda step: in_terms[step])
     gain_mlp_term = jnp.sum(grad_mlp_in * normed_two, axis=0)
     grad_hidden = grad_out + norm_back(grad_mlp_in * gain_mlp, normed_two, scale_two)
-    layer_out = hidden_res + ring.collect(lambda step: out_terms[step])
+    with jax.named_scope('layer_out_collect'):
+        layer_out = hidden_res + ring.collect(lambda step: out_terms[step])
 
     grad_gu_own = jnp.stack([dot_left_t(rows, grad_gate), dot_left_t(rows, grad_up)])
     grad_gu_own = grad_gu_own.reshape(2, n_batch, n_ctx, own_rows, ff).transpose(2, 1, 0, 3, 4)
-    grad_gu_own = batch_exchange(ctx_collect(grad_gu_own).astype(BF))
+    with jax.named_scope('grad_gate_up_collect'):
+        grad_gu_own = ctx_collect(grad_gu_own).astype(BF)
+    with jax.named_scope('grad_gate_up_exchange'):
+        grad_gu_own = batch_exchange(grad_gu_own)
     grad_gate_up = grad_gu_own.transpose(2, 1, 0, 3).reshape(own_rows, 2 * ff_all).astype(F32)
     grad_down_own = dot_left_t(activated, grad_rows)
-    grad_down = ctx_collect(grad_down_own.reshape(n_ctx, ff // n_ctx, width))
-
-    grad_att_all = ctx_gather(grad_hidden.astype(BF)).reshape(n_ctx * n_tok, width)
+    with jax.named_scope('grad_down_collect'):
+        grad_down = ctx_collect(grad_down_own.reshape(n_ctx, ff // n_ctx, width))
+
+    with jax.named_scope('grad_att_gather'):
+        grad_att_all = ctx_gather(grad_hidden.astype(BF)).reshape(n_ctx * n_tok, width)
     grad_out_own = dot_left_t(mixed, grad_att_all)
-    grad_out_own = ring.collect_rows(grad_out_own.reshape(n_batch, -1, width)).astype(BF)
-    grad_proj_out = lax.ppermute(
-        grad_out_own, ("batch", "ctx"), [(there, here) for here, there in slabs]
-    ).astype(F32)
+    with jax.named_scope('grad_proj_out_collect'):
+        grad_out_own = ring.collect_rows(grad_out_own.reshape(n_batch, -1, width)).astype(BF)
+        grad_proj_out = lax.ppermute(
+            grad_out_own, ("batch", "ctx"), [(there, here) for here, there in slabs]
+        ).astype(F32)
     grad_mixed = split_heads(dot_right_t(grad_att_all, own_out).astype(BF))
     grad_probs = jnp.einsum(
         "shtd,sud->shtu", grad_mixed, values_all, preferred_element_type=F32
@@ -387,7 +694,8 @@
     grad_qn_part = dot_right_t(grad_q, own_qup)
     grad_kv_part = by_position(jnp.concatenate([grad_keys, grad_values], axis=-1))
     back_parts = jnp.concatenate([grad_qn_part, grad_kv_part], axis=1).astype(BF)
-    back_own = ctx_collect(back_parts.reshape(n_ctx, n_tok, in_cols))
+    with jax.named_scope('back_collect'):
+        back_own = ctx_collect(back_parts.reshape(n_ctx, n_tok, in_cols))
     grad_qn = back_own[:, :QR]
     gain_query_term = jnp.sum(grad_qn * normed_query, axis=0)
     grad_latent = norm_back(grad_qn * gain_query, normed_query, scale_query)
@@ -402,7 +710,8 @@
     grad_tokens = grad_hidden + norm_back(grad_attn_in * gain_norm, normed_one, scale_one)
 
     grad_up_own = dot_left_t(q_normed_all, grad_q)
-    grad_up_own = ring.collect_rows(grad_up_own.reshape(n_batch, -1, heads * HD)).astype(BF)
+    with jax.named_scope('grad_query_up_collect'):
+        grad_up_own = ring.collect_rows(grad_up_own.reshape(n_batch, -1, heads * HD)).astype(BF)
     grad_query_up = (
         ctx_exchange(grad_up_own.reshape(n_ctx, gain_rows, heads * HD))
         .swapaxes(0, 1)
@@ -411,7 +720,8 @@
     )
     part_cols = in_cols // n_ctx
     project_parts = grad_project.reshape(n_tok, n_ctx, part_cols).swapaxes(0, 1)
-    project_all = ctx_exchange(project_parts).reshape(n_ctx * n_tok, part_cols)
+    with jax.named_scope('grad_project_exchange'):
+        project_all = ctx_exchange(project_parts).reshape(n_ctx * n_tok, part_cols)
     grad_in_own = dot_left_t(attn_in_all, project_all).reshape(
         n_batch, n_ctx, own_rows, part_cols
     )
@@ -428,7 +738,8 @@
     )
     gain_terms = jnp.pad(gain_terms, ((0, 0), (0, 0), (0, 13), (0, part_cols - own_rows)))
     joined = jnp.concatenate([grad_in_own, gain_terms], axis=2).reshape(n_batch, -1, part_cols)
-    joined = ring.collect_rows(joined).astype(BF)
+    with jax.named_scope('grad_proj_in_collect'):
+        joined = ring.collect_rows(joined).astype(BF)
     joined = ctx_exchange(joined.reshape(n_ctx, own_rows + 16, part_cols)).astype(F32)
     grad_proj_in = joined[:, :own_rows].swapaxes(0, 1).reshape(own_rows, in_cols)
     gain_sums = jnp.sum(joined[:, own_rows : own_rows + 3, :own_rows], axis=0)

time: 835 us -> 768 us (0.920)
  Pallas kernels: 0 us -> 151 us
  waiting for transfers between devices: 304 us -> 167 us
  starting transfers between devices: 135 us -> 90.3 us
  local copies, waits for them, and re-layouts: 185 us -> 162 us
  other arithmetic: 92 us -> 75.7 us
    pallas_call x0 -> x1, Pallas kernels: none -> 151 us  [spread_weights(): pl.pallas_call(functools.partial(weights_kernel, n_batch), out_shape=shap...]
    ppermute x6 -> x3, waiting for transfers between devices: 50.8 us -> 0.4 us  [ctx_gather(): pair = in_order(block, lax.ppermute(block, 'ctx', FAR), outer)]
    ppermute x14 -> x7, waiting for transfers between devices: 44.5 us -> 5.86 us  [batch_exchange(): lax.ppermute(pick(stacked, other), 'batch', pairs)]
    ppermute x15 -> x6, waiting for transfers between devices: 36.1 us -> 11 us  [spread(): upward = lax.ppermute(upward, 'batch', self.up)]
    dynamic_slice x15 -> x7, local copies, waits for them, and re-layouts: 13.9 us -> 1.53 us  [pick(): return lax.dynamic_index_in_dim(array, index, axis, keepdims=False)]
    ppermute x15 -> x6, waiting for transfers between devices: 27.8 us -> 15.6 us  [spread(): downward = lax.ppermute(downward, 'batch', self.down)]
    ppermute x14 -> x7, starting transfers between devices: 22.9 us -> 11.4 us  [batch_exchange(): lax.ppermute(pick(stacked, other), 'batch', pairs)]
    ppermute x15 -> x6, starting transfers between devices: 14.8 us -> 5.24 us  [spread(): downward = lax.ppermute(downward, 'batch', self.down)]
  transfers between devices with their start and end apart: 124 -> 84, of which waited for: 50 -> 39; matrix products, arithmetic and copies ran while one was open for 44% -> 44% of each run, Pallas kernels for 0% -> 20%
where the time goes in v2:
time: 768 us; the launch traced here: 757 us
  waiting for transfers between devices  167 us (22%)
  local copies, waits for them, and re-layouts  162 us (21%)
  Pallas kernels  151 us (20%)
  matrix products  109 us (14%)
  starting transfers between devices  90.3 us (12%)
  other arithmetic  75.7 us (10%)
    pallas_call x1, Pallas kernels, spread_weights(): pl.pallas_call(functools.partial(weights_kernel, n_batch), out_shape=shap...  151 us
    ppermute x15, waiting for transfers between devices, collect(): downward = lax.ppermute(for_lower.astype(BF), 'batch', self.down)  62.9 us
    dynamic_update_slice x8, local copies, waits for them, and re-layouts, place(): return lax.dynamic_update_index_in_dim(array, block, index, axis)  62.5 us
    dot_general x18, matrix products, dot_right_t(): lax.dot_general(left_side, right_side, (((1,), (1,)), ((), ())), preferre...  36.3 us
    dot_general x18, matrix products, dot(): return jnp.dot(left_side, right_side, preferred_element_type=F32)  32.1 us
    ppermute x15, waiting for transfers between devices, collect(): upward = lax.ppermute(for_upper.astype(BF), 'batch', self.up)  27.5 us
    dot_general x6, matrix products, dot_left_t(): lax.dot_general(left_side, right_side, (((0,), (0,)), ((), ())), preferre...  21 us
    ppermute x15, starting transfers between devices, collect(): upward = lax.ppermute(for_upper.astype(BF), 'batch', self.up)  19.5 us
  transfers between devices with their start and end apart: 84, of which 39 were waited for; matrix products, arithmetic and copies ran while one was open for 44% of the time, Pallas kernels for 20%

profile of v2, /device:TPU:4, one launch (start us, length us, event | category | flops | bytes accessed | tf_op | source)
XLA Modules:
  0.0 757.3 jit_solution(14333189186589855372)
XLA Ops:
  13.4 150.7 %spread_weights.1 = (bf16[8,4,64,1664]{3,2,1,0:T(8,128)(2,1)}, bf16[8,4,32,1024]{3,2,1,0:T(8,128)(2,1)}, bf16[8,128,2048]{2,1,0:T(8,128)(2,1)}, bf16[2,8,4,64,704]{4,3,2,1,0:T(8,128)(2,1)}, bf16[4,176,2048]{2,1,0:T(8,128)(2,1)}) custom-call(bf16[64,1664]{1,0:T(8,128)(2,1)} %fusion.103.packed_ref, bf16[4,32,1024]{2,1,0:T(8,128)(2,1)} %bitcast.615, ...), custom_call_target="tpu_custom_call" | custom-call | tf_op jit(solution)/shard_map/spread_weights/pallas_call | solution.py:476
  216.8 6.0 fusion.14
  244.5 7.0 collective-permute-done.25
  262.2 6.0 collective-permute-done.3
  363.4 10.7 %pad_maximum_fusion = f32[2,8,4,64,704]{4,3,2,1,0:T(8,128)} fusion(f32[1,8,4,64,704]{4,3,2,1,0:T(8,128)} %bitcast.577, f32[1,8,4,64,704]{4,3,2,1,0:T(8,128)} %bitcast.578), kind=kLoop, calls=%fused_computation.1 | loop fusion | flops 2883584 | bytes 23068672 | tf_op jit(solution)/shard_map/stack | solution.py:657
  390.9 9.7 %collective-permute-done.29 = bf16[128,2048]{1,0:T(8,128)(2,1)S(1)} collective-permute-done((bf16[128,2048]{1,0:T(8,128)(2,1)S(1)}, bf16[128,2048]{1,0:T(8,128)(2,1)S(1)}, u32[]{:S(2)}, u32[]{:S(2)}) %collective-permute-start.29) | collective-permute-done | bytes 524320 | tf_op jit(solution)/shard_map/grad_mlp_in_collect/ppermute | solution.py:132
  402.9 9.9 %collective-permute-done.13 = bf16[128,2048]{1,0:T(8,128)(2,1)S(1)} collective-permute-done((bf16[128,2048]{1,0:T(8,128)(2,1)S(1)}, bf16[128,2048]{1,0:T(8,128)(2,1)S(1)}, u32[]{:S(2)}, u32[]{:S(2)}) %collective-permute-start.13) | collective-permute-done | bytes 524320 | tf_op jit(solution)/shard_map/layer_out_collect/ppermute | solution.py:132
  415.2 9.7 %collective-permute-done.30 = bf16[128,2048]{1,0:T(8,128)(2,1)S(1)} collective-permute-done((bf16[128,2048]{1,0:T(8,128)(2,1)S(1)}, bf16[128,2048]{1,0:T(8,128)(2,1)S(1)}, u32[]{:S(2)}, u32[]{:S(2)}) %collective-permute-start.30) | collective-permute-done | bytes 524320 | tf_op jit(solution)/shard_map/grad_mlp_in_collect/ppermute | solution.py:132
  427.3 8.7 %collective-permute-done.14 = bf16[128,2048]{1,0:T(8,128)(2,1)S(1)} collective-permute-done((bf16[128,2048]{1,0:T(8,128)(2,1)S(1)}, bf16[128,2048]{1,0:T(8,128)(2,1)S(1)}, u32[]{:S(2)}, u32[]{:S(2)}) %collective-permute-start.14) | collective-permute-done | bytes 524320 | tf_op jit(solution)/shard_map/layer_out_collect/ppermute | solution.py:132
  442.3 8.6 %collective-permute-done.35 = bf16[128,2048]{1,0:T(8,128)(2,1)S(1)} collective-permute-done((bf16[128,2048]{1,0:T(8,128)(2,1)S(1)}, bf16[128,2048]{1,0:T(8,128)(2,1)S(1)}, u32[]{:S(2)}, u32[]{:S(2)}) %collective-permute-start.35) | collective-permute-done | bytes 524320 | tf_op jit(solution)/shard_map/grad_mlp_in_collect/ppermute | solution.py:133
  542.1 6.7 collective-permute-done.56
  575.9 7.7 %dynamic_update_slice.25 = bf16[8,2,64,704]{3,0,1,2:T(8,128)(2,1)} dynamic-update-slice(bf16[8,2,64,704]{3,0,1,2:T(8,128)(2,1)} %broadcast_in_dim.53, bf16[1,2,64,704]{3,0,1,2:T(2,128)(2,1)S(1)} %copy.290, s32[]{:T(128)S(6)} %select_n.467, s32[]{:T(128)} %constant.355.clone.1, s32[]{:T(128)} %constant.355.clone.1, s32[]{:T(128)} %constant.355.clone.1) | dynamic-update-slice | bytes 360452 | tf_op jit(solution)/shard_map/grad_gate_up_exchange/jit(dynamic_update_index_in_dim)/dynamic_update_slice | solution.py:72
  600.3 8.1 %dynamic_update_slice.26 = bf16[8,2,64,704]{3,0,1,2:T(8,128)(2,1)} dynamic-update-slice(bf16[8,2,64,704]{3,0,1,2:T(8,128)(2,1)} %dynamic_update_slice.25, bf16[1,2,64,704]{3,0,1,2:T(2,128)(2,1)S(1)} %copy.291, s32[]{:T(128)S(6)} %select_n.468, s32[]{:T(128)} %constant.355.clone.1, s32[]{:T(128)} %constant.355.clone.1, s32[]{:T(128)} %constant.355.clone.1) | dynamic-update-slice | bytes 360452 | tf_op jit(solution)/shard_map/grad_gate_up_exchange/jit(dynamic_update_index_in_dim)/dynamic_update_slice | solution.py:72
  608.4 7.8 %dynamic_update_slice.27 = bf16[8,2,64,704]{3,0,1,2:T(8,128)(2,1)} dynamic-update-slice(bf16[8,2,64,704]{3,0,1,2:T(8,128)(2,1)} %dynamic_update_slice.26, bf16[1,2,64,704]{3,0,1,2:T(2,128)(2,1)S(1)} %copy.292, s32[]{:T(128)S(6)} %select_n.469, s32[]{:T(128)} %constant.355.clone.1, s32[]{:T(128)} %constant.355.clone.1, s32[]{:T(128)} %constant.355.clone.1) | dynamic-update-slice | bytes 360452 | tf_op jit(solution)/shard_map/grad_gate_up_exchange/jit(dynamic_update_index_in_dim)/dynamic_update_slice | solution.py:72
  616.2 7.8 %dynamic_update_slice.28 = bf16[8,2,64,704]{3,0,1,2:T(8,128)(2,1)} dynamic-update-slice(bf16[8,2,64,704]{3,0,1,2:T(8,128)(2,1)} %dynamic_update_slice.27, bf16[1,2,64,704]{3,0,1,2:T(2,128)(2,1)S(1)} %copy.293, s32[]{:T(128)S(6)} %select_n.470, s32[]{:T(128)} %constant.355.clone.1, s32[]{:T(128)} %constant.355.clone.1, s32[]{:T(128)} %constant.355.clone.1) | dynamic-update-slice | bytes 360452 | tf_op jit(solution)/shard_map/grad_gate_up_exchange/jit(dynamic_update_index_in_dim)/dynamic_update_slice | solution.py:72
  624.0 7.8 %dynamic_update_slice.29 = bf16[8,2,64,704]{3,0,1,2:T(8,128)(2,1)} dynamic-update-slice(bf16[8,2,64,704]{3,0,1,2:T(8,128)(2,1)} %dynamic_update_slice.28, bf16[1,2,64,704]{3,0,1,2:T(2,128)(2,1)} %copy.294, s32[]{:T(128)S(6)} %select_n.471, s32[]{:T(128)} %constant.355.clone.1, s32[]{:T(128)} %constant.355.clone.1, s32[]{:T(128)} %constant.355.clone.1) | dynamic-update-slice | bytes 360452 | tf_op jit(solution)/shard_map/grad_gate_up_exchange/jit(dynamic_update_index_in_dim)/dynamic_update_slice | solution.py:72
  631.9 7.7 %dynamic_update_slice.30 = bf16[8,2,64,704]{3,0,1,2:T(8,128)(2,1)} dynamic-update-slice(bf16[8,2,64,704]{3,0,1,2:T(8,128)(2,1)} %dynamic_update_slice.29, bf16[1,2,64,704]{3,0,1,2:T(2,128)(2,1)S(1)} %copy-done.31, s32[]{:T(128)S(6)} %select_n.472, s32[]{:T(128)} %constant.355.clone.1, s32[]{:T(128)} %constant.355.clone.1, s32[]{:T(128)} %constant.355.clone.1) | dynamic-update-slice | bytes 360452 | tf_op jit(solution)/shard_map/grad_gate_up_exchange/jit(dynamic_update_index_in_dim)/dynamic_update_slice | solution.py:72
  639.6 7.7 %dynamic_update_slice.31 = bf16[8,2,64,704]{3,0,1,2:T(8,128)(2,1)} dynamic-update-slice(bf16[8,2,64,704]{3,0,1,2:T(8,128)(2,1)} %dynamic_update_slice.30, bf16[1,2,64,704]{3,0,1,2:T(2,128)(2,1)S(1)} %copy-done.32, s32[]{:T(128)S(6)} %select_n.473, s32[]{:T(128)} %constant.355.clone.1, s32[]{:T(128)} %constant.355.clone.1, s32[]{:T(128)} %constant.355.clone.1) | dynamic-update-slice | bytes 360452 | tf_op jit(solution)/shard_map/grad_gate_up_exchange/jit(dynamic_update_index_in_dim)/dynamic_update_slice | solution.py:72
  647.4 7.7 %dynamic_update_slice.32 = bf16[8,2,64,704]{3,0,1,2:T(8,128)(2,1)} dynamic-update-slice(bf16[8,2,64,704]{3,0,1,2:T(8,128)(2,1)} %dynamic_update_slice.31, bf16[1,2,64,704]{3,0,1,2:T(2,128)(2,1)S(1)} %copy-done.33, s32[]{:T(128)S(6)} %select_n.474, s32[]{:T(128)} %constant.355.clone.1, s32[]{:T(128)} %constant.355.clone.1, s32[]{:T(128)} %constant.355.clone.1) | dynamic-update-slice | bytes 360452 | tf_op jit(solution)/shard_map/grad_gate_up_exchange/jit(dynamic_update_index_in_dim)/dynamic_update_slice | solution.py:72
  665.5 5.9 multiply_reduce_fusion.2
  708.3 6.5 collective-permute-done.46
  718.3 5.8 collective-permute-done.50
  733.0 11.5 %collective-permute-done.52 = bf16[2,80,384]{2,1,0:T(8,128)(2,1)S(1)} collective-permute-done((bf16[2,80,384]{2,1,0:T(8,128)(2,1)S(1)}, bf16[2,80,384]{2,1,0:T(8,128)(2,1)S(1)}, u32[]{:S(2)}, u32[]{:S(2)}) %collective-permute-start.52) | collective-permute-done | bytes 122912 | tf_op jit(solution)/shard_map/ppermute | solution.py:185
  745.5 8.6 %collective-permute-done.72 = bf16[128,2048]{1,0:T(8,128)(2,1)S(1)} collective-permute-done((bf16[128,2048]{1,0:T(8,128)(2,1)S(1)}, bf16[128,2048]{1,0:T(8,128)(2,1)S(1)}, u32[]{:S(2)}, u32[]{:S(2)}) %collective-permute-start.72) | collective-permute-done | bytes 524320 | tf_op jit(solution)/shard_map/grad_proj_out_collect/ppermute | solution.py:673
  (569 shorter events, 420.0 us)
Async XLA Ops:
  4.0 193.3 %collective-permute-start.21 = (bf16[128,2048]{1,0:T(8,128)(2,1)}, bf16[128,2048]{1,0:T(8,128)(2,1)}, u32[]{:S(2)}, u32[]{:S(2)}) collective-permute-start(bf16[128,2048]{1,0:T(8,128)(2,1)} %get-tuple-element.198), channel_id=1, source_target_pairs={{8,0},{16,8},{24,16},{28,24},{20,28},{12,20},{4,12},{0,4},{9,1},{1... | collective-permute-start | bytes 1572872 | tf_op jit(solution)/shard_map/cotangent_spread/ppermute | solution.py:94
  5.6 191.7 %collective-permute-start.20 = (bf16[128,2048]{1,0:T(8,128)(2,1)}, bf16[128,2048]{1,0:T(8,128)(2,1)}, u32[]{:S(2)}, u32[]{:S(2)}) collective-permute-start(bf16[128,2048]{1,0:T(8,128)(2,1)} %get-tuple-element.198), channel_id=1, source_target_pairs={{0,8},{8,16},{16,24},{24,28},{28,20},{20,12},{12,4},{4,0},{1,9},{9... | collective-permute-start | bytes 1572872 | tf_op jit(solution)/shard_map/cotangent_spread/ppermute | solution.py:93
  167.0 27.1 %collective-permute-start.40 = (bf16[128,2048]{1,0:T(8,128)(2,1)}, bf16[128,2048]{1,0:T(8,128)(2,1)}, u32[]{:S(2)}, u32[]{:S(2)}) collective-permute-start(bf16[128,2048]{1,0:T(8,128)(2,1)} %multiply_convert_fusion.3), channel_id=1, source_target_pairs={{0,2},{1,3},{2,0},{3,1},{4,6},{5,7},{6,4},{7,5},{8,10},{9,11},{10,... | collective-permute-start | bytes 1572872 | tf_op jit(solution)/shard_map/attn_in_gather/ppermute | solution.py:167
  196.8 272.3 %collective-permute-start.41 = (bf16[2,128,2048]{2,1,0:T(8,128)(2,1)}, bf16[2,128,2048]{2,1,0:T(8,128)(2,1)}, u32[]{:S(2)}, u32[]{:S(2)}) collective-permute-start(bf16[2,128,2048]{2,1,0:T(8,128)(2,1)} %maximum_select_fusion.6), channel_id=1, source_target_pairs={{0,1},{1,0},{2,3},{3,2},{4,5},{5,4},{6,7},{7,6},{8,9},{9,8},{10,11... | collective-permute-start | bytes 3145736 | tf_op jit(solution)/shard_map/attn_in_gather/ppermute | solution.py:168
  197.3 39.5 %collective-permute-start.23 = (bf16[128,2048]{1,0:T(8,128)(2,1)}, bf16[128,2048]{1,0:T(8,128)(2,1)}, u32[]{:S(2)}, u32[]{:S(2)}) collective-permute-start(bf16[128,2048]{1,0:T(8,128)(2,1)} %collective-permute-done.21), channel_id=1, source_target_pairs={{8,0},{16,8},{24,16},{28,24},{20,28},{12,20},{4,12},{0,4},{9,1},{1... | collective-permute-start | bytes 1572872 | tf_op jit(solution)/shard_map/cotangent_spread/ppermute | solution.py:94
  197.3 40.0 %collective-permute-start.22 = (bf16[128,2048]{1,0:T(8,128)(2,1)}, bf16[128,2048]{1,0:T(8,128)(2,1)}, u32[]{:S(2)}, u32[]{:S(2)}) collective-permute-start(bf16[128,2048]{1,0:T(8,128)(2,1)} %collective-permute-done.20), channel_id=1, source_target_pairs={{0,8},{8,16},{16,24},{24,28},{28,20},{20,12},{12,4},{4,0},{1,9},{9... | collective-permute-start | bytes 1572872 | tf_op jit(solution)/shard_map/cotangent_spread/ppermute | solution.py:93
  346.7 37.9 %collective-permute-start.28 = (bf16[64,2048]{1,0:T(8,128)(2,1)}, bf16[64,2048]{1,0:T(8,128)(2,1)}, u32[]{:S(2)}, u32[]{:S(2)}) collective-permute-start(bf16[64,2048]{1,0:T(8,128)(2,1)} %get-tuple-element.145), channel_id=1, source_target_pairs={{8,0},{16,8},{24,16},{28,24},{20,28},{12,20},{4,12},{0,4},{9,1},{1... | collective-permute-start | bytes 786440 | tf_op jit(solution)/shard_map/grad_mlp_in_collect/ppermute | solution.py:117
  347.7 37.0 %collective-permute-start.32 = (bf16[64,2048]{1,0:T(8,128)(2,1)}, bf16[64,2048]{1,0:T(8,128)(2,1)}, u32[]{:S(2)}, u32[]{:S(2)}) collective-permute-start(bf16[64,2048]{1,0:T(8,128)(2,1)} %get-tuple-element.146), channel_id=1, source_target_pairs={{0,8},{8,16},{16,24},{24,28},{28,20},{20,12},{12,4},{4,0},{1,9},{9... | collective-permute-start | bytes 786440 | tf_op jit(solution)/shard_map/grad_mlp_in_collect/ppermute | solution.py:118
  350.1 37.2 %collective-permute-start.12 = (bf16[64,2048]{1,0:T(8,128)(2,1)}, bf16[64,2048]{1,0:T(8,128)(2,1)}, u32[]{:S(2)}, u32[]{:S(2)}) collective-permute-start(bf16[64,2048]{1,0:T(8,128)(2,1)} %get-tuple-element.147), channel_id=1, source_target_pairs={{8,0},{16,8},{24,16},{28,24},{20,28},{12,20},{4,12},{0,4},{9,1},{1... | collective-permute-start | bytes 786440 | tf_op jit(solution)/shard_map/layer_out_collect/ppermute | solution.py:117
  351.2 37.3 %collective-permute-start.16 = (bf16[64,2048]{1,0:T(8,128)(2,1)}, bf16[64,2048]{1,0:T(8,128)(2,1)}, u32[]{:S(2)}, u32[]{:S(2)}) collective-permute-start(bf16[64,2048]{1,0:T(8,128)(2,1)} %get-tuple-element.148), channel_id=1, source_target_pairs={{0,8},{8,16},{16,24},{24,28},{28,20},{20,12},{12,4},{4,0},{1,9},{9... | collective-permute-start | bytes 786440 | tf_op jit(solution)/shard_map/layer_out_collect/ppermute | solution.py:118
  384.6 94.3 %collective-permute-start.73 = (bf16[2,8,2,64,704]{4,3,2,1,0:T(8,128)(2,1)}, bf16[2,8,2,64,704]{4,3,2,1,0:T(8,128)(2,1)}, u32[]{:S(2)}, u32[]{:S(2)}) collective-permute-start(bf16[2,8,2,64,704]{4,3,2,1,0:T(8,128)(2,1)} %fusion.5), channel_id=1, source_target_pairs={{0,1},{1,0},{2,3},{3,2},{4,5},{5,4},{6,7},{7,6},{8,9},{9,8},{10,11... | collective-permute-start | bytes 8650760 | tf_op jit(solution)/shard_map/grad_gate_up_collect/ppermute | solution.py:176
  384.7 54.1 %collective-permute-start.82 = (bf16[2,176,2048]{2,1,0:T(8,128)(2,1)S(1)}, bf16[2,176,2048]{2,1,0:T(8,128)(2,1)S(1)}, u32[]{:S(2)}, u32[]{:S(2)}) collective-permute-start(bf16[2,176,2048]{2,1,0:T(8,128)(2,1)S(1)} %fusion.13), channel_id=1, source_target_pairs={{0,1},{1,0},{2,3},{3,2},{4,5},{5,4},{6,7},{7,6},{8,9},{9,8},{10,11... | collective-permute-start | bytes 4325384 | tf_op jit(solution)/shard_map/grad_down_collect/ppermute | solution.py:176
  485.0 67.7 %collective-permute-start.74 = (bf16[8,2,64,704]{3,2,1,0:T(8,128)(2,1)}, bf16[8,2,64,704]{3,2,1,0:T(8,128)(2,1)}, u32[]{:S(2)}, u32[]{:S(2)}) collective-permute-start(bf16[8,2,64,704]{3,2,1,0:T(8,128)(2,1)} %fusion.11), channel_id=1, source_target_pairs={{0,2},{1,3},{2,0},{3,1},{4,6},{5,7},{6,4},{7,5},{8,10},{9,11},{10,... | collective-permute-start | bytes 4325384 | tf_op jit(solution)/shard_map/grad_gate_up_collect/ppermute | solution.py:178
  518.6 32.4 %collective-permute-start.38 = (bf16[2,128,1536]{2,1,0:T(8,128)(2,1)S(1)}, bf16[2,128,1536]{2,1,0:T(8,128)(2,1)S(1)}, u32[]{:S(2)}, u32[]{:S(2)}) collective-permute-start(bf16[2,128,1536]{2,1,0:T(8,128)(2,1)S(1)} %fusion.54), channel_id=1, source_target_pairs={{0,1},{1,0},{2,3},{3,2},{4,5},{5,4},{6,7},{7,6},{8,9},{9,8},{10,11... | collective-permute-start | bytes 2359304 | tf_op jit(solution)/shard_map/back_collect/ppermute | solution.py:176
  552.2 111.2 %collective-permute-start.39 = (bf16[128,1536]{1,0:T(8,128)(2,1)}, bf16[128,1536]{1,0:T(8,128)(2,1)}, u32[]{:S(2)}, u32[]{:S(2)}) collective-permute-start(bf16[128,1536]{1,0:T(8,128)(2,1)} %fusion.90), channel_id=1, source_target_pairs={{0,2},{1,3},{2,0},{3,1},{4,6},{5,7},{6,4},{7,5},{8,10},{9,11},{10,... | collective-permute-start | bytes 1179656 | tf_op jit(solution)/shard_map/back_collect/ppermute | solution.py:178
  565.2 27.1 %collective-permute-start.79 = (bf16[2,64,704]{2,1,0:T(8,128)(2,1)}, bf16[2,64,704]{2,1,0:T(8,128)(2,1)}, u32[]{:S(2)}, u32[]{:S(2)}) collective-permute-start(bf16[2,64,704]{2,1,0:T(8,128)(2,1)} %get-tuple-element.100), channel_id=1, source_target_pairs={{0,20},{4,16},{8,28},{12,24},{16,4},{20,0},{24,12},{28,8},{1,21},{... | collective-permute-start | bytes 540680 | tf_op jit(solution)/shard_map/grad_gate_up_exchange/ppermute | solution.py:148
  566.0 28.2 %collective-permute-start.80 = (bf16[2,64,704]{2,1,0:T(8,128)(2,1)}, bf16[2,64,704]{2,1,0:T(8,128)(2,1)}, u32[]{:S(2)}, u32[]{:S(2)}) collective-permute-start(bf16[2,64,704]{2,1,0:T(8,128)(2,1)} %get-tuple-element.99), channel_id=1, source_target_pairs={{0,24},{4,28},{8,16},{12,20},{16,8},{20,12},{24,0},{28,4},{1,25},{... | collective-permute-start | bytes 540680 | tf_op jit(solution)/shard_map/grad_gate_up_exchange/ppermute | solution.py:148
  586.5 99.2 %collective-permute-start.69 = (bf16[128,2048]{1,0:T(8,128)(2,1)}, bf16[128,2048]{1,0:T(8,128)(2,1)}, u32[]{:S(2)}, u32[]{:S(2)}) collective-permute-start(bf16[128,2048]{1,0:T(8,128)(2,1)} %pad_maximum_fusion.11), channel_id=1, source_target_pairs={{0,8},{8,16},{16,24},{24,28},{28,20},{20,12},{12,4},{4,0},{1,9},{9... | collective-permute-start | bytes 1572872 | tf_op jit(solution)/shard_map/grad_proj_out_collect/ppermute | solution.py:133
  592.3 80.9 %collective-permute-start.57 = (bf16[128,1024]{1,0:T(8,128)(2,1)}, bf16[128,1024]{1,0:T(8,128)(2,1)}, u32[]{:S(2)}, u32[]{:S(2)}) collective-permute-start(bf16[128,1024]{1,0:T(8,128)(2,1)} %get-tuple-element.70), channel_id=1, source_target_pairs={{8,0},{16,8},{24,16},{28,24},{20,28},{12,20},{4,12},{0,4},{9,1},{1... | collective-permute-start | bytes 786440 | tf_op jit(solution)/shard_map/grad_query_up_collect/ppermute | solution.py:132
  594.3 91.4 %collective-permute-start.66 = (bf16[128,2048]{1,0:T(8,128)(2,1)}, bf16[128,2048]{1,0:T(8,128)(2,1)}, u32[]{:S(2)}, u32[]{:S(2)}) collective-permute-start(bf16[128,2048]{1,0:T(8,128)(2,1)} %fusion.41), channel_id=1, source_target_pairs={{8,0},{16,8},{24,16},{28,24},{20,28},{12,20},{4,12},{0,4},{9,1},{1... | collective-permute-start | bytes 1572872 | tf_op jit(solution)/shard_map/grad_proj_out_collect/ppermute | solution.py:132
  597.5 75.7 %collective-permute-start.61 = (bf16[128,1024]{1,0:T(8,128)(2,1)}, bf16[128,1024]{1,0:T(8,128)(2,1)}, u32[]{:S(2)}, u32[]{:S(2)}) collective-permute-start(bf16[128,1024]{1,0:T(8,128)(2,1)} %fusion.76), channel_id=1, source_target_pairs={{0,8},{8,16},{16,24},{24,28},{28,20},{20,12},{12,4},{4,0},{1,9},{9... | collective-permute-start | bytes 786440 | tf_op jit(solution)/shard_map/grad_query_up_collect/ppermute | solution.py:133
  679.5 53.3 %collective-permute-start.62 = (bf16[2,32,1024]{2,1,0:T(8,128)(2,1)S(1)}, bf16[2,32,1024]{2,1,0:T(8,128)(2,1)S(1)}, u32[]{:S(2)}, u32[]{:S(2)}) collective-permute-start(bf16[2,32,1024]{2,1,0:T(8,128)(2,1)S(1)} %get-tuple-element.163), channel_id=1, source_target_pairs={{0,2},{1,3},{2,0},{3,1},{4,6},{5,7},{6,4},{7,5},{8,10},{9,11},{10,... | collective-permute-start | bytes 393224 | tf_op jit(solution)/shard_map/ppermute | solution.py:185
  693.5 31.5 %collective-permute-start.67 = (bf16[128,2048]{1,0:T(8,128)(2,1)S(1)}, bf16[128,2048]{1,0:T(8,128)(2,1)S(1)}, u32[]{:S(2)}, u32[]{:S(2)}) collective-permute-start(bf16[128,2048]{1,0:T(8,128)(2,1)S(1)} %get-tuple-element.62), channel_id=1, source_target_pairs={{8,0},{16,8},{24,16},{28,24},{20,28},{12,20},{4,12},{0,4},{9,1},{1... | collective-permute-start | bytes 1572872 | tf_op jit(solution)/shard_map/grad_proj_out_collect/ppermute | solution.py:132
  725.2 28.9 %collective-permute-start.72 = (bf16[128,2048]{1,0:T(8,128)(2,1)S(1)}, bf16[128,2048]{1,0:T(8,128)(2,1)S(1)}, u32[]{:S(2)}, u32[]{:S(2)}) collective-permute-start(bf16[128,2048]{1,0:T(8,128)(2,1)S(1)} %fusion.44), channel_id=1, source_target_pairs={{0,0},{4,1},{8,2},{12,3},{16,4},{20,5},{24,6},{28,7},{1,8},{5,9},{... | collective-permute-start | bytes 1572872 | tf_op jit(solution)/shard_map/grad_proj_out_collect/ppermute | solution.py:673
  (135 other events, 1268.6 us)

commit v3 on v2

--- a/solution.py
+++ b/solution.py
@@ -138,17 +138,6 @@
         return self.collect(lambda step: pick(stacked, self.rank_of(step)))
 
 
-def batch_exchange(stacked):
-    n = lax.axis_size("batch")
-    rank = lax.axis_index("batch")
-    swapped = place(jnp.zeros_like(stacked), pick(stacked, rank), rank)
-    for offset in range(1, n):
-        pairs = [(i, i ^ offset) for i in range(n)]
-        other = rank ^ offset
-        swapped = place(swapped, lax.ppermute(pick(stacked, other), "batch", pairs), other)
-    return swapped
-
-
 FAR = [(0, 2), (1, 3), (2, 0), (3, 1)]
 NEAR = [(0, 1), (1, 0), (2, 3), (3, 2)]
 
@@ -187,10 +176,6 @@
     got = lax.ppermute(pick(parts, 1 - inner, 1), "ctx", NEAR)
     whole = in_order(pick(parts, inner, 1), got, inner)
     return jnp.swapaxes(whole, 0, 1).reshape(stacked.shape)
-
-
-def slab_pairs(n_batch, n_ctx):
-    return [(i, (i % n_batch) * n_ctx + i // n_batch) for i in range(n_batch * n_ctx)]
 
 
 MESH = pl.DeviceIdType.MESH
@@ -488,137 +473,594 @@
     )(packed, up_parts, out_rows, gu_parts, down_rows)
 
 
-def shards(
-    tokens,
-    cotangent,
-    lengths,
-    slot_sequence,
-    proj_in,
-    query_up,
-    proj_out,
-    attn_gain,
-    query_gain,
-    mlp_gain,
-    gate_up,
-    down_proj,
+def mlp_kernel(
+    n_batch,
+    rows_ref,
+    gate_ref,
+    up_ref,
+    down_ref,
+    *refs,
 ):
-    n_ctx = lax.axis_size("ctx")
-    n_batch = lax.axis_size("batch")
-    ctx_rank = lax.axis_index("ctx")
-    batch_rank = lax.axis_index("batch")
-    ring = Ring()
-    micro, pos_dev, width = tokens.shape
-    n_tok = micro * pos_dev
-    full_length = pos_dev * n_ctx
-    heads = H // n_ctx
-    score_scale = 1.0 / math.sqrt(HD)
-    in_cols = proj_in.shape[1]
-
-    slot_total = lengths.shape[0]
-    slot_ids = jnp.arange(slot_total, dtype=jnp.int32)
-    seq_lengths = jnp.sum(
-        jnp.where(slot_sequence[:, None] == slot_ids[None, :], lengths[None, :], 0), axis=1
-    )
-    own_lengths = lax.dynamic_slice_in_dim(seq_lengths, batch_rank * micro, micro)
-    query_pos = ctx_rank * pos_dev + jnp.arange(pos_dev, dtype=jnp.int32)
-    key_pos = jnp.arange(full_length, dtype=jnp.int32)
-    cos_all, sin_all = rope_tables(key_pos)
-    cos_own, sin_own = rope_tables(query_pos)
-
-    own_rows = proj_in.shape[0]
-    gain_rows = query_gain.shape[0]
-    gains = jnp.stack(
-        [attn_gain, mlp_gain, jnp.pad(query_gain, (0, own_rows - gain_rows))], axis=1
-    )
-    packed = jnp.concatenate([proj_in, jnp.pad(gains, ((0, 0), (0, 125)))], axis=1)
-    up_parts = query_up.reshape(gain_rows, n_ctx, heads * HD).swapaxes(0, 1)
-    ff_all = gate_up.shape[1] // 2
-    ff = ff_all // n_batch
-    gu_parts = gate_up.reshape(own_rows, 2, n_batch, ff).transpose(2, 1, 0, 3)
-    packed, own_qup, own_out, gu_rows, own_down = spread_weights(
-        n_batch, packed, up_parts, proj_out, gu_parts, down_proj
-    )
-    packed = packed.reshape(width, in_cols + 128)
-    own_qup = own_qup.reshape(QR, heads * HD)
-    own_out = own_out.reshape(heads * HD, width)
+    cot_refs = refs[:n_batch]
+    (
+        sum_ref,
+        down_grad,
+        term_out,
+        gu_out,
+        rows_v,
+        cot_v,
+        gate_v,
+        up_v,
+        down_v,
+        act_v,
+        ggate_v,
+        gup_v,
+        in_v,
+        term_v,
+        got_v,
+        gu_got,
+        gu_last,
+        down_got,
+        down_last,
+        send_sems,
+        recv_sems,
+        back_send,
+        back_recv,
+        load_sems,
+        store_sems,
+        part_send,
+        part_recv,
+    ) = refs[n_batch:]
+    place = Place(n_batch)
+    far = place.h
+    n_tok = rows_ref.shape[0]
+    cut = n_tok // 2
+    width = rows_ref.shape[1]
+    ff = gate_ref.shape[-1]
+    up_device, down_device = place.up(), place.down()
+    far_device, near_device = (place.b, place.far), (place.b, place.near)
+    barrier = greet(place, [up_device, down_device, far_device, near_device])
+    parts = Copies(part_send, part_recv)
+    own_rows = gate_v.shape[2]
+    block = 4 * own_rows
+
+    load_rows = pltpu.make_async_copy(rows_ref, rows_v.at[0, pl.ds(0, n_tok)], load_sems.at[0])
+    load_rows.start()
+    loads = [
+        pltpu.make_async_copy(source, target, load_sems.at[1 + i])
+        for i, (source, target) in enumerate(
+            [(gate_ref, gate_v), (up_ref, up_v), (down_ref, down_v)]
+        )
+    ]
+    spots = [(0, 0)] + [(s, k) for s in range(1, far) for k in (0, 1)] + [(0, 1)]
+    for i, (source, (group, side)) in enumerate(zip(cot_refs, spots)):
+        loads.append(
+            pltpu.make_async_copy(
+                source, cot_v.at[group, pl.ds(side * n_tok, n_tok)], load_sems.at[4 + i]
+            )
+        )
+    for copy in loads:
+        copy.start()
+    load_rows.wait()
+    pl.semaphore_wait(barrier, 4)
+
+    def piece(side, half):
+        return pl.ds(side * n_tok + half * cut, cut)
+
+    def hop(step, side, half):
+        source_group, source_side = step - 1, side
+        target_group, target_side = step, side
+        if isinstance(step, int) and step == 1:
+            source_side = 0
+        if isinstance(step, int) and step == far:
+            target_group, target_side = 0, 1
+        return pltpu.make_async_remote_copy(
+            src_ref=rows_v.at[source_group, piece(source_side, half)],
+            dst_ref=rows_v.at[target_group, piece(target_side, half)],
+            send_sem=send_sems.at[step, side, half],
+            recv_sem=recv_sems.at[step, side, half],
+            device_id=down_device if side else up_device,
+            device_id_type=MESH,
+        )
+
+    both = [(side, half) for half in (0, 1) for side in (0, 1)]
+    ends = [(0, 0), (1, 1)]
+    for side, half in both:
+        hop(1, side, half).start()
+    for copy in loads:
+        copy.wait()
+
+    def stores(group):
+        return [
+            pltpu.make_async_copy(term_v.at[group], term_out.at[group], store_sems.at[0, group])
+        ]
+
+    def compute(group):
+        rows = rows_v[group]
+        cots = cot_v[group]
+        down_all = down_v[...].reshape(ff, width)
+        start = 0
+        while start < ff:
+            size = min(256, ff - start)
+            tile = slice(start, start + size)
+            gate = dot(rows, gate_v[..., tile].reshape(width, size))
+            up = dot(rows, up_v[..., tile].reshape(width, size))
+            grad_act = dot_right_t(cots, down_all[tile])
+            sigmoid = 1.0 / (1.0 + jnp.exp(-gate))
+            silu = gate * sigmoid
+            act_v[group, :, tile] = (silu * up).astype(BF)
+            slope = sigmoid * (1.0 + gate * (1.0 - sigmoid))
+            ggate_v[group, :, tile] = (grad_act * up * slope).astype(BF)
+            gup_v[group, :, tile] = (grad_act * silu).astype(BF)
+            start += size
+        ggate = ggate_v[group]
+        gup = gup_v[group]
+        act = act_v[group]
+        tile_cols = 2 * block
+
+        @pl.loop(0, width // tile_cols)
+        def _(t):
+            cols = pl.ds(pl.multiple_of(t * tile_cols, tile_cols), tile_cols)
+            back = dot_right_t(ggate, gate_v[pl.ds(2 * t, 2)].reshape(tile_cols, ff))
+            back += dot_right_t(gup, up_v[pl.ds(2 * t, 2)].reshape(tile_cols, ff))
+            in_v[group, :, cols] = back.astype(BF)
+            down = down_v[:, :, cols].reshape(ff, tile_cols)
+            term_v[group, :, cols] = dot(act, down).astype(BF)
+
+        for copy in stores(group):
+            copy.start()
+
+    @pl.loop(1, far)
+    def _(step):
+        for side, half in both:
+            hop(step, side, half).wait_recv()
+
+        @pl.when(step < far - 1)
+        def _():
+            for side, half in both:
+                hop(step + 1, side, half).start()
+
+        @pl.when(step == far - 1)
+        def _():
+            for side, half in ends:
+                hop(far, side, half).start()
+
+        compute(step)
+
+    for side, half in ends:
+        hop(far, side, half).wait_recv()
+    compute(0)
+
+    def back_hop(step, side, half, source):
+        return pltpu.make_async_remote_copy(
+            src_ref=source,
+            dst_ref=got_v.at[step, side, half],
+            send_sem=back_send.at[step, side, half],
+            recv_sem=back_recv.at[step, side, half],
+            device_id=up_device if side else down_device,
+            device_id_type=MESH,
+        )
+
+    def held(step, side, half):
+        return in_v.at[step, piece(side, half)]
+
+    for side, half in ends:
+        back_hop(far - 1, side, half, held(0, 1, half)).start()
+
+    def pass_on(step, side, half, added):
+        own = held(step, side, half)
+        if added:
+            back_hop(step, side, half, own).wait_recv()
+            own[...] = (own[...].astype(F32) + got_v[step, side, half].astype(F32)).astype(BF)
+        back_hop(step - 1, side, half, own).start()
+
+    for side, half in both:
+        if (side, half) not in ends:
+            pass_on(far - 1, side, half, False)
+
+    def gate_up_terms(first, last):
+        @pl.loop(first, last)
+        def _(t):
+            cols = pl.ds(pl.multiple_of(t * 2 * block, 2 * block), 2 * block)
+            rows = rows_v[:, :, cols].reshape(n_batch * n_tok, 2 * block)
+            for target, grads in ((gate_v, ggate_v), (up_v, gup_v)):
+                term = dot_left_t(rows, grads[...].reshape(n_batch * n_tok, ff))
+                target[pl.ds(2 * t, 2)] = term.astype(BF).reshape(2, 4, own_rows, ff)
+
+    def down_terms():
+        @pl.loop(0, width // (2 * block))
+        def _(t):
+            cols = pl.ds(pl.multiple_of(t * 2 * block, 2 * block), 2 * block)
+            grads = cot_v[:, :, cols].reshape(n_batch * n_tok, 2 * block)
+            term = dot_left_t(act_v[...].reshape(n_batch * n_tok, ff), grads)
+            down_v[:, :, cols] = term.astype(BF).reshape(4, ff // 4, 2 * block)
+
+    def pass_all(step):
+        for side, half in [(1, 0), (0, 1), (0, 0), (1, 1)]:
+            if step < far - 1 or (side, half) in ends:
+                pass_on(step, side, half, True)
+
+    steps = iter(range(far - 1, 0, -1))
+    tiles = width // (2 * block)
+    outer, inner = place.outer, place.inner
+
+    gate_up_terms(0, tiles // 2)
+    pass_all(next(steps))
+    gate_up_terms(tiles // 2, tiles)
+    near_copies = [
+        parts.remote(
+            target.at[:, 2 * side + 1 - inner], gu_got.at[kind, side], near_device
+        )
+        for side in (0, 1)
+        for kind, target in enumerate((gate_v, up_v))
+    ]
+    for step in steps:
+        pass_all(step)
+        if step > 1:
+            down_terms()
+    down_copies = [
+        parts.remote(down_v.at[2 * side + 1 - inner], down_got.at[side], near_device)
+        for side in (0, 1)
+    ]
+    for copy in near_copies:
+        parts.arrive(copy)
+    far_copies = []
+    for kind, target in enumerate((gate_v, up_v)):
+        for side in (1 - outer, outer):
+            kept = target.at[:, 2 * side + inner]
+            kept[...] = (kept[...].astype(F32) + gu_got[kind, side].astype(F32)).astype(BF)
+            if side is not outer:
+                far_copies.append(parts.remote(kept, gu_last.at[kind], far_device))
+    for copy in down_copies:
+        parts.arrive(copy)
+    other = down_v.at[2 * (1 - outer) + inner]
+    other[...] = (other[...].astype(F32) + down_got[1 - outer].astype(F32)).astype(BF)
+    down_far = parts.remote(other, down_last, far_device)
+    for half in (0, 1):
+        for side in (0, 1):
+            back_hop(0, side, half, held(0, 0, half)).wait_recv()
+        rows = slice(half * cut, (half + 1) * cut)
+        sum_ref[rows, :] = (
+            in_v[0, rows, :].astype(F32)
+            + got_v[0, 0, half].astype(F32)
+            + got_v[0, 1, half].astype(F32)
+        )
+    for kind, target in enumerate((gate_v, up_v)):
+        parts.arrive(far_copies[kind])
+        kept = target.at[:, 2 * outer + inner]
+        kept[...] = (kept[...].astype(F32) + gu_last[kind].astype(F32)).astype(BF)
+        parts.local(kept, gu_out.at[:, kind])
+    parts.arrive(down_far)
+    down_grad[...] = (
+        down_v[2 * outer + inner].astype(F32)
+        + down_got[outer].astype(F32)
+        + down_last[...].astype(F32)
+    )
+    parts.drain()
+
+    for step in range(1, far + 1):
+        for side, half in both if step < far else ends:
+            hop(step, side, half).wait_send()
+    for side, half in ends:
+        back_hop(far - 1, side, half, held(0, 1, half)).wait_send()
+    for step in range(far - 1, 0, -1):
+        for side, half in both:
+            back_hop(step - 1, side, half, held(step, side, half)).wait_send()
+    for group in range(far):
+        for copy in stores(group):
+            copy.wait()
+
+
+def fused_mlp(n_batch, rows, cots, own_gate, own_up, own_down):
+    n_tok, width = rows.shape
+    ff = own_gate.shape[-1]
+    own_rows = own_gate.shape[2]
+    far = n_batch // 2
+    pair = 2 * n_tok
+    flops = 18 * n_batch * n_tok * width * ff
+    return pl.pallas_call(
+        functools.partial(mlp_kernel, n_batch),
+        out_shape=(
+            jax.ShapeDtypeStruct((n_tok, width), F32),
+            jax.ShapeDtypeStruct((ff // 4, width), F32),
+            jax.ShapeDtypeStruct((far, pair, width), BF),
+            jax.ShapeDtypeStruct((n_batch, 2, own_rows, ff), BF),
+        ),
+        in_specs=[pl.BlockSpec(memory_space=pl.ANY)] * (4 + n_batch),
+        out_specs=[pl.BlockSpec(memory_space=pltpu.VMEM)] * 2
+        + [pl.BlockSpec(memory_space=pl.ANY)] * 2,
+        scratch_shapes=[
+            pltpu.VMEM((far, pair, width), BF),
+            pltpu.VMEM((far, pair, width), BF),
+            pltpu.VMEM((n_batch, 4, own_rows, ff), BF),
+            pltpu.VMEM((n_batch, 4, own_rows, ff), BF),
+            pltpu.VMEM((4, ff // 4, width), BF),
+            pltpu.VMEM((far, pair, ff), BF),
+            pltpu.VMEM((far, pair, ff), BF),
+            pltpu.VMEM((far, pair, ff), BF),
+            pltpu.VMEM((far, pair, width), BF),
+            pltpu.VMEM((far, pair, width), BF),
+            pltpu.VMEM((far, 2, 2, n_tok // 2, width), BF),
+            pltpu.VMEM((2, 2, n_batch, own_rows, ff), BF),
+            pltpu.VMEM((2, n_batch, own_rows, ff), BF),
+            pltpu.VMEM((2, ff // 4, width), BF),
+            pltpu.VMEM((ff // 4, width), BF),
+            pltpu.SemaphoreType.DMA((far + 1, 2, 2)),
+            pltpu.SemaphoreType.DMA((far + 1, 2, 2)),
+            pltpu.SemaphoreType.DMA((far, 2, 2)),
+            pltpu.SemaphoreType.DMA((far, 2, 2)),
+            pltpu.SemaphoreType.DMA((4 + n_batch,)),
+            pltpu.SemaphoreType.DMA((1, far)),
+            pltpu.SemaphoreType.DMA((16,)),
+            pltpu.SemaphoreType.DMA((16,)),
+        ],
+        compiler_params=pltpu.CompilerParams(
+            collective_id=1, has_side_effects=True, vmem_limit_bytes=60 * 1024 * 1024
+        ),
+        cost_estimate=pl.CostEstimate(
+            flops=flops, bytes_accessed=24 * 1024 * 1024, transcendentals=n_batch * n_tok * ff
+        ),
+        name="fused_mlp",
+    )(rows, own_gate, own_up, own_down, *cots)
+
+
+class RingCollect:
+    def __init__(self, place, block, got, send_sems, recv_sems):
+        self.place, self.block, self.got = place, block, got
+        self.send_sems, self.recv_sems = send_sems, recv_sems
+        self.cut = got.shape[3]
+        self.step = place.h
+        self.sent = []
+
+    def held(self, step, half):
+        return self.block(self.place.rank_of(step)).at[pl.ds(half * self.cut, self.cut)]
+
+    def hop(self, step, side, half, source):
+        place = self.place
+        return pltpu.make_async_remote_copy(
+            src_ref=source,
+            dst_ref=self.got.at[step, side, half],
+            send_sem=self.send_sems.at[step, side, half],
+            recv_sem=self.recv_sems.at[step, side, half],
+            device_id=place.up() if side else place.down(),
+            device_id_type=MESH,
+        )
+
+    def send(self, step, side, half, source):
+        copy = self.hop(step, side, half, source)
+        copy.start()
+        self.sent.append(copy)
+
+    def advance(self):
+        far = self.place.h
+        step = self.step
+        self.step -= 1
+        if step == far:
+            for side in (0, 1):
+                self.send(far - 1, side, side, self.held(far, side))
+            for side in (0, 1):
+                half = 1 - side
+                self.send(far - 2, side, half, self.held((2 * side - 1) * (far - 1), half))
+            return
+        pieces = [(0, 0), (1, 1)] if step == far - 1 else [(1, 0), (0, 1), (0, 0), (1, 1)]
+        for side, half in pieces:
+            own = self.held((2 * side - 1) * step, half)
+            self.hop(step, side, half, own).wait_recv()
+            own[...] = (own[...].astype(F32) + self.got[step, side, half].astype(F32)).astype(BF)
+            self.send(step - 1, side, half, own)
+
+    def finish(self, half):
+        own = self.held(0, half)
+        for side in (0, 1):
+            self.hop(0, side, half, own).wait_recv()
+        return (
+            own[...].astype(F32)
+            + self.got[0, 0, half].astype(F32)
+            + self.got[0, 1, half].astype(F32)
+        )
+
+    def drain(self):
+        for copy in self.sent:
+            copy.wait_send()
+
+
+def tail_kernel(
+    n_batch,
+    gain_rows,
+    out_ref,
+    up_ref,
+    in_ref,
+    gu_ref,
+    out_grad,
+    up_grad,
+    in_grad,
+    gain_grad,
+    gu_grad,
+    out_v,
+    up_v,
+    in_v,
+    out_got,
+    up_got,
+    in_got,
+    out_sum,
+    out_all,
+    up_sum,
+    up_all,
+    in_sum,
+    in_all,
+    ring_send,
+    ring_recv,
+    send_sems,
+    recv_sems,
+    load_sems,
+    out_sems,
+):
+    place = Place(n_batch)
+    copies = Copies(send_sems, recv_sems)
+    b, c, n = place.b, place.c, n_batch
+    own_rows = in_grad.shape[0]
+    index = b * 4 + c
+    slab = c * n + b
+    target = (lax.div(slab, 4), lax.rem(slab, 4))
+    source = (lax.rem(index, n), lax.div(index, n))
+    stays = slab == index
+    peers = [(lax.rem(b + k, n), c) for k in range(1, n)]
+    ctx_peers = [(b, place.far), (b, place.near), (b, lax.rem(place.near + 2, 4))]
+
+    loads = [
+        pltpu.make_async_copy(held, kept, load_sems.at[i])
+        for i, (held, kept) in enumerate([(out_ref, out_v), (up_ref, up_v), (in_ref, in_v)])
+    ]
+    for copy in loads:
+        copy.start()
+    barrier = greet(place, peers + ctx_peers)
+
+    @pl.when(jnp.logical_not(stays))
+    def _():
+        for device in (target, source):
+            pl.semaphore_signal(barrier, inc=1, device_id=device, device_id_type=MESH)
+
+    pl.semaphore_wait(barrier, n + 4 - 2 * stays.astype(jnp.int32))
+
+    rings = []
+    for i, (kept, got) in enumerate([(out_v, out_got), (up_v, up_got), (in_v, in_got)]):
+        rings.append(
+            RingCollect(
+                place,
+                lambda rank, kept=kept: kept.at[rank],
+                got,
+                ring_send.at[i],
+                ring_recv.at[i],
+            )
+        )
+    for copy, ring in zip(loads, rings):
+        copy.wait()
+        ring.advance()
+    copies.local(gu_ref.at[b], gu_grad.at[b])
+    for peer in peers:
+        copies.remote(gu_ref.at[peer[0]], gu_grad.at[b], peer)
+    for _ in range(place.h - 1):
+        for ring in rings:
+            ring.advance()
+
+    in_ring, up_ring, out_ring = rings[2], rings[1], rings[0]
+    out_cut, up_cut, in_cut = out_ring.cut, up_ring.cut, in_ring.cut
+    for half in (0, 1):
+        out_sum[pl.ds(half * out_cut, out_cut), :] = out_ring.finish(half).astype(BF)
+    out_copy = pltpu.make_async_remote_copy(
+        src_ref=out_sum,
+        dst_ref=out_all,
+        send_sem=out_sems.at[0],
+        recv_sem=out_sems.at[1],
+        device_id=target,
+        device_id_type=MESH,
+    )
+    out_stay = pltpu.make_async_copy(out_sum, out_all, out_sems.at[0])
+
+    @pl.when(jnp.logical_not(stays))
+    def _():
+        out_copy.start()
+
+    @pl.when(stays)
+    def _():
+        out_stay.start()
+
+    for half in (0, 1):
+        up_sum[pl.ds(half * up_cut, up_cut), :] = up_ring.finish(half).astype(BF)
+    up_copies = [
+        copies.remote(
+            up_sum.at[pl.ds(peer[1] * gain_rows, gain_rows)], up_all.at[c], peer
+        )
+        for peer in ctx_peers
+    ]
+    up_copies.append(
+        copies.local(up_sum.at[pl.ds(c * gain_rows, gain_rows)], up_all.at[c])
+    )
+    for half in (0, 1):
+        in_sum[pl.ds(half * in_cut, in_cut), :] = in_ring.finish(half).astype(BF)
+    part_rows = own_rows + 16
+    in_copies = [
+        copies.remote(in_sum.at[pl.ds(peer[1] * part_rows, part_rows)], in_all.at[c], peer)
+        for peer in ctx_peers
+    ]
+    in_copies.append(copies.local(in_sum.at[pl.ds(c * part_rows, part_rows)], in_all.at[c]))
+
+    @pl.when(jnp.logical_not(stays))
+    def _():
+        out_copy.wait()
+
+    @pl.when(stays)
+    def _():
+        out_stay.wait()
+
+    out_grad[...] = out_all[...].astype(F32)
+    for copy in up_copies:
+        copies.arrive(copy)
+    cols = up_all.shape[2]
+    for part in range(4):
+        up_grad[:, part * cols : (part + 1) * cols] = up_all[part].astype(F32)
+    for copy in in_copies:
+        copies.arrive(copy)
+    cols = in_all.shape[2]
+    gains = jnp.zeros(gain_grad.shape, F32)
+    for part in range(4):
+        in_grad[:, part * cols : (part + 1) * cols] = in_all[part, :own_rows, :].astype(F32)
+        gains = gains + in_all[part, own_rows:, :].astype(F32)
+    gain_grad[...] = gains
+    copies.drain()
+    for ring in rings:
+        ring.drain()
+
+
+def collect_weights(n_batch, gain_rows, out_terms, up_terms, in_terms, gu_terms):
+    far = n_batch // 2
+    out_rows, width = out_terms.shape[1:]
+    up_rows, up_cols = up_terms.shape[1:]
+    in_rows, in_cols = in_terms.shape[1:]
+    own_rows = in_rows // 4 - 16
+    shapes = [out_terms.shape[1:], up_terms.shape[1:], in_terms.shape[1:]]
+    sems = 2 * n_batch + 16
+    return pl.pallas_call(
+        functools.partial(tail_kernel, n_batch, gain_rows),
+        out_shape=(
+            jax.ShapeDtypeStruct((out_rows, width), F32),
+            jax.ShapeDtypeStruct((gain_rows, 4 * up_cols), F32),
+            jax.ShapeDtypeStruct((own_rows, 4 * in_cols), F32),
+            jax.ShapeDtypeStruct((16, in_cols), F32),
+            jax.ShapeDtypeStruct(gu_terms.shape, BF),
+        ),
+        in_specs=[pl.BlockSpec(memory_space=pl.ANY)] * 4,
+        out_specs=[pl.BlockSpec(memory_space=pltpu.VMEM)] * 4
+        + [pl.BlockSpec(memory_space=pl.ANY)],
+        scratch_shapes=[pltpu.VMEM((n_batch,) + shape, BF) for shape in shapes]
+        + [pltpu.VMEM((far, 2, 2, rows // 2, cols), BF) for rows, cols in shapes]
+        + [
+            pltpu.VMEM((out_rows, width), BF),
+            pltpu.VMEM((out_rows, width), BF),
+            pltpu.VMEM((up_rows, up_cols), BF),
+            pltpu.VMEM((4, gain_rows, up_cols), BF),
+            pltpu.VMEM((in_rows, in_cols), BF),
+            pltpu.VMEM((4, own_rows + 16, in_cols), BF),
+            pltpu.SemaphoreType.DMA((3, far, 2, 2)),
+            pltpu.SemaphoreType.DMA((3, far, 2, 2)),
+            pltpu.SemaphoreType.DMA((sems,)),
+            pltpu.SemaphoreType.DMA((sems,)),
+            pltpu.SemaphoreType.DMA((3,)),
+            pltpu.SemaphoreType.DMA((2,)),
+        ],
+        compiler_params=pltpu.CompilerParams(
+            collective_id=2, has_side_effects=True, vmem_limit_bytes=48 * 1024 * 1024
+        ),
+        name="collect_weights",
+    )(out_terms, up_terms, in_terms, gu_terms)
+
+
+def permuted_mlp(ring, rows_own, grad_mo, gu_rows, own_down):
+    mlp_in = ring.spread(rows_own)
+    n_tok, width = rows_own.shape
+    _, n_batch, n_ctx, own_rows, ff = gu_rows.shape
     own_gate, own_up = gu_rows.reshape(2, width, ff)
     own_down = own_down.reshape(ff, width)
-    slabs = slab_pairs(n_batch, n_ctx)
-    full_in = packed[:, :in_cols]
-    gains = packed[:, in_cols : in_cols + 3].T.astype(F32)
-    gain_norm = gains[0]
-    gain_mlp = gains[1]
-    gain_query = gains[2].reshape(n_batch * n_ctx, own_rows)[:, :gain_rows].reshape(QR)
-
-    residual = tokens.reshape(n_tok, width).astype(F32)
-    valid_rows = (query_pos[None, :] < own_lengths[:, None]).astype(F32).reshape(n_tok, 1)
-    grad_out = cotangent.reshape(n_tok, width).astype(F32) * valid_rows
-    with jax.named_scope('cotangent_spread'):
-        grad_mo = ring.spread(grad_out.astype(BF))
-
-    scale_one = rms_scale(residual)
-    normed_one = residual * scale_one
-    attn_in = (normed_one * gain_norm).astype(BF)
-    with jax.named_scope('attn_in_gather'):
-        attn_in_all = ctx_gather(attn_in).reshape(n_ctx * n_tok, width)
-    projected = dot(attn_in, full_in)
-    q_latent = projected[:, :QR]
-    scale_query = rms_scale(q_latent)
-    normed_query = q_latent * scale_query
-    q_normed = (normed_query * gain_query).astype(BF)
-    k_rot = rotate(
-        projected[:, QR : QR + HD].reshape(micro, pos_dev, HD), cos_own, sin_own
-    ).astype(BF)
-    v_low = projected[:, QR + HD :].astype(BF)
-    with jax.named_scope('qkv_gather'):
-        qkv_all = ctx_gather(jnp.concatenate([q_normed, k_rot.reshape(n_tok, HD), v_low], axis=1))
-    q_normed_all = qkv_all[..., :QR].reshape(n_ctx * n_tok, QR)
-
-    def by_sequence(values):
-        return (
-            values.reshape(n_ctx, micro, pos_dev, -1)
-            .swapaxes(0, 1)
-            .reshape(micro, full_length, -1)
-        )
-
-    def by_position(values):
-        return (
-            values.reshape(micro, n_ctx, pos_dev, -1)
-            .swapaxes(0, 1)
-            .reshape(n_ctx * n_tok, -1)
-        )
-
-    def split_heads(values):
-        return by_sequence(values).reshape(micro, full_length, heads, HD).swapaxes(1, 2)
-
-    def join_heads(values):
-        return by_position(values.swapaxes(1, 2).reshape(micro, full_length, heads * HD))
-
-    kv_all = by_sequence(qkv_all[..., QR:])
-    keys_all = kv_all[..., :HD]
-    values_all = kv_all[..., HD:]
-    queries = split_heads(dot(q_normed_all, own_qup))
-    q_rot = rotate(queries, cos_all, sin_all).astype(BF)
-    allowed = (key_pos[None, :] <= key_pos[:, None])[None, None] & (
-        key_pos[None, None, None, :] < own_lengths[:, None, None, None]
-    )
-    scores = jnp.einsum("shtd,sud->shtu", q_rot, keys_all, preferred_element_type=F32) * score_scale
-    masked = jnp.where(allowed, scores, -1e30)
-    row_max = jnp.max(masked, axis=-1, keepdims=True)
-    raised = jnp.exp(masked - row_max)
-    weights = raised / jnp.sum(raised, axis=-1, keepdims=True)
-    weights_low = weights.astype(BF)
-    mixed = join_heads(
-        jnp.einsum("shtu,sud->shtd", weights_low, values_all, preferred_element_type=F32).astype(BF)
-    )
-    with jax.named_scope('attended_collect'):
-        attended = ctx_collect(dot(mixed, own_out).reshape(n_ctx, n_tok, width))
-    hidden_res = residual + attended
-
-    scale_two = rms_scale(hidden_res)
-    normed_two = hidden_res * scale_two
-    with jax.named_scope('mlp_in_spread'):
-        mlp_in = ring.spread((normed_two * gain_mlp).astype(BF))
     far = ring.h
     groups = [[0]] + [[-step, step] for step in range(1, far)] + [[far]]
     out_terms = {}
@@ -647,32 +1089,166 @@
     rows, grad_rows, activated, grad_gate, grad_up = (
         jnp.concatenate(items, axis=0) for items in zip(*kept)
     )
-    with jax.named_scope('grad_mlp_in_collect'):
-        grad_mlp_in = ring.collect(lambda step: in_terms[step])
+    grad_gu = jnp.stack([dot_left_t(rows, grad_gate), dot_left_t(rows, grad_up)])
+    grad_gu = grad_gu.reshape(2, n_batch, n_ctx, own_rows, ff).transpose(2, 1, 0, 3, 4)
+    grad_down = dot_left_t(activated, grad_rows)
+    return (
+        ring.collect(lambda step: in_terms[step]),
+        ctx_collect(grad_down.reshape(n_ctx, ff // n_ctx, width)),
+        out_terms,
+        ctx_collect(grad_gu).astype(BF),
+    )
+
+
+def shards(
+    tokens,
+    cotangent,
+    lengths,
+    slot_sequence,
+    proj_in,
+    query_up,
+    proj_out,
+    attn_gain,
+    query_gain,
+    mlp_gain,
+    gate_up,
+    down_proj,
+):
+    n_ctx = lax.axis_size("ctx")
+    n_batch = lax.axis_size("batch")
+    ctx_rank = lax.axis_index("ctx")
+    batch_rank = lax.axis_index("batch")
+    ring = Ring()
+    micro, pos_dev, width = tokens.shape
+    n_tok = micro * pos_dev
+    full_length = pos_dev * n_ctx
+    heads = H // n_ctx
+    score_scale = 1.0 / math.sqrt(HD)
+    in_cols = proj_in.shape[1]
+
+    slot_total = lengths.shape[0]
+    slot_ids = jnp.arange(slot_total, dtype=jnp.int32)
+    seq_lengths = jnp.sum(
+        jnp.where(slot_sequence[:, None] == slot_ids[None, :], lengths[None, :], 0), axis=1
+    )
+    own_lengths = lax.dynamic_slice_in_dim(seq_lengths, batch_rank * micro, micro)
+    query_pos = ctx_rank * pos_dev + jnp.arange(pos_dev, dtype=jnp.int32)
+    key_pos = jnp.arange(full_length, dtype=jnp.int32)
+    cos_all, sin_all = rope_tables(key_pos)
+    cos_own, sin_own = rope_tables(query_pos)
+
+    own_rows = proj_in.shape[0]
+    gain_rows = query_gain.shape[0]
+    gains = jnp.stack(
+        [attn_gain, mlp_gain, jnp.pad(query_gain, (0, own_rows - gain_rows))], axis=1
+    )
+    packed = jnp.concatenate([proj_in, jnp.pad(gains, ((0, 0), (0, 125)))], axis=1)
+    up_parts = query_up.reshape(gain_rows, n_ctx, heads * HD).swapaxes(0, 1)
+    ff_all = gate_up.shape[1] // 2
+    ff = ff_all // n_batch
+    gu_parts = gate_up.reshape(own_rows, 2, n_batch, ff).transpose(2, 1, 0, 3)
+    packed, own_qup, own_out, gu_rows, own_down = spread_weights(
+        n_batch, packed, up_parts, proj_out, gu_parts, down_proj
+    )
+    packed = packed.reshape(width, in_cols + 128)
+    own_qup = own_qup.reshape(QR, heads * HD)
+    own_out = own_out.reshape(heads * HD, width)
+    full_in = packed[:, :in_cols]
+    gains = packed[:, in_cols : in_cols + 3].T.astype(F32)
+    gain_norm = gains[0]
+    gain_mlp = gains[1]
+    gain_query = gains[2].reshape(n_batch * n_ctx, own_rows)[:, :gain_rows].reshape(QR)
+
+    residual = tokens.reshape(n_tok, width).astype(F32)
+    valid_rows = (query_pos[None, :] < own_lengths[:, None]).astype(F32).reshape(n_tok, 1)
+    grad_out = cotangent.reshape(n_tok, width).astype(F32) * valid_rows
+    with jax.named_scope('cotangent_spread'):
+        grad_mo = ring.spread(grad_out.astype(BF))
+
+    scale_one = rms_scale(residual)
+    normed_one = residual * scale_one
+    attn_in = (normed_one * gain_norm).astype(BF)
+    with jax.named_scope('attn_in_gather'):
+        attn_in_all = ctx_gather(attn_in).reshape(n_ctx * n_tok, width)
+    projected = dot(attn_in, full_in)
+    q_latent = projected[:, :QR]
+    scale_query = rms_scale(q_latent)
+    normed_query = q_latent * scale_query
+    q_normed = (normed_query * gain_query).astype(BF)
+    k_rot = rotate(
+        projected[:, QR : QR + HD].reshape(micro, pos_dev, HD), cos_own, sin_own
+    ).astype(BF)
+    v_low = projected[:, QR + HD :].astype(BF)
+    with jax.named_scope('qkv_gather'):
+        qkv_all = ctx_gather(jnp.concatenate([q_normed, k_rot.reshape(n_tok, HD), v_low], axis=1))
+    q_normed_all = qkv_all[..., :QR].reshape(n_ctx * n_tok, QR)
+
+    def by_sequence(values):
+        return (
+            values.reshape(n_ctx, micro, pos_dev, -1)
+            .swapaxes(0, 1)
+            .reshape(micro, full_length, -1)
+        )
+
+    def by_position(values):
+        return (
+            values.reshape(micro, n_ctx, pos_dev, -1)
+            .swapaxes(0, 1)
+            .reshape(n_ctx * n_tok, -1)
+        )
+
+    def split_heads(values):
+        return by_sequence(values).reshape(micro, full_length, heads, HD).swapaxes(1, 2)
+
+    def join_heads(values):
+        return by_position(values.swapaxes(1, 2).reshape(micro, full_length, heads * HD))
+
+    kv_all = by_sequence(qkv_all[..., QR:])
+    keys_all = kv_all[..., :HD]
+    values_all = kv_all[..., HD:]
+    queries = split_heads(dot(q_normed_all, own_qup))
+    q_rot = rotate(queries, cos_all, sin_all).astype(BF)
+    allowed = (key_pos[None, :] <= key_pos[:, None])[None, None] & (
+        key_pos[None, None, None, :] < own_lengths[:, None, None, None]
+    )
+    scores = jnp.einsum("shtd,sud->shtu", q_rot, keys_all, preferred_element_type=F32) * score_scale
+    masked = jnp.where(allowed, scores, -1e30)
+    row_max = jnp.max(masked, axis=-1, keepdims=True)
+    raised = jnp.exp(masked - row_max)
+    weights = raised / jnp.sum(raised, axis=-1, keepdims=True)
+    weights_low = weights.astype(BF)
+    mixed = join_heads(
+        jnp.einsum("shtu,sud->shtd", weights_low, values_all, preferred_element_type=F32).astype(BF)
+    )
+    with jax.named_scope('attended_collect'):
+        attended = ctx_collect(dot(mixed, own_out).reshape(n_ctx, n_tok, width))
+    hidden_res = residual + attended
+
+    scale_two = rms_scale(hidden_res)
+    normed_two = hidden_res * scale_two
+    mlp_in = (normed_two * gain_mlp).astype(BF)
+    far = ring.h
+    order = [0] + [side * step for step in range(1, far) for side in (-1, 1)] + [far]
+    resident = 10 * n_batch * n_tok * width <= 24 * 1024 * 1024
+    if resident:
+        grad_mlp_in, grad_down, terms, grad_gu_own = fused_mlp(
+            n_batch, mlp_in, [grad_mo[step] for step in order], gu_rows[0], gu_rows[1], own_down
+        )
+        terms = terms.reshape(n_batch, n_tok, width)
+        spots = [0, far] + [side * step for step in range(1, far) for side in (-1, 1)]
+        out_terms = {step: terms[i] for i, step in enumerate(spots)}
+    else:
+        grad_mlp_in, grad_down, out_terms, grad_gu_own = permuted_mlp(
+            ring, mlp_in, grad_mo, gu_rows, own_down
+        )
     gain_mlp_term = jnp.sum(grad_mlp_in * normed_two, axis=0)
     grad_hidden = grad_out + norm_back(grad_mlp_in * gain_mlp, normed_two, scale_two)
     with jax.named_scope('layer_out_collect'):
         layer_out = hidden_res + ring.collect(lambda step: out_terms[step])
 
-    grad_gu_own = jnp.stack([dot_left_t(rows, grad_gate), dot_left_t(rows, grad_up)])
-    grad_gu_own = grad_gu_own.reshape(2, n_batch, n_ctx, own_rows, ff).transpose(2, 1, 0, 3, 4)
-    with jax.named_scope('grad_gate_up_collect'):
-        grad_gu_own = ctx_collect(grad_gu_own).astype(BF)
-    with jax.named_scope('grad_gate_up_exchange'):
-        grad_gu_own = batch_exchange(grad_gu_own)
-    grad_gate_up = grad_gu_own.transpose(2, 1, 0, 3).reshape(own_rows, 2 * ff_all).astype(F32)
-    grad_down_own = dot_left_t(activated, grad_rows)
-    with jax.named_scope('grad_down_collect'):
-        grad_down = ctx_collect(grad_down_own.reshape(n_ctx, ff // n_ctx, width))
-
     with jax.named_scope('grad_att_gather'):
         grad_att_all = ctx_gather(grad_hidden.astype(BF)).reshape(n_ctx * n_tok, width)
     grad_out_own = dot_left_t(mixed, grad_att_all)
-    with jax.named_scope('grad_proj_out_collect'):
-        grad_out_own = ring.collect_rows(grad_out_own.reshape(n_batch, -1, width)).astype(BF)
-        grad_proj_out = lax.ppermute(
-            grad_out_own, ("batch", "ctx"), [(there, here) for here, there in slabs]
-        ).astype(F32)
     grad_mixed = split_heads(dot_right_t(grad_att_all, own_out).astype(BF))
     grad_probs = jnp.einsum(
         "shtd,sud->shtu", grad_mixed, values_all, preferred_element_type=F32
@@ -710,14 +1286,6 @@
     grad_tokens = grad_hidden + norm_back(grad_attn_in * gain_norm, normed_one, scale_one)
 
     grad_up_own = dot_left_t(q_normed_all, grad_q)
-    with jax.named_scope('grad_query_up_collect'):
-        grad_up_own = ring.collect_rows(grad_up_own.reshape(n_batch, -1, heads * HD)).astype(BF)
-    grad_query_up = (
-        ctx_exchange(grad_up_own.reshape(n_ctx, gain_rows, heads * HD))
-        .swapaxes(0, 1)
-        .reshape(gain_rows, H * HD)
-        .astype(F32)
-    )
     part_cols = in_cols // n_ctx
     project_parts = grad_project.reshape(n_tok, n_ctx, part_cols).swapaxes(0, 1)
     with jax.named_scope('grad_project_exchange'):
@@ -738,11 +1306,16 @@
     )
     gain_terms = jnp.pad(gain_terms, ((0, 0), (0, 0), (0, 13), (0, part_cols - own_rows)))
     joined = jnp.concatenate([grad_in_own, gain_terms], axis=2).reshape(n_batch, -1, part_cols)
-    with jax.named_scope('grad_proj_in_collect'):
-        joined = ring.collect_rows(joined).astype(BF)
-    joined = ctx_exchange(joined.reshape(n_ctx, own_rows + 16, part_cols)).astype(F32)
-    grad_proj_in = joined[:, :own_rows].swapaxes(0, 1).reshape(own_rows, in_cols)
-    gain_sums = jnp.sum(joined[:, own_rows : own_rows + 3, :own_rows], axis=0)
+    grad_proj_out, grad_query_up, grad_proj_in, gain_sums, grad_gu_own = collect_weights(
+        n_batch,
+        gain_rows,
+        grad_out_own.reshape(n_batch, -1, width).astype(BF),
+        grad_up_own.reshape(n_batch, -1, heads * HD).astype(BF),
+        joined.astype(BF),
+        grad_gu_own,
+    )
+    grad_gate_up = grad_gu_own.transpose(2, 1, 0, 3).reshape(own_rows, 2 * ff_all).astype(F32)
+    gain_sums = gain_sums[:, :own_rows]
 
     return (
         layer_out.reshape(tokens.shape).astype(BF),

time: 768 us -> 692 us (0.901)
  Pallas kernels: 151 us -> 421 us
  local copies, waits for them, and re-layouts: 162 us -> 64.5 us
  waiting for transfers between devices: 167 us -> 99.1 us
  starting transfers between devices: 90.3 us -> 24 us
  matrix products: 109 us -> 43 us
  other arithmetic: 75.7 us -> 31.8 us
    pallas_call x0 -> x2, Pallas kernels: none -> 269 us  [the longest x1 141 us: collect_weights(): pl.pallas_call(functools.partial(tail_kernel, n_batch, gain_rows), out_sh...]
    dynamic_update_slice x8 -> x0, local copies, waits for them, and re-layouts: 62.5 us -> none  [place(): return lax.dynamic_update_index_in_dim(array, block, index, axis)]
    ppermute x15 -> x3, waiting for transfers between devices: 62.9 us -> 21.1 us  [collect(): downward = lax.ppermute(for_lower.astype(BF), 'batch', self.down)]
    dot_general x18 -> x3, matrix products: 36.3 us -> 5.9 us  [dot_right_t(): lax.dot_general(left_side, right_side, (((1,), (1,)), ((), ())), preferre...]
    ppermute x3, waiting for transfers between devices: 0.4 us -> 29 us  [ctx_gather(): pair = in_order(block, lax.ppermute(block, 'ctx', FAR), outer)]
    dot_general x18 -> x3, matrix products: 32.1 us -> 10.1 us  [dot(): return jnp.dot(left_side, right_side, preferred_element_type=F32)]
    ppermute x15 -> x3, starting transfers between devices: 19.5 us -> 2.16 us  [collect(): upward = lax.ppermute(for_upper.astype(BF), 'batch', self.up)]
    ppermute x6 -> x3, waiting for transfers between devices: 15.6 us -> 0.01 us  [spread(): downward = lax.ppermute(downward, 'batch', self.down)]
  transfers between devices with their start and end apart: 84 -> 28, of which waited for: 39 -> 15; matrix products, arithmetic and copies ran while one was open for 44% -> 13% of each run, Pallas kernels for 20% -> 0%
where the time goes in v3:
time: 692 us; the launch traced here: 686 us
  Pallas kernels  421 us (61%)
  waiting for transfers between devices  99.1 us (14%)
  local copies, waits for them, and re-layouts  64.5 us (9%)
  matrix products  43 us (6%)
  other arithmetic  31.8 us (5%)
  starting transfers between devices  24 us (3%)
    pallas_call x1, Pallas kernels, spread_weights(): pl.pallas_call(functools.partial(weights_kernel, n_batch), out_shape=shap...  152 us
    pallas_call x1, Pallas kernels, collect_weights(): pl.pallas_call(functools.partial(tail_kernel, n_batch, gain_rows), out_sh...  141 us
    pallas_call x1, Pallas kernels, fused_mlp(): pl.pallas_call(functools.partial(mlp_kernel, n_batch), out_shape=(jax.Sha...  128 us
    ppermute x3, waiting for transfers between devices, ctx_gather(): pair = in_order(block, lax.ppermute(block, 'ctx', FAR), outer)  29 us
    ppermute x3, waiting for transfers between devices, collect(): downward = lax.ppermute(for_lower.astype(BF), 'batch', self.down)  21.1 us
    ppermute x3, waiting for transfers between devices, collect(): upward = lax.ppermute(for_upper.astype(BF), 'batch', self.up)  15.1 us
  transfers between devices with their start and end apart: 28, of which 15 were waited for; matrix products, arithmetic and copies ran while one was open for 13% of the time, Pallas kernels for 0%

profile of v3, /device:TPU:4, one launch (start us, length us, event | category | flops | bytes accessed | tf_op | source)
XLA Modules:
  0.0 685.7 jit_solution(16007962823944371813)
XLA Ops:
  0.6 3.3 reshape.748
  7.2 151.9 %spread_weights.1 = (bf16[8,4,64,1664]{3,2,1,0:T(8,128)(2,1)}, bf16[8,4,32,1024]{3,2,1,0:T(8,128)(2,1)}, bf16[8,128,2048]{2,1,0:T(8,128)(2,1)}, bf16[2,8,4,64,704]{4,3,2,1,0:T(8,128)(2,1)}, bf16[4,176,2048]{2,1,0:T(8,128)(2,1)}) custom-call(bf16[64,1664]{1,0:T(8,128)(2,1)} %fusion.51.packed_ref, bf16[4,32,1024]{2,1,0:T(8,128)(2,1)} %bitcast.348, ...), custom_call_target="tpu_custom_call" | custom-call | tf_op jit(solution)/shard_map/spread_weights/pallas_call | solution.py:461
  161.7 4.0 fusion.3
  171.7 7.9 %collective-permute-done = bf16[128,1536]{1,0:T(8,128)(2,1)S(1)} collective-permute-done((bf16[128,1536]{1,0:T(8,128)(2,1)S(1)}, bf16[128,1536]{1,0:T(8,128)(2,1)S(1)}, u32[]{:S(2)}, u32[]{:S(2)}) %collective-permute-start) | collective-permute-done | bytes 393248 | tf_op jit(solution)/shard_map/qkv_gather/ppermute | solution.py:156
  198.3 4.8 fusion.9
  204.8 4.9 fusion.69
  213.8 12.6 %collective-permute-done.8.refs_5_ = bf16[128,2048]{1,0:T(8,128)(2,1)} collective-permute-done((bf16[128,2048]{1,0:T(8,128)(2,1)}, bf16[128,2048]{1,0:T(8,128)(2,1)}, u32[]{:S(2)}, u32[]{:S(2)}) %collective-permute-start.8) | collective-permute-done | bytes 524320 | tf_op jit(solution)/shard_map/cotangent_spread/ppermute | solution.py:93
  234.2 6.2 slice_bitcast_fusion
  241.2 4.5 collective-permute-done.3
  246.9 128.3 %fused_mlp.1 = (f32[128,2048]{1,0:T(8,128)}, f32[176,2048]{1,0:T(8,128)}, bf16[4,256,2048]{2,1,0:T(8,128)(2,1)}, bf16[8,2,64,704]{3,2,1,0:T(8,128)(2,1)}) custom-call(bf16[128,2048]{1,0:T(8,128)(2,1)} %multiply_convert_fusion.1.rows_ref, bf16[8,4,64,704]{3,2,1,0:T(8,128)(2,1)} %get-tuple-element.49.gate_ref, ...), custom_call_target="tpu_custom_call" | custom-call | flops 26575110144 | bytes 25165824 | tf_op jit(solution)/shard_map/fused_mlp/pallas_call | solution.py:761
  378.7 6.2 collective-permute-done.12
  389.5 9.4 %collective-permute-done.13 = bf16[128,2048]{1,0:T(8,128)(2,1)S(1)} collective-permute-done((bf16[128,2048]{1,0:T(8,128)(2,1)S(1)}, bf16[128,2048]{1,0:T(8,128)(2,1)S(1)}, u32[]{:S(2)}, u32[]{:S(2)}) %collective-permute-start.13) | collective-permute-done | bytes 524320 | tf_op jit(solution)/shard_map/layer_out_collect/ppermute | solution.py:132
  400.9 11.6 %collective-permute-done.14 = bf16[128,2048]{1,0:T(8,128)(2,1)S(1)} collective-permute-done((bf16[128,2048]{1,0:T(8,128)(2,1)S(1)}, bf16[128,2048]{1,0:T(8,128)(2,1)S(1)}, u32[]{:S(2)}, u32[]{:S(2)}) %collective-permute-start.14) | collective-permute-done | bytes 524320 | tf_op jit(solution)/shard_map/layer_out_collect/ppermute | solution.py:132
  415.0 7.2 %collective-permute-done.18 = bf16[128,2048]{1,0:T(8,128)(2,1)S(1)} collective-permute-done((bf16[128,2048]{1,0:T(8,128)(2,1)S(1)}, bf16[128,2048]{1,0:T(8,128)(2,1)S(1)}, u32[]{:S(2)}, u32[]{:S(2)}) %collective-permute-start.18) | collective-permute-done | bytes 524320 | tf_op jit(solution)/shard_map/layer_out_collect/ppermute | solution.py:133
  423.6 7.9 %collective-permute-done.19 = bf16[128,2048]{1,0:T(8,128)(2,1)S(1)} collective-permute-done((bf16[128,2048]{1,0:T(8,128)(2,1)S(1)}, bf16[128,2048]{1,0:T(8,128)(2,1)S(1)}, u32[]{:S(2)}, u32[]{:S(2)}) %collective-permute-start.19) | collective-permute-done | bytes 524320 | tf_op jit(solution)/shard_map/layer_out_collect/ppermute | solution.py:133
  434.4 8.1 %collective-permute-done.20 = bf16[128,2048]{1,0:T(8,128)(2,1)S(1)} collective-permute-done((bf16[128,2048]{1,0:T(8,128)(2,1)S(1)}, bf16[128,2048]{1,0:T(8,128)(2,1)S(1)}, u32[]{:S(2)}, u32[]{:S(2)}) %collective-permute-start.20) | collective-permute-done | bytes 524320 | tf_op jit(solution)/shard_map/grad_att_gather/ppermute | solution.py:156
  444.2 12.9 %collective-permute-done.24 = bf16[128,2048]{1,0:T(8,128)(2,1)S(1)} collective-permute-done((bf16[128,2048]{1,0:T(8,128)(2,1)S(1)}, bf16[128,2048]{1,0:T(8,128)(2,1)S(1)}, u32[]{:S(2)}, u32[]{:S(2)}) %collective-permute-start.24) | collective-permute-done | bytes 524320 | tf_op jit(solution)/shard_map/attn_in_gather/ppermute | solution.py:156
  468.4 5.8 fusion.12
  504.4 4.4 convolution_convert_fusion.out_ref
  511.4 3.5 collective-permute-done.23
  520.8 4.1 collective-permute-done.26
  531.4 140.8 %collect_weights.1 = (f32[128,2048]{1,0:T(8,128)S(1)}, f32[32,4096]{1,0:T(8,128)S(1)}, f32[64,1536]{1,0:T(8,128)S(1)}, f32[16,384]{1,0:T(8,128)S(1)}, bf16[8,2,64,704]{3,2,1,0:T(8,128)(2,1)S(1)}) custom-call(bf16[8,128,2048]{2,1,0:T(8,128)(2,1)} %convolution_convert_fusion.out_ref, bf16[8,128,1024]{2,1,0:T(8,128)(2,1)} %convolution_convert_fusion.1.up_ref, ...), custom_call_target="tpu_custom_call" | custom-call | tf_op jit(solution)/shard_map/collect_weights/pallas_call | solution.py:1023
  673.5 3.5 copy.201
  677.0 4.7 reshape.781
  (311 shorter events, 125.0 us)
Async XLA Ops:
  168.1 11.5 %collective-permute-start = (bf16[128,1536]{1,0:T(8,128)(2,1)S(1)}, bf16[128,1536]{1,0:T(8,128)(2,1)S(1)}, u32[]{:S(2)}, u32[]{:S(2)}) collective-permute-start(bf16[128,1536]{1,0:T(8,128)(2,1)S(1)} %get-tuple-element.69), channel_id=1, source_target_pairs={{0,2},{1,3},{2,0},{3,1},{4,6},{5,7},{6,4},{7,5},{8,10},{9,11},{10,... | collective-permute-start | bytes 1179656 | tf_op jit(solution)/shard_map/qkv_gather/ppermute | solution.py:156
  169.6 14.6 %collective-permute-start.4 = (bf16[128,2048]{1,0:T(8,128)(2,1)}, bf16[128,2048]{1,0:T(8,128)(2,1)}, u32[]{:S(2)}, u32[]{:S(2)}) collective-permute-start(bf16[128,2048]{1,0:T(8,128)(2,1)} %fusion.22.refs_0_), channel_id=1, source_target_pairs={{0,8},{8,16},{16,24},{24,28},{28,20},{20,12},{12,4},{4,0},{1,9},{9... | collective-permute-start | bytes 1572872 | tf_op jit(solution)/shard_map/cotangent_spread/ppermute | solution.py:93
  171.5 14.6 %collective-permute-start.5 = (bf16[128,2048]{1,0:T(8,128)(2,1)}, bf16[128,2048]{1,0:T(8,128)(2,1)}, u32[]{:S(2)}, u32[]{:S(2)}) collective-permute-start(bf16[128,2048]{1,0:T(8,128)(2,1)} %fusion.22.refs_0_), channel_id=1, source_target_pairs={{8,0},{16,8},{24,16},{28,24},{20,28},{12,20},{4,12},{0,4},{9,1},{1... | collective-permute-start | bytes 1572872 | tf_op jit(solution)/shard_map/cotangent_spread/ppermute | solution.py:94
  184.2 27.5 %collective-permute-start.6 = (bf16[128,2048]{1,0:T(8,128)(2,1)}, bf16[128,2048]{1,0:T(8,128)(2,1)}, u32[]{:S(2)}, u32[]{:S(2)}) collective-permute-start(bf16[128,2048]{1,0:T(8,128)(2,1)} %collective-permute-done.4.refs_1_), channel_id=1, source_target_pairs={{0,8},{8,16},{16,24},{24,28},{28,20},{20,12},{12,4},{4,0},{1,9},{9... | collective-permute-start | bytes 1572872 | tf_op jit(solution)/shard_map/cotangent_spread/ppermute | solution.py:93
  186.1 27.5 %collective-permute-start.7 = (bf16[128,2048]{1,0:T(8,128)(2,1)}, bf16[128,2048]{1,0:T(8,128)(2,1)}, u32[]{:S(2)}, u32[]{:S(2)}) collective-permute-start(bf16[128,2048]{1,0:T(8,128)(2,1)} %collective-permute-done.5.refs_2_), channel_id=1, source_target_pairs={{8,0},{16,8},{24,16},{28,24},{20,28},{12,20},{4,12},{0,4},{9,1},{1... | collective-permute-start | bytes 1572872 | tf_op jit(solution)/shard_map/cotangent_spread/ppermute | solution.py:94
  211.7 18.7 %collective-permute-start.2 = (bf16[2,128,2048]{2,1,0:T(8,128)(2,1)S(1)}, bf16[2,128,2048]{2,1,0:T(8,128)(2,1)S(1)}, u32[]{:S(2)}, u32[]{:S(2)}) collective-permute-start(bf16[2,128,2048]{2,1,0:T(8,128)(2,1)S(1)} %fusion.13), channel_id=1, source_target_pairs={{0,1},{1,0},{2,3},{3,2},{4,5},{5,4},{6,7},{7,6},{8,9},{9,8},{10,11... | collective-permute-start | bytes 3145736 | tf_op jit(solution)/shard_map/attended_collect/ppermute | solution.py:165
  211.7 14.7 %collective-permute-start.8 = (bf16[128,2048]{1,0:T(8,128)(2,1)}, bf16[128,2048]{1,0:T(8,128)(2,1)}, u32[]{:S(2)}, u32[]{:S(2)}) collective-permute-start(bf16[128,2048]{1,0:T(8,128)(2,1)} %collective-permute-done.6.refs_3_), channel_id=1, source_target_pairs={{0,8},{8,16},{16,24},{24,28},{28,20},{20,12},{12,4},{4,0},{1,9},{9... | collective-permute-start | bytes 1572872 | tf_op jit(solution)/shard_map/cotangent_spread/ppermute | solution.py:93
  213.6 15.7 %collective-permute-start.9 = (bf16[128,2048]{1,0:T(8,128)(2,1)}, bf16[128,2048]{1,0:T(8,128)(2,1)}, u32[]{:S(2)}, u32[]{:S(2)}) collective-permute-start(bf16[128,2048]{1,0:T(8,128)(2,1)} %collective-permute-done.7.refs_4_), channel_id=1, source_target_pairs={{8,0},{16,8},{24,16},{28,24},{20,28},{12,20},{4,12},{0,4},{9,1},{1... | collective-permute-start | bytes 1572872 | tf_op jit(solution)/shard_map/cotangent_spread/ppermute | solution.py:94
  227.4 13.0 %collective-permute-start.10 = (bf16[64,2048]{1,0:T(8,128)(2,1)S(1)}, bf16[64,2048]{1,0:T(8,128)(2,1)S(1)}, u32[]{:S(2)}, u32[]{:S(2)}) collective-permute-start(bf16[64,2048]{1,0:T(8,128)(2,1)S(1)} %slice.235), channel_id=1, source_target_pairs={{0,8},{8,16},{16,24},{24,28},{28,20},{20,12},{12,4},{4,0},{1,9},{9... | collective-permute-start | bytes 786440 | tf_op jit(solution)/shard_map/cotangent_spread/ppermute | solution.py:100
  230.3 10.1 %collective-permute-start.11 = (bf16[64,2048]{1,0:T(8,128)(2,1)S(1)}, bf16[64,2048]{1,0:T(8,128)(2,1)S(1)}, u32[]{:S(2)}, u32[]{:S(2)}) collective-permute-start(bf16[64,2048]{1,0:T(8,128)(2,1)S(1)} %slice.236), channel_id=1, source_target_pairs={{8,0},{16,8},{24,16},{28,24},{20,28},{12,20},{4,12},{0,4},{9,1},{1... | collective-permute-start | bytes 786440 | tf_op jit(solution)/shard_map/cotangent_spread/ppermute | solution.py:101
  232.4 13.2 %collective-permute-start.3 = (bf16[128,2048]{1,0:T(8,128)(2,1)S(1)}, bf16[128,2048]{1,0:T(8,128)(2,1)S(1)}, u32[]{:S(2)}, u32[]{:S(2)}) collective-permute-start(bf16[128,2048]{1,0:T(8,128)(2,1)S(1)} %fusion.39), channel_id=1, source_target_pairs={{0,2},{1,3},{2,0},{3,1},{4,6},{5,7},{6,4},{7,5},{8,10},{9,11},{10,... | collective-permute-start | bytes 1572872 | tf_op jit(solution)/shard_map/attended_collect/ppermute | solution.py:167
  376.7 9.3 %collective-permute-start.16 = (bf16[64,2048]{1,0:T(8,128)(2,1)S(1)}, bf16[64,2048]{1,0:T(8,128)(2,1)S(1)}, u32[]{:S(2)}, u32[]{:S(2)}) collective-permute-start(bf16[64,2048]{1,0:T(8,128)(2,1)S(1)} %get-tuple-element.55), channel_id=1, source_target_pairs={{0,8},{8,16},{16,24},{24,28},{28,20},{20,12},{12,4},{4,0},{1,9},{9... | collective-permute-start | bytes 786440 | tf_op jit(solution)/shard_map/layer_out_collect/ppermute | solution.py:118
  387.2 11.8 %collective-permute-start.13 = (bf16[128,2048]{1,0:T(8,128)(2,1)S(1)}, bf16[128,2048]{1,0:T(8,128)(2,1)S(1)}, u32[]{:S(2)}, u32[]{:S(2)}) collective-permute-start(bf16[128,2048]{1,0:T(8,128)(2,1)S(1)} %pad_maximum_fusion.5), channel_id=1, source_target_pairs={{8,0},{16,8},{24,16},{28,24},{20,28},{12,20},{4,12},{0,4},{9,1},{1... | collective-permute-start | bytes 1572872 | tf_op jit(solution)/shard_map/layer_out_collect/ppermute | solution.py:132
  388.2 12.7 %collective-permute-start.17 = (bf16[128,2048]{1,0:T(8,128)(2,1)S(1)}, bf16[128,2048]{1,0:T(8,128)(2,1)S(1)}, u32[]{:S(2)}, u32[]{:S(2)}) collective-permute-start(bf16[128,2048]{1,0:T(8,128)(2,1)S(1)} %pad_maximum_fusion.6), channel_id=1, source_target_pairs={{0,8},{8,16},{16,24},{24,28},{28,20},{20,12},{12,4},{4,0},{1,9},{9... | collective-permute-start | bytes 1572872 | tf_op jit(solution)/shard_map/layer_out_collect/ppermute | solution.py:133
  399.1 13.4 %collective-permute-start.14 = (bf16[128,2048]{1,0:T(8,128)(2,1)S(1)}, bf16[128,2048]{1,0:T(8,128)(2,1)S(1)}, u32[]{:S(2)}, u32[]{:S(2)}) collective-permute-start(bf16[128,2048]{1,0:T(8,128)(2,1)S(1)} %fusion.16), channel_id=1, source_target_pairs={{8,0},{16,8},{24,16},{28,24},{20,28},{12,20},{4,12},{0,4},{9,1},{1... | collective-permute-start | bytes 1572872 | tf_op jit(solution)/shard_map/layer_out_collect/ppermute | solution.py:132
  412.9 9.2 %collective-permute-start.18 = (bf16[128,2048]{1,0:T(8,128)(2,1)S(1)}, bf16[128,2048]{1,0:T(8,128)(2,1)S(1)}, u32[]{:S(2)}, u32[]{:S(2)}) collective-permute-start(bf16[128,2048]{1,0:T(8,128)(2,1)S(1)} %get-tuple-element.51), channel_id=1, source_target_pairs={{0,8},{8,16},{16,24},{24,28},{28,20},{20,12},{12,4},{4,0},{1,9},{9... | collective-permute-start | bytes 1572872 | tf_op jit(solution)/shard_map/layer_out_collect/ppermute | solution.py:133
  413.3 10.3 %collective-permute-start.15 = (bf16[128,2048]{1,0:T(8,128)(2,1)S(1)}, bf16[128,2048]{1,0:T(8,128)(2,1)S(1)}, u32[]{:S(2)}, u32[]{:S(2)}) collective-permute-start(bf16[128,2048]{1,0:T(8,128)(2,1)S(1)} %get-tuple-element.50), channel_id=1, source_target_pairs={{8,0},{16,8},{24,16},{28,24},{20,28},{12,20},{4,12},{0,4},{9,1},{1... | collective-permute-start | bytes 1572872 | tf_op jit(solution)/shard_map/layer_out_collect/ppermute | solution.py:132
  422.3 9.2 %collective-permute-start.19 = (bf16[128,2048]{1,0:T(8,128)(2,1)S(1)}, bf16[128,2048]{1,0:T(8,128)(2,1)S(1)}, u32[]{:S(2)}, u32[]{:S(2)}) collective-permute-start(bf16[128,2048]{1,0:T(8,128)(2,1)S(1)} %fusion.15), channel_id=1, source_target_pairs={{0,8},{8,16},{16,24},{24,28},{28,20},{20,12},{12,4},{4,0},{1,9},{9... | collective-permute-start | bytes 1572872 | tf_op jit(solution)/shard_map/layer_out_collect/ppermute | solution.py:133
  433.3 9.2 %collective-permute-start.20 = (bf16[128,2048]{1,0:T(8,128)(2,1)S(1)}, bf16[128,2048]{1,0:T(8,128)(2,1)S(1)}, u32[]{:S(2)}, u32[]{:S(2)}) collective-permute-start(bf16[128,2048]{1,0:T(8,128)(2,1)S(1)} %get-tuple-element.44), channel_id=1, source_target_pairs={{0,2},{1,3},{2,0},{3,1},{4,6},{5,7},{6,4},{7,5},{8,10},{9,11},{10,... | collective-permute-start | bytes 1572872 | tf_op jit(solution)/shard_map/grad_att_gather/ppermute | solution.py:156
  442.7 15.8 %collective-permute-start.21 = (bf16[2,128,2048]{2,1,0:T(8,128)(2,1)S(1)}, bf16[2,128,2048]{2,1,0:T(8,128)(2,1)S(1)}, u32[]{:S(2)}, u32[]{:S(2)}) collective-permute-start(bf16[2,128,2048]{2,1,0:T(8,128)(2,1)S(1)} %maximum_select_fusion.4), channel_id=1, source_target_pairs={{0,1},{1,0},{2,3},{3,2},{4,5},{5,4},{6,7},{7,6},{8,9},{9,8},{10,11... | collective-permute-start | bytes 3145736 | tf_op jit(solution)/shard_map/grad_att_gather/ppermute | solution.py:157
  442.8 14.3 %collective-permute-start.24 = (bf16[128,2048]{1,0:T(8,128)(2,1)S(1)}, bf16[128,2048]{1,0:T(8,128)(2,1)S(1)}, u32[]{:S(2)}, u32[]{:S(2)}) collective-permute-start(bf16[128,2048]{1,0:T(8,128)(2,1)S(1)} %copy-done.28), channel_id=1, source_target_pairs={{0,2},{1,3},{2,0},{3,1},{4,6},{5,7},{6,4},{7,5},{8,10},{9,11},{10,... | collective-permute-start | bytes 1572872 | tf_op jit(solution)/shard_map/attn_in_gather/ppermute | solution.py:156
  458.3 38.2 %collective-permute-start.25 = (bf16[2,128,2048]{2,1,0:T(8,128)(2,1)}, bf16[2,128,2048]{2,1,0:T(8,128)(2,1)}, u32[]{:S(2)}, u32[]{:S(2)}) collective-permute-start(bf16[2,128,2048]{2,1,0:T(8,128)(2,1)} %maximum_select_fusion.6), channel_id=1, source_target_pairs={{0,1},{1,0},{2,3},{3,2},{4,5},{5,4},{6,7},{7,6},{8,9},{9,8},{10,11... | collective-permute-start | bytes 3145736 | tf_op jit(solution)/shard_map/attn_in_gather/ppermute | solution.py:157
  491.6 9.8 %collective-permute-start.22 = (bf16[2,128,1536]{2,1,0:T(8,128)(2,1)}, bf16[2,128,1536]{2,1,0:T(8,128)(2,1)}, u32[]{:S(2)}, u32[]{:S(2)}) collective-permute-start(bf16[2,128,1536]{2,1,0:T(8,128)(2,1)} %fusion.31), channel_id=1, source_target_pairs={{0,1},{1,0},{2,3},{3,2},{4,5},{5,4},{6,7},{7,6},{8,9},{9,8},{10,11... | collective-permute-start | bytes 2359304 | tf_op jit(solution)/shard_map/back_collect/ppermute | solution.py:165
  503.3 11.6 %collective-permute-start.23 = (bf16[128,1536]{1,0:T(8,128)(2,1)S(1)}, bf16[128,1536]{1,0:T(8,128)(2,1)S(1)}, u32[]{:S(2)}, u32[]{:S(2)}) collective-permute-start(bf16[128,1536]{1,0:T(8,128)(2,1)S(1)} %fusion.50), channel_id=1, source_target_pairs={{0,2},{1,3},{2,0},{3,1},{4,6},{5,7},{6,4},{7,5},{8,10},{9,11},{10,... | collective-permute-start | bytes 1179656 | tf_op jit(solution)/shard_map/back_collect/ppermute | solution.py:167
  (67 other events, 310.1 us)

commit v4 on v3

--- a/solution.py
+++ b/solution.py
@@ -479,9 +479,9 @@
     gate_ref,
     up_ref,
     down_ref,
+    cot_ref,
     *refs,
 ):
-    cot_refs = refs[:n_batch]
     (
         sum_ref,
         down_grad,
@@ -510,7 +510,7 @@
         store_sems,
         part_send,
         part_recv,
-    ) = refs[n_batch:]
+    ) = refs
     place = Place(n_batch)
     far = place.h
     n_tok = rows_ref.shape[0]
@@ -532,11 +532,12 @@
             [(gate_ref, gate_v), (up_ref, up_v), (down_ref, down_v)]
         )
     ]
-    spots = [(0, 0)] + [(s, k) for s in range(1, far) for k in (0, 1)] + [(0, 1)]
-    for i, (source, (group, side)) in enumerate(zip(cot_refs, spots)):
+    spots = [(0, 0, 0), (far, 0, 1)]
+    spots += [(side * step, step, (side + 1) // 2) for step in range(1, far) for side in (-1, 1)]
+    for i, (distance, group, side) in enumerate(spots):
         loads.append(
             pltpu.make_async_copy(
-                source, cot_v.at[group, pl.ds(side * n_tok, n_tok)], load_sems.at[4 + i]
+                cot_ref.at[place.rank_of(distance)], cot_v.at[group, pl.ds(side * n_tok, n_tok)], load_sems.at[4 + i]
             )
         )
     for copy in loads:
@@ -766,7 +767,7 @@
             jax.ShapeDtypeStruct((far, pair, width), BF),
             jax.ShapeDtypeStruct((n_batch, 2, own_rows, ff), BF),
         ),
-        in_specs=[pl.BlockSpec(memory_space=pl.ANY)] * (4 + n_batch),
+        in_specs=[pl.BlockSpec(memory_space=pl.ANY)] * 5,
         out_specs=[pl.BlockSpec(memory_space=pltpu.VMEM)] * 2
         + [pl.BlockSpec(memory_space=pl.ANY)] * 2,
         scratch_shapes=[
@@ -801,7 +802,7 @@
             flops=flops, bytes_accessed=24 * 1024 * 1024, transcendentals=n_batch * n_tok * ff
         ),
         name="fused_mlp",
-    )(rows, own_gate, own_up, own_down, *cots)
+    )(rows, own_gate, own_up, own_down, cots)
 
 
 class RingCollect:
@@ -813,7 +814,7 @@
         self.sent = []
 
     def held(self, step, half):
-        return self.block(self.place.rank_of(step)).at[pl.ds(half * self.cut, self.cut)]
+        return self.block(step).at[pl.ds(half * self.cut, self.cut)]
 
     def hop(self, step, side, half, source):
         place = self.place
@@ -869,13 +870,13 @@
     gain_rows,
     out_ref,
     up_ref,
-    in_ref,
-    gu_ref,
+    project_ref,
+    rows_ref,
+    gain_ref,
     out_grad,
     up_grad,
     in_grad,
     gain_grad,
-    gu_grad,
     out_v,
     up_v,
     in_v,
@@ -892,6 +893,8 @@
     ring_recv,
     send_sems,
     recv_sems,
+    project_v,
+    rows_v,
     load_sems,
     out_sems,
 ):
@@ -904,41 +907,63 @@
     target = (lax.div(slab, 4), lax.rem(slab, 4))
     source = (lax.rem(index, n), lax.div(index, n))
     stays = slab == index
-    peers = [(lax.rem(b + k, n), c) for k in range(1, n)]
     ctx_peers = [(b, place.far), (b, place.near), (b, lax.rem(place.near + 2, 4))]
 
     loads = [
         pltpu.make_async_copy(held, kept, load_sems.at[i])
-        for i, (held, kept) in enumerate([(out_ref, out_v), (up_ref, up_v), (in_ref, in_v)])
+        for i, (held, kept) in enumerate([(out_ref, out_v), (up_ref, up_v), (rows_ref, rows_v)])
     ]
     for copy in loads:
         copy.start()
-    barrier = greet(place, peers + ctx_peers)
+    barrier = greet(place, [place.up(), place.down()] + ctx_peers)
 
     @pl.when(jnp.logical_not(stays))
     def _():
         for device in (target, source):
             pl.semaphore_signal(barrier, inc=1, device_id=device, device_id_type=MESH)
 
-    pl.semaphore_wait(barrier, n + 4 - 2 * stays.astype(jnp.int32))
+    pl.semaphore_wait(barrier, 7 - 2 * stays.astype(jnp.int32))
 
     rings = []
     for i, (kept, got) in enumerate([(out_v, out_got), (up_v, up_got), (in_v, in_got)]):
         rings.append(
             RingCollect(
                 place,
-                lambda rank, kept=kept: kept.at[rank],
+                lambda step, kept=kept: kept.at[place.rank_of(step)],
                 got,
                 ring_send.at[i],
                 ring_recv.at[i],
             )
         )
-    for copy, ring in zip(loads, rings):
+    part_cols = project_ref.shape[2]
+    project_copies = [
+        copies.remote(project_ref.at[peer[1]], project_v.at[c], peer) for peer in ctx_peers
+    ]
+    project_copies.append(copies.local(project_ref.at[c], project_v.at[c]))
+    for copy, ring in zip(loads[:2], rings):
         copy.wait()
         ring.advance()
-    copies.local(gu_ref.at[b], gu_grad.at[b])
-    for peer in peers:
-        copies.remote(gu_ref.at[peer[0]], gu_grad.at[b], peer)
+    for copy in project_copies:
+        copies.arrive(copy)
+    loads[2].wait()
+    project = project_v[...].reshape(-1, part_cols)
+    part_rows = own_rows + 16
+    n_all = project.shape[0]
+    width = rows_ref.shape[3]
+    ahead = max(1, 256 // (4 * own_rows))
+    chunk = ahead * 4 * own_rows
+
+    @pl.loop(0, width // chunk)
+    def _(t):
+        cols = pl.ds(pl.multiple_of(t * chunk, chunk), chunk)
+        term = dot_left_t(rows_v[:, :, :, cols].reshape(n_all, chunk), project).astype(BF)
+        term = term.reshape(ahead, 4, own_rows, part_cols)
+        for part in range(4):
+            in_v[pl.ds(t * ahead, ahead), pl.ds(part * part_rows, own_rows), :] = term[:, part]
+
+    for part in range(4):
+        in_v[:, part * part_rows + own_rows : (part + 1) * part_rows, :] = gain_ref[:, part]
+    rings[2].advance()
     for _ in range(place.h - 1):
         for ring in rings:
             ring.advance()
@@ -978,7 +1003,6 @@
     )
     for half in (0, 1):
         in_sum[pl.ds(half * in_cut, in_cut), :] = in_ring.finish(half).astype(BF)
-    part_rows = own_rows + 16
     in_copies = [
         copies.remote(in_sum.at[pl.ds(peer[1] * part_rows, part_rows)], in_all.at[c], peer)
         for peer in ctx_peers
@@ -1012,13 +1036,14 @@
         ring.drain()
 
 
-def collect_weights(n_batch, gain_rows, out_terms, up_terms, in_terms, gu_terms):
+def collect_weights(n_batch, gain_rows, out_terms, up_terms, project, attn_in_all, gain_terms):
     far = n_batch // 2
     out_rows, width = out_terms.shape[1:]
     up_rows, up_cols = up_terms.shape[1:]
-    in_rows, in_cols = in_terms.shape[1:]
-    own_rows = in_rows // 4 - 16
-    shapes = [out_terms.shape[1:], up_terms.shape[1:], in_terms.shape[1:]]
+    in_cols = project.shape[2]
+    own_rows = width // (4 * n_batch)
+    in_rows = 4 * (own_rows + 16)
+    shapes = [out_terms.shape[1:], up_terms.shape[1:], (in_rows, in_cols)]
     sems = 2 * n_batch + 16
     return pl.pallas_call(
         functools.partial(tail_kernel, n_batch, gain_rows),
@@ -1027,11 +1052,9 @@
             jax.ShapeDtypeStruct((gain_rows, 4 * up_cols), F32),
             jax.ShapeDtypeStruct((own_rows, 4 * in_cols), F32),
             jax.ShapeDtypeStruct((16, in_cols), F32),
-            jax.ShapeDtypeStruct(gu_terms.shape, BF),
         ),
-        in_specs=[pl.BlockSpec(memory_space=pl.ANY)] * 4,
-        out_specs=[pl.BlockSpec(memory_space=pltpu.VMEM)] * 4
-        + [pl.BlockSpec(memory_space=pl.ANY)],
+        in_specs=[pl.BlockSpec(memory_space=pl.ANY)] * 4 + [pl.BlockSpec(memory_space=pltpu.VMEM)],
+        out_specs=[pl.BlockSpec(memory_space=pltpu.VMEM)] * 4,
         scratch_shapes=[pltpu.VMEM((n_batch,) + shape, BF) for shape in shapes]
         + [pltpu.VMEM((far, 2, 2, rows // 2, cols), BF) for rows, cols in shapes]
         + [
@@ -1045,6 +1068,8 @@
             pltpu.SemaphoreType.DMA((3, far, 2, 2)),
             pltpu.SemaphoreType.DMA((sems,)),
             pltpu.SemaphoreType.DMA((sems,)),
+            pltpu.VMEM(project.shape, BF),
+            pltpu.VMEM(attn_in_all.shape, BF),
             pltpu.SemaphoreType.DMA((3,)),
             pltpu.SemaphoreType.DMA((2,)),
         ],
@@ -1052,10 +1077,487 @@
             collective_id=2, has_side_effects=True, vmem_limit_bytes=48 * 1024 * 1024
         ),
         name="collect_weights",
-    )(out_terms, up_terms, in_terms, gu_terms)
-
-
-def permuted_mlp(ring, rows_own, grad_mo, gu_rows, own_down):
+    )(out_terms, up_terms, project, attn_in_all, gain_terms)
+
+
+class CtxCollect:
+    def __init__(self, place, copies, part, near_got, far_got):
+        self.place, self.copies, self.part = place, copies, part
+        self.near_got, self.far_got = near_got, far_got
+        self.near = {}
+        self.far = {}
+
+    def start(self, item):
+        place = self.place
+        self.near[item] = [
+            self.copies.remote(
+                self.part.at[2 * side + 1 - place.inner, item],
+                self.near_got.at[side, item],
+                (place.b, place.near),
+            )
+            for side in (0, 1)
+        ]
+
+    def cross(self, item):
+        place = self.place
+        for copy in self.near[item]:
+            self.copies.arrive(copy)
+        other = self.part.at[2 * (1 - place.outer) + place.inner, item]
+        added = other[...].astype(F32) + self.near_got[1 - place.outer, item].astype(F32)
+        other[...] = added.astype(BF)
+        self.far[item] = self.copies.remote(
+            other, self.far_got.at[item], (place.b, place.far)
+        )
+
+    def finish(self, item):
+        place = self.place
+        self.copies.arrive(self.far[item])
+        return (
+            self.part[2 * place.outer + place.inner, item].astype(F32)
+            + self.near_got[place.outer, item].astype(F32)
+            + self.far_got[item].astype(F32)
+        )
+
+
+class CtxGather:
+    def __init__(self, place, copies, everyone):
+        self.place, self.copies, self.everyone = place, copies, everyone
+        self.far = {}
+        self.near = {}
+
+    def start(self, item):
+        place = self.place
+        own = self.everyone.at[place.c, item]
+        self.far[item] = self.copies.remote(own, own, (place.b, place.far))
+        self.near[item] = [self.copies.remote(own, own, (place.b, place.near))]
+
+    def cross(self, item):
+        place = self.place
+        self.copies.arrive(self.far[item])
+        other = self.everyone.at[place.far, item]
+        self.near[item].append(self.copies.remote(other, other, (place.b, place.near)))
+
+    def finish(self, item):
+        for copy in self.near[item]:
+            self.copies.arrive(copy)
+
+
+def greet_lines(place):
+    devices = [place.up(), place.down(), (place.b, place.far), (place.b, place.near)]
+    pl.semaphore_wait(greet(place, devices), 4)
+
+
+def turn(values, cosine, sine):
+    half_size = HD // 2
+    front, back = values[:, :half_size], values[:, half_size:]
+    return front * cosine - back * sine, back * cosine + front * sine
+
+
+def softmax_rows(queries, keys, keep, score_scale):
+    scores = dot_right_t(queries, keys) * score_scale
+    rows = lax.broadcasted_iota(jnp.int32, scores.shape, 0)
+    cols = lax.broadcasted_iota(jnp.int32, scores.shape, 1)
+    masked = jnp.where((cols <= rows) & (keep > 0.5), scores, -1e30)
+    raised = jnp.exp(masked - jnp.max(masked, axis=-1, keepdims=True))
+    return raised / jnp.sum(raised, axis=-1, keepdims=True)
+
+
+def attention_kernel(
+    n_batch,
+    heads,
+    qkv_ref,
+    rows_ref,
+    cot_ref,
+    up_ref,
+    out_ref,
+    cos_ref,
+    sin_ref,
+    keep_ref,
+    attended,
+    qkv_out,
+    turned_out,
+    mixed_out,
+    rows_all,
+    cot_all,
+    qkv_v,
+    up_v,
+    out_v,
+    turned_v,
+    mixed_v,
+    part_v,
+    near_got,
+    far_got,
+    send_sems,
+    recv_sems,
+    load_sems,
+):
+    place = Place(n_batch)
+    copies = Copies(send_sems, recv_sems)
+    b, c = place.b, place.c
+    micro, pos_dev = qkv_ref.shape[:2]
+    n_tok = micro * pos_dev
+    length = 4 * pos_dev
+    score_scale = 1.0 / math.sqrt(HD)
+    loads = [
+        pltpu.make_async_copy(source, target, load_sems.at[i])
+        for i, (source, target) in enumerate(
+            [(qkv_ref, qkv_v.at[c]), (up_ref, up_v), (out_ref, out_v)]
+        )
+    ]
+    for copy in loads:
+        copy.start()
+    greet_lines(place)
+    loads[0].wait()
+    qkv = CtxGather(place, copies, qkv_v)
+    for item in range(micro):
+        qkv.start(item)
+    cot_own = copies.local(cot_ref, cot_all.at[b])
+    rows_own = copies.local(rows_ref, rows_all.at[c, 0])
+    copies.arrive(cot_own)
+    cots = RingGather(place, copies, n_tok, lambda rank, rows: cot_all.at[rank, rows])
+    cots.advance()
+    copies.arrive(rows_own)
+    rows = CtxGather(place, copies, rows_all)
+    for item in range(micro):
+        qkv.cross(item)
+    rows.start(0)
+    for copy in loads[1:]:
+        copy.wait()
+    attended_sum = CtxCollect(place, copies, part_v, near_got, far_got)
+    cosine, sine = cos_ref[...], sin_ref[...]
+    latent = qkv_v.shape[3] - 2 * HD
+    for item in range(micro):
+        qkv.finish(item)
+        q_normed = qkv_v[:, item, :, :latent].reshape(length, latent)
+        keys = qkv_v[:, item, :, latent : latent + HD].reshape(length, HD)
+        values = qkv_v[:, item, :, latent + HD :].reshape(length, HD)
+        keep = keep_ref[item]
+
+        @pl.loop(0, heads)
+        def _(head):
+            cols = pl.ds(pl.multiple_of(head * HD, HD), HD)
+            front, back = turn(dot(q_normed, up_v[:, cols]), cosine, sine)
+            turned_v[item, :, pl.ds(pl.multiple_of(head * HD, HD), HD // 2)] = front.astype(BF)
+            turned_v[item, :, pl.ds(pl.multiple_of(head * HD + HD // 2, HD // 2), HD // 2)] = (
+                back.astype(BF)
+            )
+            weights = softmax_rows(turned_v[item, :, cols], keys, keep, score_scale)
+            mixed = dot(weights.astype(BF), values).astype(BF)
+            mixed_v[:, item, :, cols] = mixed.reshape(4, pos_dev, HD)
+
+        if cots.step <= place.h:
+            cots.advance()
+        mixed = mixed_v[:, item].reshape(length, heads * HD)
+        width = out_v.shape[1]
+
+        @pl.loop(0, width // 512)
+        def _(t):
+            cols = pl.ds(pl.multiple_of(t * 512, 512), 512)
+            part = dot(mixed, out_v[:, cols]).astype(BF)
+            part_v[:, item, :, cols] = part.reshape(4, pos_dev, 512)
+
+        attended_sum.start(item)
+        if item > 0:
+            attended_sum.cross(item - 1)
+    copies.local(qkv_v, qkv_out)
+    copies.local(turned_v, turned_out)
+    copies.local(mixed_v, mixed_out)
+    if cots.step <= place.h:
+        cots.advance()
+    attended_sum.cross(micro - 1)
+    rows.cross(0)
+    for item in range(micro):
+        attended[item] = attended_sum.finish(item)
+    while cots.step <= place.h:
+        cots.advance()
+    copies.drain()
+
+
+def attention(n_batch, qkv, attn_in, grad_mo, own_qup, own_out, cos_all, sin_all, keep):
+    micro, pos_dev, qkv_cols = qkv.shape
+    n_tok, width = attn_in.shape
+    latent, head_cols = own_qup.shape
+    length = 4 * pos_dev
+    sems = 2 * n_batch + 48
+    anywhere = pl.BlockSpec(memory_space=pl.ANY)
+    near = pl.BlockSpec(memory_space=pltpu.VMEM)
+    return pl.pallas_call(
+        functools.partial(attention_kernel, n_batch, head_cols // HD),
+        out_shape=(
+            jax.ShapeDtypeStruct((micro, pos_dev, width), F32),
+            jax.ShapeDtypeStruct((4, micro, pos_dev, qkv_cols), BF),
+            jax.ShapeDtypeStruct((micro, length, head_cols), BF),
+            jax.ShapeDtypeStruct((4, micro, pos_dev, head_cols), BF),
+            jax.ShapeDtypeStruct((4, 1, n_tok, width), BF),
+            jax.ShapeDtypeStruct((n_batch, n_tok, width), BF),
+        ),
+        in_specs=[anywhere] * 5 + [near] * 3,
+        out_specs=[near] + [anywhere] * 5,
+        scratch_shapes=[
+            pltpu.VMEM((4, micro, pos_dev, qkv_cols), BF),
+            pltpu.VMEM((latent, head_cols), BF),
+            pltpu.VMEM((head_cols, width), BF),
+            pltpu.VMEM((micro, length, head_cols), BF),
+            pltpu.VMEM((4, micro, pos_dev, head_cols), BF),
+            pltpu.VMEM((4, micro, pos_dev, width), BF),
+            pltpu.VMEM((2, micro, pos_dev, width), BF),
+            pltpu.VMEM((micro, pos_dev, width), BF),
+            pltpu.SemaphoreType.DMA((sems,)),
+            pltpu.SemaphoreType.DMA((sems,)),
+            pltpu.SemaphoreType.DMA((3,)),
+        ],
+        compiler_params=pltpu.CompilerParams(
+            collective_id=3, has_side_effects=True, vmem_limit_bytes=40 * 1024 * 1024
+        ),
+        name="attention",
+    )(qkv, attn_in, grad_mo, own_qup, own_out, cos_all, sin_all, keep)
+
+
+def attention_back_kernel(
+    n_batch,
+    heads,
+    has_terms,
+    grad_ref,
+    qkv_ref,
+    turned_ref,
+    mixed_ref,
+    up_ref,
+    out_ref,
+    gu_ref,
+    *refs,
+):
+    terms_ref, refs = (refs[0], refs[1:]) if has_terms else (None, refs)
+    (
+        cos_ref,
+        sin_ref,
+        keep_ref,
+        back_out,
+        out_terms,
+        up_terms,
+        gu_grad,
+    ) = refs[:7]
+    terms_sum, refs = (refs[7], refs[8:]) if has_terms else (None, refs[7:])
+    (
+        grad_v,
+        qkv_v,
+        turned_v,
+        mixed_v,
+        up_v,
+        out_v,
+        mixgrad_v,
+        qgrad_v,
+        kgrad_v,
+        vgrad_v,
+        part_v,
+        near_got,
+        far_got,
+        outgrad_v,
+        upgrad_v,
+        send_sems,
+        recv_sems,
+        load_sems,
+    ) = refs[:18]
+    place = Place(n_batch)
+    copies = Copies(send_sems, recv_sems)
+    b, c, n = place.b, place.c, n_batch
+    micro, pos_dev, width = grad_ref.shape
+    length = 4 * pos_dev
+    head_cols = heads * HD
+    latent = qkv_ref.shape[3] - 2 * HD
+    score_scale = 1.0 / math.sqrt(HD)
+    pairs = [
+        (grad_ref, grad_v.at[c]),
+        (out_ref, out_v),
+        (qkv_ref, qkv_v),
+        (turned_ref, turned_v),
+        (up_ref, up_v),
+        (mixed_ref, mixed_v),
+    ]
+    if has_terms:
+        terms_v, terms_got, ring_send, ring_recv = refs[18:]
+        pairs.append((terms_ref, terms_v))
+    loads = [
+        pltpu.make_async_copy(source, target, load_sems.at[i])
+        for i, (source, target) in enumerate(pairs)
+    ]
+    for copy in loads:
+        copy.start()
+    peers = [(lax.rem(b + k, n), c) for k in range(1, n)]
+    others = peers + [(b, place.far), (b, place.near)]
+    pl.semaphore_wait(greet(place, others), n + 1)
+    loads[0].wait()
+    grads = CtxGather(place, copies, grad_v)
+    for item in range(micro):
+        grads.start(item)
+    steps = []
+    if has_terms:
+
+        def spot(step):
+            return 0 if step == 0 else 1 if step == place.h else 2 * abs(step) + (step > 0)
+
+        terms = RingCollect(
+            place, lambda step: terms_v.at[spot(step)], terms_got, ring_send, ring_recv
+        )
+        loads[6].wait()
+        steps = [terms.advance] * place.h
+
+    def ring_step():
+        if steps:
+            steps.pop()()
+
+    ring_step()
+    copies.local(gu_ref.at[b], gu_grad.at[b])
+    for peer in peers:
+        copies.remote(gu_ref.at[peer[0]], gu_grad.at[b], peer)
+    for item in range(micro):
+        grads.cross(item)
+    for copy in loads[1:6]:
+        copy.wait()
+    back_sum = CtxCollect(place, copies, part_v, near_got, far_got)
+    cosine, sine = cos_ref[...], sin_ref[...]
+    for item in range(micro):
+        grads.finish(item)
+        incoming = grad_v[:, item].reshape(length, width)
+        keys = qkv_v[:, item, :, latent : latent + HD].reshape(length, HD)
+        values = qkv_v[:, item, :, latent + HD :].reshape(length, HD)
+        keep = keep_ref[item]
+        kgrad_v[...] = jnp.zeros_like(kgrad_v)
+        vgrad_v[...] = jnp.zeros_like(vgrad_v)
+
+        @pl.loop(0, heads)
+        def _(head):
+            cols = pl.ds(pl.multiple_of(head * HD, HD), HD)
+            grad_mixed = dot_right_t(incoming, out_v[cols, :]).astype(BF)
+            queries = turned_v[item, :, cols]
+            weights = softmax_rows(queries, keys, keep, score_scale)
+            grad_probs = dot_right_t(grad_mixed, values)
+            row_dot = jnp.sum(weights * grad_probs, axis=-1, keepdims=True)
+            grad_scores = (weights * (grad_probs - row_dot)).astype(BF)
+            front, back = turn(dot(grad_scores, keys) * score_scale, cosine, -sine)
+            front, back = front.astype(BF), back.astype(BF)
+            base = pl.multiple_of(head * HD, HD)
+            qgrad_v[:, item, :, pl.ds(base, HD // 2)] = front.reshape(4, pos_dev, HD // 2)
+            base = pl.multiple_of(head * HD + HD // 2, HD // 2)
+            qgrad_v[:, item, :, pl.ds(base, HD // 2)] = back.reshape(4, pos_dev, HD // 2)
+            kgrad_v[...] += dot_left_t(grad_scores, queries) * score_scale
+            vgrad_v[...] += dot_left_t(weights.astype(BF), grad_mixed)
+
+        ring_step()
+        qgrad = qgrad_v[:, item].reshape(length, head_cols)
+        part_v[:, item, :, :latent] = (
+            dot_right_t(qgrad, up_v[...]).astype(BF).reshape(4, pos_dev, latent)
+        )
+        part_v[:, item, :, latent : latent + HD] = (
+            kgrad_v[...].astype(BF).reshape(4, pos_dev, HD)
+        )
+        part_v[:, item, :, latent + HD :] = vgrad_v[...].astype(BF).reshape(4, pos_dev, HD)
+        back_sum.start(item)
+        if item > 0:
+            back_sum.cross(item - 1)
+    n_all = 4 * micro * pos_dev
+    out_rows = head_cols // n
+
+    back_sum.cross(micro - 1)
+    ring_step()
+
+    @pl.loop(0, width // 512)
+    def _(t):
+        cols = pl.ds(pl.multiple_of(t * 512, 512), 512)
+        term = dot_left_t(
+            mixed_v[...].reshape(n_all, head_cols), grad_v[:, :, :, cols].reshape(n_all, 512)
+        )
+        outgrad_v[:, :, cols] = term.astype(BF).reshape(n, out_rows, 512)
+
+    copies.local(outgrad_v, out_terms)
+    for item in range(micro):
+        back_out[item] = back_sum.finish(item)
+    ring_step()
+
+    @pl.loop(0, head_cols // HD)
+    def _(t):
+        cols = pl.ds(pl.multiple_of(t * HD, HD), HD)
+        term = dot_left_t(
+            qkv_v[:, :, :, :latent].reshape(n_all, latent),
+            qgrad_v[:, :, :, cols].reshape(n_all, HD),
+        )
+        upgrad_v[:, :, cols] = term.astype(BF).reshape(n, latent // n, HD)
+
+    copies.local(upgrad_v, up_terms)
+    if has_terms:
+        while steps:
+            ring_step()
+        cut = terms.cut
+        for half in (0, 1):
+            terms_sum[half * cut : (half + 1) * cut, :] = terms.finish(half)
+        terms.drain()
+    copies.drain()
+
+
+def attention_back(
+    n_batch, grad_att, qkv_all, turned, mixed, own_qup, own_out, grad_gu, terms, tables
+):
+    micro, pos_dev, width = grad_att.shape
+    n_tok = micro * pos_dev
+    qkv_cols = qkv_all.shape[3]
+    latent, head_cols = own_qup.shape
+    length = 4 * pos_dev
+    far = n_batch // 2
+    has_terms = terms is not None
+    sems = 2 * n_batch + 48
+    anywhere = pl.BlockSpec(memory_space=pl.ANY)
+    near = pl.BlockSpec(memory_space=pltpu.VMEM)
+    out_shape = [
+        jax.ShapeDtypeStruct((micro, pos_dev, qkv_cols), F32),
+        jax.ShapeDtypeStruct((n_batch, head_cols // n_batch, width), BF),
+        jax.ShapeDtypeStruct((n_batch, latent // n_batch, head_cols), BF),
+        jax.ShapeDtypeStruct(grad_gu.shape, BF),
+    ]
+    out_specs = [near] + [anywhere] * 3
+    scratch = [
+        pltpu.VMEM((4, micro, pos_dev, width), BF),
+        pltpu.VMEM((4, micro, pos_dev, qkv_cols), BF),
+        pltpu.VMEM((micro, length, head_cols), BF),
+        pltpu.VMEM((4, micro, pos_dev, head_cols), BF),
+        pltpu.VMEM((latent, head_cols), BF),
+        pltpu.VMEM((head_cols, width), BF),
+        pltpu.VMEM((8, 128), BF),
+        pltpu.VMEM((4, micro, pos_dev, head_cols), BF),
+        pltpu.VMEM((length, HD), F32),
+        pltpu.VMEM((length, HD), F32),
+        pltpu.VMEM((4, micro, pos_dev, qkv_cols), BF),
+        pltpu.VMEM((2, micro, pos_dev, qkv_cols), BF),
+        pltpu.VMEM((micro, pos_dev, qkv_cols), BF),
+        pltpu.VMEM((n_batch, head_cols // n_batch, width), BF),
+        pltpu.VMEM((n_batch, latent // n_batch, head_cols), BF),
+        pltpu.SemaphoreType.DMA((sems,)),
+        pltpu.SemaphoreType.DMA((sems,)),
+        pltpu.SemaphoreType.DMA((7,)),
+    ]
+    args = [grad_att, qkv_all, turned, mixed, own_qup, own_out, grad_gu]
+    if has_terms:
+        args.append(terms)
+        out_shape.append(jax.ShapeDtypeStruct((n_tok, width), F32))
+        out_specs.append(near)
+        scratch += [
+            pltpu.VMEM(terms.shape, BF),
+            pltpu.VMEM((far, 2, 2, n_tok // 2, width), BF),
+            pltpu.SemaphoreType.DMA((far, 2, 2)),
+            pltpu.SemaphoreType.DMA((far, 2, 2)),
+        ]
+    return pl.pallas_call(
+        functools.partial(attention_back_kernel, n_batch, head_cols // HD, has_terms),
+        out_shape=tuple(out_shape),
+        in_specs=[anywhere] * len(args) + [near] * 3,
+        out_specs=out_specs,
+        scratch_shapes=scratch,
+        compiler_params=pltpu.CompilerParams(
+            collective_id=4, has_side_effects=True, vmem_limit_bytes=56 * 1024 * 1024
+        ),
+        name="attention_back",
+    )(*args, *tables)
+
+
+def permuted_mlp(ring, rows_own, cots, gu_rows, own_down):
     mlp_in = ring.spread(rows_own)
     n_tok, width = rows_own.shape
     _, n_batch, n_ctx, own_rows, ff = gu_rows.shape
@@ -1068,7 +1570,7 @@
     kept = []
     for group in groups:
         rows = jnp.concatenate([mlp_in[step] for step in group], axis=0)
-        grad_rows = jnp.concatenate([grad_mo[step] for step in group], axis=0)
+        grad_rows = jnp.concatenate([pick(cots, ring.rank_of(step)) for step in group], axis=0)
         gate_part = dot(rows, own_gate)
         up_part = dot(rows, own_up)
         sigmoid_gate = jax.nn.sigmoid(gate_part)
@@ -1162,14 +1664,9 @@
     residual = tokens.reshape(n_tok, width).astype(F32)
     valid_rows = (query_pos[None, :] < own_lengths[:, None]).astype(F32).reshape(n_tok, 1)
     grad_out = cotangent.reshape(n_tok, width).astype(F32) * valid_rows
-    with jax.named_scope('cotangent_spread'):
-        grad_mo = ring.spread(grad_out.astype(BF))
-
     scale_one = rms_scale(residual)
     normed_one = residual * scale_one
     attn_in = (normed_one * gain_norm).astype(BF)
-    with jax.named_scope('attn_in_gather'):
-        attn_in_all = ctx_gather(attn_in).reshape(n_ctx * n_tok, width)
     projected = dot(attn_in, full_in)
     q_latent = projected[:, :QR]
     scale_query = rms_scale(q_latent)
@@ -1179,99 +1676,52 @@
         projected[:, QR : QR + HD].reshape(micro, pos_dev, HD), cos_own, sin_own
     ).astype(BF)
     v_low = projected[:, QR + HD :].astype(BF)
-    with jax.named_scope('qkv_gather'):
-        qkv_all = ctx_gather(jnp.concatenate([q_normed, k_rot.reshape(n_tok, HD), v_low], axis=1))
-    q_normed_all = qkv_all[..., :QR].reshape(n_ctx * n_tok, QR)
-
-    def by_sequence(values):
-        return (
-            values.reshape(n_ctx, micro, pos_dev, -1)
-            .swapaxes(0, 1)
-            .reshape(micro, full_length, -1)
-        )
-
-    def by_position(values):
-        return (
-            values.reshape(micro, n_ctx, pos_dev, -1)
-            .swapaxes(0, 1)
-            .reshape(n_ctx * n_tok, -1)
-        )
-
-    def split_heads(values):
-        return by_sequence(values).reshape(micro, full_length, heads, HD).swapaxes(1, 2)
-
-    def join_heads(values):
-        return by_position(values.swapaxes(1, 2).reshape(micro, full_length, heads * HD))
-
-    kv_all = by_sequence(qkv_all[..., QR:])
-    keys_all = kv_all[..., :HD]
-    values_all = kv_all[..., HD:]
-    queries = split_heads(dot(q_normed_all, own_qup))
-    q_rot = rotate(queries, cos_all, sin_all).astype(BF)
-    allowed = (key_pos[None, :] <= key_pos[:, None])[None, None] & (
-        key_pos[None, None, None, :] < own_lengths[:, None, None, None]
-    )
-    scores = jnp.einsum("shtd,sud->shtu", q_rot, keys_all, preferred_element_type=F32) * score_scale
-    masked = jnp.where(allowed, scores, -1e30)
-    row_max = jnp.max(masked, axis=-1, keepdims=True)
-    raised = jnp.exp(masked - row_max)
-    weights = raised / jnp.sum(raised, axis=-1, keepdims=True)
-    weights_low = weights.astype(BF)
-    mixed = join_heads(
-        jnp.einsum("shtu,sud->shtd", weights_low, values_all, preferred_element_type=F32).astype(BF)
-    )
-    with jax.named_scope('attended_collect'):
-        attended = ctx_collect(dot(mixed, own_out).reshape(n_ctx, n_tok, width))
-    hidden_res = residual + attended
+    qkv = jnp.concatenate([q_normed, k_rot.reshape(n_tok, HD), v_low], axis=1)
+    keep = (key_pos[None, None, :] < own_lengths[:, None, None]).astype(F32)
+    attended, qkv_all, turned, mixed, attn_in_all, cots = attention(
+        n_batch,
+        qkv.reshape(micro, pos_dev, in_cols),
+        attn_in,
+        grad_out.astype(BF),
+        own_qup,
+        own_out,
+        cos_all,
+        sin_all,
+        keep,
+    )
+    hidden_res = residual + attended.reshape(n_tok, width)
 
     scale_two = rms_scale(hidden_res)
     normed_two = hidden_res * scale_two
     mlp_in = (normed_two * gain_mlp).astype(BF)
-    far = ring.h
-    order = [0] + [side * step for step in range(1, far) for side in (-1, 1)] + [far]
     resident = 10 * n_batch * n_tok * width <= 24 * 1024 * 1024
     if resident:
         grad_mlp_in, grad_down, terms, grad_gu_own = fused_mlp(
-            n_batch, mlp_in, [grad_mo[step] for step in order], gu_rows[0], gu_rows[1], own_down
+            n_batch, mlp_in, cots, gu_rows[0], gu_rows[1], own_down
         )
         terms = terms.reshape(n_batch, n_tok, width)
-        spots = [0, far] + [side * step for step in range(1, far) for side in (-1, 1)]
-        out_terms = {step: terms[i] for i, step in enumerate(spots)}
     else:
+        terms = None
         grad_mlp_in, grad_down, out_terms, grad_gu_own = permuted_mlp(
-            ring, mlp_in, grad_mo, gu_rows, own_down
+            ring, mlp_in, cots, gu_rows, own_down
         )
     gain_mlp_term = jnp.sum(grad_mlp_in * normed_two, axis=0)
     grad_hidden = grad_out + norm_back(grad_mlp_in * gain_mlp, normed_two, scale_two)
-    with jax.named_scope('layer_out_collect'):
-        layer_out = hidden_res + ring.collect(lambda step: out_terms[step])
-
-    with jax.named_scope('grad_att_gather'):
-        grad_att_all = ctx_gather(grad_hidden.astype(BF)).reshape(n_ctx * n_tok, width)
-    grad_out_own = dot_left_t(mixed, grad_att_all)
-    grad_mixed = split_heads(dot_right_t(grad_att_all, own_out).astype(BF))
-    grad_probs = jnp.einsum(
-        "shtd,sud->shtu", grad_mixed, values_all, preferred_element_type=F32
-    )
-    row_dot = jnp.sum(weights * grad_probs, axis=-1, keepdims=True)
-    grad_scores = (weights * (grad_probs - row_dot)).astype(BF)
-    grad_q_rot = (
-        jnp.einsum("shtu,sud->shtd", grad_scores, keys_all, preferred_element_type=F32)
-        * score_scale
-    )
-    grad_keys = (
-        jnp.einsum("shtu,shtd->sud", grad_scores, q_rot, preferred_element_type=F32)
-        * score_scale
-    )
-    grad_values = jnp.einsum(
-        "shtu,shtd->sud", weights_low, grad_mixed, preferred_element_type=F32
-    )
-    grad_q = join_heads(rotate_back(grad_q_rot, cos_all, sin_all).astype(BF))
-    grad_qn_part = dot_right_t(grad_q, own_qup)
-    grad_kv_part = by_position(jnp.concatenate([grad_keys, grad_values], axis=-1))
-    back_parts = jnp.concatenate([grad_qn_part, grad_kv_part], axis=1).astype(BF)
-    with jax.named_scope('back_collect'):
-        back_own = ctx_collect(back_parts.reshape(n_ctx, n_tok, in_cols))
+    back_own, out_grads, up_grads, grad_gu_own, *sums = attention_back(
+        n_batch,
+        grad_hidden.astype(BF).reshape(micro, pos_dev, width),
+        qkv_all,
+        turned,
+        mixed,
+        own_qup,
+        own_out,
+        grad_gu_own,
+        terms,
+        (cos_all, sin_all, keep),
+    )
+    out_sum = sums[0] if resident else ring.collect(lambda step: out_terms[step])
+    layer_out = hidden_res + out_sum
+    back_own = back_own.reshape(n_tok, in_cols)
     grad_qn = back_own[:, :QR]
     gain_query_term = jnp.sum(grad_qn * normed_query, axis=0)
     grad_latent = norm_back(grad_qn * gain_query, normed_query, scale_query)
@@ -1285,14 +1735,8 @@
     gain_norm_term = jnp.sum(grad_attn_in * normed_one, axis=0)
     grad_tokens = grad_hidden + norm_back(grad_attn_in * gain_norm, normed_one, scale_one)
 
-    grad_up_own = dot_left_t(q_normed_all, grad_q)
     part_cols = in_cols // n_ctx
     project_parts = grad_project.reshape(n_tok, n_ctx, part_cols).swapaxes(0, 1)
-    with jax.named_scope('grad_project_exchange'):
-        project_all = ctx_exchange(project_parts).reshape(n_ctx * n_tok, part_cols)
-    grad_in_own = dot_left_t(attn_in_all, project_all).reshape(
-        n_batch, n_ctx, own_rows, part_cols
-    )
     gain_terms = jnp.stack(
         [
             gain_norm_term.reshape(n_batch, n_ctx, own_rows),
@@ -1305,14 +1749,8 @@
         axis=2,
     )
     gain_terms = jnp.pad(gain_terms, ((0, 0), (0, 0), (0, 13), (0, part_cols - own_rows)))
-    joined = jnp.concatenate([grad_in_own, gain_terms], axis=2).reshape(n_batch, -1, part_cols)
-    grad_proj_out, grad_query_up, grad_proj_in, gain_sums, grad_gu_own = collect_weights(
-        n_batch,
-        gain_rows,
-        grad_out_own.reshape(n_batch, -1, width).astype(BF),
-        grad_up_own.reshape(n_batch, -1, heads * HD).astype(BF),
-        joined.astype(BF),
-        grad_gu_own,
+    grad_proj_out, grad_query_up, grad_proj_in, gain_sums = collect_weights(
+        n_batch, gain_rows, out_grads, up_grads, project_parts, attn_in_all, gain_terms.astype(BF)
     )
     grad_gate_up = grad_gu_own.transpose(2, 1, 0, 3).reshape(own_rows, 2 * ff_all).astype(F32)
     gain_sums = gain_sums[:, :own_rows]

time: 692 us -> 589 us (0.85)
  waiting for transfers between devices: 99.1 us -> 0 us
  Pallas kernels: 421 us -> 515 us
  matrix products: 43 us -> 10.3 us
  local copies, waits for them, and re-layouts: 64.5 us -> 33.8 us
  starting transfers between devices: 24 us -> 0 us
  other arithmetic: 31.8 us -> 22.6 us
    pallas_call x0 -> x2, Pallas kernels: none -> 129 us  [the longest x1 79 us: attention_back(): pl.pallas_call(functools.partial(attention_back_kernel, n_batch, head_col...]
    ppermute x28 -> x0, waiting for transfers between devices: 99.1 us -> none  [the longest x3 29 us: ctx_gather(): pair = in_order(block, lax.ppermute(block, 'ctx', FAR), outer)]
    pallas_call x1, Pallas kernels: 141 us -> 108 us  [collect_weights(): pl.pallas_call(functools.partial(tail_kernel, n_batch, gain_rows), out_sh...]
    dot_general x8 -> x0, matrix products: 24.1 us -> none  [the longest x3 8.19 us: dot_left_t(): lax.dot_general(left_side, right_side, (((0,), (0,)), ((), ())), preferre...]
    ppermute x28 -> x0, starting transfers between devices: 24 us -> none  [the longest x3 5.7 us: spread(): upward = lax.ppermute(upward, 'batch', self.up)]
    another operation x5 -> x0, local copies, waits for them, and re-layouts: 8.97 us -> none  [the longest x3 5.63 us: split_heads(): by_sequence(values).reshape(micro, full_length, heads, HD).swapaxes(1, 2)]
  transfers between devices with their start and end apart: 28 -> 0, of which waited for: 15 -> 0; matrix products, arithmetic and copies ran while one was open for 13% -> 0% of each run, Pallas kernels for 0% -> 0%
where the time goes in v4:
time: 589 us; the launch traced here: 583 us
  Pallas kernels  515 us (87%)
  local copies, waits for them, and re-layouts  33.8 us (6%)
  other arithmetic  22.6 us (4%)
  matrix products  10.3 us (2%)
    pallas_call x1, Pallas kernels, spread_weights(): pl.pallas_call(functools.partial(weights_kernel, n_batch), out_shape=shap...  152 us
    pallas_call x1, Pallas kernels, fused_mlp(): pl.pallas_call(functools.partial(mlp_kernel, n_batch), out_shape=(jax.Sha...  126 us
    pallas_call x1, Pallas kernels, collect_weights(): pl.pallas_call(functools.partial(tail_kernel, n_batch, gain_rows), out_sh...  108 us
    pallas_call x1, Pallas kernels, attention_back(): pl.pallas_call(functools.partial(attention_back_kernel, n_batch, head_col...  79 us
    pallas_call x1, Pallas kernels, attention(): pl.pallas_call(functools.partial(attention_kernel, n_batch, head_cols //...  50 us

profile of v4, /device:TPU:4, one launch (start us, length us, event | category | flops | bytes accessed | tf_op | source)
XLA Modules:
  0.0 583.2 jit_solution(7914287180019640408)
XLA Ops:
  3.1 1.2 fusion.17
  4.8 1.6 fusion.30.packed_ref
  7.0 1.8 copy.80
  8.8 2.0 fusion.5.cot_ref
  10.8 3.3 reshape.300
  14.0 1.6 copy.79
  15.7 151.9 %spread_weights.1 = (bf16[8,4,64,1664]{3,2,1,0:T(8,128)(2,1)}, bf16[8,4,32,1024]{3,2,1,0:T(8,128)(2,1)}, bf16[8,128,2048]{2,1,0:T(8,128)(2,1)}, bf16[2,8,4,64,704]{4,3,2,1,0:T(8,128)(2,1)}, bf16[4,176,2048]{2,1,0:T(8,128)(2,1)}) custom-call(bf16[64,1664]{1,0:T(8,128)(2,1)} %fusion.30.packed_ref, bf16[4,32,1024]{2,1,0:T(8,128)(2,1)} %bitcast.119, ...), custom_call_target="tpu_custom_call" | custom-call | tf_op jit(solution)/shard_map/spread_weights/pallas_call | solution.py:461
  167.6 1.1 slice_convert_fusion
  169.4 3.9 fusion.2
  173.9 3.4 slice_bitcast_fusion
  177.3 50.0 %attention.1 = (f32[2,64,2048]{2,1,0:T(8,128)S(1)}, bf16[4,2,64,1536]{3,2,1,0:T(8,128)(2,1)S(1)}, bf16[2,256,1024]{2,1,0:T(8,128)(2,1)S(1)}, bf16[4,2,64,1024]{3...) custom-call(bf16[2,64,1536]{2,1,0:T(8,128)(2,1)S(1)} %pad_maximum_fusion.qkv_ref, ...), custom_call_target="tpu_custom_call" | custom-call | tf_op jit(solution)/shard_map/attention/pallas_call | solution.py:1284
  227.3 1.3 copy-done.2
  228.6 1.2 copy-done.4
  233.1 126.5 %fused_mlp.1 = (f32[128,2048]{1,0:T(8,128)}, f32[176,2048]{1,0:T(8,128)}, bf16[4,256,2048]{2,1,0:T(8,128)(2,1)}, bf16[8,2,64,704]{3,2,1,0:T(8,128)(2,1)}) custom-call(bf16[128,2048]{1,0:T(8,128)(2,1)} %multiply_convert_fusion.rows_ref, bf16[8,4,64,704]{3,2,1,0:T(8,128)(2,1)} %get-tuple-element.67.gate_ref, bf16[8,4,64,704]{3,2,1,0:T(8,128)(2,1)} %get-tuple-element.66.up_ref, ...), custom_call_target="tpu_custom_call" | custom-call | flops 26575110144 | bytes 25165824 | tf_op jit(solution)/shard_map/fused_mlp/pallas_call | solution.py:762
  359.6 1.6 multiply_reduce_fusion
  361.9 2.8 fusion.33
  364.7 79.0 %attention_back.1 = (f32[2,64,1536]{2,1,0:T(8,128)}, bf16[8,128,2048]{2,1,0:T(8,128)(2,1)}, bf16[8,128,1024]{2,1,0:T(8,128)(2,1)}, bf16[8,2,64,704]{3,2,1,0:T(8,128)(2,1)}, f32[128,2048]{1,0:T(8,128)}) custom-call(bf16[2,64,2048]{2,1,0:T(8,128)(2,1)} %bitcast.113, bf16[4,2,64,1536]{3,2,1,0:T(8,128)(2,1)} %copy-done.4, bf16[2,256,1024]{2,1,0:T(8,128)(2,1)} %copy-done.7, ...), custom_call_target="tpu_custom_call" | custom-call | tf_op jit(solution)/shard_map/attention_back/pallas_call | solution.py:1547
  443.8 1.3 multiply_reduce_fusion.2
  445.1 1.2 subtract_multiply_fusion
  448.9 6.4 %fusion.16 = (bf16[2048]{0:T(1024)(128)(2,1)S(1)}, f32[128]{0:T(128)}, f32[128,2048]{1,0:T(8,128)}) fusion(bf16[2,64,2048]{2,1,0:T(8,128)(2,1)S(1)} %copy-done.14, f32[128]{0:T(128)S(1)} %rsqrt.31, f32[2048]{0:T(1024)S(1)} %bitcast.134, bf16[2048,1664]{1,0:T(8,128)(2,1)} %bitcast.139, bf16[128,256]{1,0:T(8,128)(2,1)S(1)} %slice.104, ...), kind=kOutput, calls=%fused_computation.25 | convolution fusion | flops 808318848 | bytes 8270848 | tf_op jit(solution)/shard_map/dot_general | solution.py:52
  456.6 3.4 fusion.15
  461.0 107.7 %collect_weights.1 = (f32[128,2048]{1,0:T(8,128)S(1)}, f32[32,4096]{1,0:T(8,128)S(1)}, f32[64,1536]{1,0:T(8,128)S(1)}, f32[16,384]{1,0:T(8,128)S(1)}) custom-call(bf16[8,128,2048]{2,1,0:T(8,128)(2,1)} %get-tuple-element.49.out_ref, bf16[8,128,1024]{2,1,0:T(8,128)(2,1)S(1)} %copy-done.3, bf16[4,128,384]{2,1,0:T(8,128)(2,1)S(1)} %bitcast.106, ...), custom_call_target="tpu_custom_call" | custom-call | tf_op jit(solution)/shard_map/collect_weights/pallas_call | solution.py:1048
  570.9 3.5 copy.71
  574.4 4.8 reshape.315
  (93 shorter events, 19.3 us)
Async XLA Ops:
  4.5 172.8 %copy-start.13 = (f32[2,1,256]{2,1,0:T(1,128)}, f32[2,1,256]{2,1,0:T(1,128)S(1)}, u32[]{:S(2)}) copy-start(f32[2,1,256]{2,1,0:T(1,128)S(1)} %compare_convert_fusion.keep_ref.refs_3_) | copy-start | bytes 6148
  7.0 170.3 %copy-start.5 = (f32[256,128]{1,0:T(8,128)}, f32[256,128]{1,0:T(8,128)S(1)}, u32[]{:S(2)}) copy-start(f32[256,128]{1,0:T(8,128)S(1)} %get-tuple-element.79.sin_ref.refs_2_) | copy-start | bytes 393220
  7.0 170.3 %copy-start.6 = (f32[256,128]{1,0:T(8,128)}, f32[256,128]{1,0:T(8,128)S(1)}, u32[]{:S(2)}) copy-start(f32[256,128]{1,0:T(8,128)S(1)} %get-tuple-element.80.cos_ref.refs_1_) | copy-start | bytes 393220
  15.7 153.6 %copy-start.14 = (bf16[2,64,2048]{2,1,0:T(8,128)(2,1)S(1)}, bf16[2,64,2048]{2,1,0:T(8,128)(2,1)}, u32[]{:S(2)}) copy-start(bf16[2,64,2048]{2,1,0:T(8,128)(2,1)} %param.12) | copy-start | bytes 1572868
  169.2 4.5 slice-start
  169.4 4.5 slice-start.1
  173.9 3.4 copy-start
  173.9 3.4 copy-start.1
  227.3 1.3 copy-start.2
  228.6 1.2 copy-start.4
  229.8 1.0 copy-start.7
  230.8 1.0 copy-start.8
  233.1 128.8 %copy-start.15 = (bf16[2,64,2048]{2,1,0:T(8,128)(2,1)S(1)}, bf16[2,64,2048]{2,1,0:T(8,128)(2,1)}, u32[]{:S(2)}) copy-start(bf16[2,64,2048]{2,1,0:T(8,128)(2,1)} %param.13) | copy-start | bytes 1572868
  455.8 5.2 copy-start.3
  461.0 109.6 %copy-start.16 = (bf16[8,2,64,704]{3,2,1,0:T(8,128)(2,1)S(1)}, bf16[8,2,64,704]{3,2,1,0:T(8,128)(2,1)}, u32[]{:S(2)}) copy-start(bf16[8,2,64,704]{3,2,1,0:T(8,128)(2,1)} %get-tuple-element.56) | copy-start | bytes 4325380
  568.7 0.8 copy-start.9
  569.5 1.4 copy-start.11
  574.4 4.8 copy-start.12
  574.4 5.5 copy-start.10
  579.1 2.5 copy-start.17

commit v5 on v4

--- a/solution.py
+++ b/solution.py
@@ -159,11 +159,16 @@
     return whole.reshape((4,) + block.shape)
 
 
-def ctx_collect(stacked):
-    outer, inner = ctx_place()
+def near_collect(stacked):
+    _, inner = ctx_place()
     parts = stacked.reshape((2, 2) + stacked.shape[1:])
     got = lax.ppermute(pick(parts, 1 - inner, 1).astype(BF), "ctx", NEAR)
-    half = pick(parts, inner, 1).astype(F32) + got.astype(F32)
+    return pick(parts, inner, 1).astype(F32) + got.astype(F32)
+
+
+def ctx_collect(stacked):
+    outer, _ = ctx_place()
+    half = near_collect(stacked)
     got = lax.ppermute(pick(half, 1 - outer).astype(BF), "ctx", FAR)
     return pick(half, outer) + got.astype(F32)
 
@@ -313,6 +318,8 @@
     send_sems,
     recv_sems,
     out_sems,
+    flat_v,
+    gu_v,
 ):
     place = Place(n_batch)
     copies = Copies(send_sems, recv_sems)
@@ -336,10 +343,15 @@
 
     pl.semaphore_wait(barrier, n + 4 - 2 * stays.astype(jnp.int32))
 
+    head_cols = up_ref.shape[1] // 4
+
+    def up_cols(rank):
+        return up_ref.at[:, pl.ds(pl.multiple_of(rank * head_cols, head_cols), head_cols)]
+
     own = [
         copies.local(packed_ref, packed_all.at[b, c]),
-        copies.local(up_ref.at[c], up_all.at[b, c]),
-        copies.local(gu_ref.at[b], gu_all.at[:, b, c]),
+        copies.local(up_cols(c), up_all.at[b, c]),
+        copies.local(gu_ref, flat_v),
         copies.local(down_ref, down_all.at[c]),
     ]
     out_copy = pltpu.make_async_remote_copy(
@@ -361,7 +373,7 @@
         out_stay.start()
 
     up_copies = [
-        copies.remote(up_ref.at[peer[1]], up_all.at[b, c], peer) for peer in ctx_peers
+        copies.remote(up_cols(peer[1]), up_all.at[b, c], peer) for peer in ctx_peers
     ]
     far_device, near_device = ctx_peers[0], ctx_peers[1]
     down_far = copies.remote(down_ref, down_all.at[c], far_device)
@@ -371,7 +383,7 @@
         place, copies, own_rows, lambda rank, rows: packed_all.at[rank, c, rows]
     )
     up_ring = RingGather(
-        place, copies, up_ref.shape[1], lambda rank, rows: up_all.at[rank, :, rows]
+        place, copies, up_ref.shape[0], lambda rank, rows: up_all.at[rank, :, rows]
     )
     out_ring = RingGather(place, copies, out_rows, lambda rank, rows: out_all.at[rank, rows])
 
@@ -385,10 +397,17 @@
             packed_far.append((rank, copies.remote(block, block, far_device)))
 
     packed_step()
+    copies.arrive(own[2])
+    ff = gu_v.shape[3]
+    for slab_at in range(n):
+        for kind in (0, 1):
+            start = (kind * n + slab_at) * ff
+            gu_v[slab_at, kind] = flat_v[:, start : start + ff]
+    own.append(copies.local(gu_v.at[b], gu_all.at[:, b, c]))
     gu_copies = [
         (
             lax.rem(b - k + n, n),
-            copies.remote(gu_ref.at[peer[0]], gu_all.at[:, b, c], peer),
+            copies.remote(gu_v.at[peer[0]], gu_all.at[:, b, c], peer),
         )
         for k, peer in zip(range(1, n), peers)
     ]
@@ -407,7 +426,7 @@
 
     out_ring.advance()
     gu_far = []
-    copies.arrive(own[2])
+    copies.arrive(own[4])
     own_gu = gu_all.at[:, b, c]
     gu_far.append(copies.remote(own_gu, own_gu, far_device))
     waiting = list(gu_copies)
@@ -446,13 +465,13 @@
     copies.drain()
 
 
-def spread_weights(n_batch, packed, up_parts, out_rows, gu_parts, down_rows):
+def spread_weights(n_batch, packed, up_rows, out_rows, gu_rows, down_rows):
     own_rows, packed_cols = packed.shape
-    _, gain_rows, up_cols = up_parts.shape
-    ff = gu_parts.shape[-1]
+    gain_rows, up_cols = up_rows.shape
+    ff = gu_rows.shape[1] // (2 * n_batch)
     shapes = (
         jax.ShapeDtypeStruct((n_batch, 4, own_rows, packed_cols), BF),
-        jax.ShapeDtypeStruct((n_batch, 4, gain_rows, up_cols), BF),
+        jax.ShapeDtypeStruct((n_batch, 4, gain_rows, up_cols // 4), BF),
         jax.ShapeDtypeStruct((n_batch,) + out_rows.shape, BF),
         jax.ShapeDtypeStruct((2, n_batch, 4, own_rows, ff), BF),
         jax.ShapeDtypeStruct((4,) + down_rows.shape, BF),
@@ -467,10 +486,12 @@
             pltpu.SemaphoreType.DMA((sems,)),
             pltpu.SemaphoreType.DMA((sems,)),
             pltpu.SemaphoreType.DMA((2,)),
+            pltpu.VMEM(gu_rows.shape, BF),
+            pltpu.VMEM((n_batch, 2, own_rows, ff), BF),
         ],
         compiler_params=pltpu.CompilerParams(collective_id=0, has_side_effects=True),
         name="spread_weights",
-    )(packed, up_parts, out_rows, gu_parts, down_rows)
+    )(packed, up_rows, out_rows, gu_rows, down_rows)
 
 
 def mlp_kernel(
@@ -484,7 +505,7 @@
 ):
     (
         sum_ref,
-        down_grad,
+        down_part,
         term_out,
         gu_out,
         rows_v,
@@ -501,7 +522,6 @@
         gu_got,
         gu_last,
         down_got,
-        down_last,
         send_sems,
         recv_sems,
         back_send,
@@ -659,14 +679,12 @@
         if (side, half) not in ends:
             pass_on(far - 1, side, half, False)
 
-    def gate_up_terms(first, last):
-        @pl.loop(first, last)
-        def _(t):
-            cols = pl.ds(pl.multiple_of(t * 2 * block, 2 * block), 2 * block)
-            rows = rows_v[:, :, cols].reshape(n_batch * n_tok, 2 * block)
-            for target, grads in ((gate_v, ggate_v), (up_v, gup_v)):
-                term = dot_left_t(rows, grads[...].reshape(n_batch * n_tok, ff))
-                target[pl.ds(2 * t, 2)] = term.astype(BF).reshape(2, 4, own_rows, ff)
+    def gate_up_terms(t):
+        cols = slice(t * 2 * block, (t + 1) * 2 * block)
+        rows = rows_v[:, :, cols].reshape(n_batch * n_tok, 2 * block)
+        for target, grads in ((gate_v, ggate_v), (up_v, gup_v)):
+            term = dot_left_t(rows, grads[...].reshape(n_batch * n_tok, ff))
+            target[2 * t : 2 * t + 2] = term.astype(BF).reshape(2, 4, own_rows, ff)
 
     def down_terms():
         @pl.loop(0, width // (2 * block))
@@ -681,42 +699,61 @@
             if step < far - 1 or (side, half) in ends:
                 pass_on(step, side, half, True)
 
-    steps = iter(range(far - 1, 0, -1))
+    steps = list(range(1, far))
+    outer, inner = place.outer, place.inner
+    kinds = list(enumerate((gate_v, up_v)))
+    near_copies, far_copies = {}, {}
+
+    def send_near(t):
+        pair = pl.ds(2 * t, 2)
+        near_copies[t] = [
+            parts.remote(
+                target.at[pair, 2 * side + 1 - inner], gu_got.at[kind, side, pair], near_device
+            )
+            for side in (0, 1)
+            for kind, target in kinds
+        ]
+
+    def send_far(t):
+        pair = pl.ds(2 * t, 2)
+        for copy in near_copies[t]:
+            parts.arrive(copy)
+        far_copies[t] = []
+        for kind, target in kinds:
+            other = target.at[pair, 2 * (1 - outer) + inner]
+            added = other[...].astype(F32) + gu_got[kind, 1 - outer, pair].astype(F32)
+            other[...] = added.astype(BF)
+            far_copies[t].append(parts.remote(other, gu_last.at[kind, pair], far_device))
+
+    def take_far(t):
+        pair = pl.ds(2 * t, 2)
+        for copy in far_copies[t]:
+            parts.arrive(copy)
+        for kind, target in kinds:
+            kept = target.at[pair, 2 * outer + inner]
+            added = kept[...].astype(F32) + gu_got[kind, outer, pair].astype(F32)
+            kept[...] = (added + gu_last[kind, pair].astype(F32)).astype(BF)
+            parts.local(kept, gu_out.at[pair, kind])
+
+    def ring_step():
+        if steps:
+            pass_all(steps.pop())
+
     tiles = width // (2 * block)
-    outer, inner = place.outer, place.inner
-
-    gate_up_terms(0, tiles // 2)
-    pass_all(next(steps))
-    gate_up_terms(tiles // 2, tiles)
-    near_copies = [
-        parts.remote(
-            target.at[:, 2 * side + 1 - inner], gu_got.at[kind, side], near_device
-        )
-        for side in (0, 1)
-        for kind, target in enumerate((gate_v, up_v))
-    ]
-    for step in steps:
-        pass_all(step)
-        if step > 1:
-            down_terms()
+    for t in range(tiles):
+        gate_up_terms(t)
+        send_near(t)
+        if t > 0:
+            send_far(t - 1)
+        ring_step()
+    while steps:
+        ring_step()
+    send_far(tiles - 1)
+    down_terms()
     down_copies = [
         parts.remote(down_v.at[2 * side + 1 - inner], down_got.at[side], near_device)
         for side in (0, 1)
     ]
-    for copy in near_copies:
-        parts.arrive(copy)
-    far_copies = []
-    for kind, target in enumerate((gate_v, up_v)):
-        for side in (1 - outer, outer):
-            kept = target.at[:, 2 * side + inner]
-            kept[...] = (kept[...].astype(F32) + gu_got[kind, side].astype(F32)).astype(BF)
-            if side is not outer:
-                far_copies.append(parts.remote(kept, gu_last.at[kind], far_device))
-    for copy in down_copies:
-        parts.arrive(copy)
-    other = down_v.at[2 * (1 - outer) + inner]
-    other[...] = (other[...].astype(F32) + down_got[1 - outer].astype(F32)).astype(BF)
-    down_far = parts.remote(other, down_last, far_device)
     for half in (0, 1):
         for side in (0, 1):
             back_hop(0, side, half, held(0, 0, half)).wait_recv()
@@ -726,17 +763,13 @@
             + got_v[0, 0, half].astype(F32)
             + got_v[0, 1, half].astype(F32)
         )
-    for kind, target in enumerate((gate_v, up_v)):
-        parts.arrive(far_copies[kind])
-        kept = target.at[:, 2 * outer + inner]
-        kept[...] = (kept[...].astype(F32) + gu_last[kind].astype(F32)).astype(BF)
-        parts.local(kept, gu_out.at[:, kind])
-    parts.arrive(down_far)
-    down_grad[...] = (
-        down_v[2 * outer + inner].astype(F32)
-        + down_got[outer].astype(F32)
-        + down_last[...].astype(F32)
-    )
+    for side in (0, 1):
+        parts.arrive(down_copies[side])
+        added = down_v[2 * side + inner].astype(F32) + down_got[side].astype(F32)
+        down_got[side] = added.astype(BF)
+    parts.local(down_got, down_part)
+    for t in range(tiles):
+        take_far(t)
     parts.drain()
 
     for step in range(1, far + 1):
@@ -763,13 +796,13 @@
         functools.partial(mlp_kernel, n_batch),
         out_shape=(
             jax.ShapeDtypeStruct((n_tok, width), F32),
-            jax.ShapeDtypeStruct((ff // 4, width), F32),
+            jax.ShapeDtypeStruct((2, ff // 4, width), BF),
             jax.ShapeDtypeStruct((far, pair, width), BF),
             jax.ShapeDtypeStruct((n_batch, 2, own_rows, ff), BF),
         ),
         in_specs=[pl.BlockSpec(memory_space=pl.ANY)] * 5,
-        out_specs=[pl.BlockSpec(memory_space=pltpu.VMEM)] * 2
-        + [pl.BlockSpec(memory_space=pl.ANY)] * 2,
+        out_specs=[pl.BlockSpec(memory_space=pltpu.VMEM)]
+        + [pl.BlockSpec(memory_space=pl.ANY)] * 3,
         scratch_shapes=[
             pltpu.VMEM((far, pair, width), BF),
             pltpu.VMEM((far, pair, width), BF),
@@ -785,15 +818,14 @@
             pltpu.VMEM((2, 2, n_batch, own_rows, ff), BF),
             pltpu.VMEM((2, n_batch, own_rows, ff), BF),
             pltpu.VMEM((2, ff // 4, width), BF),
-            pltpu.VMEM((ff // 4, width), BF),
             pltpu.SemaphoreType.DMA((far + 1, 2, 2)),
             pltpu.SemaphoreType.DMA((far + 1, 2, 2)),
             pltpu.SemaphoreType.DMA((far, 2, 2)),
             pltpu.SemaphoreType.DMA((far, 2, 2)),
             pltpu.SemaphoreType.DMA((4 + n_batch,)),
             pltpu.SemaphoreType.DMA((1, far)),
-            pltpu.SemaphoreType.DMA((16,)),
-            pltpu.SemaphoreType.DMA((16,)),
+            pltpu.SemaphoreType.DMA((72,)),
+            pltpu.SemaphoreType.DMA((72,)),
         ],
         compiler_params=pltpu.CompilerParams(
             collective_id=1, has_side_effects=True, vmem_limit_bytes=60 * 1024 * 1024
@@ -872,11 +904,13 @@
     up_ref,
     project_ref,
     rows_ref,
+    gu_ref,
     gain_ref,
     out_grad,
     up_grad,
     in_grad,
     gain_grad,
+    gu_grad,
     out_v,
     up_v,
     in_v,
@@ -895,6 +929,7 @@
     recv_sems,
     project_v,
     rows_v,
+    gu_v,
     load_sems,
     out_sems,
 ):
@@ -911,7 +946,7 @@
 
     loads = [
         pltpu.make_async_copy(held, kept, load_sems.at[i])
-        for i, (held, kept) in enumerate([(out_ref, out_v), (up_ref, up_v), (rows_ref, rows_v)])
+        for i, (held, kept) in enumerate([(out_ref, out_v), (up_ref, up_v), (rows_ref, rows_v), (gu_ref, gu_v)])
     ]
     for copy in loads:
         copy.start()
@@ -968,6 +1003,13 @@
         for ring in rings:
             ring.advance()
 
+    loads[3].wait()
+    ff = gu_v.shape[3]
+    for slab_at in range(n):
+        for kind in (0, 1):
+            start = (kind * n + slab_at) * ff
+            gu_grad[:, start : start + ff] = gu_v[slab_at, kind].astype(F32)
+
     in_ring, up_ring, out_ring = rings[2], rings[1], rings[0]
     out_cut, up_cut, in_cut = out_ring.cut, up_ring.cut, in_ring.cut
     for half in (0, 1):
@@ -1036,7 +1078,7 @@
         ring.drain()
 
 
-def collect_weights(n_batch, gain_rows, out_terms, up_terms, project, attn_in_all, gain_terms):
+def collect_weights(n_batch, gain_rows, out_terms, up_terms, project, attn_in_all, grad_gu, gain_terms):
     far = n_batch // 2
     out_rows, width = out_terms.shape[1:]
     up_rows, up_cols = up_terms.shape[1:]
@@ -1052,9 +1094,10 @@
             jax.ShapeDtypeStruct((gain_rows, 4 * up_cols), F32),
             jax.ShapeDtypeStruct((own_rows, 4 * in_cols), F32),
             jax.ShapeDtypeStruct((16, in_cols), F32),
+            jax.ShapeDtypeStruct((own_rows, 2 * n_batch * grad_gu.shape[3]), F32),
         ),
-        in_specs=[pl.BlockSpec(memory_space=pl.ANY)] * 4 + [pl.BlockSpec(memory_space=pltpu.VMEM)],
-        out_specs=[pl.BlockSpec(memory_space=pltpu.VMEM)] * 4,
+        in_specs=[pl.BlockSpec(memory_space=pl.ANY)] * 5 + [pl.BlockSpec(memory_space=pltpu.VMEM)],
+        out_specs=[pl.BlockSpec(memory_space=pltpu.VMEM)] * 5,
         scratch_shapes=[pltpu.VMEM((n_batch,) + shape, BF) for shape in shapes]
         + [pltpu.VMEM((far, 2, 2, rows // 2, cols), BF) for rows, cols in shapes]
         + [
@@ -1070,14 +1113,15 @@
             pltpu.SemaphoreType.DMA((sems,)),
             pltpu.VMEM(project.shape, BF),
             pltpu.VMEM(attn_in_all.shape, BF),
-            pltpu.SemaphoreType.DMA((3,)),
+            pltpu.VMEM(grad_gu.shape, BF),
+            pltpu.SemaphoreType.DMA((4,)),
             pltpu.SemaphoreType.DMA((2,)),
         ],
         compiler_params=pltpu.CompilerParams(
             collective_id=2, has_side_effects=True, vmem_limit_bytes=48 * 1024 * 1024
         ),
         name="collect_weights",
-    )(out_terms, up_terms, project, attn_in_all, gain_terms)
+    )(out_terms, up_terms, project, attn_in_all, grad_gu, gain_terms)
 
 
 class CtxCollect:
@@ -1324,6 +1368,7 @@
     up_ref,
     out_ref,
     gu_ref,
+    down_ref,
     *refs,
 ):
     terms_ref, refs = (refs[0], refs[1:]) if has_terms else (None, refs)
@@ -1335,8 +1380,9 @@
         out_terms,
         up_terms,
         gu_grad,
-    ) = refs[:7]
-    terms_sum, refs = (refs[7], refs[8:]) if has_terms else (None, refs[7:])
+        down_grad,
+    ) = refs[:8]
+    terms_sum, refs = (refs[8], refs[9:]) if has_terms else (None, refs[8:])
     (
         grad_v,
         qkv_v,
@@ -1344,7 +1390,6 @@
         mixed_v,
         up_v,
         out_v,
-        mixgrad_v,
         qgrad_v,
         kgrad_v,
         vgrad_v,
@@ -1353,6 +1398,7 @@
         far_got,
         outgrad_v,
         upgrad_v,
+        down_v,
         send_sems,
         recv_sems,
         load_sems,
@@ -1411,6 +1457,8 @@
         copies.remote(gu_ref.at[peer[0]], gu_grad.at[b], peer)
     for item in range(micro):
         grads.cross(item)
+    down_own = copies.local(down_ref.at[place.outer], down_v.at[0])
+    down_far = copies.remote(down_ref.at[1 - place.outer], down_v.at[1], (b, place.far))
     for copy in loads[1:6]:
         copy.wait()
     back_sum = CtxCollect(place, copies, part_v, near_got, far_got)
@@ -1483,6 +1531,9 @@
         upgrad_v[:, :, cols] = term.astype(BF).reshape(n, latent // n, HD)
 
     copies.local(upgrad_v, up_terms)
+    copies.arrive(down_own)
+    copies.arrive(down_far)
+    down_grad[...] = down_v[0].astype(F32) + down_v[1].astype(F32)
     if has_terms:
         while steps:
             ring_step()
@@ -1494,7 +1545,7 @@
 
 
 def attention_back(
-    n_batch, grad_att, qkv_all, turned, mixed, own_qup, own_out, grad_gu, terms, tables
+    n_batch, grad_att, qkv_all, turned, mixed, own_qup, own_out, grad_gu, down_part, terms, tables
 ):
     micro, pos_dev, width = grad_att.shape
     n_tok = micro * pos_dev
@@ -1511,8 +1562,9 @@
         jax.ShapeDtypeStruct((n_batch, head_cols // n_batch, width), BF),
         jax.ShapeDtypeStruct((n_batch, latent // n_batch, head_cols), BF),
         jax.ShapeDtypeStruct(grad_gu.shape, BF),
+        jax.ShapeDtypeStruct(down_part.shape[1:], F32),
     ]
-    out_specs = [near] + [anywhere] * 3
+    out_specs = [near] + [anywhere] * 3 + [near]
     scratch = [
         pltpu.VMEM((4, micro, pos_dev, width), BF),
         pltpu.VMEM((4, micro, pos_dev, qkv_cols), BF),
@@ -1520,7 +1572,6 @@
         pltpu.VMEM((4, micro, pos_dev, head_cols), BF),
         pltpu.VMEM((latent, head_cols), BF),
         pltpu.VMEM((head_cols, width), BF),
-        pltpu.VMEM((8, 128), BF),
         pltpu.VMEM((4, micro, pos_dev, head_cols), BF),
         pltpu.VMEM((length, HD), F32),
         pltpu.VMEM((length, HD), F32),
@@ -1529,11 +1580,12 @@
         pltpu.VMEM((micro, pos_dev, qkv_cols), BF),
         pltpu.VMEM((n_batch, head_cols // n_batch, width), BF),
         pltpu.VMEM((n_batch, latent // n_batch, head_cols), BF),
+        pltpu.VMEM(down_part.shape, BF),
         pltpu.SemaphoreType.DMA((sems,)),
         pltpu.SemaphoreType.DMA((sems,)),
         pltpu.SemaphoreType.DMA((7,)),
     ]
-    args = [grad_att, qkv_all, turned, mixed, own_qup, own_out, grad_gu]
+    args = [grad_att, qkv_all, turned, mixed, own_qup, own_out, grad_gu, down_part]
     if has_terms:
         args.append(terms)
         out_shape.append(jax.ShapeDtypeStruct((n_tok, width), F32))
@@ -1596,7 +1648,7 @@
     grad_down = dot_left_t(activated, grad_rows)
     return (
         ring.collect(lambda step: in_terms[step]),
-        ctx_collect(grad_down.reshape(n_ctx, ff // n_ctx, width)),
+        near_collect(grad_down.reshape(n_ctx, ff // n_ctx, width)).astype(BF),
         out_terms,
         ctx_collect(grad_gu).astype(BF),
     )
@@ -1645,12 +1697,10 @@
         [attn_gain, mlp_gain, jnp.pad(query_gain, (0, own_rows - gain_rows))], axis=1
     )
     packed = jnp.concatenate([proj_in, jnp.pad(gains, ((0, 0), (0, 125)))], axis=1)
-    up_parts = query_up.reshape(gain_rows, n_ctx, heads * HD).swapaxes(0, 1)
     ff_all = gate_up.shape[1] // 2
     ff = ff_all // n_batch
-    gu_parts = gate_up.reshape(own_rows, 2, n_batch, ff).transpose(2, 1, 0, 3)
     packed, own_qup, own_out, gu_rows, own_down = spread_weights(
-        n_batch, packed, up_parts, proj_out, gu_parts, down_proj
+        n_batch, packed, query_up, proj_out, gate_up, down_proj
     )
     packed = packed.reshape(width, in_cols + 128)
     own_qup = own_qup.reshape(QR, heads * HD)
@@ -1696,18 +1746,18 @@
     mlp_in = (normed_two * gain_mlp).astype(BF)
     resident = 10 * n_batch * n_tok * width <= 24 * 1024 * 1024
     if resident:
-        grad_mlp_in, grad_down, terms, grad_gu_own = fused_mlp(
+        grad_mlp_in, down_part, terms, grad_gu_own = fused_mlp(
             n_batch, mlp_in, cots, gu_rows[0], gu_rows[1], own_down
         )
         terms = terms.reshape(n_batch, n_tok, width)
     else:
         terms = None
-        grad_mlp_in, grad_down, out_terms, grad_gu_own = permuted_mlp(
+        grad_mlp_in, down_part, out_terms, grad_gu_own = permuted_mlp(
             ring, mlp_in, cots, gu_rows, own_down
         )
     gain_mlp_term = jnp.sum(grad_mlp_in * normed_two, axis=0)
     grad_hidden = grad_out + norm_back(grad_mlp_in * gain_mlp, normed_two, scale_two)
-    back_own, out_grads, up_grads, grad_gu_own, *sums = attention_back(
+    back_own, out_grads, up_grads, grad_gu_own, grad_down, *sums = attention_back(
         n_batch,
         grad_hidden.astype(BF).reshape(micro, pos_dev, width),
         qkv_all,
@@ -1716,6 +1766,7 @@
         own_qup,
         own_out,
         grad_gu_own,
+        down_part,
         terms,
         (cos_all, sin_all, keep),
     )
@@ -1749,10 +1800,16 @@
         axis=2,
     )
     gain_terms = jnp.pad(gain_terms, ((0, 0), (0, 0), (0, 13), (0, part_cols - own_rows)))
-    grad_proj_out, grad_query_up, grad_proj_in, gain_sums = collect_weights(
-        n_batch, gain_rows, out_grads, up_grads, project_parts, attn_in_all, gain_terms.astype(BF)
-    )
-    grad_gate_up = grad_gu_own.transpose(2, 1, 0, 3).reshape(own_rows, 2 * ff_all).astype(F32)
+    grad_proj_out, grad_query_up, grad_proj_in, gain_sums, grad_gate_up = collect_weights(
+        n_batch,
+        gain_rows,
+        out_grads,
+        up_grads,
+        project_parts,
+        attn_in_all,
+        grad_gu_own,
+        gain_terms.astype(BF),
+    )
     gain_sums = gain_sums[:, :own_rows]
 
     return (

time: 589 us -> 548 us (0.930)
  Pallas kernels: 515 us -> 493 us
  local copies, waits for them, and re-layouts: 33.8 us -> 20.5 us
    pallas_call x1, Pallas kernels: 126 us -> 102 us  [fused_mlp(): pl.pallas_call(functools.partial(mlp_kernel, n_batch), out_shape=(jax.Sha...]
    convert_element_type x2 -> x0, local copies, waits for them, and re-layouts: 8.25 us -> none  [shards(): grad_gu_own.transpose(2, 1, 0, 3).reshape(own_rows, 2 * ff_all).astype(F32)]
    reshape x3 -> x0, local copies, waits for them, and re-layouts: 6.65 us -> none  [the longest x2 4.88 us: shards(): gu_parts = gate_up.reshape(own_rows, 2, n_batch, ff).transpose(2, 1, 0, 3)]
where the time goes in v5:
time: 548 us; the launch traced here: 547 us
  Pallas kernels  493 us (90%)
  other arithmetic  22.1 us (4%)
  local copies, waits for them, and re-layouts  20.5 us (4%)
  matrix products  10.3 us (2%)
    pallas_call x1, Pallas kernels, spread_weights(): pl.pallas_call(functools.partial(weights_kernel, n_batch), out_shape=shap...  152 us
    pallas_call x1, Pallas kernels, collect_weights(): pl.pallas_call(functools.partial(tail_kernel, n_batch, gain_rows), out_sh...  110 us
    pallas_call x1, Pallas kernels, fused_mlp(): pl.pallas_call(functools.partial(mlp_kernel, n_batch), out_shape=(jax.Sha...  102 us
    pallas_call x1, Pallas kernels, attention_back(): pl.pallas_call(functools.partial(attention_back_kernel, n_batch, head_col...  79.5 us
    pallas_call x1, Pallas kernels, attention(): pl.pallas_call(functools.partial(attention_kernel, n_batch, head_cols //...  49.8 us
    unnamed x38, local copies, waits for them, and re-layouts  11 us

profile of v5, /device:TPU:4, one launch (start us, length us, event | category | flops | bytes accessed | tf_op | source)
XLA Modules:
  0.0 547.0 jit_solution(11271379662974454508)
XLA Ops:
  3.1 1.2 fusion.17
  4.8 1.6 fusion.30.packed_ref
  7.0 2.1 fusion.5.cot_ref
  9.1 151.9 %spread_weights.1 = (bf16[8,4,64,1664]{3,2,1,0:T(8,128)(2,1)}, bf16[8,4,32,1024]{3,2,1,0:T(8,128)(2,1)}, bf16[8,128,2048]{2,1,0:T(8,128)(2,1)}, bf16[2,8,4,64,704]{4,3,2,1,0:T(8,128)(2,1)}, bf16[4,176,2048]{2,1,0:T(8,128)(2,1)}) custom-call(bf16[64,1664]{1,0:T(8,128)(2,1)} %fusion.30.packed_ref, bf16[32,4096]{1,0:T(8,128)(2,1)} %up_ref.1, ...), custom_call_target="tpu_custom_call" | custom-call | tf_op jit(solution)/shard_map/spread_weights/pallas_call | solution.py:480
  161.0 1.1 slice_convert_fusion
  162.9 3.9 fusion.2
  167.4 3.4 slice_bitcast_fusion
  170.8 49.8 %attention.1 = (f32[2,64,2048]{2,1,0:T(8,128)S(1)}, bf16[4,2,64,1536]{3,2,1,0:T(8,128)(2,1)S(1)}, bf16[2,256,1024]{2,1,0:T(8,128)(2,1)S(1)}, bf16[4,2,64,1024]{3...) custom-call(bf16[2,64,1536]{2,1,0:T(8,128)(2,1)S(1)} %pad_maximum_fusion.qkv_ref, ...), custom_call_target="tpu_custom_call" | custom-call | tf_op jit(solution)/shard_map/attention/pallas_call | solution.py:1328
  220.6 1.3 copy-done.2
  221.9 1.1 copy-done.3
  224.0 1.0 copy-done.8
  225.3 1.0 multiply_convert_fusion.rows_ref
  226.3 101.6 %fused_mlp.1 = (f32[128,2048]{1,0:T(8,128)}, bf16[2,176,2048]{2,1,0:T(8,128)(2,1)}, bf16[4,256,2048]{2,1,0:T(8,128)(2,1)}, bf16[8,2,64,704]{3,2,1,0:T(8,128)(2,1)}) custom-call(bf16[128,2048]{1,0:T(8,128)(2,1)} %multiply_convert_fusion.rows_ref, bf16[8,4,64,704]{3,2,1,0:T(8,128)(2,1)} %get-tuple-element.71.gate_ref, ...), custom_call_target="tpu_custom_call" | custom-call | flops 26575110144 | bytes 25165824 | tf_op jit(solution)/shard_map/fused_mlp/pallas_call | solution.py:795
  327.9 1.7 multiply_reduce_fusion
  330.3 2.7 fusion.33
  333.1 79.5 %attention_back.1 = (f32[2,64,1536]{2,1,0:T(8,128)}, bf16[8,128,2048]{2,1,0:T(8,128)(2,1)}, bf16[8,128,1024]{2,1,0:T(8,128)(2,1)}, bf16[8,2,64,704]{3,2,1,0:T(8,...) custom-call(bf16[2,64,2048]{2,1,0:T(8,128)(2,1)} %bitcast.98, bf16[4,2,64,1536]{3,2,1,0:T(8,128)(2,1)} %copy-done.3, ...), custom_call_target="tpu_custom_call" | custom-call | tf_op jit(solution)/shard_map/attention_back/pallas_call | solution.py:1599
  412.6 1.3 multiply_reduce_fusion.2
  413.9 1.2 subtract_multiply_fusion
  417.7 6.4 %fusion.16 = (bf16[2048]{0:T(1024)(128)(2,1)S(1)}, f32[128]{0:T(128)}, f32[128,2048]{1,0:T(8,128)}) fusion(bf16[2,64,2048]{2,1,0:T(8,128)(2,1)S(1)} %copy-done.10, f32[128]{0:T(128)S(1)} %rsqrt.31, f32[2048]{0:T(1024)S(1)} %bitcast.117, bf16[2048,1664]{1,0:T(8,128)(2,1)} %bitcast.122, bf16[128,256]{1,0:T(8,128)(2,1)S(1)} %slice.104, ...), kind=kOutput, calls=%fused_computation.23 | convolution fusion | flops 808318848 | bytes 8270848 | tf_op jit(solution)/shard_map/dot_general | solution.py:52
  425.4 3.2 fusion.15
  429.6 110.3 %collect_weights.1 = (f32[128,2048]{1,0:T(8,128)S(1)}, f32[32,4096]{1,0:T(8,128)S(1)}, f32[64,1536]{1,0:T(8,128)S(1)}, f32[16,384]{1,0:T(8,128)S(1)}, f32[64,11264]{1,0:T(8,128)}) custom-call(bf16[8,128,2048]{2,1,0:T(8,128)(2,1)} %get-tuple-element.52.out_ref, bf16[8,128,1024]{2,1,0:T(8,128)(2,1)} %get-tuple-element.53.up_ref, ...), custom_call_target="tpu_custom_call" | custom-call | tf_op jit(solution)/shard_map/collect_weights/pallas_call | solution.py:1090
  542.5 1.0 copy.71
  543.5 1.6 copy.72
  545.9 1.1 copy.73
  (80 shorter events, 14.9 us)
Async XLA Ops:
  4.5 166.3 %copy-start.9 = (f32[2,1,256]{2,1,0:T(1,128)}, f32[2,1,256]{2,1,0:T(1,128)S(1)}, u32[]{:S(2)}) copy-start(f32[2,1,256]{2,1,0:T(1,128)S(1)} %compare_convert_fusion.keep_ref.refs_3_) | copy-start | bytes 6148
  7.0 163.8 %copy-start.5 = (f32[256,128]{1,0:T(8,128)}, f32[256,128]{1,0:T(8,128)S(1)}, u32[]{:S(2)}) copy-start(f32[256,128]{1,0:T(8,128)S(1)} %get-tuple-element.83.sin_ref.refs_2_) | copy-start | bytes 393220
  7.0 163.8 %copy-start.6 = (f32[256,128]{1,0:T(8,128)}, f32[256,128]{1,0:T(8,128)S(1)}, u32[]{:S(2)}) copy-start(f32[256,128]{1,0:T(8,128)S(1)} %get-tuple-element.84.cos_ref.refs_1_) | copy-start | bytes 393220
  9.1 153.5 %copy-start.10 = (bf16[2,64,2048]{2,1,0:T(8,128)(2,1)S(1)}, bf16[2,64,2048]{2,1,0:T(8,128)(2,1)}, u32[]{:S(2)}) copy-start(bf16[2,64,2048]{2,1,0:T(8,128)(2,1)} %param.12) | copy-start | bytes 1572868
  162.6 4.5 slice-start
  162.8 4.5 slice-start.1
  167.4 3.4 copy-start
  167.4 3.4 copy-start.1
  220.6 1.3 copy-start.2
  221.9 1.1 copy-start.3
  223.1 1.0 copy-start.7
  224.0 1.0 copy-start.8
  327.9 2.4 copy-start.11
  424.6 5.0 copy-start.4
  539.9 3.6 copy-start.12
  543.5 2.4 copy-start.13

commit v6 on v5

--- a/solution.py
+++ b/solution.py
@@ -303,202 +303,10 @@
         return [self.place.rank_of(-step), self.place.rank_of(step)]
 
 
-def weights_kernel(
-    n_batch,
-    packed_ref,
-    up_ref,
-    out_ref,
-    gu_ref,
-    down_ref,
-    packed_all,
-    up_all,
-    out_all,
-    gu_all,
-    down_all,
-    send_sems,
-    recv_sems,
-    out_sems,
-    flat_v,
-    gu_v,
-):
-    place = Place(n_batch)
-    copies = Copies(send_sems, recv_sems)
-    b, c, n = place.b, place.c, n_batch
-    own_rows = packed_ref.shape[0]
-    out_rows = out_ref.shape[0]
-    index = b * 4 + c
-    target = (lax.rem(index, n), lax.div(index, n))
-    slab = c * n + b
-    source = (lax.div(slab, 4), lax.rem(slab, 4))
-    stays = slab == index
-    peers = [(lax.rem(b + k, n), c) for k in range(1, n)]
-    ctx_peers = [(b, place.far), (b, place.near), (b, lax.rem(place.near + 2, 4))]
-
-    barrier = greet(place, peers + ctx_peers)
-
-    @pl.when(jnp.logical_not(stays))
-    def _():
-        for device in (target, source):
-            pl.semaphore_signal(barrier, inc=1, device_id=device, device_id_type=MESH)
-
-    pl.semaphore_wait(barrier, n + 4 - 2 * stays.astype(jnp.int32))
-
-    head_cols = up_ref.shape[1] // 4
-
-    def up_cols(rank):
-        return up_ref.at[:, pl.ds(pl.multiple_of(rank * head_cols, head_cols), head_cols)]
-
-    own = [
-        copies.local(packed_ref, packed_all.at[b, c]),
-        copies.local(up_cols(c), up_all.at[b, c]),
-        copies.local(gu_ref, flat_v),
-        copies.local(down_ref, down_all.at[c]),
-    ]
-    out_copy = pltpu.make_async_remote_copy(
-        src_ref=out_ref,
-        dst_ref=out_all.at[target[0]],
-        send_sem=out_sems.at[0],
-        recv_sem=out_sems.at[1],
-        device_id=target,
-        device_id_type=MESH,
-    )
-    out_stay = pltpu.make_async_copy(out_ref, out_all.at[b], out_sems.at[0])
-
-    @pl.when(jnp.logical_not(stays))
-    def _():
-        out_copy.start()
-
-    @pl.when(stays)
-    def _():
-        out_stay.start()
-
-    up_copies = [
-        copies.remote(up_cols(peer[1]), up_all.at[b, c], peer) for peer in ctx_peers
-    ]
-    far_device, near_device = ctx_peers[0], ctx_peers[1]
-    down_far = copies.remote(down_ref, down_all.at[c], far_device)
-
-    copies.arrive(own[0])
-    packed_ring = RingGather(
-        place, copies, own_rows, lambda rank, rows: packed_all.at[rank, c, rows]
-    )
-    up_ring = RingGather(
-        place, copies, up_ref.shape[0], lambda rank, rows: up_all.at[rank, :, rows]
-    )
-    out_ring = RingGather(place, copies, out_rows, lambda rank, rows: out_all.at[rank, rows])
-
-    packed_far = []
-
-    def packed_step():
-        packed_ring.advance()
-        ranks = packed_ring.arrived() if packed_ring.step > 1 else [b]
-        for rank in ranks:
-            block = packed_all.at[rank, c]
-            packed_far.append((rank, copies.remote(block, block, far_device)))
-
-    packed_step()
-    copies.arrive(own[2])
-    ff = gu_v.shape[3]
-    for slab_at in range(n):
-        for kind in (0, 1):
-            start = (kind * n + slab_at) * ff
-            gu_v[slab_at, kind] = flat_v[:, start : start + ff]
-    own.append(copies.local(gu_v.at[b], gu_all.at[:, b, c]))
-    gu_copies = [
-        (
-            lax.rem(b - k + n, n),
-            copies.remote(gu_v.at[peer[0]], gu_all.at[:, b, c], peer),
-        )
-        for k, peer in zip(range(1, n), peers)
-    ]
-    for copy in own[1:2] + up_copies:
-        copies.arrive(copy)
-    up_ring.advance()
-    packed_step()
-
-    @pl.when(jnp.logical_not(stays))
-    def _():
-        out_copy.wait()
-
-    @pl.when(stays)
-    def _():
-        out_stay.wait()
-
-    out_ring.advance()
-    gu_far = []
-    copies.arrive(own[4])
-    own_gu = gu_all.at[:, b, c]
-    gu_far.append(copies.remote(own_gu, own_gu, far_device))
-    waiting = list(gu_copies)
-    copies.arrive(own[3])
-    down_near = [copies.remote(down_all.at[c], down_all.at[c], near_device)]
-
-    def forward_gu(count):
-        for _ in range(min(count, len(waiting))):
-            rank, copy = waiting.pop(0)
-            copies.arrive(copy)
-            block = gu_all.at[:, rank, c]
-            gu_far.append(copies.remote(block, block, far_device))
-
-    for _ in range(place.h):
-        up_ring.advance()
-        if packed_ring.step <= place.h:
-            packed_step()
-        forward_gu(2)
-        out_ring.advance()
-    copies.arrive(down_far)
-    far = place.far
-    down_near.append(copies.remote(down_all.at[far], down_all.at[far], near_device))
-    forward_gu(n)
-    own_packed = packed_all.at[:, c]
-    copies.remote(own_packed, own_packed, near_device)
-    own_gu = gu_all.at[:, :, c]
-    copies.remote(own_gu, own_gu, near_device)
-    for _, copy in packed_far:
-        copies.arrive(copy)
-    far_packed = packed_all.at[:, far]
-    copies.remote(far_packed, far_packed, near_device)
-    for copy in gu_far:
-        copies.arrive(copy)
-    far_gu = gu_all.at[:, :, far]
-    copies.remote(far_gu, far_gu, near_device)
-    copies.drain()
-
-
-def spread_weights(n_batch, packed, up_rows, out_rows, gu_rows, down_rows):
-    own_rows, packed_cols = packed.shape
-    gain_rows, up_cols = up_rows.shape
-    ff = gu_rows.shape[1] // (2 * n_batch)
-    shapes = (
-        jax.ShapeDtypeStruct((n_batch, 4, own_rows, packed_cols), BF),
-        jax.ShapeDtypeStruct((n_batch, 4, gain_rows, up_cols // 4), BF),
-        jax.ShapeDtypeStruct((n_batch,) + out_rows.shape, BF),
-        jax.ShapeDtypeStruct((2, n_batch, 4, own_rows, ff), BF),
-        jax.ShapeDtypeStruct((4,) + down_rows.shape, BF),
-    )
-    sems = 6 * n_batch + 3 * n_batch + 32
-    return pl.pallas_call(
-        functools.partial(weights_kernel, n_batch),
-        out_shape=shapes,
-        in_specs=[pl.BlockSpec(memory_space=pl.ANY)] * 5,
-        out_specs=[pl.BlockSpec(memory_space=pl.ANY)] * 5,
-        scratch_shapes=[
-            pltpu.SemaphoreType.DMA((sems,)),
-            pltpu.SemaphoreType.DMA((sems,)),
-            pltpu.SemaphoreType.DMA((2,)),
-            pltpu.VMEM(gu_rows.shape, BF),
-            pltpu.VMEM((n_batch, 2, own_rows, ff), BF),
-        ],
-        compiler_params=pltpu.CompilerParams(collective_id=0, has_side_effects=True),
-        name="spread_weights",
-    )(packed, up_rows, out_rows, gu_rows, down_rows)
-
-
 def mlp_kernel(
     n_batch,
     rows_ref,
-    gate_ref,
-    up_ref,
+    gu_ref,
     down_ref,
     cot_ref,
     *refs,
@@ -536,7 +344,7 @@
     n_tok = rows_ref.shape[0]
     cut = n_tok // 2
     width = rows_ref.shape[1]
-    ff = gate_ref.shape[-1]
+    ff = gu_ref.shape[-1]
     up_device, down_device = place.up(), place.down()
     far_device, near_device = (place.b, place.far), (place.b, place.near)
     barrier = greet(place, [up_device, down_device, far_device, near_device])
@@ -549,7 +357,7 @@
     loads = [
         pltpu.make_async_copy(source, target, load_sems.at[1 + i])
         for i, (source, target) in enumerate(
-            [(gate_ref, gate_v), (up_ref, up_v), (down_ref, down_v)]
+            [(gu_ref.at[0], gate_v), (gu_ref.at[1], up_v), (down_ref, down_v)]
         )
     ]
     spots = [(0, 0, 0), (far, 0, 1)]
@@ -785,10 +593,10 @@
             copy.wait()
 
 
-def fused_mlp(n_batch, rows, cots, own_gate, own_up, own_down):
+def fused_mlp(n_batch, rows, cots, gu_rows, own_down):
     n_tok, width = rows.shape
-    ff = own_gate.shape[-1]
-    own_rows = own_gate.shape[2]
+    ff = gu_rows.shape[-1]
+    own_rows = gu_rows.shape[3]
     far = n_batch // 2
     pair = 2 * n_tok
     flops = 18 * n_batch * n_tok * width * ff
@@ -800,7 +608,7 @@
             jax.ShapeDtypeStruct((far, pair, width), BF),
             jax.ShapeDtypeStruct((n_batch, 2, own_rows, ff), BF),
         ),
-        in_specs=[pl.BlockSpec(memory_space=pl.ANY)] * 5,
+        in_specs=[pl.BlockSpec(memory_space=pl.ANY)] * 4,
         out_specs=[pl.BlockSpec(memory_space=pltpu.VMEM)]
         + [pl.BlockSpec(memory_space=pl.ANY)] * 3,
         scratch_shapes=[
@@ -834,7 +642,7 @@
             flops=flops, bytes_accessed=24 * 1024 * 1024, transcendentals=n_batch * n_tok * ff
         ),
         name="fused_mlp",
-    )(rows, own_gate, own_up, own_down, cots)
+    )(rows, gu_rows, own_down, cots)
 
 
 class RingCollect:
@@ -917,8 +725,6 @@
     out_got,
     up_got,
     in_got,
-    out_sum,
-    out_all,
     up_sum,
     up_all,
     in_sum,
@@ -931,17 +737,12 @@
     rows_v,
     gu_v,
     load_sems,
-    out_sems,
 ):
     place = Place(n_batch)
     copies = Copies(send_sems, recv_sems)
     b, c, n = place.b, place.c, n_batch
     own_rows = in_grad.shape[0]
-    index = b * 4 + c
-    slab = c * n + b
-    target = (lax.div(slab, 4), lax.rem(slab, 4))
-    source = (lax.rem(index, n), lax.div(index, n))
-    stays = slab == index
+    group = HeadGroup(place, out_grad.shape[0])
     ctx_peers = [(b, place.far), (b, place.near), (b, lax.rem(place.near + 2, 4))]
 
     loads = [
@@ -952,12 +753,7 @@
         copy.start()
     barrier = greet(place, [place.up(), place.down()] + ctx_peers)
 
-    @pl.when(jnp.logical_not(stays))
-    def _():
-        for device in (target, source):
-            pl.semaphore_signal(barrier, inc=1, device_id=device, device_id_type=MESH)
-
-    pl.semaphore_wait(barrier, 7 - 2 * stays.astype(jnp.int32))
+    pl.semaphore_wait(barrier, 5)
 
     rings = []
     for i, (kept, got) in enumerate([(out_v, out_got), (up_v, up_got), (in_v, in_got)]):
@@ -1013,25 +809,7 @@
     in_ring, up_ring, out_ring = rings[2], rings[1], rings[0]
     out_cut, up_cut, in_cut = out_ring.cut, up_ring.cut, in_ring.cut
     for half in (0, 1):
-        out_sum[pl.ds(half * out_cut, out_cut), :] = out_ring.finish(half).astype(BF)
-    out_copy = pltpu.make_async_remote_copy(
-        src_ref=out_sum,
-        dst_ref=out_all,
-        send_sem=out_sems.at[0],
-        recv_sem=out_sems.at[1],
-        device_id=target,
-        device_id_type=MESH,
-    )
-    out_stay = pltpu.make_async_copy(out_sum, out_all, out_sems.at[0])
-
-    @pl.when(jnp.logical_not(stays))
-    def _():
-        out_copy.start()
-
-    @pl.when(stays)
-    def _():
-        out_stay.start()
-
+        out_grad[half * out_cut : (half + 1) * out_cut, :] = out_ring.finish(half)
     for half in (0, 1):
         up_sum[pl.ds(half * up_cut, up_cut), :] = up_ring.finish(half).astype(BF)
     up_copies = [
@@ -1051,20 +829,16 @@
     ]
     in_copies.append(copies.local(in_sum.at[pl.ds(c * part_rows, part_rows)], in_all.at[c]))
 
-    @pl.when(jnp.logical_not(stays))
-    def _():
-        out_copy.wait()
-
-    @pl.when(stays)
-    def _():
-        out_stay.wait()
-
-    out_grad[...] = out_all[...].astype(F32)
     for copy in up_copies:
         copies.arrive(copy)
     cols = up_all.shape[2]
+    heads = cols // HD
     for part in range(4):
-        up_grad[:, part * cols : (part + 1) * cols] = up_all[part].astype(F32)
+        for local in range(heads):
+            head = group.head(part, local, heads)
+            up_grad[:, head * HD : (head + 1) * HD] = up_all[
+                part, :, local * HD : (local + 1) * HD
+            ].astype(F32)
     for copy in in_copies:
         copies.arrive(copy)
     cols = in_all.shape[2]
@@ -1101,8 +875,6 @@
         scratch_shapes=[pltpu.VMEM((n_batch,) + shape, BF) for shape in shapes]
         + [pltpu.VMEM((far, 2, 2, rows // 2, cols), BF) for rows, cols in shapes]
         + [
-            pltpu.VMEM((out_rows, width), BF),
-            pltpu.VMEM((out_rows, width), BF),
             pltpu.VMEM((up_rows, up_cols), BF),
             pltpu.VMEM((4, gain_rows, up_cols), BF),
             pltpu.VMEM((in_rows, in_cols), BF),
@@ -1115,7 +887,6 @@
             pltpu.VMEM(attn_in_all.shape, BF),
             pltpu.VMEM(grad_gu.shape, BF),
             pltpu.SemaphoreType.DMA((4,)),
-            pltpu.SemaphoreType.DMA((2,)),
         ],
         compiler_params=pltpu.CompilerParams(
             collective_id=2, has_side_effects=True, vmem_limit_bytes=48 * 1024 * 1024
@@ -1205,27 +976,69 @@
     raised = jnp.exp(masked - jnp.max(masked, axis=-1, keepdims=True))
     return raised / jnp.sum(raised, axis=-1, keepdims=True)
 
-
-def attention_kernel(
+def head_group(n_batch, own_rows):
+    return min(4, HD // own_rows)
+
+
+class HeadGroup:
+    def __init__(self, place, own_rows):
+        self.size = head_group(place.n, own_rows)
+        self.count = place.n // self.size
+        if self.size == 2:
+            self.me = place.inner
+            self.others = [(1 - place.inner, (place.b, place.near))]
+        else:
+            self.me = place.c
+            ranks = [place.far, place.near, lax.rem(place.near + 2, 4)]
+            self.others = [(rank, (place.b, rank)) for rank in ranks]
+
+    def blocks(self, member):
+        return pl.ds(member * self.count, self.count)
+
+    def head(self, rank, local, heads):
+        if self.size == 2:
+            return 2 * (heads * (rank % 2) + local) + rank // 2
+        return heads * rank + local
+
+
+def front_kernel(
     n_batch,
     heads,
-    qkv_ref,
-    rows_ref,
-    cot_ref,
+    packed_ref,
     up_ref,
     out_ref,
+    gu_ref,
+    down_ref,
+    tokens_ref,
+    cot_ref,
     cos_ref,
     sin_ref,
+    cos_own_ref,
+    sin_own_ref,
     keep_ref,
-    attended,
+    hidden,
+    mlp_in,
+    gains,
+    latents,
+    packed_out,
+    up_out,
+    out_out,
+    gu_all,
+    down_all,
     qkv_out,
     turned_out,
     mixed_out,
     rows_all,
     cot_all,
+    packed_v,
+    flat_v,
+    gu_v,
+    half_v,
+    out_v,
+    up_v,
+    tokens_v,
+    rows_v,
     qkv_v,
-    up_v,
-    out_v,
     turned_v,
     mixed_v,
     part_v,
@@ -1233,128 +1046,298 @@
     far_got,
     send_sems,
     recv_sems,
-    load_sems,
 ):
     place = Place(n_batch)
     copies = Copies(send_sems, recv_sems)
-    b, c = place.b, place.c
-    micro, pos_dev = qkv_ref.shape[:2]
-    n_tok = micro * pos_dev
+    b, c, n = place.b, place.c, n_batch
+    own_rows = packed_ref.shape[0]
+    gain_rows = up_ref.shape[0]
+    out_rows = out_ref.shape[0]
+    n_tok, width = tokens_ref.shape
+    micro, pos_dev = qkv_v.shape[1:3]
     length = 4 * pos_dev
+    in_cols = qkv_v.shape[3]
+    latent = in_cols - 2 * HD
+    ff = gu_v.shape[3]
     score_scale = 1.0 / math.sqrt(HD)
-    loads = [
-        pltpu.make_async_copy(source, target, load_sems.at[i])
-        for i, (source, target) in enumerate(
-            [(qkv_ref, qkv_v.at[c]), (up_ref, up_v), (out_ref, out_v)]
-        )
+    group = HeadGroup(place, out_rows)
+    peers = [(lax.rem(b + k, n), c) for k in range(1, n)]
+    ctx_peers = [(b, place.far), (b, place.near), (b, lax.rem(place.near + 2, 4))]
+    far_device, near_device = ctx_peers[0], ctx_peers[1]
+
+    barrier = greet(place, peers + ctx_peers)
+    own_packed = copies.local(packed_ref, packed_v.at[b, c])
+    own_out = copies.local(out_ref, half_v.at[b])
+    own_tokens = copies.local(tokens_ref, tokens_v)
+    own_flat = copies.local(gu_ref, flat_v)
+    own_down = copies.local(down_ref, down_all.at[c])
+    own_cot = copies.local(cot_ref, cot_all.at[b])
+
+    def up_cols(rank, local):
+        start = pl.multiple_of(group.head(rank, local, heads) * HD, HD)
+        return up_ref.at[:, pl.ds(start, HD)]
+
+    own_up = [
+        copies.local(up_cols(c, local), up_v.at[b, c, :, pl.ds(local * HD, HD)])
+        for local in range(heads)
     ]
-    for copy in loads:
-        copy.start()
-    greet_lines(place)
-    loads[0].wait()
+    pl.semaphore_wait(barrier, n + 2)
+    up_copies = [
+        copies.remote(up_cols(peer[1], local), up_v.at[b, c, :, pl.ds(local * HD, HD)], peer)
+        for peer in ctx_peers
+        for local in range(heads)
+    ]
+    copies.arrive(own_packed)
+    packed_ring = RingGather(place, copies, own_rows, lambda rank, rows: packed_v.at[rank, c, rows])
+    up_ring = RingGather(place, copies, gain_rows, lambda rank, rows: up_v.at[rank, :, rows])
+    out_ring = RingGather(place, copies, out_rows, lambda rank, rows: half_v.at[rank, rows])
+    cot_ring = RingGather(place, copies, n_tok, lambda rank, rows: cot_all.at[rank, rows])
+    packed_far = []
+
+    def packed_step():
+        packed_ring.advance()
+        ranks = packed_ring.arrived() if packed_ring.step > 1 else [b]
+        for rank in ranks:
+            block = packed_v.at[rank, c]
+            packed_far.append(copies.remote(block, block, far_device))
+
+    packed_step()
+    copies.arrive(own_out)
+    out_ring.advance()
+    for copy in own_up + up_copies:
+        copies.arrive(copy)
+    up_ring.advance()
+    packed_step()
+    copies.arrive(own_flat)
+    for slab_at in range(n):
+        for kind in (0, 1):
+            start = (kind * n + slab_at) * ff
+            gu_v[slab_at, kind] = flat_v[:, start : start + ff]
+    own_gu = copies.local(gu_v.at[b], gu_all.at[:, b, c])
+    up_ring.advance()
+    while packed_ring.step <= place.h:
+        packed_step()
+        up_ring.advance()
+        if out_ring.step < place.h - 1:
+            out_ring.advance()
+    gu_copies = []
+
+    def send_gu(count):
+        for _ in range(count):
+            k = len(gu_copies) + 1
+            if k < n:
+                peer = peers[k - 1]
+                copy = copies.remote(gu_v.at[peer[0]], gu_all.at[:, b, c], peer)
+                gu_copies.append((lax.rem(b - k + n, n), copy))
+
+    send_gu(n // 2)
+    mine = packed_v.at[:, c]
+    packed_near = [copies.remote(mine, mine, near_device)]
+    while up_ring.step <= place.h:
+        up_ring.advance()
+    out_ring.advance()
+    for copy in packed_far:
+        copies.arrive(copy)
+    theirs = packed_v.at[:, place.far]
+    packed_near.append(copies.remote(theirs, theirs, near_device))
+
+    copies.arrive(own_tokens)
+    residual = tokens_v[...].astype(F32)
+    normed = residual * rms_scale(residual)
+    for copy in packed_near:
+        copies.arrive(copy)
+    extra = packed_v[:, :, :, in_cols:].astype(F32)
+    gain_wide = jnp.transpose(extra.reshape(width, 128))
+    gain_query = jnp.transpose(extra[:, :, :gain_rows].reshape(latent, 128))[2:3]
+    gains[0:2, :] = gain_wide[0:2]
+    gains[2:3, :latent] = gain_query
+    attn_in = (normed * gain_wide[0:1]).astype(BF)
+    rows_v[...] = attn_in
+    tile = 512
+    for start in range(0, in_cols, tile):
+        weights = packed_v[:, :, :, start : start + tile].reshape(width, tile)
+        part = dot(attn_in, weights)
+        if start + tile <= latent:
+            latents[:, start : start + tile] = part
+        else:
+            front, back = turn(part[:, :HD], cos_own_ref[...], sin_own_ref[...])
+            half = HD // 2
+            qkv_v[c, :, :, latent : latent + half] = (
+                front.astype(BF).reshape(micro, pos_dev, half)
+            )
+            qkv_v[c, :, :, latent + half : latent + HD] = (
+                back.astype(BF).reshape(micro, pos_dev, half)
+            )
+            qkv_v[c, :, :, latent + HD :] = part[:, HD:].astype(BF).reshape(micro, pos_dev, HD)
+    q_latent = latents[...]
+    q_normed = q_latent * rms_scale(q_latent) * gain_query
+    qkv_v[c, :, :, :latent] = q_normed.astype(BF).reshape(micro, pos_dev, latent)
     qkv = CtxGather(place, copies, qkv_v)
     for item in range(micro):
         qkv.start(item)
-    cot_own = copies.local(cot_ref, cot_all.at[b])
-    rows_own = copies.local(rows_ref, rows_all.at[c, 0])
-    copies.arrive(cot_own)
-    cots = RingGather(place, copies, n_tok, lambda rank, rows: cot_all.at[rank, rows])
-    cots.advance()
-    copies.arrive(rows_own)
-    rows = CtxGather(place, copies, rows_all)
+    while out_ring.step <= place.h:
+        out_ring.advance()
     for item in range(micro):
         qkv.cross(item)
+    out_swaps = [
+        copies.remote(half_v.at[group.blocks(member)], out_v.at[:, group.me], device)
+        for member, device in group.others
+    ]
+    out_swaps.append(copies.local(half_v.at[group.blocks(group.me)], out_v.at[:, group.me]))
+
+    send_gu(n)
+    copies.arrive(own_cot)
+    cot_ring.advance()
+    copies.arrive(own_gu)
+    gu_far = [copies.remote(gu_all.at[:, b, c], gu_all.at[:, b, c], far_device)]
+    copies.arrive(own_down)
+    down_far = copies.remote(down_ref, down_all.at[c], far_device)
+    copies.remote(down_ref, down_all.at[c], near_device)
+    copies.arrive(copies.local(rows_v, rows_all.at[c, 0]))
+    rows = CtxGather(place, copies, rows_all)
     rows.start(0)
-    for copy in loads[1:]:
-        copy.wait()
+    waiting = list(gu_copies)
+
+    def forward_gu(count):
+        for _ in range(min(count, len(waiting))):
+            rank, copy = waiting.pop(0)
+            copies.arrive(copy)
+            block = gu_all.at[:, rank, c]
+            gu_far.append(copies.remote(block, block, far_device))
+
     attended_sum = CtxCollect(place, copies, part_v, near_got, far_got)
     cosine, sine = cos_ref[...], sin_ref[...]
-    latent = qkv_v.shape[3] - 2 * HD
     for item in range(micro):
         qkv.finish(item)
-        q_normed = qkv_v[:, item, :, :latent].reshape(length, latent)
+        q_all = qkv_v[:, item, :, :latent].reshape(length, latent)
         keys = qkv_v[:, item, :, latent : latent + HD].reshape(length, HD)
         values = qkv_v[:, item, :, latent + HD :].reshape(length, HD)
         keep = keep_ref[item]
 
         @pl.loop(0, heads)
         def _(head):
-            cols = pl.ds(pl.multiple_of(head * HD, HD), HD)
-            front, back = turn(dot(q_normed, up_v[:, cols]), cosine, sine)
-            turned_v[item, :, pl.ds(pl.multiple_of(head * HD, HD), HD // 2)] = front.astype(BF)
-            turned_v[item, :, pl.ds(pl.multiple_of(head * HD + HD // 2, HD // 2), HD // 2)] = (
-                back.astype(BF)
-            )
+            base = pl.multiple_of(head * HD, HD)
+            cols = pl.ds(base, HD)
+            up = up_v[:, :, :, cols].reshape(latent, HD)
+            front, back = turn(dot(q_all, up), cosine, sine)
+            turned_v[item, :, pl.ds(base, HD // 2)] = front.astype(BF)
+            upper = pl.multiple_of(base + HD // 2, HD // 2)
+            turned_v[item, :, pl.ds(upper, HD // 2)] = back.astype(BF)
             weights = softmax_rows(turned_v[item, :, cols], keys, keep, score_scale)
             mixed = dot(weights.astype(BF), values).astype(BF)
             mixed_v[:, item, :, cols] = mixed.reshape(4, pos_dev, HD)
 
-        if cots.step <= place.h:
-            cots.advance()
+        forward_gu(n // 4)
+        if cot_ring.step <= place.h:
+            cot_ring.advance()
         mixed = mixed_v[:, item].reshape(length, heads * HD)
-        width = out_v.shape[1]
+        for copy in out_swaps:
+            copies.arrive(copy)
+        out_swaps = []
 
         @pl.loop(0, width // 512)
         def _(t):
             cols = pl.ds(pl.multiple_of(t * 512, 512), 512)
-            part = dot(mixed, out_v[:, cols]).astype(BF)
+            weights = out_v[:, :, :, cols].reshape(heads * HD, 512)
+            part = dot(mixed, weights).astype(BF)
             part_v[:, item, :, cols] = part.reshape(4, pos_dev, 512)
 
         attended_sum.start(item)
         if item > 0:
             attended_sum.cross(item - 1)
+    copies.local(packed_v, packed_out)
+    copies.local(up_v, up_out)
+    copies.local(out_v, out_out)
     copies.local(qkv_v, qkv_out)
     copies.local(turned_v, turned_out)
     copies.local(mixed_v, mixed_out)
-    if cots.step <= place.h:
-        cots.advance()
     attended_sum.cross(micro - 1)
     rows.cross(0)
+    if cot_ring.step <= place.h:
+        cot_ring.advance()
     for item in range(micro):
-        attended[item] = attended_sum.finish(item)
-    while cots.step <= place.h:
-        cots.advance()
+        at = slice(item * pos_dev, (item + 1) * pos_dev)
+        total = tokens_v[at, :].astype(F32) + attended_sum.finish(item)
+        hidden[at, :] = total
+        mlp_in[at, :] = (total * rms_scale(total) * gains[1:2, :]).astype(BF)
+    forward_gu(n // 4)
+    while cot_ring.step <= place.h:
+        cot_ring.advance()
+        forward_gu(n // 4)
+    forward_gu(n)
+    cot_ring.advance()
+    mine = gu_all.at[:, :, c]
+    copies.remote(mine, mine, near_device)
+    copies.arrive(down_far)
+    copies.remote(down_all.at[place.far], down_all.at[place.far], near_device)
+    for copy in gu_far:
+        copies.arrive(copy)
+    theirs = gu_all.at[:, :, place.far]
+    copies.remote(theirs, theirs, near_device)
     copies.drain()
 
 
-def attention(n_batch, qkv, attn_in, grad_mo, own_qup, own_out, cos_all, sin_all, keep):
-    micro, pos_dev, qkv_cols = qkv.shape
-    n_tok, width = attn_in.shape
-    latent, head_cols = own_qup.shape
-    length = 4 * pos_dev
-    sems = 2 * n_batch + 48
+def front(n_batch, heads, packed, query_up, proj_out, gate_up, down, tokens, cots, tables):
+    own_rows, packed_cols = packed.shape
+    in_cols = packed_cols - 128
+    latent = in_cols - 2 * HD
+    gain_rows = query_up.shape[0]
+    out_rows, width = proj_out.shape
+    n_tok = cots.shape[0]
+    pos_dev = tables[0].shape[0] // 4
+    micro = n_tok // pos_dev
+    ff = gate_up.shape[1] // (2 * n_batch)
+    size = head_group(n_batch, out_rows)
+    head_cols = heads * HD
+    shapes = {
+        "packed": (n_batch, 4, own_rows, packed_cols),
+        "up": (n_batch, 4, gain_rows, head_cols),
+        "out": (n_batch // size, size, out_rows, width),
+        "gu": (2, n_batch, 4, own_rows, ff),
+        "down": (4,) + down.shape,
+        "qkv": (4, micro, pos_dev, in_cols),
+        "turned": (micro, 4 * pos_dev, head_cols),
+        "mixed": (4, micro, pos_dev, head_cols),
+        "rows": (4, 1, n_tok, width),
+        "cot": (n_batch, n_tok, width),
+    }
     anywhere = pl.BlockSpec(memory_space=pl.ANY)
     near = pl.BlockSpec(memory_space=pltpu.VMEM)
+    sems = 13 * n_batch + 100
     return pl.pallas_call(
-        functools.partial(attention_kernel, n_batch, head_cols // HD),
+        functools.partial(front_kernel, n_batch, heads),
         out_shape=(
-            jax.ShapeDtypeStruct((micro, pos_dev, width), F32),
-            jax.ShapeDtypeStruct((4, micro, pos_dev, qkv_cols), BF),
-            jax.ShapeDtypeStruct((micro, length, head_cols), BF),
-            jax.ShapeDtypeStruct((4, micro, pos_dev, head_cols), BF),
-            jax.ShapeDtypeStruct((4, 1, n_tok, width), BF),
-            jax.ShapeDtypeStruct((n_batch, n_tok, width), BF),
-        ),
-        in_specs=[anywhere] * 5 + [near] * 3,
-        out_specs=[near] + [anywhere] * 5,
+            jax.ShapeDtypeStruct((n_tok, width), F32),
+            jax.ShapeDtypeStruct((n_tok, width), BF),
+            jax.ShapeDtypeStruct((8, width), F32),
+            jax.ShapeDtypeStruct((n_tok, latent), F32),
+        )
+        + tuple(jax.ShapeDtypeStruct(shape, BF) for shape in shapes.values()),
+        in_specs=[anywhere] * 7 + [near] * 5,
+        out_specs=[near] * 4 + [anywhere] * len(shapes),
         scratch_shapes=[
-            pltpu.VMEM((4, micro, pos_dev, qkv_cols), BF),
-            pltpu.VMEM((latent, head_cols), BF),
-            pltpu.VMEM((head_cols, width), BF),
-            pltpu.VMEM((micro, length, head_cols), BF),
-            pltpu.VMEM((4, micro, pos_dev, head_cols), BF),
+            pltpu.VMEM(shapes["packed"], BF),
+            pltpu.VMEM(gate_up.shape, BF),
+            pltpu.VMEM((n_batch, 2, own_rows, ff), BF),
+            pltpu.VMEM((n_batch, out_rows, width), BF),
+            pltpu.VMEM(shapes["out"], BF),
+            pltpu.VMEM(shapes["up"], BF),
+            pltpu.VMEM((n_tok, width), BF),
+            pltpu.VMEM((n_tok, width), BF),
+            pltpu.VMEM(shapes["qkv"], BF),
+            pltpu.VMEM(shapes["turned"], BF),
+            pltpu.VMEM(shapes["mixed"], BF),
             pltpu.VMEM((4, micro, pos_dev, width), BF),
             pltpu.VMEM((2, micro, pos_dev, width), BF),
             pltpu.VMEM((micro, pos_dev, width), BF),
             pltpu.SemaphoreType.DMA((sems,)),
             pltpu.SemaphoreType.DMA((sems,)),
-            pltpu.SemaphoreType.DMA((3,)),
         ],
         compiler_params=pltpu.CompilerParams(
-            collective_id=3, has_side_effects=True, vmem_limit_bytes=40 * 1024 * 1024
+            collective_id=0, has_side_effects=True, vmem_limit_bytes=56 * 1024 * 1024
         ),
-        name="attention",
-    )(qkv, attn_in, grad_mo, own_qup, own_out, cos_all, sin_all, keep)
+        name="front",
+    )(packed, query_up, proj_out, gate_up, down, tokens, cots, *tables)
 
 
 def attention_back_kernel(
@@ -1429,8 +1412,10 @@
     for copy in loads:
         copy.start()
     peers = [(lax.rem(b + k, n), c) for k in range(1, n)]
-    others = peers + [(b, place.far), (b, place.near)]
-    pl.semaphore_wait(greet(place, others), n + 1)
+    others = peers + [(b, place.far), (b, place.near), (b, lax.rem(place.near + 2, 4))]
+    pl.semaphore_wait(greet(place, others), n + 2)
+    out_rows = out_terms.shape[1]
+    group = HeadGroup(place, out_rows)
     loads[0].wait()
     grads = CtxGather(place, copies, grad_v)
     for item in range(micro):
@@ -1475,7 +1460,7 @@
         @pl.loop(0, heads)
         def _(head):
             cols = pl.ds(pl.multiple_of(head * HD, HD), HD)
-            grad_mixed = dot_right_t(incoming, out_v[cols, :]).astype(BF)
+            grad_mixed = dot_right_t(incoming, out_v[head]).astype(BF)
             queries = turned_v[item, :, cols]
             weights = softmax_rows(queries, keys, keep, score_scale)
             grad_probs = dot_right_t(grad_mixed, values)
@@ -1503,8 +1488,6 @@
         if item > 0:
             back_sum.cross(item - 1)
     n_all = 4 * micro * pos_dev
-    out_rows = head_cols // n
-
     back_sum.cross(micro - 1)
     ring_step()
 
@@ -1514,9 +1497,12 @@
         term = dot_left_t(
             mixed_v[...].reshape(n_all, head_cols), grad_v[:, :, :, cols].reshape(n_all, 512)
         )
-        outgrad_v[:, :, cols] = term.astype(BF).reshape(n, out_rows, 512)
-
-    copies.local(outgrad_v, out_terms)
+        outgrad_v[:, :, :, cols] = term.astype(BF).reshape(group.count, group.size, out_rows, 512)
+
+    mine = out_terms.at[group.blocks(group.me)]
+    copies.local(outgrad_v.at[:, group.me], mine)
+    for member, device in group.others:
+        copies.remote(outgrad_v.at[:, member], mine, device)
     for item in range(micro):
         back_out[item] = back_sum.finish(item)
     ring_step()
@@ -1551,9 +1537,11 @@
     n_tok = micro * pos_dev
     qkv_cols = qkv_all.shape[3]
     latent, head_cols = own_qup.shape
+    own_out = own_out.reshape(head_cols // HD, HD, width)
     length = 4 * pos_dev
     far = n_batch // 2
     has_terms = terms is not None
+    size = head_group(n_batch, head_cols // n_batch)
     sems = 2 * n_batch + 48
     anywhere = pl.BlockSpec(memory_space=pl.ANY)
     near = pl.BlockSpec(memory_space=pltpu.VMEM)
@@ -1571,14 +1559,14 @@
         pltpu.VMEM((micro, length, head_cols), BF),
         pltpu.VMEM((4, micro, pos_dev, head_cols), BF),
         pltpu.VMEM((latent, head_cols), BF),
-        pltpu.VMEM((head_cols, width), BF),
+        pltpu.VMEM((head_cols // HD, HD, width), BF),
         pltpu.VMEM((4, micro, pos_dev, head_cols), BF),
         pltpu.VMEM((length, HD), F32),
         pltpu.VMEM((length, HD), F32),
         pltpu.VMEM((4, micro, pos_dev, qkv_cols), BF),
         pltpu.VMEM((2, micro, pos_dev, qkv_cols), BF),
         pltpu.VMEM((micro, pos_dev, qkv_cols), BF),
-        pltpu.VMEM((n_batch, head_cols // n_batch, width), BF),
+        pltpu.VMEM((n_batch // size, size, head_cols // n_batch, width), BF),
         pltpu.VMEM((n_batch, latent // n_batch, head_cols), BF),
         pltpu.VMEM(down_part.shape, BF),
         pltpu.SemaphoreType.DMA((sems,)),
@@ -1697,57 +1685,52 @@
         [attn_gain, mlp_gain, jnp.pad(query_gain, (0, own_rows - gain_rows))], axis=1
     )
     packed = jnp.concatenate([proj_in, jnp.pad(gains, ((0, 0), (0, 125)))], axis=1)
-    ff_all = gate_up.shape[1] // 2
-    ff = ff_all // n_batch
-    packed, own_qup, own_out, gu_rows, own_down = spread_weights(
-        n_batch, packed, query_up, proj_out, gate_up, down_proj
-    )
-    packed = packed.reshape(width, in_cols + 128)
-    own_qup = own_qup.reshape(QR, heads * HD)
-    own_out = own_out.reshape(heads * HD, width)
-    full_in = packed[:, :in_cols]
-    gains = packed[:, in_cols : in_cols + 3].T.astype(F32)
-    gain_norm = gains[0]
-    gain_mlp = gains[1]
-    gain_query = gains[2].reshape(n_batch * n_ctx, own_rows)[:, :gain_rows].reshape(QR)
-
     residual = tokens.reshape(n_tok, width).astype(F32)
     valid_rows = (query_pos[None, :] < own_lengths[:, None]).astype(F32).reshape(n_tok, 1)
     grad_out = cotangent.reshape(n_tok, width).astype(F32) * valid_rows
+    keep = (key_pos[None, None, :] < own_lengths[:, None, None]).astype(F32)
+    tables = (cos_all, sin_all, jnp.tile(cos_own, (micro, 1)), jnp.tile(sin_own, (micro, 1)), keep)
+    (
+        hidden_res,
+        mlp_in,
+        gains,
+        q_latent,
+        packed,
+        own_qup,
+        own_out,
+        gu_rows,
+        own_down,
+        qkv_all,
+        turned,
+        mixed,
+        attn_in_all,
+        cots,
+    ) = front(
+        n_batch,
+        heads,
+        packed,
+        query_up,
+        proj_out,
+        gate_up,
+        down_proj,
+        tokens.reshape(n_tok, width),
+        grad_out.astype(BF),
+        tables,
+    )
+    full_in = packed.reshape(width, in_cols + 128)[:, :in_cols]
+    own_qup = own_qup.reshape(QR, heads * HD)
+    gain_norm, gain_mlp, gain_query = gains[0], gains[1], gains[2, :QR]
     scale_one = rms_scale(residual)
     normed_one = residual * scale_one
-    attn_in = (normed_one * gain_norm).astype(BF)
-    projected = dot(attn_in, full_in)
-    q_latent = projected[:, :QR]
     scale_query = rms_scale(q_latent)
     normed_query = q_latent * scale_query
-    q_normed = (normed_query * gain_query).astype(BF)
-    k_rot = rotate(
-        projected[:, QR : QR + HD].reshape(micro, pos_dev, HD), cos_own, sin_own
-    ).astype(BF)
-    v_low = projected[:, QR + HD :].astype(BF)
-    qkv = jnp.concatenate([q_normed, k_rot.reshape(n_tok, HD), v_low], axis=1)
-    keep = (key_pos[None, None, :] < own_lengths[:, None, None]).astype(F32)
-    attended, qkv_all, turned, mixed, attn_in_all, cots = attention(
-        n_batch,
-        qkv.reshape(micro, pos_dev, in_cols),
-        attn_in,
-        grad_out.astype(BF),
-        own_qup,
-        own_out,
-        cos_all,
-        sin_all,
-        keep,
-    )
-    hidden_res = residual + attended.reshape(n_tok, width)
 
     scale_two = rms_scale(hidden_res)
     normed_two = hidden_res * scale_two
-    mlp_in = (normed_two * gain_mlp).astype(BF)
     resident = 10 * n_batch * n_tok * width <= 24 * 1024 * 1024
     if resident:
         grad_mlp_in, down_part, terms, grad_gu_own = fused_mlp(
-            n_batch, mlp_in, cots, gu_rows[0], gu_rows[1], own_down
+            n_batch, mlp_in, cots, gu_rows, own_down
         )
         terms = terms.reshape(n_batch, n_tok, width)
     else:

time: 548 us -> 512 us (0.934)
  Pallas kernels: 493 us -> 470 us
    pallas_call x2 -> x1, Pallas kernels: 202 us -> 182 us  [front(): pl.pallas_call(functools.partial(front_kernel, n_batch, heads), out_shape...]
    pallas_call x1, Pallas kernels: 110 us -> 91 us  [collect_weights(): pl.pallas_call(functools.partial(tail_kernel, n_batch, gain_rows), out_sh...]
    pallas_call x1, Pallas kernels: 102 us -> 117 us  [fused_mlp(): pl.pallas_call(functools.partial(mlp_kernel, n_batch), out_shape=(jax.Sha...]
    unnamed x38 -> x31, local copies, waits for them, and re-layouts: 11 us -> 6.07 us
where the time goes in v6:
time: 512 us; the launch traced here: 509 us
  Pallas kernels  470 us (92%)
  other arithmetic  16.7 us (3%)
  local copies, waits for them, and re-layouts  15.5 us (3%)
  matrix products  5.91 us (1%)
    pallas_call x1, Pallas kernels, front(): pl.pallas_call(functools.partial(front_kernel, n_batch, heads), out_shape...  182 us
    pallas_call x1, Pallas kernels, fused_mlp(): pl.pallas_call(functools.partial(mlp_kernel, n_batch), out_shape=(jax.Sha...  117 us
    pallas_call x1, Pallas kernels, collect_weights(): pl.pallas_call(functools.partial(tail_kernel, n_batch, gain_rows), out_sh...  91 us
    pallas_call x1, Pallas kernels, attention_back(): pl.pallas_call(functools.partial(attention_back_kernel, n_batch, head_col...  79.6 us

profile of v6, /device:TPU:4, one launch (start us, length us, event | category | flops | bytes accessed | tf_op | source)
XLA Modules:
  0.0 509.4 jit_solution(8578071427518253310)
XLA Ops:
  0.6 0.9 select_reduce_fusion
  1.7 2.0 fusion.3.cot_ref
  5.9 1.2 multiply_sine_fusion
  8.6 1.6 fusion.14.packed_ref
  10.2 182.3 %front.1 = (f32[128,2048]{1,0:T(8,128)}, bf16[128,2048]{1,0:T(8,128)(2,1)}, f32[8,2048]{1,0:T(8,128)}, f32[128,1024]{1,0:T(8,128)}, bf16[8,4,64,1664]{3,2,1,0:T(...) custom-call(bf16[64,1664]{1,0:T(8,128)(2,1)} %fusion.14.packed_ref, ...), custom_call_target="tpu_custom_call" | custom-call | tf_op jit(solution)/shard_map/front/pallas_call | solution.py:1307
  192.5 117.5 %fused_mlp.1 = (f32[128,2048]{1,0:T(8,128)}, bf16[2,176,2048]{2,1,0:T(8,128)(2,1)}, bf16[4,256,2048]{2,1,0:T(8,128)(2,1)}, bf16[8,2,64,704]{3,2,1,0:T(8,128)(2,1)}) custom-call(bf16[128,2048]{1,0:T(8,128)(2,1)} %get-tuple-element.40.rows_ref, bf16[2,8,4,64,704]{4,3,2,1,0:T(8,128)(2,1)} %get-tuple-element.41.gu_ref, ...), custom_call_target="tpu_custom_call" | custom-call | flops 26575110144 | bytes 25165824 | tf_op jit(solution)/shard_map/fused_mlp/pallas_call | solution.py:603
  310.2 1.0 fusion.19
  311.2 1.6 multiply_reduce_fusion
  312.8 1.5 fusion.17
  314.4 79.6 %attention_back.1 = (f32[2,64,1536]{2,1,0:T(8,128)}, bf16[8,128,2048]{2,1,0:T(8,128)(2,1)}, bf16[8,128,1024]{2,1,0:T(8,128)(2,1)}, bf16[8,2,64,704]{3,2,1,0:T(8,...) custom-call(bf16[2,64,2048]{2,1,0:T(8,128)(2,1)} %bitcast.43, bf16[4,2,64,1536]{3,2,1,0:T(8,128)(2,1)} %get-tuple-element.46.qkv_ref, ...), custom_call_target="tpu_custom_call" | custom-call | tf_op jit(solution)/shard_map/attention_back/pallas_call | solution.py:1587
  394.9 1.3 multiply_reduce_fusion.6
  396.2 1.2 subtract_multiply_fusion
  397.4 1.0 slice.53
  398.5 0.9 slice.56
  399.7 5.9 %multiply_reduce_fusion.1 = (bf16[2048]{0:T(1024)(128)(2,1)S(1)}, f32[128]{0:T(128)S(1)}, f32[128,2048]{1,0:T(8,128)}) fusion(f32[128]{0:T(128)S(1)} %rsqrt.29, bf16[2,64,2048]{2,1,0:T(8,128)(2,1)S(1)} %copy-done.3, f32[2048]{0:T(1024)S(1)} %bitcast.60, bf16[2048,1664]{1,0:T(8,128)(2,1)} %bitcast.64, bf16[128,256]{1,0:T(8,128)(2,1)S(1)} %slice.56, ...), kind=kOutput, calls=%fused_computation.6 | convolution fusion | flops 808318848 | bytes 8270848 | tf_op jit(solution)/shard_map/dot_general | solution.py:52
  406.0 1.0 maximum_convert_fusion
  407.1 0.9 copy.50
  408.0 1.2 copy.51
  409.2 91.0 %collect_weights.1 = (f32[128,2048]{1,0:T(8,128)S(1)}, f32[32,4096]{1,0:T(8,128)S(1)}, f32[64,1536]{1,0:T(8,128)S(1)}, f32[16,384]{1,0:T(8,128)S(1)}, f32[64,11264]{1,0:T(8,128)}) custom-call(bf16[8,128,2048]{2,1,0:T(8,128)(2,1)} %get-tuple-element.58.out_ref, bf16[8,128,1024]{2,1,0:T(8,128)(2,1)} %get-tuple-element.59.up_ref, ...), custom_call_target="tpu_custom_call" | custom-call | tf_op jit(solution)/shard_map/collect_weights/pallas_call | solution.py:864
  501.3 1.1 add_convert_fusion
  502.5 0.9 add_convert_fusion.1
  504.9 1.0 copy.65
  505.9 1.6 copy.66
  508.3 1.1 copy.67
  (62 shorter events, 9.1 us)
Async XLA Ops:
  192.5 117.5 %copy-start.1 = (f32[128,2048]{1,0:T(8,128)S(1)}, f32[128,2048]{1,0:T(8,128)}, u32[]{:S(2)}) copy-start(f32[128,2048]{1,0:T(8,128)} %get-tuple-element.39) | copy-start | bytes 3145732
  310.0 2.8 copy-start.6
  310.0 2.8 copy-start.8
  314.4 79.6 %copy-start.2 = (f32[128,1024]{1,0:T(8,128)S(1)}, f32[128,1024]{1,0:T(8,128)}, u32[]{:S(2)}) copy-start(f32[128,1024]{1,0:T(8,128)} %get-tuple-element.55) | copy-start | bytes 1572868
  394.0 5.4 %copy-start.3 = (bf16[2,64,2048]{2,1,0:T(8,128)(2,1)S(1)}, bf16[2,64,2048]{2,1,0:T(8,128)(2,1)}, u32[]{:S(2)}) copy-start(bf16[2,64,2048]{2,1,0:T(8,128)(2,1)} %param.12) | copy-start | bytes 1572868
  397.4 2.3 copy-start.12
  405.6 3.6 copy-start
  409.2 92.1 %copy-start.4 = (bf16[2,64,2048]{2,1,0:T(8,128)(2,1)S(1)}, bf16[2,64,2048]{2,1,0:T(8,128)(2,1)}, u32[]{:S(2)}) copy-start(bf16[2,64,2048]{2,1,0:T(8,128)(2,1)} %param.12) | copy-start | bytes 1572868
  409.2 92.1 %copy-start.5 = (f32[128,2048]{1,0:T(8,128)S(1)}, f32[128,2048]{1,0:T(8,128)}, u32[]{:S(2)}) copy-start(f32[128,2048]{1,0:T(8,128)} %get-tuple-element.75) | copy-start | bytes 3145732
  409.2 92.1 %copy-start.11 = (f32[128,2048]{1,0:T(8,128)S(1)}, f32[128,2048]{1,0:T(8,128)}, u32[]{:S(2)}) copy-start(f32[128,2048]{1,0:T(8,128)} %get-tuple-element.87) | copy-start | bytes 3145732
  500.3 2.2 copy-start.10
  502.5 3.4 copy-start.7
  505.9 2.4 copy-start.9

commit v7 on v6

--- a/solution.py
+++ b/solution.py
@@ -313,7 +313,7 @@
 ):
     (
         sum_ref,
-        down_part,
+        act_out,
         term_out,
         gu_out,
         rows_v,
@@ -329,7 +329,6 @@
         got_v,
         gu_got,
         gu_last,
-        down_got,
         send_sems,
         recv_sems,
         back_send,
@@ -401,7 +400,8 @@
 
     def stores(group):
         return [
-            pltpu.make_async_copy(term_v.at[group], term_out.at[group], store_sems.at[0, group])
+            pltpu.make_async_copy(term_v.at[group], term_out.at[group], store_sems.at[0, group]),
+            pltpu.make_async_copy(act_v.at[group], act_out.at[group], store_sems.at[1, group]),
         ]
 
     def compute(group):
@@ -494,14 +494,6 @@
             term = dot_left_t(rows, grads[...].reshape(n_batch * n_tok, ff))
             target[2 * t : 2 * t + 2] = term.astype(BF).reshape(2, 4, own_rows, ff)
 
-    def down_terms():
-        @pl.loop(0, width // (2 * block))
-        def _(t):
-            cols = pl.ds(pl.multiple_of(t * 2 * block, 2 * block), 2 * block)
-            grads = cot_v[:, :, cols].reshape(n_batch * n_tok, 2 * block)
-            term = dot_left_t(act_v[...].reshape(n_batch * n_tok, ff), grads)
-            down_v[:, :, cols] = term.astype(BF).reshape(4, ff // 4, 2 * block)
-
     def pass_all(step):
         for side, half in [(1, 0), (0, 1), (0, 0), (1, 1)]:
             if step < far - 1 or (side, half) in ends:
@@ -557,11 +549,6 @@
     while steps:
         ring_step()
     send_far(tiles - 1)
-    down_terms()
-    down_copies = [
-        parts.remote(down_v.at[2 * side + 1 - inner], down_got.at[side], near_device)
-        for side in (0, 1)
-    ]
     for half in (0, 1):
         for side in (0, 1):
             back_hop(0, side, half, held(0, 0, half)).wait_recv()
@@ -571,11 +558,6 @@
             + got_v[0, 0, half].astype(F32)
             + got_v[0, 1, half].astype(F32)
         )
-    for side in (0, 1):
-        parts.arrive(down_copies[side])
-        added = down_v[2 * side + inner].astype(F32) + down_got[side].astype(F32)
-        down_got[side] = added.astype(BF)
-    parts.local(down_got, down_part)
     for t in range(tiles):
         take_far(t)
     parts.drain()
@@ -604,7 +586,7 @@
         functools.partial(mlp_kernel, n_batch),
         out_shape=(
             jax.ShapeDtypeStruct((n_tok, width), F32),
-            jax.ShapeDtypeStruct((2, ff // 4, width), BF),
+            jax.ShapeDtypeStruct((far, pair, ff), BF),
             jax.ShapeDtypeStruct((far, pair, width), BF),
             jax.ShapeDtypeStruct((n_batch, 2, own_rows, ff), BF),
         ),
@@ -625,13 +607,12 @@
             pltpu.VMEM((far, 2, 2, n_tok // 2, width), BF),
             pltpu.VMEM((2, 2, n_batch, own_rows, ff), BF),
             pltpu.VMEM((2, n_batch, own_rows, ff), BF),
-            pltpu.VMEM((2, ff // 4, width), BF),
             pltpu.SemaphoreType.DMA((far + 1, 2, 2)),
             pltpu.SemaphoreType.DMA((far + 1, 2, 2)),
             pltpu.SemaphoreType.DMA((far, 2, 2)),
             pltpu.SemaphoreType.DMA((far, 2, 2)),
             pltpu.SemaphoreType.DMA((4 + n_batch,)),
-            pltpu.SemaphoreType.DMA((1, far)),
+            pltpu.SemaphoreType.DMA((2, far)),
             pltpu.SemaphoreType.DMA((72,)),
             pltpu.SemaphoreType.DMA((72,)),
         ],
@@ -710,15 +691,23 @@
     gain_rows,
     out_ref,
     up_ref,
-    project_ref,
     rows_ref,
     gu_ref,
-    gain_ref,
+    packed_ref,
+    back_ref,
+    latent_ref,
+    tokens_ref,
+    hidden_ref,
+    gains_ref,
+    mlp_term_ref,
+    cos_ref,
+    sin_ref,
     out_grad,
     up_grad,
     in_grad,
     gain_grad,
     gu_grad,
+    tokens_grad,
     out_v,
     up_v,
     in_v,
@@ -733,6 +722,8 @@
     ring_recv,
     send_sems,
     recv_sems,
+    packed_v,
+    project_own,
     project_v,
     rows_v,
     gu_v,
@@ -747,7 +738,7 @@
 
     loads = [
         pltpu.make_async_copy(held, kept, load_sems.at[i])
-        for i, (held, kept) in enumerate([(out_ref, out_v), (up_ref, up_v), (rows_ref, rows_v), (gu_ref, gu_v)])
+        for i, (held, kept) in enumerate([(out_ref, out_v), (up_ref, up_v), (rows_ref, rows_v), (gu_ref, gu_v), (packed_ref, packed_v)])
     ]
     for copy in loads:
         copy.start()
@@ -766,38 +757,83 @@
                 ring_recv.at[i],
             )
         )
-    part_cols = project_ref.shape[2]
-    project_copies = [
-        copies.remote(project_ref.at[peer[1]], project_v.at[c], peer) for peer in ctx_peers
-    ]
-    project_copies.append(copies.local(project_ref.at[c], project_v.at[c]))
     for copy, ring in zip(loads[:2], rings):
         copy.wait()
+        ring.advance()
+    part_cols = project_v.shape[2]
+    n_tok, width = tokens_ref.shape
+    latent = latent_ref.shape[1]
+
+    q_latent = latent_ref[...]
+    inverse = rms_scale(q_latent)
+    normed_query = q_latent * inverse
+    grad_qn = back_ref[:, :latent]
+    query_term = jnp.sum(grad_qn * normed_query, axis=0, keepdims=True)
+    grad_latent = norm_back(grad_qn * gains_ref[2:3, :latent], normed_query, inverse)
+    front, back = turn(back_ref[:, latent : latent + HD], cos_ref[...], -sin_ref[...])
+    project = jnp.concatenate(
+        [grad_latent, front, back, back_ref[:, latent + HD :]], axis=1
+    ).astype(BF)
+    for part in range(4):
+        project_own[part] = project[:, part * part_cols : (part + 1) * part_cols]
+    project_copies = [
+        copies.remote(project_own.at[peer[1]], project_v.at[c], peer) for peer in ctx_peers
+    ]
+    project_copies.append(copies.local(project_own.at[c], project_v.at[c]))
+    for ring in rings[:2]:
+        ring.advance()
+    loads[4].wait()
+    in_cols = 4 * part_cols
+    residual = tokens_ref[...].astype(F32)
+    inverse = rms_scale(residual)
+    normed = residual * inverse
+    weights = packed_v[:, :, :, :in_cols].reshape(width, in_cols)
+    grad_attn_in = dot_right_t(project, weights)
+    attn_term = jnp.sum(grad_attn_in * normed, axis=0, keepdims=True)
+    back = norm_back(grad_attn_in * gains_ref[0:1, :], normed, inverse)
+    tokens_grad[...] = (hidden_ref[...] + back).astype(BF)
+    for ring in rings[:2]:
         ring.advance()
     for copy in project_copies:
         copies.arrive(copy)
     loads[2].wait()
-    project = project_v[...].reshape(-1, part_cols)
+    project_all = project_v[...].reshape(-1, part_cols)
     part_rows = own_rows + 16
-    n_all = project.shape[0]
-    width = rows_ref.shape[3]
+    n_all = project_all.shape[0]
     ahead = max(1, 256 // (4 * own_rows))
     chunk = ahead * 4 * own_rows
 
     @pl.loop(0, width // chunk)
     def _(t):
         cols = pl.ds(pl.multiple_of(t * chunk, chunk), chunk)
-        term = dot_left_t(rows_v[:, :, :, cols].reshape(n_all, chunk), project).astype(BF)
+        term = dot_left_t(rows_v[:, :, :, cols].reshape(n_all, chunk), project_all).astype(BF)
         term = term.reshape(ahead, 4, own_rows, part_cols)
         for part in range(4):
             in_v[pl.ds(t * ahead, ahead), pl.ds(part * part_rows, own_rows), :] = term[:, part]
 
-    for part in range(4):
-        in_v[:, part * part_rows + own_rows : (part + 1) * part_rows, :] = gain_ref[:, part]
+    none = jnp.zeros((16, part_cols), BF)
+    wide = jnp.concatenate([attn_term, mlp_term_ref[...], jnp.zeros((14, width), F32)], axis=0)
+    short = jnp.concatenate([jnp.zeros((2, latent), F32), query_term], axis=0)
+    short = jnp.concatenate([short, jnp.zeros((13, latent), F32)], axis=0)
+    for rank in range(n):
+        for part in range(4):
+            at = pl.ds(part * part_rows + own_rows, 16)
+            device = 4 * rank + part
+            in_v[rank, at, :] = none
+            in_v[rank, at, :own_rows] = wide[
+                :, device * own_rows : (device + 1) * own_rows
+            ].astype(BF)
+            more = short[:, device * gain_rows : (device + 1) * gain_rows].astype(BF)
+            kept = in_v[rank, at, :gain_rows]
+            in_v[rank, at, :gain_rows] = kept + more
     rings[2].advance()
-    for _ in range(place.h - 1):
+    if rings[0].step > 0:
+        for ring in rings[:2]:
+            ring.advance()
+    while rings[2].step > 0:
         for ring in rings:
-            ring.advance()
+            if ring.step > 0:
+                ring.advance()
 
     loads[3].wait()
     ff = gu_v.shape[3]
@@ -852,11 +888,12 @@
         ring.drain()
 
 
-def collect_weights(n_batch, gain_rows, out_terms, up_terms, project, attn_in_all, grad_gu, gain_terms):
+def collect_weights(n_batch, gain_rows, out_terms, up_terms, attn_in_all, grad_gu, packed, own):
     far = n_batch // 2
     out_rows, width = out_terms.shape[1:]
     up_rows, up_cols = up_terms.shape[1:]
-    in_cols = project.shape[2]
+    n_tok = own[2].shape[0]
+    in_cols = own[0].shape[1] // 4
     own_rows = width // (4 * n_batch)
     in_rows = 4 * (own_rows + 16)
     shapes = [out_terms.shape[1:], up_terms.shape[1:], (in_rows, in_cols)]
@@ -869,9 +906,10 @@
             jax.ShapeDtypeStruct((own_rows, 4 * in_cols), F32),
             jax.ShapeDtypeStruct((16, in_cols), F32),
             jax.ShapeDtypeStruct((own_rows, 2 * n_batch * grad_gu.shape[3]), F32),
+            jax.ShapeDtypeStruct((n_tok, width), BF),
         ),
-        in_specs=[pl.BlockSpec(memory_space=pl.ANY)] * 5 + [pl.BlockSpec(memory_space=pltpu.VMEM)],
-        out_specs=[pl.BlockSpec(memory_space=pltpu.VMEM)] * 5,
+        in_specs=[pl.BlockSpec(memory_space=pl.ANY)] * 5 + [pl.BlockSpec(memory_space=pltpu.VMEM)] * len(own),
+        out_specs=[pl.BlockSpec(memory_space=pltpu.VMEM)] * 6,
         scratch_shapes=[pltpu.VMEM((n_batch,) + shape, BF) for shape in shapes]
         + [pltpu.VMEM((far, 2, 2, rows // 2, cols), BF) for rows, cols in shapes]
         + [
@@ -883,16 +921,18 @@
             pltpu.SemaphoreType.DMA((3, far, 2, 2)),
             pltpu.SemaphoreType.DMA((sems,)),
             pltpu.SemaphoreType.DMA((sems,)),
-            pltpu.VMEM(project.shape, BF),
+            pltpu.VMEM(packed.shape, BF),
+            pltpu.VMEM((4, n_tok, in_cols), BF),
+            pltpu.VMEM((4, n_tok, in_cols), BF),
             pltpu.VMEM(attn_in_all.shape, BF),
             pltpu.VMEM(grad_gu.shape, BF),
-            pltpu.SemaphoreType.DMA((4,)),
+            pltpu.SemaphoreType.DMA((5,)),
         ],
         compiler_params=pltpu.CompilerParams(
-            collective_id=2, has_side_effects=True, vmem_limit_bytes=48 * 1024 * 1024
+            collective_id=2, has_side_effects=True, vmem_limit_bytes=56 * 1024 * 1024
         ),
         name="collect_weights",
-    )(out_terms, up_terms, project, attn_in_all, grad_gu, gain_terms)
+    )(out_terms, up_terms, attn_in_all, grad_gu, packed, *own)
 
 
 class CtxCollect:
@@ -1028,7 +1068,7 @@
     qkv_out,
     turned_out,
     mixed_out,
-    rows_all,
+    rows_out,
     cot_all,
     packed_v,
     flat_v,
@@ -1038,6 +1078,8 @@
     up_v,
     tokens_v,
     rows_v,
+    down_v,
+    cot_v,
     qkv_v,
     turned_v,
     mixed_v,
@@ -1070,8 +1112,8 @@
     own_out = copies.local(out_ref, half_v.at[b])
     own_tokens = copies.local(tokens_ref, tokens_v)
     own_flat = copies.local(gu_ref, flat_v)
-    own_down = copies.local(down_ref, down_all.at[c])
-    own_cot = copies.local(cot_ref, cot_all.at[b])
+    own_down = copies.local(down_ref, down_v)
+    own_cot = copies.local(cot_ref, cot_v)
 
     def up_cols(rank, local):
         start = pl.multiple_of(group.head(rank, local, heads) * HD, HD)
@@ -1102,25 +1144,19 @@
             packed_far.append(copies.remote(block, block, far_device))
 
     packed_step()
-    copies.arrive(own_out)
-    out_ring.advance()
-    for copy in own_up + up_copies:
-        copies.arrive(copy)
-    up_ring.advance()
-    packed_step()
+    copies.arrive(own_down)
+    copies.local(down_v, down_all.at[c])
+    down_far = copies.remote(down_v, down_all.at[c], far_device)
+    copies.remote(down_v, down_all.at[c], near_device)
     copies.arrive(own_flat)
     for slab_at in range(n):
         for kind in (0, 1):
             start = (kind * n + slab_at) * ff
             gu_v[slab_at, kind] = flat_v[:, start : start + ff]
     own_gu = copies.local(gu_v.at[b], gu_all.at[:, b, c])
-    up_ring.advance()
-    while packed_ring.step <= place.h:
-        packed_step()
-        up_ring.advance()
-        if out_ring.step < place.h - 1:
-            out_ring.advance()
     gu_copies = []
+    gu_far = []
+    waiting = []
 
     def send_gu(count):
         for _ in range(count):
@@ -1128,18 +1164,41 @@
             if k < n:
                 peer = peers[k - 1]
                 copy = copies.remote(gu_v.at[peer[0]], gu_all.at[:, b, c], peer)
-                gu_copies.append((lax.rem(b - k + n, n), copy))
-
+                gu_copies.append(copy)
+                waiting.append((lax.rem(b - k + n, n), copy))
+
+    def forward_gu(count):
+        for _ in range(min(count, len(waiting))):
+            rank, copy = waiting.pop(0)
+            copies.arrive(copy)
+            block = gu_all.at[:, rank, c]
+            gu_far.append(copies.remote(block, block, far_device))
+
+    for copy in own_up + up_copies:
+        copies.arrive(copy)
+    up_ring.advance()
+    packed_step()
     send_gu(n // 2)
+    up_ring.advance()
+    while packed_ring.step <= place.h:
+        packed_step()
+        up_ring.advance()
+    copies.arrive(own_out)
+    out_ring.advance()
     mine = packed_v.at[:, c]
     packed_near = [copies.remote(mine, mine, near_device)]
     while up_ring.step <= place.h:
         up_ring.advance()
+    copies.arrive(own_gu)
+    gu_far.append(copies.remote(gu_all.at[:, b, c], gu_all.at[:, b, c], far_device))
+    send_gu(n)
     out_ring.advance()
     for copy in packed_far:
         copies.arrive(copy)
     theirs = packed_v.at[:, place.far]
     packed_near.append(copies.remote(theirs, theirs, near_device))
+    copies.arrive(down_far)
+    copies.remote(down_all.at[place.far], down_all.at[place.far], near_device)
 
     copies.arrive(own_tokens)
     residual = tokens_v[...].astype(F32)
@@ -1175,37 +1234,11 @@
     qkv = CtxGather(place, copies, qkv_v)
     for item in range(micro):
         qkv.start(item)
-    while out_ring.step <= place.h:
-        out_ring.advance()
+    copies.local(rows_v, rows_out)
     for item in range(micro):
         qkv.cross(item)
-    out_swaps = [
-        copies.remote(half_v.at[group.blocks(member)], out_v.at[:, group.me], device)
-        for member, device in group.others
-    ]
-    out_swaps.append(copies.local(half_v.at[group.blocks(group.me)], out_v.at[:, group.me]))
-
-    send_gu(n)
-    copies.arrive(own_cot)
-    cot_ring.advance()
-    copies.arrive(own_gu)
-    gu_far = [copies.remote(gu_all.at[:, b, c], gu_all.at[:, b, c], far_device)]
-    copies.arrive(own_down)
-    down_far = copies.remote(down_ref, down_all.at[c], far_device)
-    copies.remote(down_ref, down_all.at[c], near_device)
-    copies.arrive(copies.local(rows_v, rows_all.at[c, 0]))
-    rows = CtxGather(place, copies, rows_all)
-    rows.start(0)
-    waiting = list(gu_copies)
-
-    def forward_gu(count):
-        for _ in range(min(count, len(waiting))):
-            rank, copy = waiting.pop(0)
-            copies.arrive(copy)
-            block = gu_all.at[:, rank, c]
-            gu_far.append(copies.remote(block, block, far_device))
-
-    attended_sum = CtxCollect(place, copies, part_v, near_got, far_got)
+    out_ring.advance()
+    forward_gu(n // 2)
     cosine, sine = cos_ref[...], sin_ref[...]
     for item in range(micro):
         qkv.finish(item)
@@ -1227,13 +1260,26 @@
             mixed = dot(weights.astype(BF), values).astype(BF)
             mixed_v[:, item, :, cols] = mixed.reshape(4, pos_dev, HD)
 
-        forward_gu(n // 4)
-        if cot_ring.step <= place.h:
-            cot_ring.advance()
+        if out_ring.step < place.h:
+            out_ring.advance()
+    while out_ring.step < place.h:
+        out_ring.advance()
+
+    copies.arrive(own_cot)
+    copies.arrive(copies.local(cot_v, cot_all.at[b]))
+    cot_ring.advance()
+    out_ring.advance()
+    out_swaps = [
+        copies.remote(half_v.at[group.blocks(member)], out_v.at[:, group.me], device)
+        for member, device in group.others
+    ]
+    out_swaps.append(copies.local(half_v.at[group.blocks(group.me)], out_v.at[:, group.me]))
+    forward_gu(n)
+    for copy in out_swaps:
+        copies.arrive(copy)
+    attended_sum = CtxCollect(place, copies, part_v, near_got, far_got)
+    for item in range(micro):
         mixed = mixed_v[:, item].reshape(length, heads * HD)
-        for copy in out_swaps:
-            copies.arrive(copy)
-        out_swaps = []
 
         @pl.loop(0, width // 512)
         def _(t):
@@ -1245,31 +1291,23 @@
         attended_sum.start(item)
         if item > 0:
             attended_sum.cross(item - 1)
+    cot_ring.advance()
+    attended_sum.cross(micro - 1)
     copies.local(packed_v, packed_out)
     copies.local(up_v, up_out)
     copies.local(out_v, out_out)
     copies.local(qkv_v, qkv_out)
     copies.local(turned_v, turned_out)
     copies.local(mixed_v, mixed_out)
-    attended_sum.cross(micro - 1)
-    rows.cross(0)
-    if cot_ring.step <= place.h:
-        cot_ring.advance()
     for item in range(micro):
         at = slice(item * pos_dev, (item + 1) * pos_dev)
         total = tokens_v[at, :].astype(F32) + attended_sum.finish(item)
         hidden[at, :] = total
         mlp_in[at, :] = (total * rms_scale(total) * gains[1:2, :]).astype(BF)
-    forward_gu(n // 4)
+    mine = gu_all.at[:, :, c]
+    copies.remote(mine, mine, near_device)
     while cot_ring.step <= place.h:
         cot_ring.advance()
-        forward_gu(n // 4)
-    forward_gu(n)
-    cot_ring.advance()
-    mine = gu_all.at[:, :, c]
-    copies.remote(mine, mine, near_device)
-    copies.arrive(down_far)
-    copies.remote(down_all.at[place.far], down_all.at[place.far], near_device)
     for copy in gu_far:
         copies.arrive(copy)
     theirs = gu_all.at[:, :, place.far]
@@ -1298,7 +1336,7 @@
         "qkv": (4, micro, pos_dev, in_cols),
         "turned": (micro, 4 * pos_dev, head_cols),
         "mixed": (4, micro, pos_dev, head_cols),
-        "rows": (4, 1, n_tok, width),
+        "rows": (n_tok, width),
         "cot": (n_batch, n_tok, width),
     }
     anywhere = pl.BlockSpec(memory_space=pl.ANY)
@@ -1323,6 +1361,8 @@
             pltpu.VMEM(shapes["out"], BF),
             pltpu.VMEM(shapes["up"], BF),
             pltpu.VMEM((n_tok, width), BF),
+            pltpu.VMEM((n_tok, width), BF),
+            pltpu.VMEM(down.shape, BF),
             pltpu.VMEM((n_tok, width), BF),
             pltpu.VMEM(shapes["qkv"], BF),
             pltpu.VMEM(shapes["turned"], BF),
@@ -1352,9 +1392,10 @@
     out_ref,
     gu_ref,
     down_ref,
+    rows_ref,
     *refs,
 ):
-    terms_ref, refs = (refs[0], refs[1:]) if has_terms else (None, refs)
+    terms_ref, cot_ref, refs = (refs[0], refs[1], refs[2:]) if has_terms else (None, None, refs)
     (
         cos_ref,
         sin_ref,
@@ -1364,8 +1405,9 @@
         up_terms,
         gu_grad,
         down_grad,
-    ) = refs[:8]
-    terms_sum, refs = (refs[8], refs[9:]) if has_terms else (None, refs[8:])
+        rows_all,
+    ) = refs[:9]
+    terms_sum, refs = (refs[9], refs[10:]) if has_terms else (None, refs[9:])
     (
         grad_v,
         qkv_v,
@@ -1382,10 +1424,12 @@
         outgrad_v,
         upgrad_v,
         down_v,
+        gu_v,
+        rows_v,
         send_sems,
         recv_sems,
         load_sems,
-    ) = refs[:18]
+    ) = refs[:20]
     place = Place(n_batch)
     copies = Copies(send_sems, recv_sems)
     b, c, n = place.b, place.c, n_batch
@@ -1403,8 +1447,26 @@
         (mixed_ref, mixed_v),
     ]
     if has_terms:
-        terms_v, terms_got, ring_send, ring_recv = refs[18:]
-        pairs.append((terms_ref, terms_v))
+        (
+            terms_v,
+            terms_got,
+            ring_send,
+            ring_recv,
+            act_v,
+            cot_v,
+            down_all,
+            down_got,
+        ) = refs[20:]
+        pairs += [(terms_ref, terms_v), (down_ref, act_v)]
+        n_tok = terms_v.shape[1]
+        spots = [(0, 0, 0), (place.h, 0, 1)]
+        spots += [
+            (side * step, step, (side + 1) // 2) for step in range(1, place.h) for side in (-1, 1)
+        ]
+        pairs += [
+            (cot_ref.at[place.rank_of(step)], cot_v.at[pair, pl.ds(side * n_tok, n_tok)])
+            for step, pair, side in spots
+        ]
     loads = [
         pltpu.make_async_copy(source, target, load_sems.at[i])
         for i, (source, target) in enumerate(pairs)
@@ -1437,15 +1499,45 @@
             steps.pop()()
 
     ring_step()
-    copies.local(gu_ref.at[b], gu_grad.at[b])
+    own_gu = copies.local(gu_ref.at[b], gu_v)
+    own_rows = copies.local(rows_ref, rows_v.at[c, 0])
     for peer in peers:
         copies.remote(gu_ref.at[peer[0]], gu_grad.at[b], peer)
     for item in range(micro):
         grads.cross(item)
-    down_own = copies.local(down_ref.at[place.outer], down_v.at[0])
-    down_far = copies.remote(down_ref.at[1 - place.outer], down_v.at[1], (b, place.far))
+    outer, inner = place.outer, place.inner
+    if has_terms:
+        for copy in loads[7:]:
+            copy.wait()
+        n_rows = cot_v.shape[0] * cot_v.shape[1]
+        ff = act_v.shape[2]
+
+        @pl.loop(0, width // 512)
+        def _(t):
+            cols = pl.ds(pl.multiple_of(t * 512, 512), 512)
+            term = dot_left_t(
+                act_v[...].reshape(n_rows, ff), cot_v[:, :, cols].reshape(n_rows, 512)
+            )
+            down_all[:, :, cols] = term.astype(BF).reshape(4, ff // 4, 512)
+
+        down_near = [
+            copies.remote(down_all.at[2 * side + 1 - inner], down_got.at[side], (b, place.near))
+            for side in (0, 1)
+        ]
+    else:
+        down_own = copies.local(down_ref.at[outer], down_v.at[0])
+        down_far = copies.remote(down_ref.at[1 - outer], down_v.at[1], (b, place.far))
     for copy in loads[1:6]:
         copy.wait()
+    if has_terms:
+        for copy in down_near:
+            copies.arrive(copy)
+        other = down_all.at[2 * (1 - outer) + inner]
+        other[...] = (other[...].astype(F32) + down_got[1 - outer].astype(F32)).astype(BF)
+        down_far = copies.remote(other, down_v.at[1], (b, place.far))
+    copies.arrive(own_rows)
+    rows = CtxGather(place, copies, rows_v)
+    rows.start(0)
     back_sum = CtxCollect(place, copies, part_v, near_got, far_got)
     cosine, sine = cos_ref[...], sin_ref[...]
     for item in range(micro):
@@ -1517,9 +1609,21 @@
         upgrad_v[:, :, cols] = term.astype(BF).reshape(n, latent // n, HD)
 
     copies.local(upgrad_v, up_terms)
-    copies.arrive(down_own)
+    rows.cross(0)
+    rows.finish(0)
+    copies.local(rows_v, rows_all)
+    copies.arrive(own_gu)
+    copies.local(gu_v, gu_grad.at[b])
     copies.arrive(down_far)
-    down_grad[...] = down_v[0].astype(F32) + down_v[1].astype(F32)
+    if has_terms:
+        down_grad[...] = (
+            down_all[2 * outer + inner].astype(F32)
+            + down_got[outer].astype(F32)
+            + down_v[1].astype(F32)
+        )
+    else:
+        copies.arrive(down_own)
+        down_grad[...] = down_v[0].astype(F32) + down_v[1].astype(F32)
     if has_terms:
         while steps:
             ring_step()
@@ -1531,7 +1635,7 @@
 
 
 def attention_back(
-    n_batch, grad_att, qkv_all, turned, mixed, own_qup, own_out, grad_gu, down_part, terms, tables
+    n_batch, grad_att, qkv_all, turned, mixed, own_qup, own_out, grad_gu, down_part, attn_in, terms, cots, tables
 ):
     micro, pos_dev, width = grad_att.shape
     n_tok = micro * pos_dev
@@ -1541,6 +1645,7 @@
     length = 4 * pos_dev
     far = n_batch // 2
     has_terms = terms is not None
+    down_rows = down_part.shape[2] // 4 if has_terms else down_part.shape[1]
     size = head_group(n_batch, head_cols // n_batch)
     sems = 2 * n_batch + 48
     anywhere = pl.BlockSpec(memory_space=pl.ANY)
@@ -1550,9 +1655,10 @@
         jax.ShapeDtypeStruct((n_batch, head_cols // n_batch, width), BF),
         jax.ShapeDtypeStruct((n_batch, latent // n_batch, head_cols), BF),
         jax.ShapeDtypeStruct(grad_gu.shape, BF),
-        jax.ShapeDtypeStruct(down_part.shape[1:], F32),
+        jax.ShapeDtypeStruct((down_rows, width), F32),
+        jax.ShapeDtypeStruct((4, 1) + attn_in.shape, BF),
     ]
-    out_specs = [near] + [anywhere] * 3 + [near]
+    out_specs = [near] + [anywhere] * 3 + [near, anywhere]
     scratch = [
         pltpu.VMEM((4, micro, pos_dev, width), BF),
         pltpu.VMEM((4, micro, pos_dev, qkv_cols), BF),
@@ -1568,14 +1674,16 @@
         pltpu.VMEM((micro, pos_dev, qkv_cols), BF),
         pltpu.VMEM((n_batch // size, size, head_cols // n_batch, width), BF),
         pltpu.VMEM((n_batch, latent // n_batch, head_cols), BF),
-        pltpu.VMEM(down_part.shape, BF),
+        pltpu.VMEM((2, down_rows, width), BF),
+        pltpu.VMEM(grad_gu.shape[1:], BF),
+        pltpu.VMEM((4, 1) + attn_in.shape, BF),
         pltpu.SemaphoreType.DMA((sems,)),
         pltpu.SemaphoreType.DMA((sems,)),
-        pltpu.SemaphoreType.DMA((7,)),
+        pltpu.SemaphoreType.DMA((8 + n_batch,)),
     ]
-    args = [grad_att, qkv_all, turned, mixed, own_qup, own_out, grad_gu, down_part]
+    args = [grad_att, qkv_all, turned, mixed, own_qup, own_out, grad_gu, down_part, attn_in]
     if has_terms:
-        args.append(terms)
+        args += [terms, cots]
         out_shape.append(jax.ShapeDtypeStruct((n_tok, width), F32))
         out_specs.append(near)
         scratch += [
@@ -1583,6 +1691,10 @@
             pltpu.VMEM((far, 2, 2, n_tok // 2, width), BF),
             pltpu.SemaphoreType.DMA((far, 2, 2)),
             pltpu.SemaphoreType.DMA((far, 2, 2)),
+            pltpu.VMEM(down_part.shape, BF),
+            pltpu.VMEM((far, 2 * n_tok, width), BF),
+            pltpu.VMEM((4, down_rows, width), BF),
+            pltpu.VMEM((2, down_rows, width), BF),
         ]
     return pl.pallas_call(
         functools.partial(attention_back_kernel, n_batch, head_cols // HD, has_terms),
@@ -1685,7 +1797,6 @@
         [attn_gain, mlp_gain, jnp.pad(query_gain, (0, own_rows - gain_rows))], axis=1
     )
     packed = jnp.concatenate([proj_in, jnp.pad(gains, ((0, 0), (0, 125)))], axis=1)
-    residual = tokens.reshape(n_tok, width).astype(F32)
     valid_rows = (query_pos[None, :] < own_lengths[:, None]).astype(F32).reshape(n_tok, 1)
     grad_out = cotangent.reshape(n_tok, width).astype(F32) * valid_rows
     keep = (key_pos[None, None, :] < own_lengths[:, None, None]).astype(F32)
@@ -1703,7 +1814,7 @@
         qkv_all,
         turned,
         mixed,
-        attn_in_all,
+        attn_in,
         cots,
     ) = front(
         n_batch,
@@ -1717,13 +1828,8 @@
         grad_out.astype(BF),
         tables,
     )
-    full_in = packed.reshape(width, in_cols + 128)[:, :in_cols]
     own_qup = own_qup.reshape(QR, heads * HD)
-    gain_norm, gain_mlp, gain_query = gains[0], gains[1], gains[2, :QR]
-    scale_one = rms_scale(residual)
-    normed_one = residual * scale_one
-    scale_query = rms_scale(q_latent)
-    normed_query = q_latent * scale_query
+    gain_mlp = gains[1]
 
     scale_two = rms_scale(hidden_res)
     normed_two = hidden_res * scale_two
@@ -1740,7 +1846,7 @@
         )
     gain_mlp_term = jnp.sum(grad_mlp_in * normed_two, axis=0)
     grad_hidden = grad_out + norm_back(grad_mlp_in * gain_mlp, normed_two, scale_two)
-    back_own, out_grads, up_grads, grad_gu_own, grad_down, *sums = attention_back(
+    back_own, out_grads, up_grads, grad_gu_own, grad_down, attn_in_all, *sums = attention_back(
         n_batch,
         grad_hidden.astype(BF).reshape(micro, pos_dev, width),
         qkv_all,
@@ -1750,54 +1856,45 @@
         own_out,
         grad_gu_own,
         down_part,
+        attn_in,
         terms,
+        cots,
         (cos_all, sin_all, keep),
     )
     out_sum = sums[0] if resident else ring.collect(lambda step: out_terms[step])
     layer_out = hidden_res + out_sum
     back_own = back_own.reshape(n_tok, in_cols)
-    grad_qn = back_own[:, :QR]
-    gain_query_term = jnp.sum(grad_qn * normed_query, axis=0)
-    grad_latent = norm_back(grad_qn * gain_query, normed_query, scale_query)
-    grad_key_raw = rotate_back(
-        back_own[:, QR : QR + HD].reshape(micro, pos_dev, HD), cos_own, sin_own
-    ).reshape(n_tok, HD)
-    grad_project = jnp.concatenate(
-        [grad_latent, grad_key_raw, back_own[:, QR + HD :]], axis=1
-    ).astype(BF)
-    grad_attn_in = dot_right_t(grad_project, full_in)
-    gain_norm_term = jnp.sum(grad_attn_in * normed_one, axis=0)
-    grad_tokens = grad_hidden + norm_back(grad_attn_in * gain_norm, normed_one, scale_one)
-
-    part_cols = in_cols // n_ctx
-    project_parts = grad_project.reshape(n_tok, n_ctx, part_cols).swapaxes(0, 1)
-    gain_terms = jnp.stack(
-        [
-            gain_norm_term.reshape(n_batch, n_ctx, own_rows),
-            gain_mlp_term.reshape(n_batch, n_ctx, own_rows),
-            jnp.pad(
-                gain_query_term.reshape(n_batch, n_ctx, gain_rows),
-                ((0, 0), (0, 0), (0, own_rows - gain_rows)),
-            ),
-        ],
-        axis=2,
-    )
-    gain_terms = jnp.pad(gain_terms, ((0, 0), (0, 0), (0, 13), (0, part_cols - own_rows)))
-    grad_proj_out, grad_query_up, grad_proj_in, gain_sums, grad_gate_up = collect_weights(
+    (
+        grad_proj_out,
+        grad_query_up,
+        grad_proj_in,
+        gain_sums,
+        grad_gate_up,
+        grad_tokens,
+    ) = collect_weights(
         n_batch,
         gain_rows,
         out_grads,
         up_grads,
-        project_parts,
         attn_in_all,
         grad_gu_own,
-        gain_terms.astype(BF),
+        packed,
+        (
+            back_own,
+            q_latent,
+            tokens.reshape(n_tok, width),
+            grad_hidden,
+            gains,
+            gain_mlp_term[None, :],
+            tables[2],
+            tables[3],
+        ),
     )
     gain_sums = gain_sums[:, :own_rows]
 
     return (
         layer_out.reshape(tokens.shape).astype(BF),
-        grad_tokens.reshape(tokens.shape).astype(BF),
+        grad_tokens.reshape(tokens.shape),
         grad_proj_in,
         grad_query_up,
         grad_proj_out,

time: 512 us -> 483 us (0.943)
  Pallas kernels: 470 us -> 455 us
  matrix products: 5.91 us -> 0 us
    pallas_call x1, Pallas kernels: 117 us -> 106 us  [fused_mlp(): pl.pallas_call(functools.partial(mlp_kernel, n_batch), out_shape=(jax.Sha...]
    pallas_call x1, Pallas kernels: 182 us -> 175 us  [front(): pl.pallas_call(functools.partial(front_kernel, n_batch, heads), out_shape...]
    dot_general x1 -> x0, matrix products: 5.91 us -> none  [dot_right_t(): lax.dot_general(left_side, right_side, (((1,), (1,)), ((), ())), preferre...]
where the time goes in v7:
time: 483 us; the launch traced here: 480 us
  Pallas kernels  455 us (94%)
  local copies, waits for them, and re-layouts  12.5 us (3%)
  other arithmetic  12.1 us (3%)
    pallas_call x1, Pallas kernels, front(): pl.pallas_call(functools.partial(front_kernel, n_batch, heads), out_shape...  175 us
    pallas_call x1, Pallas kernels, fused_mlp(): pl.pallas_call(functools.partial(mlp_kernel, n_batch), out_shape=(jax.Sha...  106 us
    pallas_call x1, Pallas kernels, collect_weights(): pl.pallas_call(functools.partial(tail_kernel, n_batch, gain_rows), out_sh...  93.8 us
    pallas_call x1, Pallas kernels, attention_back(): pl.pallas_call(functools.partial(attention_back_kernel, n_batch, head_col...  79.7 us

profile of v7, /device:TPU:4, one launch (start us, length us, event | category | flops | bytes accessed | tf_op | source)
XLA Modules:
  0.0 480.1 jit_solution(1482569698037033515)
XLA Ops:
  0.7 0.9 select_reduce_fusion
  1.6 0.7 pad_bitcast_fusion
  2.3 0.7 pad_maximum_fusion
  3.1 0.6 compare_convert_fusion.keep_ref.refs_4_
  5.3 1.6 fusion.3.packed_ref
  7.0 1.2 multiply_sine_fusion
  8.2 2.0 fusion.1.cot_ref
  10.2 174.8 %front.1 = (f32[128,2048]{1,0:T(8,128)}, bf16[128,2048]{1,0:T(8,128)(2,1)}, f32[8,2048]{1,0:T(8,128)}, f32[128,1024]{1,0:T(8,128)}, bf16[8,4,64,1664]{3,2,1,0:T(...) custom-call(bf16[64,1664]{1,0:T(8,128)(2,1)} %fusion.3.packed_ref, ...), custom_call_target="tpu_custom_call" | custom-call | tf_op jit(solution)/shard_map/front/pallas_call | solution.py:1345
  185.0 106.5 %fused_mlp.1 = (f32[128,2048]{1,0:T(8,128)}, bf16[4,256,704]{2,1,0:T(8,128)(2,1)}, bf16[4,256,2048]{2,1,0:T(8,128)(2,1)}, bf16[8,2,64,704]{3,2,1,0:T(8,128)(2,1)}) custom-call(bf16[128,2048]{1,0:T(8,128)(2,1)} %get-tuple-element.42.rows_ref, bf16[2,8,4,64,704]{4,3,2,1,0:T(8,128)(2,1)} %get-tuple-element.43.gu_ref, ...), custom_call_target="tpu_custom_call" | custom-call | flops 26575110144 | bytes 25165824 | tf_op jit(solution)/shard_map/fused_mlp/pallas_call | solution.py:585
  291.7 1.0 slice.16
  292.6 2.2 multiply_reduce_fusion
  294.8 1.5 fusion.5
  296.3 79.7 %attention_back.1 = (f32[2,64,1536]{2,1,0:T(8,128)}, bf16[8,128,2048]{2,1,0:T(8,128)(2,1)}, bf16[8,128,1024]{2,1,0:T(8,128)(2,1)}, bf16[8,2,64,704]{3,2,1,0:T(8,...) custom-call(bf16[2,64,2048]{2,1,0:T(8,128)(2,1)} %bitcast.30, ...), custom_call_target="tpu_custom_call" | custom-call | tf_op jit(solution)/shard_map/attention_back/pallas_call | solution.py:1699
  376.0 93.8 %collect_weights.1 = (f32[128,2048]{1,0:T(8,128)}, f32[32,4096]{1,0:T(8,128)}, f32[64,1536]{1,0:T(8,128)}, f32[16,384]{1,0:T(8,128)}, f32[64,11264]{1,0:T(8,128)}, /*index=5*/bf16[128,2048]{1,0:T(8,128)(2,1)}) custom-call(bf16[8,128,2048]{2,1,0:T(8,128)(2,1)} %get-tuple-element.58.out_ref, bf16[8,128,1024]{2,1,0:T(8,128)(2,1)} %get-tuple-element.59.up_ref, ...), custom_call_target="tpu_custom_call" | custom-call | tf_op jit(solution)/shard_map/collect_weights/pallas_call | solution.py:901
  469.8 0.9 add_convert_fusion
  470.7 1.3 slice_bitcast_fusion.1
  472.0 1.3 slice_bitcast_fusion
  473.3 0.8 copy.33
  474.1 0.7 copy.34
  474.8 0.8 copy.35
  475.6 1.0 copy.36
  476.6 1.6 copy.37
  478.2 0.8 copy-done.4
  479.0 1.1 copy.38
  (32 shorter events, 2.0 us)
Async XLA Ops:
  185.0 106.5 %copy-start = (f32[128,2048]{1,0:T(8,128)S(1)}, f32[128,2048]{1,0:T(8,128)}, u32[]{:S(2)}) copy-start(f32[128,2048]{1,0:T(8,128)} %get-tuple-element.41) | copy-start | bytes 3145732
  291.5 3.3 copy-start.1
  291.5 3.3 copy-start.3
  376.0 93.8 %copy-start.5 = (f32[128,2048]{1,0:T(8,128)S(1)}, f32[128,2048]{1,0:T(8,128)}, u32[]{:S(2)}) copy-start(f32[128,2048]{1,0:T(8,128)} %get-tuple-element.57) | copy-start | bytes 3145732
  469.8 3.5 copy-start.8
  469.8 4.3 copy-start.9
  469.8 5.0 %copy-start.7 = (f32[32,4096]{1,0:T(8,128)S(1)}, f32[32,4096]{1,0:T(8,128)}, u32[]{:S(2)}) copy-start(f32[32,4096]{1,0:T(8,128)} %get-tuple-element.97) | copy-start | bytes 1572868
  470.7 4.9 %copy-start.6 = (f32[128,2048]{1,0:T(8,128)S(1)}, f32[128,2048]{1,0:T(8,128)}, u32[]{:S(2)}) copy-start(f32[128,2048]{1,0:T(8,128)} %get-tuple-element.98) | copy-start | bytes 3145732
  474.1 2.5 copy-start.2
  476.6 2.4 copy-start.4

commit v8 on v7

--- a/solution.py
+++ b/solution.py
@@ -3,6 +3,7 @@
 
 import jax
 import jax.numpy as jnp
+import numpy as np
 from jax import lax
 from jax.experimental import pallas as pl
 from jax.experimental.pallas import tpu as pltpu
@@ -20,11 +21,12 @@
     return lax.rsqrt(jnp.mean(values * values, axis=-1, keepdims=True) + EPSILON)
 
 
-def rope_tables(positions):
+def rope_tables(length):
     half_size = HD // 2
-    frequency = 10000.0 ** (-(jnp.arange(half_size, dtype=F32) * 2.0 / HD))
-    angles = positions.astype(F32)[:, None] * frequency[None, :]
-    return (jnp.cos(angles), jnp.sin(angles))
+    frequency = np.float32(10000.0) ** (-(np.arange(half_size, dtype=np.float32) * 2.0 / HD))
+    angles = np.arange(length, dtype=np.float32)[:, None] * frequency.astype(np.float32)[None, :]
+    cosine, sine = np.cos(angles), np.sin(angles)
+    return jnp.asarray(cosine, F32), jnp.asarray(sine, F32)
 
 
 def rotate(values, cosine_table, sine_table):
@@ -444,15 +446,15 @@
         for side, half in both:
             hop(step, side, half).wait_recv()
 
-        @pl.when(step < far - 1)
-        def _():
-            for side, half in both:
+            @pl.when(step < far - 1)
+            def _():
                 hop(step + 1, side, half).start()
 
-        @pl.when(step == far - 1)
-        def _():
-            for side, half in ends:
-                hop(far, side, half).start()
+            if (side, half) in ends:
+
+                @pl.when(step == far - 1)
+                def _():
+                    hop(far, side, half).start()
 
         compute(step)
 
@@ -762,6 +764,10 @@
         ring.advance()
     part_cols = project_v.shape[2]
     n_tok, width = tokens_ref.shape
+    pos_dev = cos_ref.shape[0] // 4
+    own_at = pl.ds(pl.multiple_of(c * pos_dev, pos_dev), pos_dev)
+    cos_own = jnp.concatenate([cos_ref[own_at, :]] * (n_tok // pos_dev), axis=0)
+    sin_own = jnp.concatenate([sin_ref[own_at, :]] * (n_tok // pos_dev), axis=0)
     latent = latent_ref.shape[1]
 
     q_latent = latent_ref[...]
@@ -770,7 +776,7 @@
     grad_qn = back_ref[:, :latent]
     query_term = jnp.sum(grad_qn * normed_query, axis=0, keepdims=True)
     grad_latent = norm_back(grad_qn * gains_ref[2:3, :latent], normed_query, inverse)
-    front, back = turn(back_ref[:, latent : latent + HD], cos_ref[...], -sin_ref[...])
+    front, back = turn(back_ref[:, latent : latent + HD], cos_own, -sin_own)
     project = jnp.concatenate(
         [grad_latent, front, back, back_ref[:, latent + HD :]], axis=1
     ).astype(BF)
@@ -1044,7 +1050,8 @@
 def front_kernel(
     n_batch,
     heads,
-    packed_ref,
+    proj_ref,
+    gain_ref,
     up_ref,
     out_ref,
     gu_ref,
@@ -1053,9 +1060,8 @@
     cot_ref,
     cos_ref,
     sin_ref,
-    cos_own_ref,
-    sin_own_ref,
     keep_ref,
+    valid_ref,
     hidden,
     mlp_in,
     gains,
@@ -1092,7 +1098,7 @@
     place = Place(n_batch)
     copies = Copies(send_sems, recv_sems)
     b, c, n = place.b, place.c, n_batch
-    own_rows = packed_ref.shape[0]
+    own_rows = proj_ref.shape[0]
     gain_rows = up_ref.shape[0]
     out_rows = out_ref.shape[0]
     n_tok, width = tokens_ref.shape
@@ -1108,7 +1114,10 @@
     far_device, near_device = ctx_peers[0], ctx_peers[1]
 
     barrier = greet(place, peers + ctx_peers)
-    own_packed = copies.local(packed_ref, packed_v.at[b, c])
+    own_packed = [
+        copies.local(proj_ref, packed_v.at[b, c, :, pl.ds(0, in_cols)]),
+        copies.local(gain_ref, packed_v.at[b, c, :, pl.ds(in_cols, 128)]),
+    ]
     own_out = copies.local(out_ref, half_v.at[b])
     own_tokens = copies.local(tokens_ref, tokens_v)
     own_flat = copies.local(gu_ref, flat_v)
@@ -1129,7 +1138,8 @@
         for peer in ctx_peers
         for local in range(heads)
     ]
-    copies.arrive(own_packed)
+    for copy in own_packed:
+        copies.arrive(copy)
     packed_ring = RingGather(place, copies, own_rows, lambda rank, rows: packed_v.at[rank, c, rows])
     up_ring = RingGather(place, copies, gain_rows, lambda rank, rows: up_v.at[rank, :, rows])
     out_ring = RingGather(place, copies, out_rows, lambda rank, rows: half_v.at[rank, rows])
@@ -1179,12 +1189,12 @@
     up_ring.advance()
     packed_step()
     send_gu(n // 2)
+    copies.arrive(own_out)
+    out_ring.advance()
     up_ring.advance()
     while packed_ring.step <= place.h:
         packed_step()
         up_ring.advance()
-    copies.arrive(own_out)
-    out_ring.advance()
     mine = packed_v.at[:, c]
     packed_near = [copies.remote(mine, mine, near_device)]
     while up_ring.step <= place.h:
@@ -1193,14 +1203,16 @@
     gu_far.append(copies.remote(gu_all.at[:, b, c], gu_all.at[:, b, c], far_device))
     send_gu(n)
     out_ring.advance()
+    forward_gu(2)
     for copy in packed_far:
         copies.arrive(copy)
     theirs = packed_v.at[:, place.far]
     packed_near.append(copies.remote(theirs, theirs, near_device))
-    copies.arrive(down_far)
-    copies.remote(down_all.at[place.far], down_all.at[place.far], near_device)
 
     copies.arrive(own_tokens)
+    own_at = pl.ds(pl.multiple_of(c * pos_dev, pos_dev), pos_dev)
+    cos_own = jnp.concatenate([cos_ref[own_at, :]] * micro, axis=0)
+    sin_own = jnp.concatenate([sin_ref[own_at, :]] * micro, axis=0)
     residual = tokens_v[...].astype(F32)
     normed = residual * rms_scale(residual)
     for copy in packed_near:
@@ -1219,7 +1231,7 @@
         if start + tile <= latent:
             latents[:, start : start + tile] = part
         else:
-            front, back = turn(part[:, :HD], cos_own_ref[...], sin_own_ref[...])
+            front, back = turn(part[:, :HD], cos_own, sin_own)
             half = HD // 2
             qkv_v[c, :, :, latent : latent + half] = (
                 front.astype(BF).reshape(micro, pos_dev, half)
@@ -1235,9 +1247,14 @@
     for item in range(micro):
         qkv.start(item)
     copies.local(rows_v, rows_out)
+    copies.arrive(own_cot)
+    cot_v[...] = (cot_v[...].astype(F32) * valid_ref[...]).astype(BF)
+    copies.arrive(copies.local(cot_v, cot_all.at[b]))
+    cot_ring.advance()
     for item in range(micro):
         qkv.cross(item)
-    out_ring.advance()
+    if out_ring.step < place.h:
+        out_ring.advance()
     forward_gu(n // 2)
     cosine, sine = cos_ref[...], sin_ref[...]
     for item in range(micro):
@@ -1265,10 +1282,9 @@
     while out_ring.step < place.h:
         out_ring.advance()
 
-    copies.arrive(own_cot)
-    copies.arrive(copies.local(cot_v, cot_all.at[b]))
     cot_ring.advance()
-    out_ring.advance()
+    while out_ring.step <= place.h:
+        out_ring.advance()
     out_swaps = [
         copies.remote(half_v.at[group.blocks(member)], out_v.at[:, group.me], device)
         for member, device in group.others
@@ -1277,6 +1293,8 @@
     forward_gu(n)
     for copy in out_swaps:
         copies.arrive(copy)
+    copies.arrive(down_far)
+    copies.remote(down_all.at[place.far], down_all.at[place.far], near_device)
     attended_sum = CtxCollect(place, copies, part_v, near_got, far_got)
     for item in range(micro):
         mixed = mixed_v[:, item].reshape(length, heads * HD)
@@ -1315,9 +1333,9 @@
     copies.drain()
 
 
-def front(n_batch, heads, packed, query_up, proj_out, gate_up, down, tokens, cots, tables):
-    own_rows, packed_cols = packed.shape
-    in_cols = packed_cols - 128
+def front(n_batch, heads, proj_in, gain_cols, query_up, proj_out, gate_up, down, tokens, cots, tables):
+    own_rows, in_cols = proj_in.shape
+    packed_cols = in_cols + 128
     latent = in_cols - 2 * HD
     gain_rows = query_up.shape[0]
     out_rows, width = proj_out.shape
@@ -1351,7 +1369,7 @@
             jax.ShapeDtypeStruct((n_tok, latent), F32),
         )
         + tuple(jax.ShapeDtypeStruct(shape, BF) for shape in shapes.values()),
-        in_specs=[anywhere] * 7 + [near] * 5,
+        in_specs=[anywhere] * 8 + [near] * 4,
         out_specs=[near] * 4 + [anywhere] * len(shapes),
         scratch_shapes=[
             pltpu.VMEM(shapes["packed"], BF),
@@ -1377,7 +1395,7 @@
             collective_id=0, has_side_effects=True, vmem_limit_bytes=56 * 1024 * 1024
         ),
         name="front",
-    )(packed, query_up, proj_out, gate_up, down, tokens, cots, *tables)
+    )(proj_in, gain_cols, query_up, proj_out, gate_up, down, tokens, cots, *tables)
 
 
 def attention_back_kernel(
@@ -1788,19 +1806,17 @@
     own_lengths = lax.dynamic_slice_in_dim(seq_lengths, batch_rank * micro, micro)
     query_pos = ctx_rank * pos_dev + jnp.arange(pos_dev, dtype=jnp.int32)
     key_pos = jnp.arange(full_length, dtype=jnp.int32)
-    cos_all, sin_all = rope_tables(key_pos)
-    cos_own, sin_own = rope_tables(query_pos)
+    cos_all, sin_all = rope_tables(full_length)
 
     own_rows = proj_in.shape[0]
     gain_rows = query_gain.shape[0]
     gains = jnp.stack(
         [attn_gain, mlp_gain, jnp.pad(query_gain, (0, own_rows - gain_rows))], axis=1
     )
-    packed = jnp.concatenate([proj_in, jnp.pad(gains, ((0, 0), (0, 125)))], axis=1)
+    gain_cols = jnp.pad(gains, ((0, 0), (0, 125)))
     valid_rows = (query_pos[None, :] < own_lengths[:, None]).astype(F32).reshape(n_tok, 1)
     grad_out = cotangent.reshape(n_tok, width).astype(F32) * valid_rows
     keep = (key_pos[None, None, :] < own_lengths[:, None, None]).astype(F32)
-    tables = (cos_all, sin_all, jnp.tile(cos_own, (micro, 1)), jnp.tile(sin_own, (micro, 1)), keep)
     (
         hidden_res,
         mlp_in,
@@ -1819,14 +1835,15 @@
     ) = front(
         n_batch,
         heads,
-        packed,
+        proj_in,
+        gain_cols,
         query_up,
         proj_out,
         gate_up,
         down_proj,
         tokens.reshape(n_tok, width),
-        grad_out.astype(BF),
-        tables,
+        cotangent.reshape(n_tok, width),
+        (cos_all, sin_all, keep, valid_rows),
     )
     own_qup = own_qup.reshape(QR, heads * HD)
     gain_mlp = gains[1]
@@ -1886,8 +1903,8 @@
             grad_hidden,
             gains,
             gain_mlp_term[None, :],
-            tables[2],
-            tables[3],
+            cos_all,
+            sin_all,
         ),
     )
     gain_sums = gain_sums[:, :own_rows]

time: 483 us -> 470 us (0.973)
  Pallas kernels: 455 us -> 448 us
  other arithmetic: 12.1 us -> 7.05 us
    pallas_call x1, Pallas kernels: 175 us -> 170 us  [front(): pl.pallas_call(functools.partial(front_kernel, n_batch, heads), out_shape...]
where the time goes in v8:
time: 470 us; the launch traced here: 469 us
  Pallas kernels  448 us (95%)
  local copies, waits for them, and re-layouts  12.7 us (3%)
  other arithmetic  7.05 us (2%)
    pallas_call x1, Pallas kernels, front(): pl.pallas_call(functools.partial(front_kernel, n_batch, heads), out_shape...  170 us
    pallas_call x1, Pallas kernels, fused_mlp(): pl.pallas_call(functools.partial(mlp_kernel, n_batch), out_shape=(jax.Sha...  103 us
    pallas_call x1, Pallas kernels, collect_weights(): pl.pallas_call(functools.partial(tail_kernel, n_batch, gain_rows), out_sh...  95.2 us
    pallas_call x1, Pallas kernels, attention_back(): pl.pallas_call(functools.partial(attention_back_kernel, n_batch, head_col...  79.6 us

profile of v8, /device:TPU:4, one launch (start us, length us, event | category | flops | bytes accessed | tf_op | source)
XLA Modules:
  0.0 468.5 jit_solution(14725978834380452746)
XLA Ops:
  0.7 0.9 select_reduce_fusion
  1.8 0.7 pad_bitcast_fusion
  2.4 0.7 pad_maximum_fusion
  3.1 0.6 compare_convert_fusion.keep_ref.refs_4_
  3.9 0.6 pad.9.gain_ref
  4.5 0.8 reshape.145.valid_ref
  5.2 170.0 %front.1 = (f32[128,2048]{1,0:T(8,128)}, bf16[128,2048]{1,0:T(8,128)(2,1)}, f32[8,2048]{1,0:T(8,128)}, f32[128,1024]{1,0:T(8,128)}, bf16[8,4,64,1664]{3,2,1,0:T(...) custom-call(bf16[64,1536]{1,0:T(8,128)(2,1)} %proj_ref.1, ...), custom_call_target="tpu_custom_call" | custom-call | tf_op jit(solution)/shard_map/front/pallas_call | solution.py:1363
  175.2 103.2 %fused_mlp.1 = (f32[128,2048]{1,0:T(8,128)}, bf16[4,256,704]{2,1,0:T(8,128)(2,1)}, bf16[4,256,2048]{2,1,0:T(8,128)(2,1)}, bf16[8,2,64,704]{3,2,1,0:T(8,128)(2,1)}) custom-call(bf16[128,2048]{1,0:T(8,128)(2,1)} %get-tuple-element.42.rows_ref, bf16[2,8,4,64,704]{4,3,2,1,0:T(8,128)(2,1)} %get-tuple-element.43.gu_ref, ...), custom_call_target="tpu_custom_call" | custom-call | flops 26575110144 | bytes 25165824 | tf_op jit(solution)/shard_map/fused_mlp/pallas_call | solution.py:587
  278.5 0.2 multiply_reduce_fusion.2
  278.7 1.0 slice.16
  279.6 2.2 multiply_reduce_fusion
  281.8 1.5 fusion
  283.3 79.6 %attention_back.1 = (f32[2,64,1536]{2,1,0:T(8,128)}, bf16[8,128,2048]{2,1,0:T(8,128)(2,1)}, bf16[8,128,1024]{2,1,0:T(8,128)(2,1)}, bf16[8,2,64,704]{3,2,1,0:T(8,...) custom-call(bf16[2,64,2048]{2,1,0:T(8,128)(2,1)} %bitcast.26, ...), custom_call_target="tpu_custom_call" | custom-call | tf_op jit(solution)/shard_map/attention_back/pallas_call | solution.py:1717
  363.0 95.2 %collect_weights.1 = (f32[128,2048]{1,0:T(8,128)}, f32[32,4096]{1,0:T(8,128)}, f32[64,1536]{1,0:T(8,128)}, f32[16,384]{1,0:T(8,128)}, f32[64,11264]{1,0:T(8,128)}, /*index=5*/bf16[128,2048]{1,0:T(8,128)(2,1)}) custom-call(bf16[8,128,2048]{2,1,0:T(8,128)(2,1)} %get-tuple-element.58.out_ref, bf16[8,128,1024]{2,1,0:T(8,128)(2,1)} %get-tuple-element.59.up_ref, ...), custom_call_target="tpu_custom_call" | custom-call | tf_op jit(solution)/shard_map/collect_weights/pallas_call | solution.py:907
  458.2 0.9 add_convert_fusion
  459.1 1.3 slice_bitcast_fusion.1
  460.4 1.3 slice_bitcast_fusion
  461.7 0.8 copy.38
  462.5 0.7 copy.39
  463.2 0.8 copy.40
  464.0 1.0 copy.41
  465.0 1.6 copy.42
  466.6 0.8 copy-done.4
  467.4 1.1 copy.43
  (26 shorter events, 0.4 us)
Async XLA Ops:
  175.2 103.3 %copy-start = (f32[128,2048]{1,0:T(8,128)S(1)}, f32[128,2048]{1,0:T(8,128)}, u32[]{:S(2)}) copy-start(f32[128,2048]{1,0:T(8,128)} %get-tuple-element.41) | copy-start | bytes 3145732
  278.5 3.3 copy-start.1
  278.5 3.3 copy-start.3
  363.0 95.2 %copy-start.5 = (f32[128,2048]{1,0:T(8,128)S(1)}, f32[128,2048]{1,0:T(8,128)}, u32[]{:S(2)}) copy-start(f32[128,2048]{1,0:T(8,128)} %get-tuple-element.57) | copy-start | bytes 3145732
  458.2 3.5 copy-start.8
  458.2 4.3 copy-start.9
  458.2 5.0 %copy-start.7 = (f32[32,4096]{1,0:T(8,128)S(1)}, f32[32,4096]{1,0:T(8,128)}, u32[]{:S(2)}) copy-start(f32[32,4096]{1,0:T(8,128)} %get-tuple-element.91) | copy-start | bytes 1572868
  459.1 4.9 %copy-start.6 = (f32[128,2048]{1,0:T(8,128)S(1)}, f32[128,2048]{1,0:T(8,128)}, u32[]{:S(2)}) copy-start(f32[128,2048]{1,0:T(8,128)} %get-tuple-element.92) | copy-start | bytes 3145732
  462.5 2.5 copy-start.2
  465.0 2.4 copy-start.4

commit v9 on v8

--- a/solution.py
+++ b/solution.py
@@ -311,10 +311,14 @@
     gu_ref,
     down_ref,
     cot_ref,
+    hidden_ref,
+    gains_ref,
     *refs,
 ):
     (
-        sum_ref,
+        grad_ref,
+        low_ref,
+        gain_term,
         act_out,
         term_out,
         gu_out,
@@ -551,15 +555,24 @@
     while steps:
         ring_step()
     send_far(tiles - 1)
+    totals = []
     for half in (0, 1):
         for side in (0, 1):
             back_hop(0, side, half, held(0, 0, half)).wait_recv()
-        rows = slice(half * cut, (half + 1) * cut)
-        sum_ref[rows, :] = (
-            in_v[0, rows, :].astype(F32)
+        totals.append(
+            in_v[0, half * cut : (half + 1) * cut, :].astype(F32)
             + got_v[0, 0, half].astype(F32)
             + got_v[0, 1, half].astype(F32)
         )
+    total = jnp.concatenate(totals, axis=0)
+    hidden = hidden_ref[...]
+    inverse = rms_scale(hidden)
+    normed = hidden * inverse
+    gain_term[...] = jnp.sum(total * normed, axis=0, keepdims=True)
+    back = norm_back(total * gains_ref[1:2, :], normed, inverse)
+    grad_hidden = cot_v[0, :n_tok, :].astype(F32) + back
+    grad_ref[...] = grad_hidden
+    low_ref[...] = grad_hidden.astype(BF)
     for t in range(tiles):
         take_far(t)
     parts.drain()
@@ -577,7 +590,7 @@
             copy.wait()
 
 
-def fused_mlp(n_batch, rows, cots, gu_rows, own_down):
+def fused_mlp(n_batch, rows, cots, hidden_res, gains, gu_rows, own_down):
     n_tok, width = rows.shape
     ff = gu_rows.shape[-1]
     own_rows = gu_rows.shape[3]
@@ -588,12 +601,15 @@
         functools.partial(mlp_kernel, n_batch),
         out_shape=(
             jax.ShapeDtypeStruct((n_tok, width), F32),
+            jax.ShapeDtypeStruct((n_tok, width), BF),
+            jax.ShapeDtypeStruct((1, width), F32),
             jax.ShapeDtypeStruct((far, pair, ff), BF),
             jax.ShapeDtypeStruct((far, pair, width), BF),
             jax.ShapeDtypeStruct((n_batch, 2, own_rows, ff), BF),
         ),
-        in_specs=[pl.BlockSpec(memory_space=pl.ANY)] * 4,
-        out_specs=[pl.BlockSpec(memory_space=pltpu.VMEM)]
+        in_specs=[pl.BlockSpec(memory_space=pl.ANY)] * 4
+        + [pl.BlockSpec(memory_space=pltpu.VMEM)] * 2,
+        out_specs=[pl.BlockSpec(memory_space=pltpu.VMEM)] * 3
         + [pl.BlockSpec(memory_space=pl.ANY)] * 3,
         scratch_shapes=[
             pltpu.VMEM((far, pair, width), BF),
@@ -625,7 +641,7 @@
             flops=flops, bytes_accessed=24 * 1024 * 1024, transcendentals=n_batch * n_tok * ff
         ),
         name="fused_mlp",
-    )(rows, gu_rows, own_down, cots)
+    )(rows, gu_rows, own_down, cots, hidden_res, gains)
 
 
 class RingCollect:
@@ -707,7 +723,9 @@
     out_grad,
     up_grad,
     in_grad,
-    gain_grad,
+    attn_gain_grad,
+    query_gain_grad,
+    mlp_gain_grad,
     gu_grad,
     tokens_grad,
     out_v,
@@ -884,11 +902,13 @@
     for copy in in_copies:
         copies.arrive(copy)
     cols = in_all.shape[2]
-    gains = jnp.zeros(gain_grad.shape, F32)
+    gains = jnp.zeros((16, cols), F32)
     for part in range(4):
         in_grad[:, part * cols : (part + 1) * cols] = in_all[part, :own_rows, :].astype(F32)
         gains = gains + in_all[part, own_rows:, :].astype(F32)
-    gain_grad[...] = gains
+    attn_gain_grad[...] = gains[0:1, :own_rows]
+    mlp_gain_grad[...] = gains[1:2, :own_rows]
+    query_gain_grad[...] = gains[2:3, :gain_rows]
     copies.drain()
     for ring in rings:
         ring.drain()
@@ -910,12 +930,14 @@
             jax.ShapeDtypeStruct((out_rows, width), F32),
             jax.ShapeDtypeStruct((gain_rows, 4 * up_cols), F32),
             jax.ShapeDtypeStruct((own_rows, 4 * in_cols), F32),
-            jax.ShapeDtypeStruct((16, in_cols), F32),
+            jax.ShapeDtypeStruct((1, own_rows), F32),
+            jax.ShapeDtypeStruct((1, gain_rows), F32),
+            jax.ShapeDtypeStruct((1, own_rows), F32),
             jax.ShapeDtypeStruct((own_rows, 2 * n_batch * grad_gu.shape[3]), F32),
             jax.ShapeDtypeStruct((n_tok, width), BF),
         ),
         in_specs=[pl.BlockSpec(memory_space=pl.ANY)] * 5 + [pl.BlockSpec(memory_space=pltpu.VMEM)] * len(own),
-        out_specs=[pl.BlockSpec(memory_space=pltpu.VMEM)] * 6,
+        out_specs=[pl.BlockSpec(memory_space=pltpu.VMEM)] * 8,
         scratch_shapes=[pltpu.VMEM((n_batch,) + shape, BF) for shape in shapes]
         + [pltpu.VMEM((far, 2, 2, rows // 2, cols), BF) for rows, cols in shapes]
         + [
@@ -1815,7 +1837,6 @@
     )
     gain_cols = jnp.pad(gains, ((0, 0), (0, 125)))
     valid_rows = (query_pos[None, :] < own_lengths[:, None]).astype(F32).reshape(n_tok, 1)
-    grad_out = cotangent.reshape(n_tok, width).astype(F32) * valid_rows
     keep = (key_pos[None, None, :] < own_lengths[:, None, None]).astype(F32)
     (
         hidden_res,
@@ -1846,26 +1867,27 @@
         (cos_all, sin_all, keep, valid_rows),
     )
     own_qup = own_qup.reshape(QR, heads * HD)
-    gain_mlp = gains[1]
-
-    scale_two = rms_scale(hidden_res)
-    normed_two = hidden_res * scale_two
+
     resident = 10 * n_batch * n_tok * width <= 24 * 1024 * 1024
     if resident:
-        grad_mlp_in, down_part, terms, grad_gu_own = fused_mlp(
-            n_batch, mlp_in, cots, gu_rows, own_down
+        grad_hidden, grad_att, gain_mlp_term, down_part, terms, grad_gu_own = fused_mlp(
+            n_batch, mlp_in, cots, hidden_res, gains, gu_rows, own_down
         )
         terms = terms.reshape(n_batch, n_tok, width)
     else:
         terms = None
+        scale_two = rms_scale(hidden_res)
+        normed_two = hidden_res * scale_two
         grad_mlp_in, down_part, out_terms, grad_gu_own = permuted_mlp(
             ring, mlp_in, cots, gu_rows, own_down
         )
-    gain_mlp_term = jnp.sum(grad_mlp_in * normed_two, axis=0)
-    grad_hidden = grad_out + norm_back(grad_mlp_in * gain_mlp, normed_two, scale_two)
+        gain_mlp_term = jnp.sum(grad_mlp_in * normed_two, axis=0)[None, :]
+        grad_hidden = cotangent.reshape(n_tok, width).astype(F32) * valid_rows
+        grad_hidden += norm_back(grad_mlp_in * gains[1], normed_two, scale_two)
+        grad_att = grad_hidden.astype(BF)
     back_own, out_grads, up_grads, grad_gu_own, grad_down, attn_in_all, *sums = attention_back(
         n_batch,
-        grad_hidden.astype(BF).reshape(micro, pos_dev, width),
+        grad_att.reshape(micro, pos_dev, width),
         qkv_all,
         turned,
         mixed,
@@ -1885,7 +1907,9 @@
         grad_proj_out,
         grad_query_up,
         grad_proj_in,
-        gain_sums,
+        grad_attn_gain,
+        grad_query_gain,
+        grad_mlp_gain,
         grad_gate_up,
         grad_tokens,
     ) = collect_weights(
@@ -1902,22 +1926,20 @@
             tokens.reshape(n_tok, width),
             grad_hidden,
             gains,
-            gain_mlp_term[None, :],
+            gain_mlp_term,
             cos_all,
             sin_all,
         ),
     )
-    gain_sums = gain_sums[:, :own_rows]
-
     return (
         layer_out.reshape(tokens.shape).astype(BF),
         grad_tokens.reshape(tokens.shape),
         grad_proj_in,
         grad_query_up,
         grad_proj_out,
-        gain_sums[0],
-        gain_sums[2, :gain_rows],
-        gain_sums[1],
+        grad_attn_gain.reshape(-1),
+        grad_query_gain.reshape(-1),
+        grad_mlp_gain.reshape(-1),
         grad_gate_up,
         grad_down,
     )

time: 470 us -> 465 us (0.989)
  no operation moved by 1% of the time
where the time goes in v9:
time: 465 us; the launch traced here: 464 us
  Pallas kernels  449 us (97%)
  local copies, waits for them, and re-layouts  10.7 us (2%)
    pallas_call x1, Pallas kernels, front(): pl.pallas_call(functools.partial(front_kernel, n_batch, heads), out_shape...  170 us
    pallas_call x1, Pallas kernels, fused_mlp(): pl.pallas_call(functools.partial(mlp_kernel, n_batch), out_shape=(jax.Sha...  104 us
    pallas_call x1, Pallas kernels, collect_weights(): pl.pallas_call(functools.partial(tail_kernel, n_batch, gain_rows), out_sh...  95.4 us
    pallas_call x1, Pallas kernels, attention_back(): pl.pallas_call(functools.partial(attention_back_kernel, n_batch, head_col...  79.7 us

profile of v9, /device:TPU:4, one launch (start us, length us, event | category | flops | bytes accessed | tf_op | source)
XLA Modules:
  0.0 463.8 jit_solution(8528591138816164465)
XLA Ops:
  0.7 0.9 select_reduce_fusion
  1.5 0.1 dynamic_slice.3
  1.7 0.7 pad_bitcast_fusion
  2.3 0.7 pad_maximum_fusion
  3.0 0.6 compare_convert_fusion.keep_ref.refs_4_
  3.7 0.1 copy.30
  3.8 0.6 pad.9.gain_ref
  4.4 0.8 reshape.138.valid_ref
  5.2 169.9 %front.1 = (f32[128,2048]{1,0:T(8,128)}, bf16[128,2048]{1,0:T(8,128)(2,1)}, f32[8,2048]{1,0:T(8,128)}, f32[128,1024]{1,0:T(8,128)}, bf16[8,4,64,1664]{3,2,1,0:T(...) custom-call(bf16[64,1536]{1,0:T(8,128)(2,1)} %proj_ref.1, ...), custom_call_target="tpu_custom_call" | custom-call | tf_op jit(solution)/shard_map/front/pallas_call | solution.py:1385
  175.1 104.1 %fused_mlp.1 = (f32[128,2048]{1,0:T(8,128)}, bf16[128,2048]{1,0:T(8,128)(2,1)}, f32[1,2048]{1,0:T(1,128)}, bf16[4,256,704]{2,1,0:T(8,128)(2,1)}, bf16[4,256,2048...) custom-call(bf16[128,2048]{1,0:T(8,128)(2,1)} %get-tuple-element.46.rows_ref, ...), custom_call_target="tpu_custom_call" | custom-call | flops 26575110144 | bytes 25165824 | tf_op jit(solution)/shard_map/fused_mlp/pallas_call | solution.py:600
  279.2 79.7 %attention_back.1 = (f32[2,64,1536]{2,1,0:T(8,128)}, bf16[8,128,2048]{2,1,0:T(8,128)(2,1)}, bf16[8,128,1024]{2,1,0:T(8,128)(2,1)}, bf16[8,2,64,704]{3,2,1,0:T(8,...) custom-call(bf16[2,64,2048]{2,1,0:T(8,128)(2,1)} %bitcast.23, ...), custom_call_target="tpu_custom_call" | custom-call | tf_op jit(solution)/shard_map/attention_back/pallas_call | solution.py:1739
  358.9 95.4 %collect_weights.1 = (f32[128,2048]{1,0:T(8,128)}, f32[32,4096]{1,0:T(8,128)}, f32[64,1536]{1,0:T(8,128)}, f32[1,64]{1,0:T(1,128)}, f32[1,32]{1,0:T(1,128)}, /*i...) custom-call(bf16[8,128,2048]{2,1,0:T(8,128)(2,1)} %get-tuple-element.62.out_ref, ...), custom_call_target="tpu_custom_call" | custom-call | tf_op jit(solution)/shard_map/collect_weights/pallas_call | solution.py:927
  454.4 0.9 add_convert_fusion
  455.3 0.1 copy-done.6
  455.4 0.8 copy.41
  456.2 0.7 copy.42
  456.9 0.8 copy.43
  457.7 1.0 copy.44
  458.7 0.5 copy.45
  459.2 0.5 copy.46
  459.7 0.5 copy.47
  460.3 1.6 copy.48
  461.8 0.8 copy-done.1
  462.7 1.1 copy.49
  (22 shorter events, 0.1 us)
Async XLA Ops:
  358.9 95.5 %copy-start.2 = (f32[128,2048]{1,0:T(8,128)S(1)}, f32[128,2048]{1,0:T(8,128)}, u32[]{:S(2)}) copy-start(f32[128,2048]{1,0:T(8,128)} %get-tuple-element.45.hidden_ref) | copy-start | bytes 3145732
  358.9 95.5 %copy-start.3 = (f32[128,2048]{1,0:T(8,128)S(1)}, f32[128,2048]{1,0:T(8,128)}, u32[]{:S(2)}) copy-start(f32[128,2048]{1,0:T(8,128)} %get-tuple-element.61) | copy-start | bytes 3145732
  454.3 1.0 copy-start.6
  454.3 1.8 copy-start.7
  454.4 2.6 copy-start.5
  455.3 2.4 copy-start.4
  456.2 2.5 copy-start.10
  456.2 3.1 copy-start.9
  456.2 3.6 copy-start.8
  456.2 4.1 copy-start
  460.3 2.4 copy-start.1

commit v10 on v9

--- a/solution.py
+++ b/solution.py
@@ -760,7 +760,7 @@
         pltpu.make_async_copy(held, kept, load_sems.at[i])
         for i, (held, kept) in enumerate([(out_ref, out_v), (up_ref, up_v), (rows_ref, rows_v), (gu_ref, gu_v), (packed_ref, packed_v)])
     ]
-    for copy in loads:
+    for copy in (loads[1], loads[0], *loads[2:]):
         copy.start()
     barrier = greet(place, [place.up(), place.down()] + ctx_peers)
 
@@ -777,9 +777,9 @@
                 ring_recv.at[i],
             )
         )
-    for copy, ring in zip(loads[:2], rings):
-        copy.wait()
-        ring.advance()
+    for at in (1, 0):
+        loads[at].wait()
+        rings[at].advance()
     part_cols = project_v.shape[2]
     n_tok, width = tokens_ref.shape
     pos_dev = cos_ref.shape[0] // 4
@@ -1511,7 +1511,7 @@
         pltpu.make_async_copy(source, target, load_sems.at[i])
         for i, (source, target) in enumerate(pairs)
     ]
-    for copy in loads:
+    for copy in loads[:1] + loads[6:] + loads[1:6]:
         copy.start()
     peers = [(lax.rem(b + k, n), c) for k in range(1, n)]
     others = peers + [(b, place.far), (b, place.near), (b, lax.rem(place.near + 2, 4))]

time: 465 us -> 462 us (level)
  no operation moved by 1% of the time
where the time goes in v10:
time: 462 us; the launch traced here: 461 us
  Pallas kernels  446 us (97%)
  local copies, waits for them, and re-layouts  10.7 us (2%)
    pallas_call x1, Pallas kernels, front(): pl.pallas_call(functools.partial(front_kernel, n_batch, heads), out_shape...  170 us
    pallas_call x1, Pallas kernels, fused_mlp(): pl.pallas_call(functools.partial(mlp_kernel, n_batch), out_shape=(jax.Sha...  104 us
    pallas_call x1, Pallas kernels, collect_weights(): pl.pallas_call(functools.partial(tail_kernel, n_batch, gain_rows), out_sh...  95.1 us
    pallas_call x1, Pallas kernels, attention_back(): pl.pallas_call(functools.partial(attention_back_kernel, n_batch, head_col...  76.8 us

profile of v10, /device:TPU:4, one launch (start us, length us, event | category | flops | bytes accessed | tf_op | source)
XLA Modules:
  0.0 460.6 jit_solution(13601506606631936687)
XLA Ops:
  0.7 0.9 select_reduce_fusion
  1.5 0.1 dynamic_slice.3
  1.7 0.7 pad_bitcast_fusion
  2.3 0.7 pad_maximum_fusion
  3.0 0.6 compare_convert_fusion.keep_ref.refs_4_
  3.7 0.1 copy.30
  3.8 0.6 pad.9.gain_ref
  4.4 0.8 reshape.138.valid_ref
  5.2 169.9 %front.1 = (f32[128,2048]{1,0:T(8,128)}, bf16[128,2048]{1,0:T(8,128)(2,1)}, f32[8,2048]{1,0:T(8,128)}, f32[128,1024]{1,0:T(8,128)}, bf16[8,4,64,1664]{3,2,1,0:T(...) custom-call(bf16[64,1536]{1,0:T(8,128)(2,1)} %proj_ref.1, ...), custom_call_target="tpu_custom_call" | custom-call | tf_op jit(solution)/shard_map/front/pallas_call | solution.py:1385
  175.1 104.1 %fused_mlp.1 = (f32[128,2048]{1,0:T(8,128)}, bf16[128,2048]{1,0:T(8,128)(2,1)}, f32[1,2048]{1,0:T(1,128)}, bf16[4,256,704]{2,1,0:T(8,128)(2,1)}, bf16[4,256,2048...) custom-call(bf16[128,2048]{1,0:T(8,128)(2,1)} %get-tuple-element.46.rows_ref, ...), custom_call_target="tpu_custom_call" | custom-call | flops 26575110144 | bytes 25165824 | tf_op jit(solution)/shard_map/fused_mlp/pallas_call | solution.py:600
  279.2 76.8 %attention_back.1 = (f32[2,64,1536]{2,1,0:T(8,128)}, bf16[8,128,2048]{2,1,0:T(8,128)(2,1)}, bf16[8,128,1024]{2,1,0:T(8,128)(2,1)}, bf16[8,2,64,704]{3,2,1,0:T(8,...) custom-call(bf16[2,64,2048]{2,1,0:T(8,128)(2,1)} %bitcast.23, ...), custom_call_target="tpu_custom_call" | custom-call | tf_op jit(solution)/shard_map/attention_back/pallas_call | solution.py:1739
  356.1 95.1 %collect_weights.1 = (f32[128,2048]{1,0:T(8,128)}, f32[32,4096]{1,0:T(8,128)}, f32[64,1536]{1,0:T(8,128)}, f32[1,64]{1,0:T(1,128)}, f32[1,32]{1,0:T(1,128)}, /*i...) custom-call(bf16[8,128,2048]{2,1,0:T(8,128)(2,1)} %get-tuple-element.62.out_ref, ...), custom_call_target="tpu_custom_call" | custom-call | tf_op jit(solution)/shard_map/collect_weights/pallas_call | solution.py:927
  451.3 0.9 add_convert_fusion
  452.2 0.1 copy-done.6
  452.3 0.8 copy.41
  453.1 0.7 copy.42
  453.8 0.8 copy.43
  454.6 1.0 copy.44
  455.6 0.5 copy.45
  456.1 0.5 copy.46
  456.6 0.5 copy.47
  457.1 1.6 copy.48
  458.7 0.8 copy-done.1
  459.5 1.1 copy.49
  (22 shorter events, 0.1 us)
Async XLA Ops:
  356.1 95.2 %copy-start.2 = (f32[128,2048]{1,0:T(8,128)S(1)}, f32[128,2048]{1,0:T(8,128)}, u32[]{:S(2)}) copy-start(f32[128,2048]{1,0:T(8,128)} %get-tuple-element.45.hidden_ref) | copy-start | bytes 3145732
  356.1 95.2 %copy-start.3 = (f32[128,2048]{1,0:T(8,128)S(1)}, f32[128,2048]{1,0:T(8,128)}, u32[]{:S(2)}) copy-start(f32[128,2048]{1,0:T(8,128)} %get-tuple-element.61) | copy-start | bytes 3145732
  451.2 1.0 copy-start.6
  451.2 1.8 copy-start.7
  451.3 2.6 copy-start.5
  452.2 2.4 copy-start.4
  453.1 2.5 copy-start.10
  453.1 3.1 copy-start.9
  453.1 3.6 copy-start.8
  453.1 4.1 copy-start
  457.1 2.4 copy-start.1
